TPU v7x, 32 devices: a whole 2x2x4 slice. The times are simulated.
32 devices in a mesh: chain: 4 (over x, core), rows: 8 (over z, y).
Axes of the slice: x: 2, y: 2, z: 4, core: 2. Of those that a mesh axis runs over, the one named last changes fastest.
Arguments:
- right_side: bfloat16 [8, 64, 128, 256], P('chain', 'rows'), may hold values from -3 to 3
- lower_blocks: bfloat16 [8, 64, 6, 128, 128], P('chain', 'rows'), may hold values from -0.5 to 0.5
- block_scale: float32 [8, 64, 6], P('chain', 'rows'), may hold values from 0.1 to 0.6
- diag_inverse: bfloat16 [8, 64, 128, 128], P('chain', 'rows'), may hold values from -0.11 to 1.11
- depend_rows: int32 [8, 64, 6], P('chain', 'rows'), may hold values from 0 to 63, as said below
Outputs:
- solution: bfloat16 [8, 64, 128, 256], P('chain', 'rows')
Inputs may be any that keep to these rules, and one draw needn't show every extreme that they name: depend_rows[l, q, k] names a block row of level l - 1 (unused at level 0) from q - 2 to q + 2.
All inputs are finite; a program needn't handle non-finite values.
Results may differ from a plain program's by a relative error of at most 0.03.
Values may be sent and summed in bfloat16 or wider, within the bound.
No kernel may reach another device: no remote copies, remote signals or barrier semaphores. Data moves between devices by JAX's collectives and lax.ppermute only.
A program may use at most 64 MiB of HBM per device.

v0:
```python
import jax
import jax.numpy as jnp
from jax import lax
from jax.sharding import PartitionSpec as P

REACH = 2


def padded(cells, sides, width):
    for axis, dim in sides:
        count = lax.axis_size(axis)
        ends = count - 1
        head = lax.slice_in_dim(cells, 0, width, axis=dim)
        tail = lax.slice_in_dim(cells, cells.shape[dim] - width, cells.shape[dim], axis=dim)
        cells = jnp.concatenate(
            [
                lax.ppermute(tail, axis, [(i, (i + 1) % count) for i in range(ends)]),
                cells,
                lax.ppermute(head, axis, [((i + 1) % count, i) for i in range(ends)]),
            ],
            axis=dim,
        )
    return cells


def passed_along(value, axis, steps):
    count = lax.axis_size(axis)
    first, last = (max(0, -steps), min(count, count - steps))
    return lax.ppermute(value, axis, [(source, source + steps) for source in range(first, last)])


def level_solve(widened, dep_local, right_level, blocks, scales, inverse):
    picked_rows = jnp.take(widened, dep_local, axis=0)
    scaled = (scales[:, :, None, None] * picked_rows.astype(jnp.float32)).astype(jnp.bfloat16)
    totals = jnp.einsum("qkab,qkbn->qan", blocks, scaled, preferred_element_type=jnp.float32)
    remainder = (right_level.astype(jnp.float32) - totals).astype(jnp.bfloat16)
    return jnp.einsum(
        "qab,qbn->qan", inverse, remainder, preferred_element_type=jnp.float32
    ).astype(jnp.bfloat16)


def solve_group(right_side, lower_blocks, block_scale, diag_inverse, depend_rows, incoming, spread):
    row_count = right_side.shape[1]
    row_index = lax.axis_index("rows")
    first_row = row_index * row_count - REACH
    dep_local = jnp.clip(depend_rows - first_row, 0, row_count + 2 * REACH - 1)
    previous = incoming
    results = []
    for section_level in range(right_side.shape[0]):
        widened = spread(previous)
        previous = level_solve(
            widened,
            dep_local[section_level],
            right_side[section_level],
            lower_blocks[section_level],
            block_scale[section_level],
            diag_inverse[section_level],
        )
        results.append(previous)
    return jnp.stack(results)


def per_device(right_side, lower_blocks, block_scale, diag_inverse, depend_rows):

    def spread(values):
        return padded(values, (("rows", 0),), REACH)

    def advance(moment, state_pair):
        boundary, solved = state_pair
        incoming = passed_along(boundary, "chain", 1)
        solved = solve_group(
            right_side, lower_blocks, block_scale, diag_inverse, depend_rows, incoming, spread
        )
        return (solved[-1], solved)

    initial = (jnp.zeros(right_side.shape[1:], jnp.bfloat16), jnp.zeros_like(right_side))
    _, solution = lax.fori_loop(0, lax.axis_size("chain"), advance, initial)
    return solution


def solution(mesh):
    placed = (
        P("chain", "rows", None, None),
        P("chain", "rows", None, None, None),
        P("chain", "rows", None),
        P("chain", "rows", None, None),
        P("chain", "rows", None),
    )
    return jax.shard_map(
        per_device,
        mesh=mesh,
        in_specs=placed,
        out_specs=P("chain", "rows", None, None),
        check_vma=False,
    )
```

profile of v0, /device:TPU:26, one launch (start us, length us, event | category | flops | bytes accessed | tf_op | source)
XLA Modules:
  0.0 183.4 jit_solution(12706704244872375838)
XLA Ops:
  3.3 177.9 %while.14 = (s32[]{:T(128)}, bf16[8,128,256]{1,2,0:T(8,128)(2,1)S(1)}, bf16[2,8,128,256]{2,3,1,0:T(8,128)(2,1)}, bf16[2,8,128,256]{2,3,1,0:T(8,128)(2,1)S(1)}, f...) while((s32[]{:T(128)}, ...), condition=%wide.region_1.0_spmd, body=%wide.region_0.2_spmd.sunk | while | flops 956304384 | bytes 37247592 | solution.py:77
  3.3 1.9 %collective-permute-start = (bf16[8,128,256]{1,2,0:T(8,128)(2,1)S(1)}, bf16[8,128,256]{1,2,0:T(8,128)(2,1)S(1)}, u32[]{:S(2)}, u32[]{:S(2)}) collective-permute-start(bf16[8,128,256]{1,2,0:T(8,128)(2,1)S(1)} %get-tuple-element.218), channel_id=1, source_target_pairs={{0,8},{8,16},{16,24},{1,9},{9,17},{17,25},{2,10},{10,18},{18,26},{... | collective-permute-start | bytes 1572872 | tf_op jit(solution)/shard_map/while/body/eval_jaxpr/ppermute | solution.py:29
  5.2 8.5 %collective-permute-done = bf16[8,128,256]{1,2,0:T(8,128)(2,1)S(1)} collective-permute-done((bf16[8,128,256]{1,2,0:T(8,128)(2,1)S(1)}, bf16[8,128,256]{1,2,0:T(8,128)(2,1)S(1)}, u32[]{:S(2)}, u32[]{:S(2)}) %collective-permute-start) | collective-permute-done | bytes 524320 | tf_op jit(solution)/shard_map/while/body/eval_jaxpr/ppermute | solution.py:29
  13.8 3.3 %collective-permute-start.1 = (bf16[2,128,256]{1,2,0:T(8,128)(2,1)S(1)}, bf16[2,128,256]{1,2,0:T(8,128)(2,1)S(1)}, u32[]{:S(2)}, u32[]{:S(2)}) collective-permute-start(bf16[2,128,256]{1,2,0:T(8,128)(2,1)S(1)} %get-tuple-element.195), channel_id=1, source_target_pairs={{1,0},{2,1},{3,2},{4,3},{5,4},{6,5},{7,6},{9,8},{10,9},{11,10},{12... | collective-permute-start | bytes 393224 | tf_op jit(solution)/shard_map/while/body/eval_jaxpr/ppermute | solution.py:19
  17.1 2.5 %collective-permute-start.2 = (bf16[2,128,256]{1,2,0:T(8,128)(2,1)S(1)}, bf16[2,128,256]{1,2,0:T(8,128)(2,1)S(1)}, u32[]{:S(2)}, u32[]{:S(2)}) collective-permute-start(bf16[2,128,256]{1,2,0:T(8,128)(2,1)S(1)} %get-tuple-element.196), channel_id=1, source_target_pairs={{0,1},{1,2},{2,3},{3,4},{4,5},{5,6},{6,7},{8,9},{9,10},{10,11},{11... | collective-permute-start | bytes 393224 | tf_op jit(solution)/shard_map/while/body/eval_jaxpr/ppermute | solution.py:17
  20.6 4.2 %collective-permute-done.2 = bf16[2,128,256]{1,2,0:T(8,128)(2,1)S(1)} collective-permute-done((bf16[2,128,256]{1,2,0:T(8,128)(2,1)S(1)}, bf16[2,128,256]{1,2,0:T(8,128)(2,1)S(1)}, u32[]{:S(2)}, u32[]{:S(2)}) %collective-permute-start.2) | collective-permute-done | bytes 131104 | tf_op jit(solution)/shard_map/while/body/eval_jaxpr/ppermute | solution.py:17
  25.0 2.7 %gather_fusion = bf16[48,128,256]{1,2,0:T(8,128)(2,1)} fusion(bf16[12,128,256]{1,2,0:T(8,128)(2,1)S(1)} %pad_maximum_fusion.6, s32[1024]{0:T(1024)S(1)} %pad_clamp_fusion.4), kind=kCustom, calls=%fused_computation.clone.clone.1 | custom fusion | bytes 6291648 | tf_op jit(solution)/shard_map/while/body/eval_jaxpr/jit(_take)/gather | solution.py:33
  27.6 3.5 %convolution_convert_fusion.4 = bf16[8,256,128]{2,1,0:T(8,128)(2,1)S(1)} fusion(bf16[2,8,6,128,128]{4,3,2,1,0:T(8,128)(2,1)} %get-tuple-element.235, bf16[8,6,128,256]{2,3,1,0:T(8,128)(2,1)} %bitcast.124, f32[8,6]{1,0:T(8,128)S(1)} %get-tuple-element.198, pred[8,6]{1,0:T(8,128)(4,1)S(1)} %get-tuple-element.199, ...), kind=kOutput, calls=%fused_computation.23.clone.1 | convolution fusion | flops 477102080 | bytes 6034432 | tf_op jit(solution)/shard_map/while/body/eval_jaxpr/qab,qbn->qan/dot_general | solution.py:37
  31.2 1.9 %collective-permute-start.3 = (bf16[2,128,256]{1,2,0:T(8,128)(2,1)S(1)}, bf16[2,128,256]{1,2,0:T(8,128)(2,1)S(1)}, u32[]{:S(2)}, u32[]{:S(2)}) collective-permute-start(bf16[2,128,256]{1,2,0:T(8,128)(2,1)S(1)} %get-tuple-element.200), channel_id=1, source_target_pairs={{1,0},{2,1},{3,2},{4,3},{5,4},{6,5},{7,6},{9,8},{10,9},{11,10},{12... | collective-permute-start | bytes 393224 | tf_op jit(solution)/shard_map/while/body/eval_jaxpr/ppermute | solution.py:19
  33.1 3.9 %collective-permute-start.4 = (bf16[2,128,256]{1,2,0:T(8,128)(2,1)S(1)}, bf16[2,128,256]{1,2,0:T(8,128)(2,1)S(1)}, u32[]{:S(2)}, u32[]{:S(2)}) collective-permute-start(bf16[2,128,256]{1,2,0:T(8,128)(2,1)S(1)} %get-tuple-element.201), channel_id=1, source_target_pairs={{0,1},{1,2},{2,3},{3,4},{4,5},{5,6},{6,7},{8,9},{9,10},{10,11},{11... | collective-permute-start | bytes 393224 | tf_op jit(solution)/shard_map/while/body/eval_jaxpr/ppermute | solution.py:17
  38.1 2.8 %collective-permute-done.4 = bf16[2,128,256]{1,2,0:T(8,128)(2,1)S(1)} collective-permute-done((bf16[2,128,256]{1,2,0:T(8,128)(2,1)S(1)}, bf16[2,128,256]{1,2,0:T(8,128)(2,1)S(1)}, u32[]{:S(2)}, u32[]{:S(2)}) %collective-permute-start.4) | collective-permute-done | bytes 131104 | tf_op jit(solution)/shard_map/while/body/eval_jaxpr/ppermute | solution.py:17
  41.0 2.7 %gather_fusion.1 = bf16[48,128,256]{1,2,0:T(8,128)(2,1)} fusion(bf16[12,128,256]{1,2,0:T(8,128)(2,1)S(1)} %pad_maximum_fusion.7, s32[1024]{0:T(1024)S(1)} %pad_clamp_fusion.5), kind=kCustom, calls=%fused_computation.1.clone.clone.1 | custom fusion | bytes 6291648 | tf_op jit(solution)/shard_map/while/body/eval_jaxpr/jit(_take)/gather | solution.py:33
  43.7 3.5 %convolution_convert_fusion.5 = bf16[8,256,128]{2,1,0:T(8,128)(2,1)S(1)} fusion(bf16[2,8,6,128,128]{4,3,2,1,0:T(8,128)(2,1)} %get-tuple-element.235, bf16[8,6,128,256]{2,3,1,0:T(8,128)(2,1)} %bitcast.123, f32[8,6]{1,0:T(8,128)S(1)} %get-tuple-element.203, pred[8,6]{1,0:T(8,128)(4,1)S(1)} %get-tuple-element.204, ...), kind=kOutput, calls=%fused_computation.22.clone.1 | convolution fusion | flops 477102080 | bytes 6034432 | tf_op jit(solution)/shard_map/while/body/eval_jaxpr/qab,qbn->qan/dot_general | solution.py:37
  50.3 8.5 %collective-permute-done = bf16[8,128,256]{1,2,0:T(8,128)(2,1)S(1)} collective-permute-done((bf16[8,128,256]{1,2,0:T(8,128)(2,1)S(1)}, bf16[8,128,256]{1,2,0:T(8,128)(2,1)S(1)}, u32[]{:S(2)}, u32[]{:S(2)}) %collective-permute-start) | collective-permute-done | bytes 524320 | tf_op jit(solution)/shard_map/while/body/eval_jaxpr/ppermute | solution.py:29
  58.8 2.9 %collective-permute-start.1 = (bf16[2,128,256]{1,2,0:T(8,128)(2,1)S(1)}, bf16[2,128,256]{1,2,0:T(8,128)(2,1)S(1)}, u32[]{:S(2)}, u32[]{:S(2)}) collective-permute-start(bf16[2,128,256]{1,2,0:T(8,128)(2,1)S(1)} %get-tuple-element.195), channel_id=1, source_target_pairs={{1,0},{2,1},{3,2},{4,3},{5,4},{6,5},{7,6},{9,8},{10,9},{11,10},{12... | collective-permute-start | bytes 393224 | tf_op jit(solution)/shard_map/while/body/eval_jaxpr/ppermute | solution.py:19
  61.7 2.9 %collective-permute-start.2 = (bf16[2,128,256]{1,2,0:T(8,128)(2,1)S(1)}, bf16[2,128,256]{1,2,0:T(8,128)(2,1)S(1)}, u32[]{:S(2)}, u32[]{:S(2)}) collective-permute-start(bf16[2,128,256]{1,2,0:T(8,128)(2,1)S(1)} %get-tuple-element.196), channel_id=1, source_target_pairs={{0,1},{1,2},{2,3},{3,4},{4,5},{5,6},{6,7},{8,9},{9,10},{10,11},{11... | collective-permute-start | bytes 393224 | tf_op jit(solution)/shard_map/while/body/eval_jaxpr/ppermute | solution.py:17
  65.7 3.8 %collective-permute-done.2 = bf16[2,128,256]{1,2,0:T(8,128)(2,1)S(1)} collective-permute-done((bf16[2,128,256]{1,2,0:T(8,128)(2,1)S(1)}, bf16[2,128,256]{1,2,0:T(8,128)(2,1)S(1)}, u32[]{:S(2)}, u32[]{:S(2)}) %collective-permute-start.2) | collective-permute-done | bytes 131104 | tf_op jit(solution)/shard_map/while/body/eval_jaxpr/ppermute | solution.py:17
  69.6 2.7 %gather_fusion = bf16[48,128,256]{1,2,0:T(8,128)(2,1)} fusion(bf16[12,128,256]{1,2,0:T(8,128)(2,1)S(1)} %pad_maximum_fusion.6, s32[1024]{0:T(1024)S(1)} %pad_clamp_fusion.4), kind=kCustom, calls=%fused_computation.clone.clone.1 | custom fusion | bytes 6291648 | tf_op jit(solution)/shard_map/while/body/eval_jaxpr/jit(_take)/gather | solution.py:33
  72.3 3.5 %convolution_convert_fusion.4 = bf16[8,256,128]{2,1,0:T(8,128)(2,1)S(1)} fusion(bf16[2,8,6,128,128]{4,3,2,1,0:T(8,128)(2,1)} %get-tuple-element.235, bf16[8,6,128,256]{2,3,1,0:T(8,128)(2,1)} %bitcast.124, f32[8,6]{1,0:T(8,128)S(1)} %get-tuple-element.198, pred[8,6]{1,0:T(8,128)(4,1)S(1)} %get-tuple-element.199, ...), kind=kOutput, calls=%fused_computation.23.clone.1 | convolution fusion | flops 477102080 | bytes 6034432 | tf_op jit(solution)/shard_map/while/body/eval_jaxpr/qab,qbn->qan/dot_general | solution.py:37
  75.8 1.9 %collective-permute-start.3 = (bf16[2,128,256]{1,2,0:T(8,128)(2,1)S(1)}, bf16[2,128,256]{1,2,0:T(8,128)(2,1)S(1)}, u32[]{:S(2)}, u32[]{:S(2)}) collective-permute-start(bf16[2,128,256]{1,2,0:T(8,128)(2,1)S(1)} %get-tuple-element.200), channel_id=1, source_target_pairs={{1,0},{2,1},{3,2},{4,3},{5,4},{6,5},{7,6},{9,8},{10,9},{11,10},{12... | collective-permute-start | bytes 393224 | tf_op jit(solution)/shard_map/while/body/eval_jaxpr/ppermute | solution.py:19
  77.8 3.9 %collective-permute-start.4 = (bf16[2,128,256]{1,2,0:T(8,128)(2,1)S(1)}, bf16[2,128,256]{1,2,0:T(8,128)(2,1)S(1)}, u32[]{:S(2)}, u32[]{:S(2)}) collective-permute-start(bf16[2,128,256]{1,2,0:T(8,128)(2,1)S(1)} %get-tuple-element.201), channel_id=1, source_target_pairs={{0,1},{1,2},{2,3},{3,4},{4,5},{5,6},{6,7},{8,9},{9,10},{10,11},{11... | collective-permute-start | bytes 393224 | tf_op jit(solution)/shard_map/while/body/eval_jaxpr/ppermute | solution.py:17
  82.7 2.8 %collective-permute-done.4 = bf16[2,128,256]{1,2,0:T(8,128)(2,1)S(1)} collective-permute-done((bf16[2,128,256]{1,2,0:T(8,128)(2,1)S(1)}, bf16[2,128,256]{1,2,0:T(8,128)(2,1)S(1)}, u32[]{:S(2)}, u32[]{:S(2)}) %collective-permute-start.4) | collective-permute-done | bytes 131104 | tf_op jit(solution)/shard_map/while/body/eval_jaxpr/ppermute | solution.py:17
  85.6 2.7 %gather_fusion.1 = bf16[48,128,256]{1,2,0:T(8,128)(2,1)} fusion(bf16[12,128,256]{1,2,0:T(8,128)(2,1)S(1)} %pad_maximum_fusion.7, s32[1024]{0:T(1024)S(1)} %pad_clamp_fusion.5), kind=kCustom, calls=%fused_computation.1.clone.clone.1 | custom fusion | bytes 6291648 | tf_op jit(solution)/shard_map/while/body/eval_jaxpr/jit(_take)/gather | solution.py:33
  88.3 3.5 %convolution_convert_fusion.5 = bf16[8,256,128]{2,1,0:T(8,128)(2,1)S(1)} fusion(bf16[2,8,6,128,128]{4,3,2,1,0:T(8,128)(2,1)} %get-tuple-element.235, bf16[8,6,128,256]{2,3,1,0:T(8,128)(2,1)} %bitcast.123, f32[8,6]{1,0:T(8,128)S(1)} %get-tuple-element.203, pred[8,6]{1,0:T(8,128)(4,1)S(1)} %get-tuple-element.204, ...), kind=kOutput, calls=%fused_computation.22.clone.1 | convolution fusion | flops 477102080 | bytes 6034432 | tf_op jit(solution)/shard_map/while/body/eval_jaxpr/qab,qbn->qan/dot_general | solution.py:37
  94.9 8.5 %collective-permute-done = bf16[8,128,256]{1,2,0:T(8,128)(2,1)S(1)} collective-permute-done((bf16[8,128,256]{1,2,0:T(8,128)(2,1)S(1)}, bf16[8,128,256]{1,2,0:T(8,128)(2,1)S(1)}, u32[]{:S(2)}, u32[]{:S(2)}) %collective-permute-start) | collective-permute-done | bytes 524320 | tf_op jit(solution)/shard_map/while/body/eval_jaxpr/ppermute | solution.py:29
  103.4 2.9 %collective-permute-start.1 = (bf16[2,128,256]{1,2,0:T(8,128)(2,1)S(1)}, bf16[2,128,256]{1,2,0:T(8,128)(2,1)S(1)}, u32[]{:S(2)}, u32[]{:S(2)}) collective-permute-start(bf16[2,128,256]{1,2,0:T(8,128)(2,1)S(1)} %get-tuple-element.195), channel_id=1, source_target_pairs={{1,0},{2,1},{3,2},{4,3},{5,4},{6,5},{7,6},{9,8},{10,9},{11,10},{12... | collective-permute-start | bytes 393224 | tf_op jit(solution)/shard_map/while/body/eval_jaxpr/ppermute | solution.py:19
  106.3 2.9 %collective-permute-start.2 = (bf16[2,128,256]{1,2,0:T(8,128)(2,1)S(1)}, bf16[2,128,256]{1,2,0:T(8,128)(2,1)S(1)}, u32[]{:S(2)}, u32[]{:S(2)}) collective-permute-start(bf16[2,128,256]{1,2,0:T(8,128)(2,1)S(1)} %get-tuple-element.196), channel_id=1, source_target_pairs={{0,1},{1,2},{2,3},{3,4},{4,5},{5,6},{6,7},{8,9},{9,10},{10,11},{11... | collective-permute-start | bytes 393224 | tf_op jit(solution)/shard_map/while/body/eval_jaxpr/ppermute | solution.py:17
  110.3 3.8 %collective-permute-done.2 = bf16[2,128,256]{1,2,0:T(8,128)(2,1)S(1)} collective-permute-done((bf16[2,128,256]{1,2,0:T(8,128)(2,1)S(1)}, bf16[2,128,256]{1,2,0:T(8,128)(2,1)S(1)}, u32[]{:S(2)}, u32[]{:S(2)}) %collective-permute-start.2) | collective-permute-done | bytes 131104 | tf_op jit(solution)/shard_map/while/body/eval_jaxpr/ppermute | solution.py:17
  114.2 2.7 %gather_fusion = bf16[48,128,256]{1,2,0:T(8,128)(2,1)} fusion(bf16[12,128,256]{1,2,0:T(8,128)(2,1)S(1)} %pad_maximum_fusion.6, s32[1024]{0:T(1024)S(1)} %pad_clamp_fusion.4), kind=kCustom, calls=%fused_computation.clone.clone.1 | custom fusion | bytes 6291648 | tf_op jit(solution)/shard_map/while/body/eval_jaxpr/jit(_take)/gather | solution.py:33
  116.9 3.5 %convolution_convert_fusion.4 = bf16[8,256,128]{2,1,0:T(8,128)(2,1)S(1)} fusion(bf16[2,8,6,128,128]{4,3,2,1,0:T(8,128)(2,1)} %get-tuple-element.235, bf16[8,6,128,256]{2,3,1,0:T(8,128)(2,1)} %bitcast.124, f32[8,6]{1,0:T(8,128)S(1)} %get-tuple-element.198, pred[8,6]{1,0:T(8,128)(4,1)S(1)} %get-tuple-element.199, ...), kind=kOutput, calls=%fused_computation.23.clone.1 | convolution fusion | flops 477102080 | bytes 6034432 | tf_op jit(solution)/shard_map/while/body/eval_jaxpr/qab,qbn->qan/dot_general | solution.py:37
  120.4 1.9 %collective-permute-start.3 = (bf16[2,128,256]{1,2,0:T(8,128)(2,1)S(1)}, bf16[2,128,256]{1,2,0:T(8,128)(2,1)S(1)}, u32[]{:S(2)}, u32[]{:S(2)}) collective-permute-start(bf16[2,128,256]{1,2,0:T(8,128)(2,1)S(1)} %get-tuple-element.200), channel_id=1, source_target_pairs={{1,0},{2,1},{3,2},{4,3},{5,4},{6,5},{7,6},{9,8},{10,9},{11,10},{12... | collective-permute-start | bytes 393224 | tf_op jit(solution)/shard_map/while/body/eval_jaxpr/ppermute | solution.py:19
  122.4 3.9 %collective-permute-start.4 = (bf16[2,128,256]{1,2,0:T(8,128)(2,1)S(1)}, bf16[2,128,256]{1,2,0:T(8,128)(2,1)S(1)}, u32[]{:S(2)}, u32[]{:S(2)}) collective-permute-start(bf16[2,128,256]{1,2,0:T(8,128)(2,1)S(1)} %get-tuple-element.201), channel_id=1, source_target_pairs={{0,1},{1,2},{2,3},{3,4},{4,5},{5,6},{6,7},{8,9},{9,10},{10,11},{11... | collective-permute-start | bytes 393224 | tf_op jit(solution)/shard_map/while/body/eval_jaxpr/ppermute | solution.py:17
  127.3 2.8 %collective-permute-done.4 = bf16[2,128,256]{1,2,0:T(8,128)(2,1)S(1)} collective-permute-done((bf16[2,128,256]{1,2,0:T(8,128)(2,1)S(1)}, bf16[2,128,256]{1,2,0:T(8,128)(2,1)S(1)}, u32[]{:S(2)}, u32[]{:S(2)}) %collective-permute-start.4) | collective-permute-done | bytes 131104 | tf_op jit(solution)/shard_map/while/body/eval_jaxpr/ppermute | solution.py:17
  130.2 2.7 %gather_fusion.1 = bf16[48,128,256]{1,2,0:T(8,128)(2,1)} fusion(bf16[12,128,256]{1,2,0:T(8,128)(2,1)S(1)} %pad_maximum_fusion.7, s32[1024]{0:T(1024)S(1)} %pad_clamp_fusion.5), kind=kCustom, calls=%fused_computation.1.clone.clone.1 | custom fusion | bytes 6291648 | tf_op jit(solution)/shard_map/while/body/eval_jaxpr/jit(_take)/gather | solution.py:33
  132.9 3.5 %convolution_convert_fusion.5 = bf16[8,256,128]{2,1,0:T(8,128)(2,1)S(1)} fusion(bf16[2,8,6,128,128]{4,3,2,1,0:T(8,128)(2,1)} %get-tuple-element.235, bf16[8,6,128,256]{2,3,1,0:T(8,128)(2,1)} %bitcast.123, f32[8,6]{1,0:T(8,128)S(1)} %get-tuple-element.203, pred[8,6]{1,0:T(8,128)(4,1)S(1)} %get-tuple-element.204, ...), kind=kOutput, calls=%fused_computation.22.clone.1 | convolution fusion | flops 477102080 | bytes 6034432 | tf_op jit(solution)/shard_map/while/body/eval_jaxpr/qab,qbn->qan/dot_general | solution.py:37
  137.5 1.9 %collective-permute-start = (bf16[8,128,256]{1,2,0:T(8,128)(2,1)S(1)}, bf16[8,128,256]{1,2,0:T(8,128)(2,1)S(1)}, u32[]{:S(2)}, u32[]{:S(2)}) collective-permute-start(bf16[8,128,256]{1,2,0:T(8,128)(2,1)S(1)} %get-tuple-element.218), channel_id=1, source_target_pairs={{0,8},{8,16},{16,24},{1,9},{9,17},{17,25},{2,10},{10,18},{18,26},{... | collective-permute-start | bytes 1572872 | tf_op jit(solution)/shard_map/while/body/eval_jaxpr/ppermute | solution.py:29
  139.5 8.5 %collective-permute-done = bf16[8,128,256]{1,2,0:T(8,128)(2,1)S(1)} collective-permute-done((bf16[8,128,256]{1,2,0:T(8,128)(2,1)S(1)}, bf16[8,128,256]{1,2,0:T(8,128)(2,1)S(1)}, u32[]{:S(2)}, u32[]{:S(2)}) %collective-permute-start) | collective-permute-done | bytes 524320 | tf_op jit(solution)/shard_map/while/body/eval_jaxpr/ppermute | solution.py:29
  148.0 1.9 %collective-permute-start.1 = (bf16[2,128,256]{1,2,0:T(8,128)(2,1)S(1)}, bf16[2,128,256]{1,2,0:T(8,128)(2,1)S(1)}, u32[]{:S(2)}, u32[]{:S(2)}) collective-permute-start(bf16[2,128,256]{1,2,0:T(8,128)(2,1)S(1)} %get-tuple-element.195), channel_id=1, source_target_pairs={{1,0},{2,1},{3,2},{4,3},{5,4},{6,5},{7,6},{9,8},{10,9},{11,10},{12... | collective-permute-start | bytes 393224 | tf_op jit(solution)/shard_map/while/body/eval_jaxpr/ppermute | solution.py:19
  150.0 3.9 %collective-permute-start.2 = (bf16[2,128,256]{1,2,0:T(8,128)(2,1)S(1)}, bf16[2,128,256]{1,2,0:T(8,128)(2,1)S(1)}, u32[]{:S(2)}, u32[]{:S(2)}) collective-permute-start(bf16[2,128,256]{1,2,0:T(8,128)(2,1)S(1)} %get-tuple-element.196), channel_id=1, source_target_pairs={{0,1},{1,2},{2,3},{3,4},{4,5},{5,6},{6,7},{8,9},{9,10},{10,11},{11... | collective-permute-start | bytes 393224 | tf_op jit(solution)/shard_map/while/body/eval_jaxpr/ppermute | solution.py:17
  154.9 2.8 %collective-permute-done.2 = bf16[2,128,256]{1,2,0:T(8,128)(2,1)S(1)} collective-permute-done((bf16[2,128,256]{1,2,0:T(8,128)(2,1)S(1)}, bf16[2,128,256]{1,2,0:T(8,128)(2,1)S(1)}, u32[]{:S(2)}, u32[]{:S(2)}) %collective-permute-start.2) | collective-permute-done | bytes 131104 | tf_op jit(solution)/shard_map/while/body/eval_jaxpr/ppermute | solution.py:17
  157.8 2.7 %gather_fusion = bf16[48,128,256]{1,2,0:T(8,128)(2,1)} fusion(bf16[12,128,256]{1,2,0:T(8,128)(2,1)S(1)} %pad_maximum_fusion.6, s32[1024]{0:T(1024)S(1)} %pad_clamp_fusion.4), kind=kCustom, calls=%fused_computation.clone.clone.1 | custom fusion | bytes 6291648 | tf_op jit(solution)/shard_map/while/body/eval_jaxpr/jit(_take)/gather | solution.py:33
  160.5 3.5 %convolution_convert_fusion.4 = bf16[8,256,128]{2,1,0:T(8,128)(2,1)S(1)} fusion(bf16[2,8,6,128,128]{4,3,2,1,0:T(8,128)(2,1)} %get-tuple-element.235, bf16[8,6,128,256]{2,3,1,0:T(8,128)(2,1)} %bitcast.124, f32[8,6]{1,0:T(8,128)S(1)} %get-tuple-element.198, pred[8,6]{1,0:T(8,128)(4,1)S(1)} %get-tuple-element.199, ...), kind=kOutput, calls=%fused_computation.23.clone.1 | convolution fusion | flops 477102080 | bytes 6034432 | tf_op jit(solution)/shard_map/while/body/eval_jaxpr/qab,qbn->qan/dot_general | solution.py:37
  164.1 1.9 %collective-permute-start.3 = (bf16[2,128,256]{1,2,0:T(8,128)(2,1)S(1)}, bf16[2,128,256]{1,2,0:T(8,128)(2,1)S(1)}, u32[]{:S(2)}, u32[]{:S(2)}) collective-permute-start(bf16[2,128,256]{1,2,0:T(8,128)(2,1)S(1)} %get-tuple-element.200), channel_id=1, source_target_pairs={{1,0},{2,1},{3,2},{4,3},{5,4},{6,5},{7,6},{9,8},{10,9},{11,10},{12... | collective-permute-start | bytes 393224 | tf_op jit(solution)/shard_map/while/body/eval_jaxpr/ppermute | solution.py:19
  166.0 3.9 %collective-permute-start.4 = (bf16[2,128,256]{1,2,0:T(8,128)(2,1)S(1)}, bf16[2,128,256]{1,2,0:T(8,128)(2,1)S(1)}, u32[]{:S(2)}, u32[]{:S(2)}) collective-permute-start(bf16[2,128,256]{1,2,0:T(8,128)(2,1)S(1)} %get-tuple-element.201), channel_id=1, source_target_pairs={{0,1},{1,2},{2,3},{3,4},{4,5},{5,6},{6,7},{8,9},{9,10},{10,11},{11... | collective-permute-start | bytes 393224 | tf_op jit(solution)/shard_map/while/body/eval_jaxpr/ppermute | solution.py:17
  170.9 2.8 %collective-permute-done.4 = bf16[2,128,256]{1,2,0:T(8,128)(2,1)S(1)} collective-permute-done((bf16[2,128,256]{1,2,0:T(8,128)(2,1)S(1)}, bf16[2,128,256]{1,2,0:T(8,128)(2,1)S(1)}, u32[]{:S(2)}, u32[]{:S(2)}) %collective-permute-start.4) | collective-permute-done | bytes 131104 | tf_op jit(solution)/shard_map/while/body/eval_jaxpr/ppermute | solution.py:17
  173.9 2.7 %gather_fusion.1 = bf16[48,128,256]{1,2,0:T(8,128)(2,1)} fusion(bf16[12,128,256]{1,2,0:T(8,128)(2,1)S(1)} %pad_maximum_fusion.7, s32[1024]{0:T(1024)S(1)} %pad_clamp_fusion.5), kind=kCustom, calls=%fused_computation.1.clone.clone.1 | custom fusion | bytes 6291648 | tf_op jit(solution)/shard_map/while/body/eval_jaxpr/jit(_take)/gather | solution.py:33
  176.6 3.5 %convolution_convert_fusion.5 = bf16[8,256,128]{2,1,0:T(8,128)(2,1)S(1)} fusion(bf16[2,8,6,128,128]{4,3,2,1,0:T(8,128)(2,1)} %get-tuple-element.235, bf16[8,6,128,256]{2,3,1,0:T(8,128)(2,1)} %bitcast.123, f32[8,6]{1,0:T(8,128)S(1)} %get-tuple-element.203, pred[8,6]{1,0:T(8,128)(4,1)S(1)} %get-tuple-element.204, ...), kind=kOutput, calls=%fused_computation.22.clone.1 | convolution fusion | flops 477102080 | bytes 6034432 | tf_op jit(solution)/shard_map/while/body/eval_jaxpr/qab,qbn->qan/dot_general | solution.py:37
  181.1 2.3 %copy.9 = bf16[2,8,128,256]{3,2,1,0:T(8,128)(2,1)} copy(bf16[2,8,128,256]{2,3,1,0:T(8,128)(2,1)} %get-tuple-element.103) | data formatting | bytes 2097152 | tf_op jit(solution)/shard_map/while | solution.py:77
  (75 shorter events, 20.3 us)
Async XLA Ops:
  3.3 10.5 %collective-permute-start = (bf16[8,128,256]{1,2,0:T(8,128)(2,1)S(1)}, bf16[8,128,256]{1,2,0:T(8,128)(2,1)S(1)}, u32[]{:S(2)}, u32[]{:S(2)}) collective-permute-start(bf16[8,128,256]{1,2,0:T(8,128)(2,1)S(1)} %get-tuple-element.218), channel_id=1, source_target_pairs={{0,8},{8,16},{16,24},{1,9},{9,17},{17,25},{2,10},{10,18},{18,26},{... | collective-permute-start | bytes 1572872 | tf_op jit(solution)/shard_map/while/body/eval_jaxpr/ppermute | solution.py:29
  13.8 6.9 %collective-permute-start.1 = (bf16[2,128,256]{1,2,0:T(8,128)(2,1)S(1)}, bf16[2,128,256]{1,2,0:T(8,128)(2,1)S(1)}, u32[]{:S(2)}, u32[]{:S(2)}) collective-permute-start(bf16[2,128,256]{1,2,0:T(8,128)(2,1)S(1)} %get-tuple-element.195), channel_id=1, source_target_pairs={{1,0},{2,1},{3,2},{4,3},{5,4},{6,5},{7,6},{9,8},{10,9},{11,10},{12... | collective-permute-start | bytes 393224 | tf_op jit(solution)/shard_map/while/body/eval_jaxpr/ppermute | solution.py:19
  17.1 7.8 %collective-permute-start.2 = (bf16[2,128,256]{1,2,0:T(8,128)(2,1)S(1)}, bf16[2,128,256]{1,2,0:T(8,128)(2,1)S(1)}, u32[]{:S(2)}, u32[]{:S(2)}) collective-permute-start(bf16[2,128,256]{1,2,0:T(8,128)(2,1)S(1)} %get-tuple-element.196), channel_id=1, source_target_pairs={{0,1},{1,2},{2,3},{3,4},{4,5},{5,6},{6,7},{8,9},{9,10},{10,11},{11... | collective-permute-start | bytes 393224 | tf_op jit(solution)/shard_map/while/body/eval_jaxpr/ppermute | solution.py:17
  31.2 6.9 %collective-permute-start.3 = (bf16[2,128,256]{1,2,0:T(8,128)(2,1)S(1)}, bf16[2,128,256]{1,2,0:T(8,128)(2,1)S(1)}, u32[]{:S(2)}, u32[]{:S(2)}) collective-permute-start(bf16[2,128,256]{1,2,0:T(8,128)(2,1)S(1)} %get-tuple-element.200), channel_id=1, source_target_pairs={{1,0},{2,1},{3,2},{4,3},{5,4},{6,5},{7,6},{9,8},{10,9},{11,10},{12... | collective-permute-start | bytes 393224 | tf_op jit(solution)/shard_map/while/body/eval_jaxpr/ppermute | solution.py:19
  33.1 7.8 %collective-permute-start.4 = (bf16[2,128,256]{1,2,0:T(8,128)(2,1)S(1)}, bf16[2,128,256]{1,2,0:T(8,128)(2,1)S(1)}, u32[]{:S(2)}, u32[]{:S(2)}) collective-permute-start(bf16[2,128,256]{1,2,0:T(8,128)(2,1)S(1)} %get-tuple-element.201), channel_id=1, source_target_pairs={{0,1},{1,2},{2,3},{3,4},{4,5},{5,6},{6,7},{8,9},{9,10},{10,11},{11... | collective-permute-start | bytes 393224 | tf_op jit(solution)/shard_map/while/body/eval_jaxpr/ppermute | solution.py:17
  41.0 2.7 %copy-start = (bf16[2,8,128,128]{3,2,1,0:T(8,128)(2,1)S(1)}, bf16[2,8,128,128]{3,2,1,0:T(8,128)(2,1)}, u32[]{:S(2)}) copy-start(bf16[2,8,128,128]{3,2,1,0:T(8,128)(2,1)} %get-tuple-element.236) | copy-start | bytes 1572868 | tf_op jit(solution)/shard_map/while
  48.3 10.5 %collective-permute-start = (bf16[8,128,256]{1,2,0:T(8,128)(2,1)S(1)}, bf16[8,128,256]{1,2,0:T(8,128)(2,1)S(1)}, u32[]{:S(2)}, u32[]{:S(2)}) collective-permute-start(bf16[8,128,256]{1,2,0:T(8,128)(2,1)S(1)} %get-tuple-element.218), channel_id=1, source_target_pairs={{0,8},{8,16},{16,24},{1,9},{9,17},{17,25},{2,10},{10,18},{18,26},{... | collective-permute-start | bytes 1572872 | tf_op jit(solution)/shard_map/while/body/eval_jaxpr/ppermute | solution.py:29
  58.8 6.9 %collective-permute-start.1 = (bf16[2,128,256]{1,2,0:T(8,128)(2,1)S(1)}, bf16[2,128,256]{1,2,0:T(8,128)(2,1)S(1)}, u32[]{:S(2)}, u32[]{:S(2)}) collective-permute-start(bf16[2,128,256]{1,2,0:T(8,128)(2,1)S(1)} %get-tuple-element.195), channel_id=1, source_target_pairs={{1,0},{2,1},{3,2},{4,3},{5,4},{6,5},{7,6},{9,8},{10,9},{11,10},{12... | collective-permute-start | bytes 393224 | tf_op jit(solution)/shard_map/while/body/eval_jaxpr/ppermute | solution.py:19
  61.7 7.8 %collective-permute-start.2 = (bf16[2,128,256]{1,2,0:T(8,128)(2,1)S(1)}, bf16[2,128,256]{1,2,0:T(8,128)(2,1)S(1)}, u32[]{:S(2)}, u32[]{:S(2)}) collective-permute-start(bf16[2,128,256]{1,2,0:T(8,128)(2,1)S(1)} %get-tuple-element.196), channel_id=1, source_target_pairs={{0,1},{1,2},{2,3},{3,4},{4,5},{5,6},{6,7},{8,9},{9,10},{10,11},{11... | collective-permute-start | bytes 393224 | tf_op jit(solution)/shard_map/while/body/eval_jaxpr/ppermute | solution.py:17
  75.8 6.9 %collective-permute-start.3 = (bf16[2,128,256]{1,2,0:T(8,128)(2,1)S(1)}, bf16[2,128,256]{1,2,0:T(8,128)(2,1)S(1)}, u32[]{:S(2)}, u32[]{:S(2)}) collective-permute-start(bf16[2,128,256]{1,2,0:T(8,128)(2,1)S(1)} %get-tuple-element.200), channel_id=1, source_target_pairs={{1,0},{2,1},{3,2},{4,3},{5,4},{6,5},{7,6},{9,8},{10,9},{11,10},{12... | collective-permute-start | bytes 393224 | tf_op jit(solution)/shard_map/while/body/eval_jaxpr/ppermute | solution.py:19
  77.8 7.8 %collective-permute-start.4 = (bf16[2,128,256]{1,2,0:T(8,128)(2,1)S(1)}, bf16[2,128,256]{1,2,0:T(8,128)(2,1)S(1)}, u32[]{:S(2)}, u32[]{:S(2)}) collective-permute-start(bf16[2,128,256]{1,2,0:T(8,128)(2,1)S(1)} %get-tuple-element.201), channel_id=1, source_target_pairs={{0,1},{1,2},{2,3},{3,4},{4,5},{5,6},{6,7},{8,9},{9,10},{10,11},{11... | collective-permute-start | bytes 393224 | tf_op jit(solution)/shard_map/while/body/eval_jaxpr/ppermute | solution.py:17
  85.6 2.7 %copy-start = (bf16[2,8,128,128]{3,2,1,0:T(8,128)(2,1)S(1)}, bf16[2,8,128,128]{3,2,1,0:T(8,128)(2,1)}, u32[]{:S(2)}) copy-start(bf16[2,8,128,128]{3,2,1,0:T(8,128)(2,1)} %get-tuple-element.236) | copy-start | bytes 1572868 | tf_op jit(solution)/shard_map/while
  92.9 10.5 %collective-permute-start = (bf16[8,128,256]{1,2,0:T(8,128)(2,1)S(1)}, bf16[8,128,256]{1,2,0:T(8,128)(2,1)S(1)}, u32[]{:S(2)}, u32[]{:S(2)}) collective-permute-start(bf16[8,128,256]{1,2,0:T(8,128)(2,1)S(1)} %get-tuple-element.218), channel_id=1, source_target_pairs={{0,8},{8,16},{16,24},{1,9},{9,17},{17,25},{2,10},{10,18},{18,26},{... | collective-permute-start | bytes 1572872 | tf_op jit(solution)/shard_map/while/body/eval_jaxpr/ppermute | solution.py:29
  103.4 6.9 %collective-permute-start.1 = (bf16[2,128,256]{1,2,0:T(8,128)(2,1)S(1)}, bf16[2,128,256]{1,2,0:T(8,128)(2,1)S(1)}, u32[]{:S(2)}, u32[]{:S(2)}) collective-permute-start(bf16[2,128,256]{1,2,0:T(8,128)(2,1)S(1)} %get-tuple-element.195), channel_id=1, source_target_pairs={{1,0},{2,1},{3,2},{4,3},{5,4},{6,5},{7,6},{9,8},{10,9},{11,10},{12... | collective-permute-start | bytes 393224 | tf_op jit(solution)/shard_map/while/body/eval_jaxpr/ppermute | solution.py:19
  106.3 7.8 %collective-permute-start.2 = (bf16[2,128,256]{1,2,0:T(8,128)(2,1)S(1)}, bf16[2,128,256]{1,2,0:T(8,128)(2,1)S(1)}, u32[]{:S(2)}, u32[]{:S(2)}) collective-permute-start(bf16[2,128,256]{1,2,0:T(8,128)(2,1)S(1)} %get-tuple-element.196), channel_id=1, source_target_pairs={{0,1},{1,2},{2,3},{3,4},{4,5},{5,6},{6,7},{8,9},{9,10},{10,11},{11... | collective-permute-start | bytes 393224 | tf_op jit(solution)/shard_map/while/body/eval_jaxpr/ppermute | solution.py:17
  120.4 6.9 %collective-permute-start.3 = (bf16[2,128,256]{1,2,0:T(8,128)(2,1)S(1)}, bf16[2,128,256]{1,2,0:T(8,128)(2,1)S(1)}, u32[]{:S(2)}, u32[]{:S(2)}) collective-permute-start(bf16[2,128,256]{1,2,0:T(8,128)(2,1)S(1)} %get-tuple-element.200), channel_id=1, source_target_pairs={{1,0},{2,1},{3,2},{4,3},{5,4},{6,5},{7,6},{9,8},{10,9},{11,10},{12... | collective-permute-start | bytes 393224 | tf_op jit(solution)/shard_map/while/body/eval_jaxpr/ppermute | solution.py:19
  122.4 7.8 %collective-permute-start.4 = (bf16[2,128,256]{1,2,0:T(8,128)(2,1)S(1)}, bf16[2,128,256]{1,2,0:T(8,128)(2,1)S(1)}, u32[]{:S(2)}, u32[]{:S(2)}) collective-permute-start(bf16[2,128,256]{1,2,0:T(8,128)(2,1)S(1)} %get-tuple-element.201), channel_id=1, source_target_pairs={{0,1},{1,2},{2,3},{3,4},{4,5},{5,6},{6,7},{8,9},{9,10},{10,11},{11... | collective-permute-start | bytes 393224 | tf_op jit(solution)/shard_map/while/body/eval_jaxpr/ppermute | solution.py:17
  130.2 2.7 %copy-start = (bf16[2,8,128,128]{3,2,1,0:T(8,128)(2,1)S(1)}, bf16[2,8,128,128]{3,2,1,0:T(8,128)(2,1)}, u32[]{:S(2)}) copy-start(bf16[2,8,128,128]{3,2,1,0:T(8,128)(2,1)} %get-tuple-element.236) | copy-start | bytes 1572868 | tf_op jit(solution)/shard_map/while
  137.5 10.5 %collective-permute-start = (bf16[8,128,256]{1,2,0:T(8,128)(2,1)S(1)}, bf16[8,128,256]{1,2,0:T(8,128)(2,1)S(1)}, u32[]{:S(2)}, u32[]{:S(2)}) collective-permute-start(bf16[8,128,256]{1,2,0:T(8,128)(2,1)S(1)} %get-tuple-element.218), channel_id=1, source_target_pairs={{0,8},{8,16},{16,24},{1,9},{9,17},{17,25},{2,10},{10,18},{18,26},{... | collective-permute-start | bytes 1572872 | tf_op jit(solution)/shard_map/while/body/eval_jaxpr/ppermute | solution.py:29
  148.0 6.9 %collective-permute-start.1 = (bf16[2,128,256]{1,2,0:T(8,128)(2,1)S(1)}, bf16[2,128,256]{1,2,0:T(8,128)(2,1)S(1)}, u32[]{:S(2)}, u32[]{:S(2)}) collective-permute-start(bf16[2,128,256]{1,2,0:T(8,128)(2,1)S(1)} %get-tuple-element.195), channel_id=1, source_target_pairs={{1,0},{2,1},{3,2},{4,3},{5,4},{6,5},{7,6},{9,8},{10,9},{11,10},{12... | collective-permute-start | bytes 393224 | tf_op jit(solution)/shard_map/while/body/eval_jaxpr/ppermute | solution.py:19
  150.0 7.8 %collective-permute-start.2 = (bf16[2,128,256]{1,2,0:T(8,128)(2,1)S(1)}, bf16[2,128,256]{1,2,0:T(8,128)(2,1)S(1)}, u32[]{:S(2)}, u32[]{:S(2)}) collective-permute-start(bf16[2,128,256]{1,2,0:T(8,128)(2,1)S(1)} %get-tuple-element.196), channel_id=1, source_target_pairs={{0,1},{1,2},{2,3},{3,4},{4,5},{5,6},{6,7},{8,9},{9,10},{10,11},{11... | collective-permute-start | bytes 393224 | tf_op jit(solution)/shard_map/while/body/eval_jaxpr/ppermute | solution.py:17
  164.1 6.9 %collective-permute-start.3 = (bf16[2,128,256]{1,2,0:T(8,128)(2,1)S(1)}, bf16[2,128,256]{1,2,0:T(8,128)(2,1)S(1)}, u32[]{:S(2)}, u32[]{:S(2)}) collective-permute-start(bf16[2,128,256]{1,2,0:T(8,128)(2,1)S(1)} %get-tuple-element.200), channel_id=1, source_target_pairs={{1,0},{2,1},{3,2},{4,3},{5,4},{6,5},{7,6},{9,8},{10,9},{11,10},{12... | collective-permute-start | bytes 393224 | tf_op jit(solution)/shard_map/while/body/eval_jaxpr/ppermute | solution.py:19
  166.0 7.8 %collective-permute-start.4 = (bf16[2,128,256]{1,2,0:T(8,128)(2,1)S(1)}, bf16[2,128,256]{1,2,0:T(8,128)(2,1)S(1)}, u32[]{:S(2)}, u32[]{:S(2)}) collective-permute-start(bf16[2,128,256]{1,2,0:T(8,128)(2,1)S(1)} %get-tuple-element.201), channel_id=1, source_target_pairs={{0,1},{1,2},{2,3},{3,4},{4,5},{5,6},{6,7},{8,9},{9,10},{10,11},{11... | collective-permute-start | bytes 393224 | tf_op jit(solution)/shard_map/while/body/eval_jaxpr/ppermute | solution.py:17
  173.9 2.7 %copy-start = (bf16[2,8,128,128]{3,2,1,0:T(8,128)(2,1)S(1)}, bf16[2,8,128,128]{3,2,1,0:T(8,128)(2,1)}, u32[]{:S(2)}) copy-start(bf16[2,8,128,128]{3,2,1,0:T(8,128)(2,1)} %get-tuple-element.236) | copy-start | bytes 1572868 | tf_op jit(solution)/shard_map/while
where the time goes:
time: 184 us; the launch traced here: 183 us
  waiting for transfers between devices  67.3 us (37%)
  starting transfers between devices  54.4 us (30%)
  matrix products  28.2 us (15%)
  local copies, waits for them, and re-layouts  27.7 us (15%)
  other arithmetic  5.16 us (3%)
    ppermute x4, waiting for transfers between devices, passed_along(): lax.ppermute(value, axis, [(source, source + steps) for source in range(f...  34.1 us
    dot_general x8, matrix products, level_solve(): jnp.einsum('qab,qbn->qan', inverse, remainder, preferred_element_type=jnp...  28.2 us
    ppermute x8, starting transfers between devices, padded(): lax.ppermute(tail, axis, [(i, (i + 1) % count) for i in range(ends)])  28 us
    ppermute x8, waiting for transfers between devices, padded(): lax.ppermute(tail, axis, [(i, (i + 1) % count) for i in range(ends)])  26 us
    gather x8, local copies, waits for them, and re-layouts, level_solve(): picked_rows = jnp.take(widened, dep_local, axis=0)  21.4 us
    ppermute x8, starting transfers between devices, padded(): lax.ppermute(head, axis, [((i + 1) % count, i) for i in range(ends)])  18.7 us
    ppermute x4, starting transfers between devices, passed_along(): lax.ppermute(value, axis, [(source, source + steps) for source in range(f...  7.65 us
    ppermute x8, waiting for transfers between devices, padded(): lax.ppermute(head, axis, [((i + 1) % count, i) for i in range(ends)])  7.23 us
  transfers between devices with their start and end apart: 20, of which 20 were waited for; matrix products, arithmetic and copies ran while one was open for 0% of the time, Pallas kernels for 0%

commit v1 on v0

v1 whole, which is shorter than its diff:
```python
import functools

import jax
import jax.numpy as jnp
from jax import lax
from jax.experimental import pallas as pl
from jax.experimental.pallas import tpu as pltpu
from jax.sharding import PartitionSpec as P

REACH = 2
SPAN = 2 * REACH + 1
AXES = ("chain", "rows")
VMEM = pl.BlockSpec(memory_space=pltpu.VMEM)
SMEM = pl.BlockSpec(memory_space=pltpu.SMEM)
ANY = pl.BlockSpec(memory_space=pl.ANY)


def even_mate(row, rows):
    return row ^ 1


def odd_mate(row, rows):
    mate = row + 1 if row % 2 else row - 1
    return mate if 0 <= mate < rows else row


def same_row(row, rows):
    return row


def swap_groups(chain, taken=()):
    return {g: g ^ 1 for g in range(chain) if g not in taken}


def hop_pairs(group, mate, chain, rows):
    if group % 2 == 0:
        moves = swap_groups(chain)
    else:
        moves = swap_groups(chain, range(group - 1, group + 3))
        moves.update({group: group + 1, group - 1: group, group + 1: group + 2, group + 2: group - 1})
    return [
        (source * rows + r, target * rows + (mate(r, rows) if source == group else r))
        for source, target in moves.items()
        for r in range(rows)
    ]


def first_pairs(mate, chain, rows):
    pairs = []
    for r in range(rows):
        target = mate(r, rows)
        if target == r:
            moves = swap_groups(chain)
        else:
            pairs.append((r, target))
            moves = swap_groups(chain, range(4))
            moves.update({1: 2, 2: 3, 3: 1})
        pairs += [(a * rows + r, b * rows + r) for a, b in moves.items()]
    return pairs


def inner_pairs(mate, chain, rows):
    return [
        (g * rows + r, g * rows + mate(r, rows))
        for g in range(1, chain)
        for r in range(rows)
        if mate(r, rows) != r
    ]


def dot(a, b):
    return jnp.dot(a, b, preferred_element_type=jnp.float32)


def by_parity(odd, low_value, high_value, even_ref, odd_ref):
    @pl.when(odd == 0)
    def _():
        even_ref[...] = high_value()
        odd_ref[...] = low_value()

    @pl.when(odd == 1)
    def _():
        even_ref[...] = low_value()
        odd_ref[...] = high_value()


def first_kernel(meta, inverse, right, solved, even_out, odd_out):
    count = right.shape[1]
    for q in range(count):
        solved[q] = dot(inverse[0, q], right[0, q]).astype(solved.dtype)
    by_parity(
        meta[1],
        lambda: solved[:REACH],
        lambda: solved[count - REACH :],
        even_out,
        odd_out,
    )


def prepare_kernel(meta, depend, scale, lower, inverse, right, first, wide_a, wide_b, base_b, even_out, odd_out, acc, row_form):
    step = pl.program_id(0)
    last = pl.num_programs(0) - 1
    block = lower.shape[-1]
    width = SPAN * block
    for level, wide in ((0, wide_a), (1, wide_b)):
        wide[...] = jnp.zeros_like(wide)
        for half in range(2):
            q = 2 * step + half
            acc[...] = jnp.zeros_like(acc)
            for k in range(lower.shape[2]):
                product = dot(inverse[level, half], lower[level, half, k])
                acc[depend[level, q, k]] += scale[level, q, k] * product
            for d in range(SPAN):
                column = (d + half) * block
                value = (-acc[d]).astype(wide.dtype)
                wide[0, half * block : (half + 1) * block, column : column + block] = value
                if level == 0:
                    row_form[half, :, d * block : (d + 1) * block] = value
    for half in range(2):
        base_b[half] = dot(inverse[1, half], right[0, half])

    def emit(ref):
        ref[:, :, :width] = row_form[...]
        ref[:, :, width:] = first[...]

    odd = meta[1]
    at_low, at_high = step == 0, step == last

    @pl.when((at_low & (odd == 1)) | (at_high & (odd == 0)))
    def _():
        emit(even_out)

    @pl.when((at_low & (odd == 0)) | (at_high & (odd == 1)))
    def _():
        emit(odd_out)


def order_kernel(meta, even_in, odd_in, edges):
    odd = meta[1]
    edges[1 - odd] = even_in[...]
    edges[odd] = odd_in[...]


def flat(ref, start, count):
    block = ref[start : start + count]
    return block.reshape(count * block.shape[1], block.shape[2])


def second_level(wide_b, base_b, level_a, solved):
    for p in range(wide_b.shape[0]):
        rows = dot(wide_b[p], flat(level_a, 2 * p, SPAN + 1)) + flat(base_b, 2 * p, 2)
        solved[2 * p : 2 * p + 2] = rows.astype(solved.dtype).reshape(2, *solved.shape[1:])


def finish(odd, level_a, solved, out, sends, sem_a, sem_b, copy_a):
    count = solved.shape[0]
    copy_b = pltpu.make_async_copy(solved, out.at[1], sem_b)
    copy_b.start()
    if sends:
        by_parity(
            odd,
            lambda: solved[: 2 * REACH],
            lambda: solved[count - 2 * REACH :],
            *sends,
        )
    copy_a.wait()
    copy_b.wait()


def first_step(group, meta, first, even_in, odd_in, wide_b, base_b, out, solved, *rest):
    *sends, level_a, sem_a, sem_b = rest

    @pl.when(meta[0] == group)
    def _():
        odd = meta[1]
        count = first.shape[0]
        low, high = 0, count + REACH
        level_a[REACH : REACH + count] = first[...]
        level_a[pl.ds(jnp.where(odd == 1, low, high), REACH)] = even_in[...]
        level_a[pl.ds(jnp.where(odd == 1, high, low), REACH)] = odd_in[...]
        copy_a = pltpu.make_async_copy(level_a.at[pl.ds(REACH, count)], out.at[0], sem_a)
        copy_a.start()
        second_level(wide_b, base_b, level_a, solved)
        finish(odd, level_a, solved, out, sends, sem_a, sem_b, copy_a)


def later_step(group, meta, centre, even_in, odd_in, edges, first, wide_a, wide_b, base_b, out_in, out, solved, *rest):
    *sends, window, level_a, sem_a, sem_b = rest

    @pl.when(meta[0] == group)
    def _():
        odd = meta[1]
        count, block = first.shape[0], first.shape[1]
        width = SPAN * block
        halo = 2 * REACH
        low, high = 0, count + halo
        window[halo : halo + count] = centre[...]
        window[pl.ds(jnp.where(odd == 1, low, high), halo)] = even_in[...]
        window[pl.ds(jnp.where(odd == 1, high, low), halo)] = odd_in[...]
        for p in range(wide_a.shape[0]):
            rows = dot(wide_a[p], flat(window, REACH + 2 * p, SPAN + 1)) + flat(first, 2 * p, 2).astype(jnp.float32)
            level_a[REACH + 2 * p : REACH + 2 * p + 2] = rows.astype(level_a.dtype).reshape(2, *level_a.shape[1:])
        copy_a = pltpu.make_async_copy(level_a.at[pl.ds(REACH, count)], out.at[0], sem_a)
        copy_a.start()
        for side in range(2):
            for i in range(REACH):
                at = side * (count + REACH) + i
                row = dot(edges[side, i, :, :width], flat(window, at, SPAN)) + edges[side, i, :, width:].astype(jnp.float32)
                level_a[at] = row.astype(level_a.dtype)
        second_level(wide_b, base_b, level_a, solved)
        finish(odd, level_a, solved, out, sends, sem_a, sem_b, copy_a)


def shaped(shape, dtype=jnp.bfloat16):
    return jax.ShapeDtypeStruct(shape, dtype)


def params(**more):
    return pltpu.CompilerParams(vmem_limit_bytes=32 * 1024 * 1024, **more)


def per_device(chain, rows, right_side, lower_blocks, block_scale, diag_inverse, depend_rows):
    _, count, block, cases = right_side.shape
    terms = lower_blocks.shape[2]
    width = SPAN * block
    row = lax.axis_index("rows")
    meta = jnp.stack([lax.axis_index("chain"), row % 2]).astype(jnp.int32)
    offset = depend_rows - (row * count + jnp.arange(count, dtype=jnp.int32))[None, :, None] + REACH
    offset = jnp.clip(offset, 0, SPAN - 1)

    first, even_edge, odd_edge = pl.pallas_call(
        first_kernel,
        grid=(1,),
        in_specs=[
            SMEM,
            pl.BlockSpec((1, count, block, block), lambda i: (0, 0, 0, 0)),
            pl.BlockSpec((1, count, block, cases), lambda i: (0, 0, 0, 0)),
        ],
        out_specs=[
            pl.BlockSpec((count, block, cases), lambda i: (0, 0, 0)),
            pl.BlockSpec((REACH, block, cases), lambda i: (0, 0, 0)),
            pl.BlockSpec((REACH, block, cases), lambda i: (0, 0, 0)),
        ],
        out_shape=[shaped((count, block, cases)), shaped((REACH, block, cases)), shaped((REACH, block, cases))],
        compiler_params=params(),
        name="first_level",
    )(meta, diag_inverse, right_side)
    even_x = lax.ppermute(even_edge, AXES, first_pairs(even_mate, chain, rows))
    odd_x = lax.ppermute(odd_edge, AXES, first_pairs(odd_mate, chain, rows))

    pairs = count // 2
    wide_a, wide_b, base_b, even_w, odd_w = pl.pallas_call(
        prepare_kernel,
        grid=(pairs,),
        in_specs=[
            SMEM,
            SMEM,
            SMEM,
            pl.BlockSpec((2, 2, terms, block, block), lambda i: (0, i, 0, 0, 0)),
            pl.BlockSpec((2, 2, block, block), lambda i: (0, i, 0, 0)),
            pl.BlockSpec((1, 2, block, cases), lambda i: (1, i, 0, 0)),
            pl.BlockSpec((2, block, cases), lambda i: (i, 0, 0)),
        ],
        out_specs=[
            pl.BlockSpec((1, 2 * block, width + block), lambda i: (i, 0, 0)),
            pl.BlockSpec((1, 2 * block, width + block), lambda i: (i, 0, 0)),
            pl.BlockSpec((2, block, cases), lambda i: (i, 0, 0)),
            pl.BlockSpec((REACH, block, width + cases), lambda i: (0, 0, 0)),
            pl.BlockSpec((REACH, block, width + cases), lambda i: (0, 0, 0)),
        ],
        out_shape=[
            shaped((pairs, 2 * block, width + block)),
            shaped((pairs, 2 * block, width + block)),
            shaped((count, block, cases), jnp.float32),
            shaped((REACH, block, width + cases)),
            shaped((REACH, block, width + cases)),
        ],
        scratch_shapes=[
            pltpu.VMEM((SPAN, block, block), jnp.float32),
            pltpu.VMEM((2, block, width), jnp.bfloat16),
        ],
        compiler_params=params(),
        name="prepare",
    )(meta, offset, block_scale, lower_blocks, diag_inverse, right_side, first)
    even_w = lax.ppermute(even_w, AXES, inner_pairs(even_mate, chain, rows))
    odd_w = lax.ppermute(odd_w, AXES, inner_pairs(odd_mate, chain, rows))

    halo = 2 * REACH
    sem = [pltpu.SemaphoreType.DMA, pltpu.SemaphoreType.DMA]
    level_a = pltpu.VMEM((count + 2 * REACH, block, cases), jnp.bfloat16)
    solved_shape = shaped((count, block, cases))
    send_shape = [shaped((halo, block, cases))] * 2

    out, *sent = pl.pallas_call(
        functools.partial(first_step, 0),
        in_specs=[SMEM] + [VMEM] * 5,
        out_specs=[ANY] + [VMEM] * 3,
        out_shape=[shaped(right_side.shape), solved_shape, *send_shape],
        scratch_shapes=[level_a, *sem],
        compiler_params=params(),
        name="step_0",
    )(meta, first, even_x, odd_x, wide_b, base_b)

    edges = pl.pallas_call(
        order_kernel,
        in_specs=[SMEM, VMEM, VMEM],
        out_specs=VMEM,
        out_shape=shaped((2, *even_w.shape)),
        compiler_params=params(),
        name="order",
    )(meta, even_w, odd_w)

    for group in range(1, chain):
        mates = (same_row, even_mate, odd_mate)
        received = [
            lax.ppermute(value, AXES, hop_pairs(group - 1, mate, chain, rows))
            for value, mate in zip(sent, mates)
        ]
        final = group == chain - 1
        outs = [solved_shape] + ([] if final else send_shape)
        out, *sent = pl.pallas_call(
            functools.partial(later_step, group),
            in_specs=[SMEM] + [VMEM] * 8 + [ANY],
            out_specs=[ANY] + [VMEM] * len(outs),
            out_shape=[shaped(right_side.shape), *outs],
            scratch_shapes=[
                pltpu.VMEM((count + 2 * halo, block, cases), jnp.bfloat16),
                level_a,
                *sem,
            ],
            input_output_aliases={9: 0},
            compiler_params=params(),
            name=f"step_{group}",
        )(meta, *received, edges, first, wide_a, wide_b, base_b, out)
    return out


def solution(mesh):
    placed = (
        P("chain", "rows", None, None),
        P("chain", "rows", None, None, None),
        P("chain", "rows", None),
        P("chain", "rows", None, None),
        P("chain", "rows", None),
    )
    return jax.shard_map(
        functools.partial(per_device, mesh.shape["chain"], mesh.shape["rows"]),
        mesh=mesh,
        in_specs=placed,
        out_specs=P("chain", "rows", None, None),
        check_vma=False,
    )
```

time: 184 us -> 68.2 us (0.37)
  the two profiles are of different devices: /device:TPU:26 before, /device:TPU:11 now
where the time goes in v1:
time: 68.2 us; the launch traced here: 67.9 us
  waiting for transfers between devices  34 us (50%)
  starting transfers between devices  18.7 us (27%)
  Pallas kernels  10.5 us (15%)
  local copies, waits for them, and re-layouts  4.34 us (6%)
    ppermute x1, waiting for transfers between devices, per_device(): even_w = lax.ppermute(even_w, AXES, inner_pairs(even_mate, chain, rows))  17.4 us
    ppermute x9, waiting for transfers between devices, per_device(): lax.ppermute(value, AXES, hop_pairs(group - 1, mate, chain, rows))  16.7 us
    ppermute x9, starting transfers between devices, per_device(): lax.ppermute(value, AXES, hop_pairs(group - 1, mate, chain, rows))  11.6 us
    pallas_call x3, Pallas kernels, per_device(): pl.pallas_call(functools.partial(later_step, group), in_specs=[SMEM] + [V...  4.58 us
    unnamed x16, local copies, waits for them, and re-layouts  4.34 us
    pallas_call x1, Pallas kernels, per_device(): pl.pallas_call(prepare_kernel, grid=(pairs,), in_specs=[SMEM, SMEM, SMEM,...  3.9 us
    ppermute x1, starting transfers between devices, per_device(): even_w = lax.ppermute(even_w, AXES, inner_pairs(even_mate, chain, rows))  3.15 us
    ppermute x1, starting transfers between devices, per_device(): odd_w = lax.ppermute(odd_w, AXES, inner_pairs(odd_mate, chain, rows))  1.92 us
  transfers between devices with their start and end apart: 13, of which 4 were waited for; matrix products, arithmetic and copies ran while one was open for 0% of the time, Pallas kernels for 7%

profile of v1, /device:TPU:11, one launch (start us, length us, event | category | flops | bytes accessed | tf_op | source)
XLA Modules:
  0.0 67.9 jit_solution(8026161040998220064)
XLA Ops:
  0.0 0.0 copy-start.5
  0.0 0.0 copy-start.6
  0.0 0.1 pad_add_fusion.meta
  0.1 0.0 copy-start
  0.1 1.2 %copy-done = bf16[2,8,128,256]{3,2,1,0:T(8,128)(2,1)S(1)} copy-done((bf16[2,8,128,256]{3,2,1,0:T(8,128)(2,1)S(1)}, bf16[2,8,128,256]{3,2,1,0:T(8,128)(2,1)}, u32[]{:S(2)}) %copy-start) | copy-done | bytes 1048600
  1.3 0.0 copy-start.3
  1.3 1.0 %copy-done.3 = bf16[2,8,128,128]{3,2,1,0:T(8,128)(2,1)S(1)} copy-done((bf16[2,8,128,128]{3,2,1,0:T(8,128)(2,1)S(1)}, bf16[2,8,128,128]{3,2,1,0:T(8,128)(2,1)}, u32[]{:S(2)}) %copy-start.3) | copy-done | bytes 524312
  2.4 0.8 %first_level.1 = (bf16[8,128,256]{2,1,0:T(8,128)(2,1)S(1)}, bf16[2,128,256]{2,1,0:T(8,128)(2,1)S(1)}, bf16[2,128,256]{2,1,0:T(8,128)(2,1)S(1)}) custom-call(s32[2]{0:T(128)S(1)} %pad_add_fusion.meta, bf16[2,8,128,128]{3,2,1,0:T(8,128)(2,1)S(1)} %copy-done.3, bf16[2,8,128,256]{3,2,1,0:T(8,128)(2,1)S(1)} %copy-done), custom_call_target="tpu_custom_call" | custom-call | tf_op jit(solution)/shard_map/first_level/pallas_call | solution.py:231
  3.2 0.3 collective-permute-start
  3.5 1.8 %collective-permute-start.1 = (bf16[2,128,256]{2,1,0:T(8,128)(2,1)S(1)}, bf16[2,128,256]{2,1,0:T(8,128)(2,1)S(1)}, u32[]{:S(2)}, u32[]{:S(2)}) collective-permute-start(bf16[2,128,256]{2,1,0:T(8,128)(2,1)S(1)} %get-tuple-element.28), channel_id=1, source_target_pairs={{0,8},{8,0},{16,24},{24,16},{1,2},{9,17},{17,25},{25,9},{2,1},{10,... | collective-permute-start | bytes 393224 | tf_op jit(solution)/shard_map/ppermute | solution.py:249
  5.3 0.0 copy-done.5
  5.3 0.1 copy.10.scale
  5.4 0.0 copy-done.6
  5.4 0.1 copy.9
  5.5 0.1 add_clamp_fusion.depend
  5.5 0.0 copy-done.1
  5.5 0.0 copy-done.4
  5.6 1.9 %copy-done.2 = bf16[2,8,6,128,128]{4,3,2,1,0:T(8,128)(2,1)S(1)} copy-done((bf16[2,8,6,128,128]{4,3,2,1,0:T(8,128)(2,1)S(1)}, bf16[2,8,6,128,128]{4,3,2,1,0:T(8,128)(2,1)}, u32[]{:S(2)}) %copy-start.2) | copy-done | bytes 3145752
  7.4 3.9 %prepare.1 = (bf16[4,256,768]{2,1,0:T(8,128)(2,1)S(1)}, bf16[4,256,768]{2,1,0:T(8,128)(2,1)S(1)}, f32[8,128,256]{2,1,0:T(8,128)S(1)}, bf16[2,128,896]{2,1,0:T(8,128)(2,1)S(1)}, bf16[2,128,896]{2,1,0:T(8,128)(2,1)S(1)}) custom-call(s32[2]{0:T(128)S(1)} %pad_add_fusion.meta, s32[2,8,6]{2,1,0:T(8,128)S(1)} %add_clamp_fusion.depend, f32[2,8,6]{2,1,0:T(8,128)S(1)} %copy.10.scale, ...), custom_call_target="tpu_custom_call" | custom-call | tf_op jit(solution)/shard_map/prepare/pallas_call | solution.py:252
  11.3 0.0 collective-permute-done.even_in
  11.4 0.0 collective-permute-done.1.odd_in
  11.4 0.6 step_0.1
  11.9 0.1 collective-permute-start.2
  12.0 3.1 %collective-permute-start.5 = (bf16[2,128,896]{2,1,0:T(8,128)(2,1)S(1)}, bf16[2,128,896]{2,1,0:T(8,128)(2,1)S(1)}, u32[]{:S(2)}, u32[]{:S(2)}) collective-permute-start(bf16[2,128,896]{2,1,0:T(8,128)(2,1)S(1)} %get-tuple-element.34), channel_id=1, source_target_pairs={{8,9},{9,8},{10,11},{11,10},{12,13},{13,12},{14,15},{15,14},{16,17... | collective-permute-start | bytes 1376264 | tf_op jit(solution)/shard_map/ppermute | solution.py:285
  15.2 1.9 %collective-permute-start.6 = (bf16[2,128,896]{2,1,0:T(8,128)(2,1)S(1)}, bf16[2,128,896]{2,1,0:T(8,128)(2,1)S(1)}, u32[]{:S(2)}, u32[]{:S(2)}) collective-permute-start(bf16[2,128,896]{2,1,0:T(8,128)(2,1)S(1)} %get-tuple-element.35), channel_id=1, source_target_pairs={{9,10},{10,9},{11,12},{12,11},{13,14},{14,13},{17,18},{18,17},{19,... | collective-permute-start | bytes 1376264 | tf_op jit(solution)/shard_map/ppermute | solution.py:286
  17.1 0.8 %collective-permute-start.3 = (bf16[4,128,256]{2,1,0:T(8,128)(2,1)S(1)}, bf16[4,128,256]{2,1,0:T(8,128)(2,1)S(1)}, u32[]{:S(2)}, u32[]{:S(2)}) collective-permute-start(bf16[4,128,256]{2,1,0:T(8,128)(2,1)S(1)} %get-tuple-element.32), channel_id=1, source_target_pairs={{0,9},{1,8},{2,11},{3,10},{4,13},{5,12},{6,15},{7,14},{8,0},{9,1},... | collective-permute-start | bytes 786440 | tf_op jit(solution)/shard_map/ppermute | solution.py:316
  17.9 0.1 collective-permute-start.4
  18.0 17.4 %collective-permute-done.5.even_in = bf16[2,128,896]{2,1,0:T(8,128)(2,1)S(1)} collective-permute-done((bf16[2,128,896]{2,1,0:T(8,128)(2,1)S(1)}, bf16[2,128,896]{2,1,0:T(8,128)(2,1)S(1)}, u32[]{:S(2)}, u32[]{:S(2)}) %collective-permute-start.5) | collective-permute-done | bytes 458784 | tf_op jit(solution)/shard_map/ppermute | solution.py:285
  35.4 0.0 collective-permute-done.6.odd_in
  35.4 0.6 order.1.edges
  36.0 0.0 collective-permute-done.3.even_in
  36.0 0.0 collective-permute-done.4.odd_in
  36.0 0.0 collective-permute-done.2.centre
  36.0 0.6 step_1.1
  36.6 0.1 collective-permute-start.7
  36.7 1.3 %collective-permute-start.8 = (bf16[4,128,256]{2,1,0:T(8,128)(2,1)S(1)}, bf16[4,128,256]{2,1,0:T(8,128)(2,1)S(1)}, u32[]{:S(2)}, u32[]{:S(2)}) collective-permute-start(bf16[4,128,256]{2,1,0:T(8,128)(2,1)S(1)} %get-tuple-element.39), channel_id=1, source_target_pairs={{8,17},{9,16},{10,19},{11,18},{12,21},{13,20},{14,23},{15,22},{0,8... | collective-permute-start | bytes 786440 | tf_op jit(solution)/shard_map/ppermute | solution.py:316
  38.0 1.7 %collective-permute-start.9 = (bf16[4,128,256]{2,1,0:T(8,128)(2,1)S(1)}, bf16[4,128,256]{2,1,0:T(8,128)(2,1)S(1)}, u32[]{:S(2)}, u32[]{:S(2)}) collective-permute-start(bf16[4,128,256]{2,1,0:T(8,128)(2,1)S(1)} %get-tuple-element.40), channel_id=1, source_target_pairs={{8,16},{9,18},{10,17},{11,20},{12,19},{13,22},{14,21},{15,23},{0,8... | collective-permute-start | bytes 786440 | tf_op jit(solution)/shard_map/ppermute | solution.py:316
  39.7 5.9 %collective-permute-done.8.even_in = bf16[4,128,256]{2,1,0:T(8,128)(2,1)S(1)} collective-permute-done((bf16[4,128,256]{2,1,0:T(8,128)(2,1)S(1)}, bf16[4,128,256]{2,1,0:T(8,128)(2,1)S(1)}, u32[]{:S(2)}, u32[]{:S(2)}) %collective-permute-start.8) | collective-permute-done | bytes 262176 | tf_op jit(solution)/shard_map/ppermute | solution.py:316
  45.6 2.8 %collective-permute-done.9.odd_in = bf16[4,128,256]{2,1,0:T(8,128)(2,1)S(1)} collective-permute-done((bf16[4,128,256]{2,1,0:T(8,128)(2,1)S(1)}, bf16[4,128,256]{2,1,0:T(8,128)(2,1)S(1)}, u32[]{:S(2)}, u32[]{:S(2)}) %collective-permute-start.9) | collective-permute-done | bytes 262176 | tf_op jit(solution)/shard_map/ppermute | solution.py:316
  48.4 0.0 collective-permute-done.7.centre
  48.4 0.6 step_2.1
  49.0 6.9 %collective-permute-start.10 = (bf16[8,128,256]{2,1,0:T(8,128)(2,1)S(1)}, bf16[8,128,256]{2,1,0:T(8,128)(2,1)S(1)}, u32[]{:S(2)}, u32[]{:S(2)}) collective-permute-start(bf16[8,128,256]{2,1,0:T(8,128)(2,1)S(1)} %get-tuple-element.42), channel_id=1, source_target_pairs={{0,8},{1,9},{2,10},{3,11},{4,12},{5,13},{6,14},{7,15},{8,0},{9,1},... | collective-permute-start | bytes 1572872 | tf_op jit(solution)/shard_map/ppermute | solution.py:316
  55.9 0.1 collective-permute-start.11
  55.9 0.6 collective-permute-start.12
  56.5 8.0 %collective-permute-done.11.even_in = bf16[4,128,256]{2,1,0:T(8,128)(2,1)S(1)} collective-permute-done((bf16[4,128,256]{2,1,0:T(8,128)(2,1)S(1)}, bf16[4,128,256]{2,1,0:T(8,128)(2,1)S(1)}, u32[]{:S(2)}, u32[]{:S(2)}) %collective-permute-start.11) | collective-permute-done | bytes 262176 | tf_op jit(solution)/shard_map/ppermute | solution.py:316
  64.5 0.0 collective-permute-done.12.odd_in
  64.5 0.0 collective-permute-done.10.centre
  64.5 3.4 %step_3.1 = (bf16[2,8,128,256]{3,2,1,0:T(8,128)(2,1)}, bf16[8,128,256]{2,1,0:T(8,128)(2,1)}) custom-call(s32[2]{0:T(128)S(1)} %pad_add_fusion.meta, bf16[8,128,256]{2,1,0:T(8,128)(2,1)S(1)} %collective-permute-done.10.centre, bf16[4,128,256]{2,1,0:T(8,128)(2,1)S(1)} %collective-permute-done.11.even_in, ...), custom_call_target="tpu_custom_call", output_to_operand_aliasing={{0}: (9, {})} | custom-call | tf_op jit(solution)/shard_map/step_3/pallas_call | solution.py:321
  (4 shorter events, 0.0 us)
Async XLA Ops:
  0.0 5.3 %copy-start.5 = (f32[2,8,6]{1,0,2:T(2,128)S(1)}, f32[2,8,6]{1,0,2:T(2,128)}, u32[]{:S(2)}) copy-start(f32[2,8,6]{1,0,2:T(2,128)} %param.7) | copy-start | bytes 1156
  0.0 5.4 %copy-start.6 = (s32[2,8,6]{1,0,2:T(2,128)S(1)}, s32[2,8,6]{1,0,2:T(2,128)}, u32[]{:S(2)}) copy-start(s32[2,8,6]{1,0,2:T(2,128)} %param.9) | copy-start | bytes 1156
  0.1 1.2 %copy-start = (bf16[2,8,128,256]{3,2,1,0:T(8,128)(2,1)S(1)}, bf16[2,8,128,256]{3,2,1,0:T(8,128)(2,1)}, u32[]{:S(2)}) copy-start(bf16[2,8,128,256]{3,2,1,0:T(8,128)(2,1)} %right.3) | copy-start | bytes 3145732
  1.3 1.0 %copy-start.3 = (bf16[2,8,128,128]{3,2,1,0:T(8,128)(2,1)S(1)}, bf16[2,8,128,128]{3,2,1,0:T(8,128)(2,1)}, u32[]{:S(2)}) copy-start(bf16[2,8,128,128]{3,2,1,0:T(8,128)(2,1)} %inverse.3) | copy-start | bytes 1572868
  2.3 3.2 %copy-start.1 = (bf16[2,8,128,256]{3,2,1,0:T(8,128)(2,1)S(1)}, bf16[2,8,128,256]{3,2,1,0:T(8,128)(2,1)}, u32[]{:S(2)}) copy-start(bf16[2,8,128,256]{3,2,1,0:T(8,128)(2,1)} %right.3) | copy-start | bytes 3145732
  2.3 3.2 %copy-start.4 = (bf16[2,8,128,128]{3,2,1,0:T(8,128)(2,1)S(1)}, bf16[2,8,128,128]{3,2,1,0:T(8,128)(2,1)}, u32[]{:S(2)}) copy-start(bf16[2,8,128,128]{3,2,1,0:T(8,128)(2,1)} %inverse.3) | copy-start | bytes 1572868
  3.2 8.2 %collective-permute-start = (bf16[2,128,256]{2,1,0:T(8,128)(2,1)S(1)}, bf16[2,128,256]{2,1,0:T(8,128)(2,1)S(1)}, u32[]{:S(2)}, u32[]{:S(2)}) collective-permute-start(bf16[2,128,256]{2,1,0:T(8,128)(2,1)S(1)} %get-tuple-element.27), channel_id=1, source_target_pairs={{0,1},{8,16},{16,24},{24,8},{1,0},{9,17},{17,25},{25,9},{2,3},{10,... | collective-permute-start | bytes 393224 | tf_op jit(solution)/shard_map/ppermute | solution.py:248
  3.5 7.9 %collective-permute-start.1 = (bf16[2,128,256]{2,1,0:T(8,128)(2,1)S(1)}, bf16[2,128,256]{2,1,0:T(8,128)(2,1)S(1)}, u32[]{:S(2)}, u32[]{:S(2)}) collective-permute-start(bf16[2,128,256]{2,1,0:T(8,128)(2,1)S(1)} %get-tuple-element.28), channel_id=1, source_target_pairs={{0,8},{8,0},{16,24},{24,16},{1,2},{9,17},{17,25},{25,9},{2,1},{10,... | collective-permute-start | bytes 393224 | tf_op jit(solution)/shard_map/ppermute | solution.py:249
  5.5 1.9 %copy-start.2 = (bf16[2,8,6,128,128]{4,3,2,1,0:T(8,128)(2,1)S(1)}, bf16[2,8,6,128,128]{4,3,2,1,0:T(8,128)(2,1)}, u32[]{:S(2)}) copy-start(bf16[2,8,6,128,128]{4,3,2,1,0:T(8,128)(2,1)} %lower.1) | copy-start | bytes 9437188
  11.9 24.1 %collective-permute-start.2 = (bf16[8,128,256]{2,1,0:T(8,128)(2,1)S(1)}, bf16[8,128,256]{2,1,0:T(8,128)(2,1)S(1)}, u32[]{:S(2)}, u32[]{:S(2)}) collective-permute-start(bf16[8,128,256]{2,1,0:T(8,128)(2,1)S(1)} %get-tuple-element.31), channel_id=1, source_target_pairs={{0,8},{1,9},{2,10},{3,11},{4,12},{5,13},{6,14},{7,15},{8,0},{9,1},... | collective-permute-start | bytes 1572872 | tf_op jit(solution)/shard_map/ppermute | solution.py:316
  12.0 23.3 %collective-permute-start.5 = (bf16[2,128,896]{2,1,0:T(8,128)(2,1)S(1)}, bf16[2,128,896]{2,1,0:T(8,128)(2,1)S(1)}, u32[]{:S(2)}, u32[]{:S(2)}) collective-permute-start(bf16[2,128,896]{2,1,0:T(8,128)(2,1)S(1)} %get-tuple-element.34), channel_id=1, source_target_pairs={{8,9},{9,8},{10,11},{11,10},{12,13},{13,12},{14,15},{15,14},{16,17... | collective-permute-start | bytes 1376264 | tf_op jit(solution)/shard_map/ppermute | solution.py:285
  15.2 20.2 %collective-permute-start.6 = (bf16[2,128,896]{2,1,0:T(8,128)(2,1)S(1)}, bf16[2,128,896]{2,1,0:T(8,128)(2,1)S(1)}, u32[]{:S(2)}, u32[]{:S(2)}) collective-permute-start(bf16[2,128,896]{2,1,0:T(8,128)(2,1)S(1)} %get-tuple-element.35), channel_id=1, source_target_pairs={{9,10},{10,9},{11,12},{12,11},{13,14},{14,13},{17,18},{18,17},{19,... | collective-permute-start | bytes 1376264 | tf_op jit(solution)/shard_map/ppermute | solution.py:286
  17.1 18.9 %collective-permute-start.3 = (bf16[4,128,256]{2,1,0:T(8,128)(2,1)S(1)}, bf16[4,128,256]{2,1,0:T(8,128)(2,1)S(1)}, u32[]{:S(2)}, u32[]{:S(2)}) collective-permute-start(bf16[4,128,256]{2,1,0:T(8,128)(2,1)S(1)} %get-tuple-element.32), channel_id=1, source_target_pairs={{0,9},{1,8},{2,11},{3,10},{4,13},{5,12},{6,15},{7,14},{8,0},{9,1},... | collective-permute-start | bytes 786440 | tf_op jit(solution)/shard_map/ppermute | solution.py:316
  17.9 18.1 %collective-permute-start.4 = (bf16[4,128,256]{2,1,0:T(8,128)(2,1)S(1)}, bf16[4,128,256]{2,1,0:T(8,128)(2,1)S(1)}, u32[]{:S(2)}, u32[]{:S(2)}) collective-permute-start(bf16[4,128,256]{2,1,0:T(8,128)(2,1)S(1)} %get-tuple-element.33), channel_id=1, source_target_pairs={{0,8},{1,10},{2,9},{3,12},{4,11},{5,14},{6,13},{7,15},{8,0},{9,1},... | collective-permute-start | bytes 786440 | tf_op jit(solution)/shard_map/ppermute | solution.py:316
  36.6 11.8 %collective-permute-start.7 = (bf16[8,128,256]{2,1,0:T(8,128)(2,1)S(1)}, bf16[8,128,256]{2,1,0:T(8,128)(2,1)S(1)}, u32[]{:S(2)}, u32[]{:S(2)}) collective-permute-start(bf16[8,128,256]{2,1,0:T(8,128)(2,1)S(1)} %get-tuple-element.38), channel_id=1, source_target_pairs={{8,16},{9,17},{10,18},{11,19},{12,20},{13,21},{14,22},{15,23},{0,8... | collective-permute-start | bytes 1572872 | tf_op jit(solution)/shard_map/ppermute | solution.py:316
  36.7 8.9 %collective-permute-start.8 = (bf16[4,128,256]{2,1,0:T(8,128)(2,1)S(1)}, bf16[4,128,256]{2,1,0:T(8,128)(2,1)S(1)}, u32[]{:S(2)}, u32[]{:S(2)}) collective-permute-start(bf16[4,128,256]{2,1,0:T(8,128)(2,1)S(1)} %get-tuple-element.39), channel_id=1, source_target_pairs={{8,17},{9,16},{10,19},{11,18},{12,21},{13,20},{14,23},{15,22},{0,8... | collective-permute-start | bytes 786440 | tf_op jit(solution)/shard_map/ppermute | solution.py:316
  38.0 10.4 %collective-permute-start.9 = (bf16[4,128,256]{2,1,0:T(8,128)(2,1)S(1)}, bf16[4,128,256]{2,1,0:T(8,128)(2,1)S(1)}, u32[]{:S(2)}, u32[]{:S(2)}) collective-permute-start(bf16[4,128,256]{2,1,0:T(8,128)(2,1)S(1)} %get-tuple-element.40), channel_id=1, source_target_pairs={{8,16},{9,18},{10,17},{11,20},{12,19},{13,22},{14,21},{15,23},{0,8... | collective-permute-start | bytes 786440 | tf_op jit(solution)/shard_map/ppermute | solution.py:316
  49.0 15.5 %collective-permute-start.10 = (bf16[8,128,256]{2,1,0:T(8,128)(2,1)S(1)}, bf16[8,128,256]{2,1,0:T(8,128)(2,1)S(1)}, u32[]{:S(2)}, u32[]{:S(2)}) collective-permute-start(bf16[8,128,256]{2,1,0:T(8,128)(2,1)S(1)} %get-tuple-element.42), channel_id=1, source_target_pairs={{0,8},{1,9},{2,10},{3,11},{4,12},{5,13},{6,14},{7,15},{8,0},{9,1},... | collective-permute-start | bytes 1572872 | tf_op jit(solution)/shard_map/ppermute | solution.py:316
  55.9 8.6 %collective-permute-start.11 = (bf16[4,128,256]{2,1,0:T(8,128)(2,1)S(1)}, bf16[4,128,256]{2,1,0:T(8,128)(2,1)S(1)}, u32[]{:S(2)}, u32[]{:S(2)}) collective-permute-start(bf16[4,128,256]{2,1,0:T(8,128)(2,1)S(1)} %get-tuple-element.43), channel_id=1, source_target_pairs={{0,8},{1,9},{2,10},{3,11},{4,12},{5,13},{6,14},{7,15},{8,0},{9,1},... | collective-permute-start | bytes 786440 | tf_op jit(solution)/shard_map/ppermute | solution.py:316
  55.9 8.5 %collective-permute-start.12 = (bf16[4,128,256]{2,1,0:T(8,128)(2,1)S(1)}, bf16[4,128,256]{2,1,0:T(8,128)(2,1)S(1)}, u32[]{:S(2)}, u32[]{:S(2)}) collective-permute-start(bf16[4,128,256]{2,1,0:T(8,128)(2,1)S(1)} %get-tuple-element.44), channel_id=1, source_target_pairs={{0,8},{1,9},{2,10},{3,11},{4,12},{5,13},{6,14},{7,15},{8,0},{9,1},... | collective-permute-start | bytes 786440 | tf_op jit(solution)/shard_map/ppermute | solution.py:316

commit v2 on v0

v2 whole, which is shorter than its diff:
```python
import functools

import jax
import jax.numpy as jnp
from jax import lax
from jax.experimental import pallas as pl
from jax.experimental.pallas import tpu as pltpu
from jax.sharding import PartitionSpec as P

REACH = 2
SPAN = 2 * REACH + 1
CHUNKS = 2
EDGE = SPAN + CHUNKS
AXES = ("chain", "rows")
VMEM = pl.BlockSpec(memory_space=pltpu.VMEM)
SMEM = pl.BlockSpec(memory_space=pltpu.SMEM)
ANY = pl.BlockSpec(memory_space=pl.ANY)
HBM = pl.BlockSpec(memory_space=pltpu.HBM)


def even_mate(row, rows):
    return row ^ 1


def odd_mate(row, rows):
    mate = row + 1 if row % 2 else row - 1
    return mate if 0 <= mate < rows else row


def same_row(row, rows):
    return row


def swap_groups(chain, taken=()):
    return {g: g ^ 1 for g in range(chain) if g not in taken}


def hop_pairs(group, mate, chain, rows, within):
    if group % 2 == 0:
        moves = swap_groups(chain)
    else:
        moves = swap_groups(chain, range(group - 1, group + 3))
        moves.update({group: group + 1, group - 1: group, group + 1: group + 2, group + 2: group - 1})
    stay = ()
    if within and group < 2:
        stay = range(2, chain) if group == 0 else range(3, chain)
        moves = {0: 1, 1: 0} if group == 0 else {0: 1, 1: 2, 2: 0}
    pairs = []
    for r in range(rows):
        target = mate(r, rows)
        own = dict(moves)
        if stay and target == r:
            own = {0: 1, 1: 0, **swap_groups(chain, (0, 1))} if group == 0 else {0: 1, 1: 2, 2: 3, 3: 0, **swap_groups(chain, range(4))}
        else:
            own.update({g: g for g in stay})
        pairs += [
            (source * rows + r, dest * rows + (target if source == group or source in stay and target != r else r))
            for source, dest in own.items()
        ]
    return pairs


def first_pairs(mate, chain, rows):
    pairs = []
    for r in range(rows):
        target = mate(r, rows)
        if target == r:
            moves = swap_groups(chain)
        else:
            pairs.append((r, target))
            moves = swap_groups(chain, range(4))
            moves.update({1: 2, 2: 3, 3: 1})
        pairs += [(a * rows + r, b * rows + r) for a, b in moves.items()]
    return pairs


def inner_pairs(mate, chain, rows):
    pairs = []
    for r in range(rows):
        target = mate(r, rows)
        if target == r:
            moves = swap_groups(chain)
        else:
            pairs += [(g * rows + r, g * rows + target) for g in (1, 2)]
            moves = swap_groups(chain, range(4))
            moves.update({0: 3, 3: 0})
        pairs += [(a * rows + r, b * rows + r) for a, b in moves.items()]
    return pairs


def dot(a, b):
    return jnp.dot(a, b, preferred_element_type=jnp.float32)


def by_parity(odd, low_value, high_value, even_ref, odd_ref):
    @pl.when(odd == 0)
    def _():
        even_ref[...] = high_value()
        odd_ref[...] = low_value()

    @pl.when(odd == 1)
    def _():
        even_ref[...] = low_value()
        odd_ref[...] = high_value()


def first_kernel(meta, inverse_hbm, right_hbm, solved, *rest):
    *sends, inverse, right, sems = rest
    count = inverse.shape[0]
    parts = 2
    size = count // parts
    loads = []
    for part in range(parts):
        rows = pl.ds(part * size, size)
        loads.append(
            (
                pltpu.make_async_copy(inverse_hbm.at[0, rows], inverse.at[rows], sems.at[0, part]),
                pltpu.make_async_copy(right_hbm.at[0, rows], right.at[rows], sems.at[1, part]),
            )
        )
    for pair in loads:
        for load in pair:
            load.start()
    for part in range(parts):
        for load in loads[part]:
            load.wait()
        for q in range(part * size, (part + 1) * size):
            solved[q] = dot(inverse[q], right[q]).astype(solved.dtype)
    by_parity(meta[1], lambda: solved[:REACH], lambda: solved[count - REACH :], *sends)


def premultiply(depend, scale, lower, inverse, wide, acc, level, q, half, keep=None):
    block = lower.shape[-1]
    terms = lower.shape[2]
    acc[...] = jnp.zeros_like(acc)
    beside = jnp.concatenate([lower[0, half, k] for k in range(terms)], axis=1)
    products = dot(inverse[0, half], beside)
    for k in range(terms):
        acc[depend[level, q, k]] += scale[level, q, k] * products[:, k * block : (k + 1) * block]
    at = slice(half * block, (half + 1) * block)
    for d in range(SPAN):
        value = (-acc[d]).astype(wide.dtype)
        wide[0, at, (d + half) * block : (d + half + 1) * block] = value
        if keep is not None:
            keep[half, d] = value
    other = 0 if half else SPAN
    wide[0, at, other * block : (other + 1) * block] = jnp.zeros((block, block), wide.dtype)


def prepare_a_kernel(meta, depend, scale, lower, inverse, first, wide, even_out, odd_out, acc, keep):
    step = pl.program_id(0)
    last = pl.num_programs(0) - 1
    block = lower.shape[-1]
    for half in range(2):
        premultiply(depend, scale, lower, inverse, wide, acc, 0, 2 * step + half, half, keep)

    def emit(ref):
        for half in range(2):
            for d in range(SPAN):
                ref[half * EDGE + d] = keep[half, d]
            for chunk in range(CHUNKS):
                ref[half * EDGE + SPAN + chunk] = first[half, :, chunk * block : (chunk + 1) * block]

    odd = meta[1]
    at_low, at_high = step == 0, step == last

    @pl.when((at_low & (odd == 1)) | (at_high & (odd == 0)))
    def _():
        emit(even_out)

    @pl.when((at_low & (odd == 0)) | (at_high & (odd == 1)))
    def _():
        emit(odd_out)


def prepare_b_kernel(depend, scale, lower, inverse, right, wide, base, acc):
    step = pl.program_id(0)
    for half in range(2):
        premultiply(depend, scale, lower, inverse, wide, acc, 1, 2 * step + half, half)
        base[half] = dot(inverse[0, half], right[0, half])


def order_kernel(applies, meta, *refs):
    *pieces, edges = refs

    @pl.when(applies(meta[0]))
    def _():
        odd = meta[1]
        size = pieces[0].shape[0]
        for i in range(len(pieces) // 2):
            edges[1 - odd, i * size : (i + 1) * size] = pieces[2 * i][...]
            edges[odd, i * size : (i + 1) * size] = pieces[2 * i + 1][...]


def flat(ref, start, count, at=slice(None)):
    block = ref[start : start + count, :, at]
    return block.reshape(count * block.shape[1], block.shape[2])


def place(window, odd, even_in, odd_in, at=slice(None)):
    halo = even_in.shape[0]
    low, high = 0, window.shape[0] - halo
    window[pl.ds(jnp.where(odd == 1, low, high), halo)] = even_in[:, :, at]
    window[pl.ds(jnp.where(odd == 1, high, low), halo)] = odd_in[:, :, at]


def second_level(wide_b, base_b, level_a, solved, at):
    for p in range(wide_b.shape[0]):
        rows = dot(wide_b[p], flat(level_a, 2 * p, SPAN + 1)) + flat(base_b, 2 * p, 2, at)
        solved[2 * p : 2 * p + 2] = rows.astype(solved.dtype).reshape(2, *solved.shape[1:])


def emit_sends(odd, solved, sends):
    half = solved.shape[0] // 2
    if sends:
        by_parity(odd, lambda: solved[:half], lambda: solved[half:], *sends)


def store(first_level, second, out, at, sems):
    copies = [
        pltpu.make_async_copy(source, out.at[level, :, :, at], sems.at[level])
        for level, source in ((0, first_level), (1, second))
    ]
    for copy in copies:
        copy.start()
    for copy in copies:
        copy.wait()


def ride(turn, meta, even_w, odd_w, sends):
    size = sends[0].shape[0]

    @pl.when(meta[0] > 2)
    def _():
        for send, source in zip(sends, (even_w, odd_w)):
            send[...] = source[turn * size : (turn + 1) * size]


def first_step(chunk, meta, first, even_in, odd_in, wide_b, base_b, even_w, odd_w, *rest):
    solved, even_out, odd_out, level_a = rest[-4:]

    @pl.when(meta[0] == 0)
    def _():
        cases = solved.shape[-1]
        at = slice(chunk * cases, (chunk + 1) * cases)
        count = first.shape[0]
        level_a[REACH : REACH + count] = first[:, :, at]
        place(level_a, meta[1], even_in, odd_in, at)
        second_level(wide_b, base_b, level_a, solved, at)
        emit_sends(meta[1], solved, (even_out, odd_out))

    ride(chunk, meta, even_w, odd_w, (even_out, odd_out))


def later_step(group, chunk, final, aliased, meta, centre, even_in, odd_in, edges, first, wide_a, wide_b, base_b, old_a, old_b, even_w, odd_w, *rest):
    rest = rest[1:] if aliased else rest
    out, solved, solved_a, *sends, window, level_a, sems = rest
    cases = solved.shape[-1]
    at = slice(chunk * cases, (chunk + 1) * cases)
    on_out = pl.ds(chunk * cases, cases)
    count = first.shape[0]

    @pl.when(meta[0] == group)
    def _():
        odd = meta[1]
        halo = 2 * REACH
        window[halo : halo + count] = centre[...]
        place(window, odd, even_in, odd_in)
        for p in range(wide_a.shape[0]):
            rows = dot(wide_a[p], flat(window, REACH + 2 * p, SPAN + 1)) + flat(first, 2 * p, 2, at).astype(jnp.float32)
            level_a[REACH + 2 * p : REACH + 2 * p + 2] = rows.astype(level_a.dtype).reshape(2, *level_a.shape[1:])
        for side in range(2):
            for i in range(REACH):
                put = side * (count + REACH) + i
                base = edges[side, i * EDGE + SPAN + chunk]
                blocks = jnp.concatenate([edges[side, i * EDGE + d] for d in range(SPAN)], axis=1)
                row = dot(blocks, flat(window, put, SPAN)) + base.astype(jnp.float32)
                level_a[put] = row.astype(level_a.dtype)
        second_level(wide_b, base_b, level_a, solved, at)
        emit_sends(odd, solved, sends)
        if final:
            store(level_a.at[pl.ds(REACH, count)], solved, out, on_out, sems)
        else:
            solved_a[...] = level_a[REACH : REACH + count]

    @pl.when(meta[0] == group - 1)
    def _():
        if group == 1:
            store(old_a.at[:, :, on_out], old_b, out, on_out, sems)
        else:
            store(old_a, old_b, out, on_out, sems)

    if group == 1 and not final:
        ride(CHUNKS + chunk, meta, even_w, odd_w, sends)


def shaped(shape, dtype=jnp.bfloat16):
    return jax.ShapeDtypeStruct(shape, dtype)


def params(**more):
    return pltpu.CompilerParams(vmem_limit_bytes=24 * 1024 * 1024, **more)


def in_hbm(value):
    return pltpu.with_memory_space_constraint(value, pltpu.HBM)


def after(values, *earlier):
    return lax.optimization_barrier((values, earlier))[0]


def per_device(chain, rows, right_side, lower_blocks, block_scale, diag_inverse, depend_rows):
    _, count, block, cases = right_side.shape
    terms = lower_blocks.shape[2]
    width = SPAN * block
    part = cases // CHUNKS
    row = lax.axis_index("rows")
    meta = jnp.stack([lax.axis_index("chain"), row % 2]).astype(jnp.int32)
    offset = depend_rows - (row * count + jnp.arange(count, dtype=jnp.int32))[None, :, None] + REACH
    offset = jnp.clip(offset, 0, SPAN - 1)
    right_side, lower_blocks, diag_inverse = in_hbm(right_side), in_hbm(lower_blocks), in_hbm(diag_inverse)
    mates = (even_mate, odd_mate)

    first, *sides = pl.pallas_call(
        first_kernel,
        in_specs=[SMEM, HBM, HBM],
        out_specs=[VMEM] * 3,
        out_shape=[shaped((count, block, cases))] + [shaped((REACH, block, cases))] * 2,
        scratch_shapes=[
            pltpu.VMEM((count, block, block), jnp.bfloat16),
            pltpu.VMEM((count, block, cases), jnp.bfloat16),
            pltpu.SemaphoreType.DMA((2, 2)),
        ],
        compiler_params=params(),
        name="first_level",
    )(meta, diag_inverse, right_side)
    sides = [lax.ppermute(side, AXES, first_pairs(mate, chain, rows)) for side, mate in zip(sides, mates)]

    pairs = count // 2
    wide_shape = shaped((pairs, 2 * block, width + block))
    wide_spec = pl.BlockSpec((1, 2 * block, width + block), lambda i: (i, 0, 0))
    halo = 2 * REACH
    pieces = 2 * CHUNKS * halo
    edge_shape = shaped((pieces, block, block))
    edge_spec = pl.BlockSpec((pieces, block, block), lambda i: (0, 0, 0))

    def of_level(level):
        return [
            pl.BlockSpec((1, 2, terms, block, block), lambda i: (level, i, 0, 0, 0)),
            pl.BlockSpec((1, 2, block, block), lambda i: (level, i, 0, 0)),
        ]

    def ordered(applies, moved):
        return pl.pallas_call(
            functools.partial(order_kernel, applies),
            in_specs=[SMEM] + [VMEM] * len(moved),
            out_specs=VMEM,
            out_shape=shaped((2, *edge_shape.shape)),
            compiler_params=params(),
            name="order",
        )(meta, *moved)

    acc = pltpu.VMEM((SPAN, block, block), jnp.float32)
    wide_a, *edge_w = pl.pallas_call(
        prepare_a_kernel,
        grid=(pairs,),
        in_specs=[SMEM, SMEM, SMEM, *of_level(0), pl.BlockSpec((2, block, cases), lambda i: (i, 0, 0))],
        out_specs=[wide_spec, edge_spec, edge_spec],
        out_shape=[wide_shape, edge_shape, edge_shape],
        scratch_shapes=[acc, pltpu.VMEM((2, SPAN, block, block), jnp.bfloat16)],
        compiler_params=params(),
        name="prepare_a",
    )(meta, offset, block_scale, lower_blocks, diag_inverse, first)
    moved_w = [lax.ppermute(value, AXES, inner_pairs(mate, chain, rows)) for value, mate in zip(edge_w, mates)]
    wide_b, base_b = pl.pallas_call(
        prepare_b_kernel,
        grid=(pairs,),
        in_specs=[SMEM, SMEM, *of_level(1), pl.BlockSpec((1, 2, block, cases), lambda i: (1, i, 0, 0))],
        out_specs=[wide_spec, pl.BlockSpec((2, block, cases), lambda i: (i, 0, 0))],
        out_shape=[wide_shape, shaped((count, block, cases), jnp.float32)],
        scratch_shapes=[acc],
        compiler_params=params(),
        name="prepare_b",
    )(offset, block_scale, lower_blocks, diag_inverse, right_side)

    level_a = pltpu.VMEM((count + 2 * REACH, block, part), jnp.bfloat16)
    solved_shape = shaped((count, block, part))
    send_shape = shaped((halo, block, part))

    sent, made_a = [], [first] * CHUNKS
    for chunk in range(CHUNKS):
        sent.append(
            pl.pallas_call(
                functools.partial(first_step, chunk),
                in_specs=[SMEM] + [VMEM] * 7 + [ANY] * chunk,
                out_specs=[VMEM] * 3,
                out_shape=[solved_shape, send_shape, send_shape],
                scratch_shapes=[level_a],
                compiler_params=params(),
                name=f"step_0_{chunk}",
            )(meta, first, *sides, wide_b, base_b, *edge_w, *(values[0] for values in sent))
        )
    edges = ordered(lambda group: (group == 1) | (group == 2), moved_w)

    def travel(group, chunk, before_sides, before_centre):
        solved, *halves = sent[chunk]
        halves = after(halves, before_sides)
        side = [
            lax.ppermute(value, AXES, hop_pairs(group, mate, chain, rows, True))
            for value, mate in zip(halves, mates)
        ]
        centre = lax.ppermute(
            after(solved, before_centre), AXES, hop_pairs(group, same_row, chain, rows, False)
        )
        return [centre, *side]

    out = None
    flying = None
    ridden = []
    for group in range(1, chain):
        final = group == chain - 1
        arrived = [travel(group - 1, 0, [], [])]
        wait = moved_w if group == 1 else []
        arrived.append(travel(group - 1, 1, wait, wait))
        flying = arrived[1][0]
        if group < 3:
            ridden += [side for chunk in range(CHUNKS) for side in arrived[chunk][1:]]
        if group == 3:
            edges = ordered(lambda group: group > 2, after(ridden, sent))
        made = []
        for chunk in range(CHUNKS):
            outs = [solved_shape, solved_shape] + ([] if final else [send_shape] * 2)
            aliased = out is not None
            out, solved, level, *sends = pl.pallas_call(
                functools.partial(later_step, group, chunk, final, aliased),
                in_specs=[SMEM] + [VMEM] * 12 + [ANY] * aliased,
                out_specs=[ANY] + [VMEM] * len(outs),
                out_shape=[shaped(right_side.shape), *outs],
                scratch_shapes=[
                    pltpu.VMEM((count + 2 * halo, block, part), jnp.bfloat16),
                    level_a,
                    pltpu.SemaphoreType.DMA((2,)),
                ],
                input_output_aliases={13: 0} if aliased else {},
                compiler_params=params(),
                name=f"step_{group}_{chunk}",
            )(
                meta,
                *arrived[chunk],
                edges,
                first,
                wide_a,
                wide_b,
                base_b,
                made_a[chunk],
                sent[chunk][0],
                *edge_w,
                *([out] if aliased else []),
            )
            made.append(((solved, *sends), level))
        sent, made_a = [values[0] for values in made], [values[1] for values in made]
    return out


def solution(mesh):
    placed = (
        P("chain", "rows", None, None),
        P("chain", "rows", None, None, None),
        P("chain", "rows", None),
        P("chain", "rows", None, None),
        P("chain", "rows", None),
    )
    return jax.shard_map(
        functools.partial(per_device, mesh.shape["chain"], mesh.shape["rows"]),
        mesh=mesh,
        in_specs=placed,
        out_specs=P("chain", "rows", None, None),
        check_vma=False,
    )
```

time: 184 us -> 69.3 us (0.38)
  the two profiles are of different devices: /device:TPU:26 before, /device:TPU:19 now
where the time goes in v2:
time: 69.3 us; the launch traced here: 69 us
  starting transfers between devices  26.4 us (38%)
  waiting for transfers between devices  20.7 us (30%)
  Pallas kernels  20 us (29%)
  local copies, waits for them, and re-layouts  1.54 us (2%)
    ppermute x12, waiting for transfers between devices, travel(): lax.ppermute(value, AXES, hop_pairs(group, mate, chain, rows, True))  12.6 us
    ppermute x12, starting transfers between devices, travel(): lax.ppermute(value, AXES, hop_pairs(group, mate, chain, rows, True))  12 us
    ppermute x6, starting transfers between devices, travel(): lax.ppermute(after(solved, before_centre), AXES, hop_pairs(group, same_ro...  10.5 us
    pallas_call x6, Pallas kernels, per_device(): pl.pallas_call(functools.partial(later_step, group, chunk, final, aliased...  8.98 us
    ppermute x2, waiting for transfers between devices, per_device(): lax.ppermute(side, AXES, first_pairs(mate, chain, rows))  8.1 us
    pallas_call x1, Pallas kernels, per_device(): pl.pallas_call(prepare_a_kernel, grid=(pairs,), in_specs=[SMEM, SMEM, SME...  3.34 us
    pallas_call x1, Pallas kernels, per_device(): pl.pallas_call(prepare_b_kernel, grid=(pairs,), in_specs=[SMEM, SMEM, *of...  3.33 us
    ppermute x2, starting transfers between devices, per_device(): lax.ppermute(side, AXES, first_pairs(mate, chain, rows))  2.2 us
  transfers between devices with their start and end apart: 22, of which 8 were waited for; matrix products, arithmetic and copies ran while one was open for 0% of the time, Pallas kernels for 16%

profile of v2, /device:TPU:19, one launch (start us, length us, event | category | flops | bytes accessed | tf_op | source)
XLA Modules:
  0.0 69.0 jit_solution(16949007364167344351)
XLA Ops:
  0.0 0.8 %copy.12.scale = f32[2,8,6]{2,1,0:T(8,128)S(1)} copy(f32[2,8,6]{1,0,2:T(2,128)} %param.7) | data formatting | bytes 768 | tf_op args[2]
  0.8 0.8 %copy.11 = s32[2,8,6]{2,1,0:T(8,128)S(1)} copy(s32[2,8,6]{1,0,2:T(2,128)} %param.9) | data formatting | bytes 768 | tf_op args[4]
  1.5 0.1 pad_add_fusion.meta
  1.6 0.1 add_clamp_fusion.depend
  1.7 2.0 %first_level.1 = (bf16[8,128,256]{2,1,0:T(8,128)(2,1)S(1)}, bf16[2,128,256]{2,1,0:T(8,128)(2,1)S(1)}, bf16[2,128,256]{2,1,0:T(8,128)(2,1)S(1)}) custom-call(s32[2]{0:T(128)S(1)} %pad_add_fusion.meta, bf16[2,8,128,128]{3,2,1,0:T(8,128)(2,1)} %inverse.3, bf16[2,8,128,256]{3,2,1,0:T(8,128)(2,1)} %right.1), custom_call_target="tpu_custom_call" | custom-call | tf_op jit(solution)/shard_map/first_level/pallas_call | solution.py:325
  3.7 3.3 %prepare_a.1 = (bf16[4,256,768]{2,1,0:T(8,128)(2,1)S(1)}, bf16[16,128,128]{2,1,0:T(8,128)(2,1)S(1)}, bf16[16,128,128]{2,1,0:T(8,128)(2,1)S(1)}) custom-call(s32[2]{0:T(128)S(1)} %pad_add_fusion.meta, s32[2,8,6]{2,1,0:T(8,128)S(1)} %add_clamp_fusion.depend, f32[2,8,6]{2,1,0:T(8,128)S(1)} %copy.12.scale, bf16[2,8,6,128,128]{4,3,2,1,0:T(8,128)(2,1)} %lower.3, ...), custom_call_target="tpu_custom_call" | custom-call | tf_op jit(solution)/shard_map/prepare_a/pallas_call | solution.py:365
  7.1 0.9 %collective-permute-start.2 = (bf16[16,128,128]{2,1,0:T(8,128)(2,1)S(1)}, bf16[16,128,128]{2,1,0:T(8,128)(2,1)S(1)}, u32[]{:S(2)}, u32[]{:S(2)}) collective-permute-start(bf16[16,128,128]{2,1,0:T(8,128)(2,1)S(1)} %get-tuple-element.67.even_w), channel_id=1, source_target_pairs={{8,9},{16,17},{0,24},{24,0},{9,8},{17,16},{1,25},{25,1},{10,11},{1... | collective-permute-start | bytes 1572872 | tf_op jit(solution)/shard_map/ppermute | solution.py:375
  8.0 0.9 %collective-permute-start.3 = (bf16[16,128,128]{2,1,0:T(8,128)(2,1)S(1)}, bf16[16,128,128]{2,1,0:T(8,128)(2,1)S(1)}, u32[]{:S(2)}, u32[]{:S(2)}) collective-permute-start(bf16[16,128,128]{2,1,0:T(8,128)(2,1)S(1)} %get-tuple-element.68.odd_w), channel_id=1, source_target_pairs={{0,8},{8,0},{16,24},{24,16},{9,10},{17,18},{1,25},{25,1},{10,9},{1... | collective-permute-start | bytes 1572872 | tf_op jit(solution)/shard_map/ppermute | solution.py:375
  8.9 2.2 %collective-permute-start.1 = (bf16[2,128,256]{2,1,0:T(8,128)(2,1)S(1)}, bf16[2,128,256]{2,1,0:T(8,128)(2,1)S(1)}, u32[]{:S(2)}, u32[]{:S(2)}) collective-permute-start(bf16[2,128,256]{2,1,0:T(8,128)(2,1)S(1)} %get-tuple-element.64), channel_id=1, source_target_pairs={{0,8},{8,0},{16,24},{24,16},{1,2},{9,17},{17,25},{25,9},{2,1},{10,... | collective-permute-start | bytes 393224 | tf_op jit(solution)/shard_map/ppermute | solution.py:338
  11.1 3.3 %prepare_b.1 = (bf16[4,256,768]{2,1,0:T(8,128)(2,1)S(1)}, f32[8,128,256]{2,1,0:T(8,128)S(1)}) custom-call(s32[2,8,6]{2,1,0:T(8,128)S(1)} %add_clamp_fusion.depend, f32[2,8,6]{2,1,0:T(8,128)S(1)} %copy.12.scale, bf16[2,8,6,128,128]{4,3,2,1,0:T(8,128)(2,1)} %lower.3, bf16[2,8,128,128]{3,2,1,0:T(8,128)(2,1)} %inverse.3, bf16[2,8,128,256]{3,2,1,0:T(8,128)(2,1)} %right.1), custom_call_target="tpu_custom_call" | custom-call | tf_op jit(solution)/shard_map/prepare_b/pallas_call | solution.py:376
  14.4 6.7 %collective-permute-done.even_in = bf16[2,128,256]{2,1,0:T(8,128)(2,1)S(1)} collective-permute-done((bf16[2,128,256]{2,1,0:T(8,128)(2,1)S(1)}, bf16[2,128,256]{2,1,0:T(8,128)(2,1)S(1)}, u32[]{:S(2)}, u32[]{:S(2)}) %collective-permute-start) | collective-permute-done | bytes 131104 | tf_op jit(solution)/shard_map/ppermute | solution.py:338
  21.1 1.4 %collective-permute-done.1.odd_in = bf16[2,128,256]{2,1,0:T(8,128)(2,1)S(1)} collective-permute-done((bf16[2,128,256]{2,1,0:T(8,128)(2,1)S(1)}, bf16[2,128,256]{2,1,0:T(8,128)(2,1)S(1)}, u32[]{:S(2)}, u32[]{:S(2)}) %collective-permute-start.1) | collective-permute-done | bytes 131104 | tf_op jit(solution)/shard_map/ppermute | solution.py:338
  22.5 0.6 step_0_0.1
  23.1 0.1 collective-permute-start.7
  23.2 1.3 %collective-permute-start.8 = (bf16[4,128,128]{2,1,0:T(8,128)(2,1)S(1)}, bf16[4,128,128]{2,1,0:T(8,128)(2,1)S(1)}, u32[]{:S(2)}, u32[]{:S(2)}) collective-permute-start(bf16[4,128,128]{2,1,0:T(8,128)(2,1)S(1)} %get-tuple-element.79), channel_id=1, source_target_pairs={{0,9},{8,0},{16,17},{24,25},{1,8},{9,1},{17,16},{25,24},{2,11},{10... | collective-permute-start | bytes 393224 | tf_op jit(solution)/shard_map/ppermute | solution.py:410
  24.5 0.6 step_0_1.1
  25.1 0.0 collective-permute-done.3.refs_1_
  25.1 0.8 %collective-permute-start.4 = (bf16[8,128,128]{2,1,0:T(8,128)(2,1)S(1)}, bf16[8,128,128]{2,1,0:T(8,128)(2,1)S(1)}, u32[]{:S(2)}, u32[]{:S(2)}) collective-permute-start(bf16[8,128,128]{2,1,0:T(8,128)(2,1)S(1)} %get-tuple-element.71.old_b), channel_id=1, source_target_pairs={{0,8},{8,0},{16,24},{24,16},{1,9},{9,1},{17,25},{25,17},{2,10},{10... | collective-permute-start | bytes 786440 | tf_op jit(solution)/shard_map/ppermute | solution.py:413
  25.9 0.1 collective-permute-start.9
  26.0 0.8 %collective-permute-start.5 = (bf16[4,128,128]{2,1,0:T(8,128)(2,1)S(1)}, bf16[4,128,128]{2,1,0:T(8,128)(2,1)S(1)}, u32[]{:S(2)}, u32[]{:S(2)}) collective-permute-start(bf16[4,128,128]{2,1,0:T(8,128)(2,1)S(1)} %get-tuple-element.74), channel_id=1, source_target_pairs={{0,9},{8,0},{16,17},{24,25},{1,8},{9,1},{17,16},{25,24},{2,11},{10... | collective-permute-start | bytes 393224 | tf_op jit(solution)/shard_map/ppermute | solution.py:410
  26.8 1.0 %collective-permute-done.8.even_in.refs_0_ = bf16[4,128,128]{2,1,0:T(8,128)(2,1)S(1)} collective-permute-done((bf16[4,128,128]{2,1,0:T(8,128)(2,1)S(1)}, bf16[4,128,128]{2,1,0:T(8,128)(2,1)S(1)}, u32[]{:S(2)}, u32[]{:S(2)}) %collective-permute-start.8) | collective-permute-done | bytes 131104 | tf_op jit(solution)/shard_map/ppermute | solution.py:410
  27.9 1.1 %collective-permute-start.6 = (bf16[4,128,128]{2,1,0:T(8,128)(2,1)S(1)}, bf16[4,128,128]{2,1,0:T(8,128)(2,1)S(1)}, u32[]{:S(2)}, u32[]{:S(2)}) collective-permute-start(bf16[4,128,128]{2,1,0:T(8,128)(2,1)S(1)} %get-tuple-element.75), channel_id=1, source_target_pairs={{0,8},{8,0},{16,24},{24,16},{1,10},{9,1},{17,18},{25,26},{2,9},{10... | collective-permute-start | bytes 393224 | tf_op jit(solution)/shard_map/ppermute | solution.py:410
  29.0 0.5 order.2.edges
  29.6 2.3 %collective-permute-done.9.odd_in.refs_1_ = bf16[4,128,128]{2,1,0:T(8,128)(2,1)S(1)} collective-permute-done((bf16[4,128,128]{2,1,0:T(8,128)(2,1)S(1)}, bf16[4,128,128]{2,1,0:T(8,128)(2,1)S(1)}, u32[]{:S(2)}, u32[]{:S(2)}) %collective-permute-start.9) | collective-permute-done | bytes 131104 | tf_op jit(solution)/shard_map/ppermute | solution.py:410
  31.9 0.0 collective-permute-done.7.centre
  31.9 0.6 step_1_0.1
  32.5 0.6 collective-permute-start.13
  33.1 1.2 %collective-permute-start.14 = (bf16[4,128,128]{2,1,0:T(8,128)(2,1)S(1)}, bf16[4,128,128]{2,1,0:T(8,128)(2,1)S(1)}, u32[]{:S(2)}, u32[]{:S(2)}) collective-permute-start(bf16[4,128,128]{2,1,0:T(8,128)(2,1)S(1)} %get-tuple-element.91), channel_id=1, source_target_pairs={{0,8},{8,17},{16,0},{24,25},{1,9},{9,16},{17,1},{25,24},{2,10},{10... | collective-permute-start | bytes 393224 | tf_op jit(solution)/shard_map/ppermute | solution.py:410
  34.3 0.8 %collective-permute-done.5.even_in.refs_2_ = bf16[4,128,128]{2,1,0:T(8,128)(2,1)S(1)} collective-permute-done((bf16[4,128,128]{2,1,0:T(8,128)(2,1)S(1)}, bf16[4,128,128]{2,1,0:T(8,128)(2,1)S(1)}, u32[]{:S(2)}, u32[]{:S(2)}) %collective-permute-start.5) | collective-permute-done | bytes 131104 | tf_op jit(solution)/shard_map/ppermute | solution.py:410
  35.1 0.6 step_1_1.1
  35.7 3.7 %collective-permute-start.10 = (bf16[8,128,128]{2,1,0:T(8,128)(2,1)S(1)}, bf16[8,128,128]{2,1,0:T(8,128)(2,1)S(1)}, u32[]{:S(2)}, u32[]{:S(2)}) collective-permute-start(bf16[8,128,128]{2,1,0:T(8,128)(2,1)S(1)} %get-tuple-element.82.old_b), channel_id=1, source_target_pairs={{8,16},{0,8},{16,24},{24,0},{9,17},{1,9},{17,25},{25,1},{10,18},{2... | collective-permute-start | bytes 786440 | tf_op jit(solution)/shard_map/ppermute | solution.py:413
  39.4 0.4 collective-permute-start.15
  39.8 2.3 %collective-permute-start.11 = (bf16[4,128,128]{2,1,0:T(8,128)(2,1)S(1)}, bf16[4,128,128]{2,1,0:T(8,128)(2,1)S(1)}, u32[]{:S(2)}, u32[]{:S(2)}) collective-permute-start(bf16[4,128,128]{2,1,0:T(8,128)(2,1)S(1)} %get-tuple-element.85), channel_id=1, source_target_pairs={{0,8},{8,17},{16,0},{24,25},{1,9},{9,16},{17,1},{25,24},{2,10},{10... | collective-permute-start | bytes 393224 | tf_op jit(solution)/shard_map/ppermute | solution.py:410
  42.2 0.0 collective-permute-done.14.even_in.refs_4_
  42.2 3.4 %collective-permute-done.15.odd_in.refs_5_ = bf16[4,128,128]{2,1,0:T(8,128)(2,1)S(1)} collective-permute-done((bf16[4,128,128]{2,1,0:T(8,128)(2,1)S(1)}, bf16[4,128,128]{2,1,0:T(8,128)(2,1)S(1)}, u32[]{:S(2)}, u32[]{:S(2)}) %collective-permute-start.15) | collective-permute-done | bytes 131104 | tf_op jit(solution)/shard_map/ppermute | solution.py:410
  45.6 0.6 step_2_0.1
  46.1 4.4 %collective-permute-start.20 = (bf16[4,128,128]{2,1,0:T(8,128)(2,1)S(1)}, bf16[4,128,128]{2,1,0:T(8,128)(2,1)S(1)}, u32[]{:S(2)}, u32[]{:S(2)}) collective-permute-start(bf16[4,128,128]{2,1,0:T(8,128)(2,1)S(1)} %get-tuple-element.113), channel_id=1, source_target_pairs={{0,8},{8,0},{16,25},{24,16},{1,9},{9,1},{17,24},{25,17},{2,10},{10... | collective-permute-start | bytes 393224 | tf_op jit(solution)/shard_map/ppermute | solution.py:410
  50.6 0.1 collective-permute-start.19
  50.7 0.4 collective-permute-done.11.even_in.refs_6_
  51.1 0.6 step_2_1.1
  51.7 5.2 %collective-permute-start.16 = (bf16[8,128,128]{2,1,0:T(8,128)(2,1)S(1)}, bf16[8,128,128]{2,1,0:T(8,128)(2,1)S(1)}, u32[]{:S(2)}, u32[]{:S(2)}) collective-permute-start(bf16[8,128,128]{2,1,0:T(8,128)(2,1)S(1)} %get-tuple-element.96.old_b), channel_id=1, source_target_pairs={{0,8},{8,0},{16,24},{24,16},{1,9},{9,1},{17,25},{25,17},{2,10},{10... | collective-permute-start | bytes 786440 | tf_op jit(solution)/shard_map/ppermute | solution.py:413
  56.9 0.1 collective-permute-start.21
  57.0 0.1 collective-permute-start.17
  57.0 0.1 collective-permute-start.18
  57.1 0.6 order.3.edges
  57.7 4.6 %collective-permute-done.21.odd_in = bf16[4,128,128]{2,1,0:T(8,128)(2,1)S(1)} collective-permute-done((bf16[4,128,128]{2,1,0:T(8,128)(2,1)S(1)}, bf16[4,128,128]{2,1,0:T(8,128)(2,1)S(1)}, u32[]{:S(2)}, u32[]{:S(2)}) %collective-permute-start.21) | collective-permute-done | bytes 131104 | tf_op jit(solution)/shard_map/ppermute | solution.py:410
  62.3 3.3 %step_3_0.1 = (bf16[2,8,128,256]{3,2,1,0:T(8,128)(2,1)}, bf16[8,128,128]{2,1,0:T(8,128)(2,1)}, bf16[8,128,128]{2,1,0:T(8,128)(2,1)}) custom-call(s32[2]{0:T(128)S(1)} %pad_add_fusion.meta, bf16[8,128,128]{2,1,0:T(8,128)(2,1)S(1)} %collective-permute-done.19.centre, ...), custom_call_target="tpu_custom_call", output_to_operand_aliasing={{0}: (13, {})} | custom-call | tf_op jit(solution)/shard_map/step_3_0/pallas_call | solution.py:435
  65.6 3.3 %step_3_1.1 = (bf16[2,8,128,256]{3,2,1,0:T(8,128)(2,1)}, bf16[8,128,128]{2,1,0:T(8,128)(2,1)}, bf16[8,128,128]{2,1,0:T(8,128)(2,1)}) custom-call(s32[2]{0:T(128)S(1)} %pad_add_fusion.meta, bf16[8,128,128]{2,1,0:T(8,128)(2,1)S(1)} %collective-permute-done.16.centre, ...), custom_call_target="tpu_custom_call", output_to_operand_aliasing={{0}: (13, {})} | custom-call | tf_op jit(solution)/shard_map/step_3_1/pallas_call | solution.py:435
  (14 shorter events, 0.0 us)
Async XLA Ops:
  7.1 18.0 %collective-permute-start.2 = (bf16[16,128,128]{2,1,0:T(8,128)(2,1)S(1)}, bf16[16,128,128]{2,1,0:T(8,128)(2,1)S(1)}, u32[]{:S(2)}, u32[]{:S(2)}) collective-permute-start(bf16[16,128,128]{2,1,0:T(8,128)(2,1)S(1)} %get-tuple-element.67.even_w), channel_id=1, source_target_pairs={{8,9},{16,17},{0,24},{24,0},{9,8},{17,16},{1,25},{25,1},{10,11},{1... | collective-permute-start | bytes 1572872 | tf_op jit(solution)/shard_map/ppermute | solution.py:375
  8.0 17.1 %collective-permute-start.3 = (bf16[16,128,128]{2,1,0:T(8,128)(2,1)S(1)}, bf16[16,128,128]{2,1,0:T(8,128)(2,1)S(1)}, u32[]{:S(2)}, u32[]{:S(2)}) collective-permute-start(bf16[16,128,128]{2,1,0:T(8,128)(2,1)S(1)} %get-tuple-element.68.odd_w), channel_id=1, source_target_pairs={{0,8},{8,0},{16,24},{24,16},{9,10},{17,18},{1,25},{25,1},{10,9},{1... | collective-permute-start | bytes 1572872 | tf_op jit(solution)/shard_map/ppermute | solution.py:375
  8.9 12.2 %collective-permute-start = (bf16[2,128,256]{2,1,0:T(8,128)(2,1)S(1)}, bf16[2,128,256]{2,1,0:T(8,128)(2,1)S(1)}, u32[]{:S(2)}, u32[]{:S(2)}) collective-permute-start(bf16[2,128,256]{2,1,0:T(8,128)(2,1)S(1)} %get-tuple-element.63), channel_id=1, source_target_pairs={{0,1},{8,16},{16,24},{24,8},{1,0},{9,17},{17,25},{25,9},{2,3},{10,... | collective-permute-start | bytes 393224 | tf_op jit(solution)/shard_map/ppermute | solution.py:338
  8.9 13.6 %collective-permute-start.1 = (bf16[2,128,256]{2,1,0:T(8,128)(2,1)S(1)}, bf16[2,128,256]{2,1,0:T(8,128)(2,1)S(1)}, u32[]{:S(2)}, u32[]{:S(2)}) collective-permute-start(bf16[2,128,256]{2,1,0:T(8,128)(2,1)S(1)} %get-tuple-element.64), channel_id=1, source_target_pairs={{0,8},{8,0},{16,24},{24,16},{1,2},{9,17},{17,25},{25,9},{2,1},{10,... | collective-permute-start | bytes 393224 | tf_op jit(solution)/shard_map/ppermute | solution.py:338
  23.1 8.8 %collective-permute-start.7 = (bf16[8,128,128]{2,1,0:T(8,128)(2,1)S(1)}, bf16[8,128,128]{2,1,0:T(8,128)(2,1)S(1)}, u32[]{:S(2)}, u32[]{:S(2)}) collective-permute-start(bf16[8,128,128]{2,1,0:T(8,128)(2,1)S(1)} %get-tuple-element.69.rest_0_.old_b), channel_id=1, source_target_pairs={{0,8},{8,0},{16,24},{24,16},{1,9},{9,1},{17,25},{25,17},{2,10},{10... | collective-permute-start | bytes 786440 | tf_op jit(solution)/shard_map/ppermute | solution.py:413
  23.2 4.7 %collective-permute-start.8 = (bf16[4,128,128]{2,1,0:T(8,128)(2,1)S(1)}, bf16[4,128,128]{2,1,0:T(8,128)(2,1)S(1)}, u32[]{:S(2)}, u32[]{:S(2)}) collective-permute-start(bf16[4,128,128]{2,1,0:T(8,128)(2,1)S(1)} %get-tuple-element.79), channel_id=1, source_target_pairs={{0,9},{8,0},{16,17},{24,25},{1,8},{9,1},{17,16},{25,24},{2,11},{10... | collective-permute-start | bytes 393224 | tf_op jit(solution)/shard_map/ppermute | solution.py:410
  25.1 10.0 %collective-permute-start.4 = (bf16[8,128,128]{2,1,0:T(8,128)(2,1)S(1)}, bf16[8,128,128]{2,1,0:T(8,128)(2,1)S(1)}, u32[]{:S(2)}, u32[]{:S(2)}) collective-permute-start(bf16[8,128,128]{2,1,0:T(8,128)(2,1)S(1)} %get-tuple-element.71.old_b), channel_id=1, source_target_pairs={{0,8},{8,0},{16,24},{24,16},{1,9},{9,1},{17,25},{25,17},{2,10},{10... | collective-permute-start | bytes 786440 | tf_op jit(solution)/shard_map/ppermute | solution.py:413
  25.9 6.0 %collective-permute-start.9 = (bf16[4,128,128]{2,1,0:T(8,128)(2,1)S(1)}, bf16[4,128,128]{2,1,0:T(8,128)(2,1)S(1)}, u32[]{:S(2)}, u32[]{:S(2)}) collective-permute-start(bf16[4,128,128]{2,1,0:T(8,128)(2,1)S(1)} %get-tuple-element.80), channel_id=1, source_target_pairs={{0,8},{8,0},{16,24},{24,16},{1,10},{9,1},{17,18},{25,26},{2,9},{10... | collective-permute-start | bytes 393224 | tf_op jit(solution)/shard_map/ppermute | solution.py:410
  26.0 9.1 %collective-permute-start.5 = (bf16[4,128,128]{2,1,0:T(8,128)(2,1)S(1)}, bf16[4,128,128]{2,1,0:T(8,128)(2,1)S(1)}, u32[]{:S(2)}, u32[]{:S(2)}) collective-permute-start(bf16[4,128,128]{2,1,0:T(8,128)(2,1)S(1)} %get-tuple-element.74), channel_id=1, source_target_pairs={{0,9},{8,0},{16,17},{24,25},{1,8},{9,1},{17,16},{25,24},{2,11},{10... | collective-permute-start | bytes 393224 | tf_op jit(solution)/shard_map/ppermute | solution.py:410
  27.9 7.2 %collective-permute-start.6 = (bf16[4,128,128]{2,1,0:T(8,128)(2,1)S(1)}, bf16[4,128,128]{2,1,0:T(8,128)(2,1)S(1)}, u32[]{:S(2)}, u32[]{:S(2)}) collective-permute-start(bf16[4,128,128]{2,1,0:T(8,128)(2,1)S(1)} %get-tuple-element.75), channel_id=1, source_target_pairs={{0,8},{8,0},{16,24},{24,16},{1,10},{9,1},{17,18},{25,26},{2,9},{10... | collective-permute-start | bytes 393224 | tf_op jit(solution)/shard_map/ppermute | solution.py:410
  32.5 13.1 %collective-permute-start.13 = (bf16[8,128,128]{2,1,0:T(8,128)(2,1)S(1)}, bf16[8,128,128]{2,1,0:T(8,128)(2,1)S(1)}, u32[]{:S(2)}, u32[]{:S(2)}) collective-permute-start(bf16[8,128,128]{2,1,0:T(8,128)(2,1)S(1)} %get-tuple-element.88.old_b), channel_id=1, source_target_pairs={{8,16},{0,8},{16,24},{24,0},{9,17},{1,9},{17,25},{25,1},{10,18},{2... | collective-permute-start | bytes 786440 | tf_op jit(solution)/shard_map/ppermute | solution.py:413
  33.1 9.1 %collective-permute-start.14 = (bf16[4,128,128]{2,1,0:T(8,128)(2,1)S(1)}, bf16[4,128,128]{2,1,0:T(8,128)(2,1)S(1)}, u32[]{:S(2)}, u32[]{:S(2)}) collective-permute-start(bf16[4,128,128]{2,1,0:T(8,128)(2,1)S(1)} %get-tuple-element.91), channel_id=1, source_target_pairs={{0,8},{8,17},{16,0},{24,25},{1,9},{9,16},{17,1},{25,24},{2,10},{10... | collective-permute-start | bytes 393224 | tf_op jit(solution)/shard_map/ppermute | solution.py:410
  35.7 15.4 %collective-permute-start.10 = (bf16[8,128,128]{2,1,0:T(8,128)(2,1)S(1)}, bf16[8,128,128]{2,1,0:T(8,128)(2,1)S(1)}, u32[]{:S(2)}, u32[]{:S(2)}) collective-permute-start(bf16[8,128,128]{2,1,0:T(8,128)(2,1)S(1)} %get-tuple-element.82.old_b), channel_id=1, source_target_pairs={{8,16},{0,8},{16,24},{24,0},{9,17},{1,9},{17,25},{25,1},{10,18},{2... | collective-permute-start | bytes 786440 | tf_op jit(solution)/shard_map/ppermute | solution.py:413
  39.4 6.2 %collective-permute-start.15 = (bf16[4,128,128]{2,1,0:T(8,128)(2,1)S(1)}, bf16[4,128,128]{2,1,0:T(8,128)(2,1)S(1)}, u32[]{:S(2)}, u32[]{:S(2)}) collective-permute-start(bf16[4,128,128]{2,1,0:T(8,128)(2,1)S(1)} %get-tuple-element.92), channel_id=1, source_target_pairs={{0,8},{8,16},{16,24},{24,0},{1,9},{9,18},{17,1},{25,26},{2,10},{10... | collective-permute-start | bytes 393224 | tf_op jit(solution)/shard_map/ppermute | solution.py:410
  39.8 11.3 %collective-permute-start.11 = (bf16[4,128,128]{2,1,0:T(8,128)(2,1)S(1)}, bf16[4,128,128]{2,1,0:T(8,128)(2,1)S(1)}, u32[]{:S(2)}, u32[]{:S(2)}) collective-permute-start(bf16[4,128,128]{2,1,0:T(8,128)(2,1)S(1)} %get-tuple-element.85), channel_id=1, source_target_pairs={{0,8},{8,17},{16,0},{24,25},{1,9},{9,16},{17,1},{25,24},{2,10},{10... | collective-permute-start | bytes 393224 | tf_op jit(solution)/shard_map/ppermute | solution.py:410
  42.2 8.9 %collective-permute-start.12 = (bf16[4,128,128]{2,1,0:T(8,128)(2,1)S(1)}, bf16[4,128,128]{2,1,0:T(8,128)(2,1)S(1)}, u32[]{:S(2)}, u32[]{:S(2)}) collective-permute-start(bf16[4,128,128]{2,1,0:T(8,128)(2,1)S(1)} %get-tuple-element.86), channel_id=1, source_target_pairs={{0,8},{8,16},{16,24},{24,0},{1,9},{9,18},{17,1},{25,26},{2,10},{10... | collective-permute-start | bytes 393224 | tf_op jit(solution)/shard_map/ppermute | solution.py:410
  46.1 10.9 %collective-permute-start.20 = (bf16[4,128,128]{2,1,0:T(8,128)(2,1)S(1)}, bf16[4,128,128]{2,1,0:T(8,128)(2,1)S(1)}, u32[]{:S(2)}, u32[]{:S(2)}) collective-permute-start(bf16[4,128,128]{2,1,0:T(8,128)(2,1)S(1)} %get-tuple-element.113), channel_id=1, source_target_pairs={{0,8},{8,0},{16,25},{24,16},{1,9},{9,1},{17,24},{25,17},{2,10},{10... | collective-permute-start | bytes 393224 | tf_op jit(solution)/shard_map/ppermute | solution.py:410
  50.6 11.7 %collective-permute-start.19 = (bf16[8,128,128]{2,1,0:T(8,128)(2,1)S(1)}, bf16[8,128,128]{2,1,0:T(8,128)(2,1)S(1)}, u32[]{:S(2)}, u32[]{:S(2)}) collective-permute-start(bf16[8,128,128]{2,1,0:T(8,128)(2,1)S(1)} %get-tuple-element.101.old_b), channel_id=1, source_target_pairs={{0,8},{8,0},{16,24},{24,16},{1,9},{9,1},{17,25},{25,17},{2,10},{10... | collective-permute-start | bytes 786440 | tf_op jit(solution)/shard_map/ppermute | solution.py:413
  51.7 14.0 %collective-permute-start.16 = (bf16[8,128,128]{2,1,0:T(8,128)(2,1)S(1)}, bf16[8,128,128]{2,1,0:T(8,128)(2,1)S(1)}, u32[]{:S(2)}, u32[]{:S(2)}) collective-permute-start(bf16[8,128,128]{2,1,0:T(8,128)(2,1)S(1)} %get-tuple-element.96.old_b), channel_id=1, source_target_pairs={{0,8},{8,0},{16,24},{24,16},{1,9},{9,1},{17,25},{25,17},{2,10},{10... | collective-permute-start | bytes 786440 | tf_op jit(solution)/shard_map/ppermute | solution.py:413
  56.9 5.4 %collective-permute-start.21 = (bf16[4,128,128]{2,1,0:T(8,128)(2,1)S(1)}, bf16[4,128,128]{2,1,0:T(8,128)(2,1)S(1)}, u32[]{:S(2)}, u32[]{:S(2)}) collective-permute-start(bf16[4,128,128]{2,1,0:T(8,128)(2,1)S(1)} %get-tuple-element.114), channel_id=1, source_target_pairs={{0,8},{8,0},{16,24},{24,16},{1,9},{9,1},{17,26},{25,17},{2,10},{10... | collective-permute-start | bytes 393224 | tf_op jit(solution)/shard_map/ppermute | solution.py:410
  57.0 8.7 %collective-permute-start.17 = (bf16[4,128,128]{2,1,0:T(8,128)(2,1)S(1)}, bf16[4,128,128]{2,1,0:T(8,128)(2,1)S(1)}, u32[]{:S(2)}, u32[]{:S(2)}) collective-permute-start(bf16[4,128,128]{2,1,0:T(8,128)(2,1)S(1)} %get-tuple-element.99), channel_id=1, source_target_pairs={{0,8},{8,0},{16,25},{24,16},{1,9},{9,1},{17,24},{25,17},{2,10},{10... | collective-permute-start | bytes 393224 | tf_op jit(solution)/shard_map/ppermute | solution.py:410
  57.0 8.6 %collective-permute-start.18 = (bf16[4,128,128]{2,1,0:T(8,128)(2,1)S(1)}, bf16[4,128,128]{2,1,0:T(8,128)(2,1)S(1)}, u32[]{:S(2)}, u32[]{:S(2)}) collective-permute-start(bf16[4,128,128]{2,1,0:T(8,128)(2,1)S(1)} %get-tuple-element.100), channel_id=1, source_target_pairs={{0,8},{8,0},{16,24},{24,16},{1,9},{9,1},{17,26},{25,17},{2,10},{10... | collective-permute-start | bytes 393224 | tf_op jit(solution)/shard_map/ppermute | solution.py:410

commit v3 on v2

v3 whole, which is shorter than its diff:
```python
import functools

import jax
import jax.numpy as jnp
from jax import lax
from jax.experimental import pallas as pl
from jax.experimental.pallas import tpu as pltpu
from jax.sharding import PartitionSpec as P

REACH = 2
SPAN = 2 * REACH + 1
CHUNKS = 2
EDGE = SPAN + CHUNKS
AXES = ("chain", "rows")
VMEM = pl.BlockSpec(memory_space=pltpu.VMEM)
SMEM = pl.BlockSpec(memory_space=pltpu.SMEM)
ANY = pl.BlockSpec(memory_space=pl.ANY)
HBM = pl.BlockSpec(memory_space=pltpu.HBM)


def even_mate(row, rows):
    return row ^ 1


def odd_mate(row, rows):
    mate = row + 1 if row % 2 else row - 1
    return mate if 0 <= mate < rows else row


def same_row(row, rows):
    return row


def swap_groups(chain, taken=()):
    return {g: g ^ 1 for g in range(chain) if g not in taken}


def hop_pairs(group, mate, chain, rows):
    if group % 2 == 0:
        moves = swap_groups(chain)
    else:
        moves = swap_groups(chain, range(group - 1, group + 3))
        moves.update({group: group + 1, group - 1: group, group + 1: group + 2, group + 2: group - 1})
    return [
        (source * rows + r, target * rows + (mate(r, rows) if source == group else r))
        for source, target in moves.items()
        for r in range(rows)
    ]


def inner_pairs(groups, mate, chain, rows):
    pairs = []
    for r in range(rows):
        target = mate(r, rows)
        if target == r:
            moves = swap_groups(chain)
        else:
            pairs += [(g * rows + r, g * rows + target) for g in groups]
            others = [g for g in range(min(chain, 4)) if g not in groups]
            moves = dict(zip(others, others[1:] + others[:1]))
            moves.update(swap_groups(chain, [*range(4), *groups]))
        pairs += [(a * rows + r, b * rows + r) for a, b in moves.items()]
    return pairs


def dot(a, b):
    return jnp.dot(a, b, preferred_element_type=jnp.float32)


def by_parity(odd, low_value, high_value, even_ref, odd_ref):
    @pl.when(odd == 0)
    def _():
        even_ref[...] = high_value()
        odd_ref[...] = low_value()

    @pl.when(odd == 1)
    def _():
        even_ref[...] = low_value()
        odd_ref[...] = high_value()


def first_kernel(meta, inverse_hbm, right_hbm, solved, *rest):
    *sends, inverse, right, sems = rest
    count = inverse.shape[0]
    parts = 2
    size = count // parts
    loads = []
    for part in range(parts):
        rows = pl.ds(part * size, size)
        loads.append(
            (
                pltpu.make_async_copy(inverse_hbm.at[0, rows], inverse.at[rows], sems.at[0, part]),
                pltpu.make_async_copy(right_hbm.at[0, rows], right.at[rows], sems.at[1, part]),
            )
        )
    for pair in loads:
        for load in pair:
            load.start()
    for part in range(parts):
        for load in loads[part]:
            load.wait()
        for q in range(part * size, (part + 1) * size):
            solved[q] = dot(inverse[q], right[q]).astype(solved.dtype)
    by_parity(meta[1], lambda: solved[:REACH], lambda: solved[count - REACH :], *sends)


def premultiply(meta, depend, scale, lower, inverse, wide, acc, level, q, half, keep=None):
    block = lower.shape[-1]
    terms = lower.shape[2]
    acc[...] = jnp.zeros_like(acc)
    beside = jnp.concatenate([lower[level, half, k] for k in range(terms)], axis=1)
    products = dot(inverse[level, half], beside)
    for k in range(terms):
        column = jnp.clip(depend[k, level, q] - (meta[2] + q) + REACH, 0, SPAN - 1)
        acc[column] += scale[k, level, q] * products[:, k * block : (k + 1) * block]
    at = slice(half * block, (half + 1) * block)
    for d in range(SPAN):
        value = (-acc[d]).astype(wide.dtype)
        wide[0, at, (d + half) * block : (d + half + 1) * block] = value
        if keep is not None:
            keep[half, d] = value
    other = 0 if half else SPAN
    wide[0, at, other * block : (other + 1) * block] = jnp.zeros((block, block), wide.dtype)


def prepare_kernel(meta, depend, scale, lower, inverse, right, first, wide_a, wide_b, base, even_out, odd_out, acc, keep):
    step = pl.program_id(0)
    last = pl.num_programs(0) - 1
    block = lower.shape[-1]
    for half in range(2):
        for level, wide in ((0, wide_a), (1, wide_b)):
            premultiply(meta, depend, scale, lower, inverse, wide, acc, level, 2 * step + half, half, None if level else keep)
        base[half] = dot(inverse[1, half], right[0, half])

    def emit(ref):
        for half in range(2):
            for d in range(SPAN):
                ref[half * EDGE + d] = keep[half, d]
            for chunk in range(CHUNKS):
                ref[half * EDGE + SPAN + chunk] = first[half, :, chunk * block : (chunk + 1) * block]

    odd = meta[1]
    at_low, at_high = step == 0, step == last

    @pl.when((at_low & (odd == 1)) | (at_high & (odd == 0)))
    def _():
        emit(even_out)

    @pl.when((at_low & (odd == 0)) | (at_high & (odd == 1)))
    def _():
        emit(odd_out)


def order_kernel(meta, even_in, odd_in, edges):
    @pl.when(meta[0] > 1)
    def _():
        odd = meta[1]
        edges[1 - odd] = even_in[...]
        edges[odd] = odd_in[...]


def flat(ref, start, count, at=slice(None)):
    block = ref[start : start + count, :, at]
    return block.reshape(count * block.shape[1], block.shape[2])


def place(window, odd, even_in, odd_in, at=slice(None)):
    halo = even_in.shape[0]
    low, high = 0, window.shape[0] - halo
    window[pl.ds(jnp.where(odd == 1, low, high), halo)] = even_in[:, :, at]
    window[pl.ds(jnp.where(odd == 1, high, low), halo)] = odd_in[:, :, at]


def columns(chunk, cases):
    return slice(None) if chunk is None else slice(chunk * cases, (chunk + 1) * cases)


def first_of_group(wide_a, first, window, level_a, put, at):
    for p in range(wide_a.shape[0]):
        rows = dot(wide_a[p], flat(window, 2 * p, SPAN + 1)) + flat(first, 2 * p, 2, at).astype(jnp.float32)
        level_a[put + 2 * p : put + 2 * p + 2] = rows.astype(level_a.dtype).reshape(2, *level_a.shape[1:])


def second_of_group(wide_b, base_b, level_a, solved, at, ready=None):
    for p in range(wide_b.shape[0]):
        rows = dot(wide_b[p], flat(level_a, 2 * p, SPAN + 1)) + flat(base_b, 2 * p, 2, at)
        solved[2 * p : 2 * p + 2] = rows.astype(solved.dtype).reshape(2, *solved.shape[1:])
        if ready is not None:
            ready[p].start()


def emit_sends(odd, solved, sends):
    if sends:
        size = sends[0].shape[0]
        count = solved.shape[0]
        by_parity(odd, lambda: solved[:size], lambda: solved[count - size :], *sends)


def store(level_a, solved, out, at, sems):
    copies = [
        pltpu.make_async_copy(source, out.at[level, :, :, at], sems.at[level])
        for level, source in ((0, level_a), (1, solved))
    ]
    for copy in copies:
        copy.start()
    for copy in copies:
        copy.wait()


def exchanged_step(group, chunk, meta, own, even_in, odd_in, wide_b, base_b, solved, even_out, odd_out, level_a):
    @pl.when(meta[0] == group)
    def _():
        at = columns(chunk, solved.shape[-1])
        count = own.shape[0]
        level_a[REACH : REACH + count] = own[:, :, at]
        place(level_a, meta[1], even_in, odd_in, at)
        second_of_group(wide_b, base_b, level_a, solved, at)
        emit_sends(meta[1], solved, (even_out, odd_out))


def level_step(group, meta, centre, even_in, odd_in, first, wide_a, old_b, out, solved, even_out, odd_out, window, sems):
    count = first.shape[0]

    @pl.when(meta[0] == group)
    def _():
        window[REACH : REACH + count] = centre[...]
        place(window, meta[1], even_in, odd_in)
        first_of_group(wide_a, first, window, solved, 0, slice(None))
        emit_sends(meta[1], solved, (even_out, odd_out))

    @pl.when(meta[0] == group - 1)
    def _():
        store(first, old_b, out, slice(None), sems)


def later_step(group, chunk, final, meta, centre, even_in, odd_in, edges, first, wide_a, wide_b, base_b, old_a, old_b, out_in, out, solved, solved_a, *rest):
    *sends, window, level_a, sems = rest
    cases = solved.shape[-1]
    at = columns(chunk, cases)
    on_out = pl.ds(chunk * cases, cases)
    count = first.shape[0]

    @pl.when(meta[0] == group)
    def _():
        odd = meta[1]
        halo = 2 * REACH
        window[halo : halo + count] = centre[...]
        place(window, odd, even_in, odd_in)
        first_of_group(wide_a, first, window.at[pl.ds(REACH, count + halo)], level_a, REACH, at)
        copy_a, copies_b = None, None
        if final:
            copy_a = pltpu.make_async_copy(level_a.at[pl.ds(REACH, count)], out.at[0, :, :, on_out], sems.at[0])
            copies_b = [
                pltpu.make_async_copy(solved.at[pl.ds(p, 2)], out.at[1, pl.ds(p, 2), :, on_out], sems.at[1 + p // 2])
                for p in range(0, count, 2)
            ]
            copy_a.start()
        for side in range(2):
            for i in range(REACH):
                put = side * (count + REACH) + i
                base = edges[side, i * EDGE + SPAN + chunk]
                blocks = jnp.concatenate([edges[side, i * EDGE + d] for d in range(SPAN)], axis=1)
                row = dot(blocks, flat(window, put, SPAN)) + base.astype(jnp.float32)
                level_a[put] = row.astype(level_a.dtype)
        second_of_group(wide_b, base_b, level_a, solved, at, copies_b)
        emit_sends(odd, solved, sends)
        if final:
            copy_a.wait()
            for copy in copies_b:
                copy.wait()
        else:
            solved_a[...] = level_a[REACH : REACH + count]

    @pl.when(meta[0] == group - 1)
    def _():
        store(old_a.at[:, :, at] if old_a.shape[-1] > cases else old_a, old_b, out, on_out, sems)


def shaped(shape, dtype=jnp.bfloat16):
    return jax.ShapeDtypeStruct(shape, dtype)


def params(**more):
    return pltpu.CompilerParams(vmem_limit_bytes=24 * 1024 * 1024, **more)


def in_hbm(value):
    return pltpu.with_memory_space_constraint(value, pltpu.HBM)


def after(values, *earlier):
    return lax.optimization_barrier((values, earlier))[0]


def per_device(chain, rows, right_side, lower_blocks, block_scale, diag_inverse, depend_rows):
    _, count, block, cases = right_side.shape
    terms = lower_blocks.shape[2]
    width = SPAN * block
    part = cases // CHUNKS
    halo = 2 * REACH
    row = lax.axis_index("rows")
    meta = jnp.stack([lax.axis_index("chain"), row % 2, row * count]).astype(jnp.int32)
    depend = depend_rows.transpose(2, 0, 1)
    scale = block_scale.transpose(2, 0, 1)
    right_side, lower_blocks, diag_inverse = in_hbm(right_side), in_hbm(lower_blocks), in_hbm(diag_inverse)
    mates = (even_mate, odd_mate)

    def exchange(groups, values):
        return [lax.ppermute(value, AXES, inner_pairs(groups, mate, chain, rows)) for value, mate in zip(values, mates)]

    def travel(group, centre, sides):
        return [
            lax.ppermute(value, AXES, hop_pairs(group, mate, chain, rows))
            for value, mate in zip((centre, *sides), (same_row, *mates))
        ]

    def call(kernel, name, in_specs, out_shape, out_specs=None, **more):
        return pl.pallas_call(
            kernel,
            in_specs=in_specs,
            out_specs=out_specs or [VMEM] * len(out_shape),
            out_shape=out_shape,
            compiler_params=params(),
            name=name,
            **more,
        )

    whole, half = shaped((count, block, cases)), shaped((count, block, part))
    whole_edge, half_edge = shaped((REACH, block, cases)), shaped((halo, block, part))

    first, *sides = call(
        first_kernel,
        "first_level",
        [SMEM, HBM, HBM],
        [whole, whole_edge, whole_edge],
        scratch_shapes=[
            pltpu.VMEM((count, block, block), jnp.bfloat16),
            pltpu.VMEM(whole.shape, jnp.bfloat16),
            pltpu.SemaphoreType.DMA((2, 2)),
        ],
    )(meta, diag_inverse, right_side)
    sides = exchange([0], sides)

    pairs = count // 2
    wide_shape = shaped((pairs, 2 * block, width + block))
    wide_spec = pl.BlockSpec((1, 2 * block, width + block), lambda i: (i, 0, 0))
    edge_shape = shaped((REACH * EDGE, block, block))
    edge_spec = pl.BlockSpec(edge_shape.shape, lambda i: (0, 0, 0))

    wide_a, wide_b, base_b, *edge_w = call(
        prepare_kernel,
        "prepare",
        [
            SMEM,
            SMEM,
            SMEM,
            pl.BlockSpec((2, 2, terms, block, block), lambda i: (0, i, 0, 0, 0)),
            pl.BlockSpec((2, 2, block, block), lambda i: (0, i, 0, 0)),
            pl.BlockSpec((1, 2, block, cases), lambda i: (1, i, 0, 0)),
            pl.BlockSpec((2, block, cases), lambda i: (i, 0, 0)),
        ],
        [wide_shape, wide_shape, shaped((count, block, cases), jnp.float32), edge_shape, edge_shape],
        [wide_spec, wide_spec, pl.BlockSpec((2, block, cases), lambda i: (i, 0, 0)), edge_spec, edge_spec],
        grid=(pairs,),
        scratch_shapes=[pltpu.VMEM((SPAN, block, block), jnp.float32), pltpu.VMEM((2, SPAN, block, block), jnp.bfloat16)],
    )(meta, depend, scale, lower_blocks, diag_inverse, right_side, first)

    padded = pltpu.VMEM((count + halo, block, cases), jnp.bfloat16)
    padded_half = pltpu.VMEM((count + halo, block, part), jnp.bfloat16)
    solved, *sends = call(
        functools.partial(exchanged_step, 0, None),
        "step_0",
        [SMEM] + [VMEM] * 5,
        [whole, whole_edge, whole_edge],
        scratch_shapes=[padded],
    )(meta, first, *sides, wide_b, base_b)
    arrived = travel(0, solved, sends)

    edge_w = exchange(range(2, chain), after(edge_w, sides))
    edges, = call(order_kernel, "order", [SMEM, VMEM, VMEM], [shaped((2, *edge_shape.shape))])(meta, *edge_w)

    out, own, *sides = call(
        functools.partial(level_step, 1),
        "step_1",
        [SMEM] + [VMEM] * 6,
        [shaped(right_side.shape), whole, whole_edge, whole_edge],
        [ANY] + [VMEM] * 3,
        scratch_shapes=[padded, pltpu.SemaphoreType.DMA((2,))],
    )(meta, *arrived, first, wide_a, solved)
    sides = exchange([1], sides)
    made_a = [own] * CHUNKS
    sent = []
    for chunk in range(CHUNKS):
        sent.append(
            call(
                functools.partial(exchanged_step, 1, chunk),
                f"step_1_{chunk}",
                [SMEM] + [VMEM] * 5,
                [half, half_edge, half_edge],
                scratch_shapes=[padded_half],
            )(meta, own, *sides, wide_b, base_b)
        )

    for group in range(2, chain):
        final = group == chain - 1
        arrived = [travel(group - 1, solved, sends) for solved, *sends in sent]
        made = []
        for chunk in range(CHUNKS):
            outs = [half, half] + ([] if final else [half_edge] * 2)
            out, solved, level, *sends = call(
                functools.partial(later_step, group, chunk, final),
                f"step_{group}_{chunk}",
                [SMEM] + [VMEM] * 10 + [ANY],
                [shaped(right_side.shape), *outs],
                [ANY] + [VMEM] * len(outs),
                scratch_shapes=[
                    pltpu.VMEM((count + 2 * halo, block, part), jnp.bfloat16),
                    padded_half,
                    pltpu.SemaphoreType.DMA((1 + pairs,)),
                ],
                input_output_aliases={11: 0},
            )(meta, *arrived[chunk], edges, first, wide_a, wide_b, base_b, made_a[chunk], sent[chunk][0], out)
            made.append(((solved, *sends), level))
        sent, made_a = [values[0] for values in made], [values[1] for values in made]
    return out


def solution(mesh):
    placed = (
        P("chain", "rows", None, None),
        P("chain", "rows", None, None, None),
        P("chain", "rows", None),
        P("chain", "rows", None, None),
        P("chain", "rows", None),
    )
    return jax.shard_map(
        functools.partial(per_device, mesh.shape["chain"], mesh.shape["rows"]),
        mesh=mesh,
        in_specs=placed,
        out_specs=P("chain", "rows", None, None),
        check_vma=False,
    )
```

time: 69.3 us -> 56.8 us (0.82)
  the two profiles are of different devices: /device:TPU:19 before, /device:TPU:11 now
where the time goes in v3:
time: 56.8 us; the launch traced here: 56.6 us
  starting transfers between devices  27.4 us (48%)
  Pallas kernels  17.2 us (30%)
  waiting for transfers between devices  11.7 us (21%)
    ppermute x15, starting transfers between devices, travel(): lax.ppermute(value, AXES, hop_pairs(group, mate, chain, rows))  17.8 us
    ppermute x6, starting transfers between devices, exchange(): lax.ppermute(value, AXES, inner_pairs(groups, mate, chain, rows))  9.63 us
    pallas_call x4, Pallas kernels, per_device(): call(functools.partial(later_step, group, chunk, final), f'step_{group}_{...  7.77 us
    ppermute x6, waiting for transfers between devices, exchange(): lax.ppermute(value, AXES, inner_pairs(groups, mate, chain, rows))  6.42 us
    ppermute x15, waiting for transfers between devices, travel(): lax.ppermute(value, AXES, hop_pairs(group, mate, chain, rows))  5.31 us
    pallas_call x1, Pallas kernels, per_device(): call(prepare_kernel, 'prepare', [SMEM, SMEM, SMEM, pl.BlockSpec((2, 2, te...  4.52 us
    pallas_call x1, Pallas kernels, per_device(): call(first_kernel, 'first_level', [SMEM, HBM, HBM], [whole, whole_edge, w...  2.04 us
  transfers between devices with their start and end apart: 21, of which 6 were waited for; matrix products, arithmetic and copies ran while one was open for 0% of the time, Pallas kernels for 20%

profile of v3, /device:TPU:11, one launch (start us, length us, event | category | flops | bytes accessed | tf_op | source)
XLA Modules:
  0.0 56.6 jit_solution(5239646236469217127)
XLA Ops:
  0.0 0.1 pad_add_fusion.meta
  0.1 2.0 %first_level.1 = (bf16[8,128,256]{2,1,0:T(8,128)(2,1)S(1)}, bf16[2,128,256]{2,1,0:T(8,128)(2,1)S(1)}, bf16[2,128,256]{2,1,0:T(8,128)(2,1)S(1)}) custom-call(s32[3]{0:T(128)S(1)} %pad_add_fusion.meta, bf16[2,8,128,128]{3,2,1,0:T(8,128)(2,1)} %inverse.1, bf16[2,8,128,256]{3,2,1,0:T(8,128)(2,1)} %right.1), custom_call_target="tpu_custom_call" | custom-call | tf_op jit(solution)/shard_map/first_level/pallas_call | solution.py:331
  2.1 0.3 collective-permute-start
  2.4 1.8 %collective-permute-start.1 = (bf16[2,128,256]{2,1,0:T(8,128)(2,1)S(1)}, bf16[2,128,256]{2,1,0:T(8,128)(2,1)S(1)}, u32[]{:S(2)}, u32[]{:S(2)}) collective-permute-start(bf16[2,128,256]{2,1,0:T(8,128)(2,1)S(1)} %get-tuple-element.42), channel_id=1, source_target_pairs={{0,8},{8,0},{16,24},{24,16},{1,2},{9,17},{17,25},{25,9},{2,1},{10,... | collective-permute-start | bytes 393224 | tf_op jit(solution)/shard_map/ppermute | solution.py:309
  4.2 4.5 %prepare.1 = (bf16[4,256,768]{2,1,0:T(8,128)(2,1)S(1)}, bf16[4,256,768]{2,1,0:T(8,128)(2,1)S(1)}, f32[8,128,256]{2,1,0:T(8,128)S(1)}, bf16[14,128,128]{2,1,0:T(8,128)(2,1)S(1)}, bf16[14,128,128]{2,1,0:T(8,128)(2,1)S(1)}) custom-call(s32[3]{0:T(128)S(1)} %pad_add_fusion.meta, s32[6,2,8]{2,1,0:T(2,128)S(1)} %bitcast.5, f32[6,2,8]{2,1,0:T(2,128)S(1)} %bitcast.6, ...), custom_call_target="tpu_custom_call" | custom-call | tf_op jit(solution)/shard_map/prepare/pallas_call | solution.py:350
  8.7 0.0 collective-permute-done.even_in
  8.8 0.0 collective-permute-done.1.odd_in
  8.8 0.6 step_0.1
  9.3 0.1 collective-permute-start.2
  9.4 1.3 %collective-permute-start.10 = (bf16[14,128,128]{2,1,0:T(8,128)(2,1)S(1)}, bf16[14,128,128]{2,1,0:T(8,128)(2,1)S(1)}, u32[]{:S(2)}, u32[]{:S(2)}) collective-permute-start(bf16[14,128,128]{2,1,0:T(8,128)(2,1)S(1)} %get-tuple-element.57), channel_id=1, source_target_pairs={{16,17},{24,25},{0,8},{8,0},{17,16},{25,24},{1,9},{9,1},{18,19},{2... | collective-permute-start | bytes 1376264 | tf_op jit(solution)/shard_map/ppermute | solution.py:309
  10.7 0.0 collective-permute-start.11
  10.7 0.7 %collective-permute-start.3 = (bf16[2,128,256]{2,1,0:T(8,128)(2,1)S(1)}, bf16[2,128,256]{2,1,0:T(8,128)(2,1)S(1)}, u32[]{:S(2)}, u32[]{:S(2)}) collective-permute-start(bf16[2,128,256]{2,1,0:T(8,128)(2,1)S(1)} %get-tuple-element.46), channel_id=1, source_target_pairs={{0,9},{1,8},{2,11},{3,10},{4,13},{5,12},{6,15},{7,14},{8,0},{9,1},... | collective-permute-start | bytes 393224 | tf_op jit(solution)/shard_map/ppermute | solution.py:313
  11.4 0.0 collective-permute-start.4
  11.4 1.0 %collective-permute-done.3.even_in = bf16[2,128,256]{2,1,0:T(8,128)(2,1)S(1)} collective-permute-done((bf16[2,128,256]{2,1,0:T(8,128)(2,1)S(1)}, bf16[2,128,256]{2,1,0:T(8,128)(2,1)S(1)}, u32[]{:S(2)}, u32[]{:S(2)}) %collective-permute-start.3) | collective-permute-done | bytes 131104 | tf_op jit(solution)/shard_map/ppermute | solution.py:313
  12.4 0.4 collective-permute-done.4.odd_in
  12.8 0.0 collective-permute-done.2.centre
  12.8 0.6 %step_1.1 = (bf16[2,8,128,256]{3,2,1,0:T(8,128)(2,1)}, bf16[8,128,256]{2,1,0:T(8,128)(2,1)S(1)}, bf16[2,128,256]{2,1,0:T(8,128)(2,1)S(1)}, bf16[2,128,256]{2,1,0:T(8,128)(2,1)S(1)}) custom-call(s32[3]{0:T(128)S(1)} %pad_add_fusion.meta, bf16[8,128,256]{2,1,0:T(8,128)(2,1)S(1)} %collective-permute-done.2.centre, ...), custom_call_target="tpu_custom_call" | custom-call | tf_op jit(solution)/shard_map/step_1/pallas_call | solution.py:382
  13.4 6.2 %collective-permute-start.5 = (bf16[2,128,256]{2,1,0:T(8,128)(2,1)S(1)}, bf16[2,128,256]{2,1,0:T(8,128)(2,1)S(1)}, u32[]{:S(2)}, u32[]{:S(2)}) collective-permute-start(bf16[2,128,256]{2,1,0:T(8,128)(2,1)S(1)} %get-tuple-element.50), channel_id=1, source_target_pairs={{8,9},{0,16},{16,24},{24,0},{9,8},{1,17},{17,25},{25,1},{10,11},{2... | collective-permute-start | bytes 393224 | tf_op jit(solution)/shard_map/ppermute | solution.py:309
  19.5 0.1 collective-permute-start.6
  19.6 1.9 %collective-permute-done.5.even_in = bf16[2,128,256]{2,1,0:T(8,128)(2,1)S(1)} collective-permute-done((bf16[2,128,256]{2,1,0:T(8,128)(2,1)S(1)}, bf16[2,128,256]{2,1,0:T(8,128)(2,1)S(1)}, u32[]{:S(2)}, u32[]{:S(2)}) %collective-permute-start.5) | collective-permute-done | bytes 131104 | tf_op jit(solution)/shard_map/ppermute | solution.py:309
  21.5 1.4 %collective-permute-done.6.odd_in = bf16[2,128,256]{2,1,0:T(8,128)(2,1)S(1)} collective-permute-done((bf16[2,128,256]{2,1,0:T(8,128)(2,1)S(1)}, bf16[2,128,256]{2,1,0:T(8,128)(2,1)S(1)}, u32[]{:S(2)}, u32[]{:S(2)}) %collective-permute-start.6) | collective-permute-done | bytes 131104 | tf_op jit(solution)/shard_map/ppermute | solution.py:309
  22.8 0.5 step_1_0.1
  23.4 2.5 %collective-permute-start.12 = (bf16[8,128,128]{2,1,0:T(8,128)(2,1)S(1)}, bf16[8,128,128]{2,1,0:T(8,128)(2,1)S(1)}, u32[]{:S(2)}, u32[]{:S(2)}) collective-permute-start(bf16[8,128,128]{2,1,0:T(8,128)(2,1)S(1)} %get-tuple-element.59.old_b), channel_id=1, source_target_pairs={{8,16},{9,17},{10,18},{11,19},{12,20},{13,21},{14,22},{15,23},{0,8... | collective-permute-start | bytes 786440 | tf_op jit(solution)/shard_map/ppermute | solution.py:313
  25.9 1.2 %collective-permute-start.13 = (bf16[4,128,128]{2,1,0:T(8,128)(2,1)S(1)}, bf16[4,128,128]{2,1,0:T(8,128)(2,1)S(1)}, u32[]{:S(2)}, u32[]{:S(2)}) collective-permute-start(bf16[4,128,128]{2,1,0:T(8,128)(2,1)S(1)} %get-tuple-element.60), channel_id=1, source_target_pairs={{8,17},{9,16},{10,19},{11,18},{12,21},{13,20},{14,23},{15,22},{0,8... | collective-permute-start | bytes 393224 | tf_op jit(solution)/shard_map/ppermute | solution.py:313
  27.1 0.5 step_1_1.1
  27.7 0.1 collective-permute-start.7
  27.8 3.2 %collective-permute-done.10.even_in = bf16[14,128,128]{2,1,0:T(8,128)(2,1)S(1)} collective-permute-done((bf16[14,128,128]{2,1,0:T(8,128)(2,1)S(1)}, bf16[14,128,128]{2,1,0:T(8,128)(2,1)S(1)}, u32[]{:S(2)}, u32[]{:S(2)}) %collective-permute-start.10) | collective-permute-done | bytes 458784 | tf_op jit(solution)/shard_map/ppermute | solution.py:309
  31.0 0.0 collective-permute-start.14
  31.0 0.0 collective-permute-done.11.odd_in
  31.0 0.0 collective-permute-start.8
  31.0 5.3 %collective-permute-start.9 = (bf16[4,128,128]{2,1,0:T(8,128)(2,1)S(1)}, bf16[4,128,128]{2,1,0:T(8,128)(2,1)S(1)}, u32[]{:S(2)}, u32[]{:S(2)}) collective-permute-start(bf16[4,128,128]{2,1,0:T(8,128)(2,1)S(1)} %get-tuple-element.54), channel_id=1, source_target_pairs={{8,16},{9,18},{10,17},{11,20},{12,19},{13,22},{14,21},{15,23},{0,8... | collective-permute-start | bytes 393224 | tf_op jit(solution)/shard_map/ppermute | solution.py:313
  36.2 0.6 %order.1.edges = bf16[2,14,128,128]{3,2,1,0:T(8,128)(2,1)S(1)} custom-call(s32[3]{0:T(128)S(1)} %pad_add_fusion.meta, bf16[14,128,128]{2,1,0:T(8,128)(2,1)S(1)} %collective-permute-done.10.even_in, bf16[14,128,128]{2,1,0:T(8,128)(2,1)S(1)} %collective-permute-done.11.odd_in), custom_call_target="tpu_custom_call" | custom-call | tf_op jit(solution)/shard_map/order/pallas_call | solution.py:380
  36.9 0.0 collective-permute-done.14.odd_in
  36.9 0.0 collective-permute-done.12.centre
  36.9 0.6 %step_2_0.1 = (bf16[2,8,128,256]{3,2,1,0:T(8,128)(2,1)}, bf16[8,128,128]{2,1,0:T(8,128)(2,1)S(1)}, bf16[8,128,128]{2,1,0:T(8,128)(2,1)S(1)}, bf16[4,128,128]{2,1,0:T(8,128)(2,1)S(1)}, bf16[4,128,128]{2,1,0:T(8,128)(2,1)S(1)}) custom-call(s32[3]{0:T(128)S(1)} %pad_add_fusion.meta, ...), custom_call_target="tpu_custom_call", output_to_operand_aliasing={{0}: (11, {})} | custom-call | tf_op jit(solution)/shard_map/step_2_0/pallas_call | solution.py:410
  37.5 4.4 %collective-permute-start.19 = (bf16[4,128,128]{2,1,0:T(8,128)(2,1)S(1)}, bf16[4,128,128]{2,1,0:T(8,128)(2,1)S(1)}, u32[]{:S(2)}, u32[]{:S(2)}) collective-permute-start(bf16[4,128,128]{2,1,0:T(8,128)(2,1)S(1)} %get-tuple-element.69), channel_id=1, source_target_pairs={{0,8},{1,9},{2,10},{3,11},{4,12},{5,13},{6,14},{7,15},{8,0},{9,1},... | collective-permute-start | bytes 393224 | tf_op jit(solution)/shard_map/ppermute | solution.py:313
  41.9 0.1 collective-permute-start.18
  41.9 0.0 collective-permute-done.8.even_in
  41.9 0.6 %step_2_1.1 = (bf16[2,8,128,256]{3,2,1,0:T(8,128)(2,1)}, bf16[8,128,128]{2,1,0:T(8,128)(2,1)S(1)}, bf16[8,128,128]{2,1,0:T(8,128)(2,1)S(1)}, bf16[4,128,128]{2,1,0:T(8,128)(2,1)S(1)}, bf16[4,128,128]{2,1,0:T(8,128)(2,1)S(1)}) custom-call(s32[3]{0:T(128)S(1)} %pad_add_fusion.meta, ...), custom_call_target="tpu_custom_call", output_to_operand_aliasing={{0}: (11, {})} | custom-call | tf_op jit(solution)/shard_map/step_2_1/pallas_call | solution.py:410
  42.6 2.0 %collective-permute-start.15 = (bf16[8,128,128]{2,1,0:T(8,128)(2,1)S(1)}, bf16[8,128,128]{2,1,0:T(8,128)(2,1)S(1)}, u32[]{:S(2)}, u32[]{:S(2)}) collective-permute-start(bf16[8,128,128]{2,1,0:T(8,128)(2,1)S(1)} %get-tuple-element.64.old_b), channel_id=1, source_target_pairs={{0,8},{1,9},{2,10},{3,11},{4,12},{5,13},{6,14},{7,15},{8,0},{9,1},... | collective-permute-start | bytes 786440 | tf_op jit(solution)/shard_map/ppermute | solution.py:313
  44.6 0.1 collective-permute-start.20
  44.7 1.2 %collective-permute-start.16 = (bf16[4,128,128]{2,1,0:T(8,128)(2,1)S(1)}, bf16[4,128,128]{2,1,0:T(8,128)(2,1)S(1)}, u32[]{:S(2)}, u32[]{:S(2)}) collective-permute-start(bf16[4,128,128]{2,1,0:T(8,128)(2,1)S(1)} %get-tuple-element.65), channel_id=1, source_target_pairs={{0,8},{1,9},{2,10},{3,11},{4,12},{5,13},{6,14},{7,15},{8,0},{9,1},... | collective-permute-start | bytes 393224 | tf_op jit(solution)/shard_map/ppermute | solution.py:313
  45.9 0.2 collective-permute-start.17
  46.1 3.9 %collective-permute-done.20.odd_in = bf16[4,128,128]{2,1,0:T(8,128)(2,1)S(1)} collective-permute-done((bf16[4,128,128]{2,1,0:T(8,128)(2,1)S(1)}, bf16[4,128,128]{2,1,0:T(8,128)(2,1)S(1)}, u32[]{:S(2)}, u32[]{:S(2)}) %collective-permute-start.20) | collective-permute-done | bytes 131104 | tf_op jit(solution)/shard_map/ppermute | solution.py:313
  50.0 3.3 %step_3_0.1 = (bf16[2,8,128,256]{3,2,1,0:T(8,128)(2,1)}, bf16[8,128,128]{2,1,0:T(8,128)(2,1)}, bf16[8,128,128]{2,1,0:T(8,128)(2,1)}) custom-call(s32[3]{0:T(128)S(1)} %pad_add_fusion.meta, bf16[8,128,128]{2,1,0:T(8,128)(2,1)S(1)} %collective-permute-done.18.centre, ...), custom_call_target="tpu_custom_call", output_to_operand_aliasing={{0}: (11, {})} | custom-call | tf_op jit(solution)/shard_map/step_3_0/pallas_call | solution.py:410
  53.3 0.0 collective-permute-done.16.even_in
  53.3 0.0 collective-permute-done.17.odd_in
  53.3 3.3 %step_3_1.1 = (bf16[2,8,128,256]{3,2,1,0:T(8,128)(2,1)}, bf16[8,128,128]{2,1,0:T(8,128)(2,1)}, bf16[8,128,128]{2,1,0:T(8,128)(2,1)}) custom-call(s32[3]{0:T(128)S(1)} %pad_add_fusion.meta, bf16[8,128,128]{2,1,0:T(8,128)(2,1)S(1)} %collective-permute-done.15.centre, ...), custom_call_target="tpu_custom_call", output_to_operand_aliasing={{0}: (11, {})} | custom-call | tf_op jit(solution)/shard_map/step_3_1/pallas_call | solution.py:410
  (10 shorter events, 0.0 us)
Async XLA Ops:
  0.0 4.2 %copy-start = (s32[2,8,6]{1,0,2:T(2,128)S(1)}, s32[2,8,6]{1,0,2:T(2,128)}, u32[]{:S(2)}) copy-start(s32[2,8,6]{1,0,2:T(2,128)} %param.9) | copy-start | bytes 1156
  0.0 4.2 %copy-start.1 = (f32[2,8,6]{1,0,2:T(2,128)S(1)}, f32[2,8,6]{1,0,2:T(2,128)}, u32[]{:S(2)}) copy-start(f32[2,8,6]{1,0,2:T(2,128)} %param.7) | copy-start | bytes 1156
  2.1 6.6 %collective-permute-start = (bf16[2,128,256]{2,1,0:T(8,128)(2,1)S(1)}, bf16[2,128,256]{2,1,0:T(8,128)(2,1)S(1)}, u32[]{:S(2)}, u32[]{:S(2)}) collective-permute-start(bf16[2,128,256]{2,1,0:T(8,128)(2,1)S(1)} %get-tuple-element.41), channel_id=1, source_target_pairs={{0,1},{8,16},{16,24},{24,8},{1,0},{9,17},{17,25},{25,9},{2,3},{10,... | collective-permute-start | bytes 393224 | tf_op jit(solution)/shard_map/ppermute | solution.py:309
  2.4 6.3 %collective-permute-start.1 = (bf16[2,128,256]{2,1,0:T(8,128)(2,1)S(1)}, bf16[2,128,256]{2,1,0:T(8,128)(2,1)S(1)}, u32[]{:S(2)}, u32[]{:S(2)}) collective-permute-start(bf16[2,128,256]{2,1,0:T(8,128)(2,1)S(1)} %get-tuple-element.42), channel_id=1, source_target_pairs={{0,8},{8,0},{16,24},{24,16},{1,2},{9,17},{17,25},{25,9},{2,1},{10,... | collective-permute-start | bytes 393224 | tf_op jit(solution)/shard_map/ppermute | solution.py:309
  9.3 3.5 %collective-permute-start.2 = (bf16[8,128,256]{2,1,0:T(8,128)(2,1)S(1)}, bf16[8,128,256]{2,1,0:T(8,128)(2,1)S(1)}, u32[]{:S(2)}, u32[]{:S(2)}) collective-permute-start(bf16[8,128,256]{2,1,0:T(8,128)(2,1)S(1)} %get-tuple-element.45.old_b), channel_id=1, source_target_pairs={{0,8},{1,9},{2,10},{3,11},{4,12},{5,13},{6,14},{7,15},{8,0},{9,1},... | collective-permute-start | bytes 1572872 | tf_op jit(solution)/shard_map/ppermute | solution.py:313
  9.4 21.6 %collective-permute-start.10 = (bf16[14,128,128]{2,1,0:T(8,128)(2,1)S(1)}, bf16[14,128,128]{2,1,0:T(8,128)(2,1)S(1)}, u32[]{:S(2)}, u32[]{:S(2)}) collective-permute-start(bf16[14,128,128]{2,1,0:T(8,128)(2,1)S(1)} %get-tuple-element.57), channel_id=1, source_target_pairs={{16,17},{24,25},{0,8},{8,0},{17,16},{25,24},{1,9},{9,1},{18,19},{2... | collective-permute-start | bytes 1376264 | tf_op jit(solution)/shard_map/ppermute | solution.py:309
  10.7 20.3 %collective-permute-start.11 = (bf16[14,128,128]{2,1,0:T(8,128)(2,1)S(1)}, bf16[14,128,128]{2,1,0:T(8,128)(2,1)S(1)}, u32[]{:S(2)}, u32[]{:S(2)}) collective-permute-start(bf16[14,128,128]{2,1,0:T(8,128)(2,1)S(1)} %get-tuple-element.58), channel_id=1, source_target_pairs={{0,8},{8,0},{16,24},{24,16},{17,18},{25,26},{1,9},{9,1},{18,17},{2... | collective-permute-start | bytes 1376264 | tf_op jit(solution)/shard_map/ppermute | solution.py:309
  10.7 1.7 %collective-permute-start.3 = (bf16[2,128,256]{2,1,0:T(8,128)(2,1)S(1)}, bf16[2,128,256]{2,1,0:T(8,128)(2,1)S(1)}, u32[]{:S(2)}, u32[]{:S(2)}) collective-permute-start(bf16[2,128,256]{2,1,0:T(8,128)(2,1)S(1)} %get-tuple-element.46), channel_id=1, source_target_pairs={{0,9},{1,8},{2,11},{3,10},{4,13},{5,12},{6,15},{7,14},{8,0},{9,1},... | collective-permute-start | bytes 393224 | tf_op jit(solution)/shard_map/ppermute | solution.py:313
  11.4 1.3 %collective-permute-start.4 = (bf16[2,128,256]{2,1,0:T(8,128)(2,1)S(1)}, bf16[2,128,256]{2,1,0:T(8,128)(2,1)S(1)}, u32[]{:S(2)}, u32[]{:S(2)}) collective-permute-start(bf16[2,128,256]{2,1,0:T(8,128)(2,1)S(1)} %get-tuple-element.47), channel_id=1, source_target_pairs={{0,8},{1,10},{2,9},{3,12},{4,11},{5,14},{6,13},{7,15},{8,0},{9,1},... | collective-permute-start | bytes 393224 | tf_op jit(solution)/shard_map/ppermute | solution.py:313
  13.4 8.1 %collective-permute-start.5 = (bf16[2,128,256]{2,1,0:T(8,128)(2,1)S(1)}, bf16[2,128,256]{2,1,0:T(8,128)(2,1)S(1)}, u32[]{:S(2)}, u32[]{:S(2)}) collective-permute-start(bf16[2,128,256]{2,1,0:T(8,128)(2,1)S(1)} %get-tuple-element.50), channel_id=1, source_target_pairs={{8,9},{0,16},{16,24},{24,0},{9,8},{1,17},{17,25},{25,1},{10,11},{2... | collective-permute-start | bytes 393224 | tf_op jit(solution)/shard_map/ppermute | solution.py:309
  19.5 3.3 %collective-permute-start.6 = (bf16[2,128,256]{2,1,0:T(8,128)(2,1)S(1)}, bf16[2,128,256]{2,1,0:T(8,128)(2,1)S(1)}, u32[]{:S(2)}, u32[]{:S(2)}) collective-permute-start(bf16[2,128,256]{2,1,0:T(8,128)(2,1)S(1)} %get-tuple-element.51), channel_id=1, source_target_pairs={{0,8},{8,0},{16,24},{24,16},{9,10},{1,17},{17,25},{25,1},{10,9},{2... | collective-permute-start | bytes 393224 | tf_op jit(solution)/shard_map/ppermute | solution.py:309
  23.4 13.5 %collective-permute-start.12 = (bf16[8,128,128]{2,1,0:T(8,128)(2,1)S(1)}, bf16[8,128,128]{2,1,0:T(8,128)(2,1)S(1)}, u32[]{:S(2)}, u32[]{:S(2)}) collective-permute-start(bf16[8,128,128]{2,1,0:T(8,128)(2,1)S(1)} %get-tuple-element.59.old_b), channel_id=1, source_target_pairs={{8,16},{9,17},{10,18},{11,19},{12,20},{13,21},{14,22},{15,23},{0,8... | collective-permute-start | bytes 786440 | tf_op jit(solution)/shard_map/ppermute | solution.py:313
  25.9 5.0 %collective-permute-start.13 = (bf16[4,128,128]{2,1,0:T(8,128)(2,1)S(1)}, bf16[4,128,128]{2,1,0:T(8,128)(2,1)S(1)}, u32[]{:S(2)}, u32[]{:S(2)}) collective-permute-start(bf16[4,128,128]{2,1,0:T(8,128)(2,1)S(1)} %get-tuple-element.60), channel_id=1, source_target_pairs={{8,17},{9,16},{10,19},{11,18},{12,21},{13,20},{14,23},{15,22},{0,8... | collective-permute-start | bytes 393224 | tf_op jit(solution)/shard_map/ppermute | solution.py:313
  27.7 14.3 %collective-permute-start.7 = (bf16[8,128,128]{2,1,0:T(8,128)(2,1)S(1)}, bf16[8,128,128]{2,1,0:T(8,128)(2,1)S(1)}, u32[]{:S(2)}, u32[]{:S(2)}) collective-permute-start(bf16[8,128,128]{2,1,0:T(8,128)(2,1)S(1)} %get-tuple-element.52.old_b), channel_id=1, source_target_pairs={{8,16},{9,17},{10,18},{11,19},{12,20},{13,21},{14,22},{15,23},{0,8... | collective-permute-start | bytes 786440 | tf_op jit(solution)/shard_map/ppermute | solution.py:313
  31.0 5.9 %collective-permute-start.14 = (bf16[4,128,128]{2,1,0:T(8,128)(2,1)S(1)}, bf16[4,128,128]{2,1,0:T(8,128)(2,1)S(1)}, u32[]{:S(2)}, u32[]{:S(2)}) collective-permute-start(bf16[4,128,128]{2,1,0:T(8,128)(2,1)S(1)} %get-tuple-element.61), channel_id=1, source_target_pairs={{8,16},{9,18},{10,17},{11,20},{12,19},{13,22},{14,21},{15,23},{0,8... | collective-permute-start | bytes 393224 | tf_op jit(solution)/shard_map/ppermute | solution.py:313
  31.0 11.0 %collective-permute-start.8 = (bf16[4,128,128]{2,1,0:T(8,128)(2,1)S(1)}, bf16[4,128,128]{2,1,0:T(8,128)(2,1)S(1)}, u32[]{:S(2)}, u32[]{:S(2)}) collective-permute-start(bf16[4,128,128]{2,1,0:T(8,128)(2,1)S(1)} %get-tuple-element.53), channel_id=1, source_target_pairs={{8,17},{9,16},{10,19},{11,18},{12,21},{13,20},{14,23},{15,22},{0,8... | collective-permute-start | bytes 393224 | tf_op jit(solution)/shard_map/ppermute | solution.py:313
  31.0 11.0 %collective-permute-start.9 = (bf16[4,128,128]{2,1,0:T(8,128)(2,1)S(1)}, bf16[4,128,128]{2,1,0:T(8,128)(2,1)S(1)}, u32[]{:S(2)}, u32[]{:S(2)}) collective-permute-start(bf16[4,128,128]{2,1,0:T(8,128)(2,1)S(1)} %get-tuple-element.54), channel_id=1, source_target_pairs={{8,16},{9,18},{10,17},{11,20},{12,19},{13,22},{14,21},{15,23},{0,8... | collective-permute-start | bytes 393224 | tf_op jit(solution)/shard_map/ppermute | solution.py:313
  37.5 8.4 %collective-permute-start.19 = (bf16[4,128,128]{2,1,0:T(8,128)(2,1)S(1)}, bf16[4,128,128]{2,1,0:T(8,128)(2,1)S(1)}, u32[]{:S(2)}, u32[]{:S(2)}) collective-permute-start(bf16[4,128,128]{2,1,0:T(8,128)(2,1)S(1)} %get-tuple-element.69), channel_id=1, source_target_pairs={{0,8},{1,9},{2,10},{3,11},{4,12},{5,13},{6,14},{7,15},{8,0},{9,1},... | collective-permute-start | bytes 393224 | tf_op jit(solution)/shard_map/ppermute | solution.py:313
  41.9 8.1 %collective-permute-start.18 = (bf16[8,128,128]{2,1,0:T(8,128)(2,1)S(1)}, bf16[8,128,128]{2,1,0:T(8,128)(2,1)S(1)}, u32[]{:S(2)}, u32[]{:S(2)}) collective-permute-start(bf16[8,128,128]{2,1,0:T(8,128)(2,1)S(1)} %get-tuple-element.68.old_b), channel_id=1, source_target_pairs={{0,8},{1,9},{2,10},{3,11},{4,12},{5,13},{6,14},{7,15},{8,0},{9,1},... | collective-permute-start | bytes 786440 | tf_op jit(solution)/shard_map/ppermute | solution.py:313
  42.6 10.7 %collective-permute-start.15 = (bf16[8,128,128]{2,1,0:T(8,128)(2,1)S(1)}, bf16[8,128,128]{2,1,0:T(8,128)(2,1)S(1)}, u32[]{:S(2)}, u32[]{:S(2)}) collective-permute-start(bf16[8,128,128]{2,1,0:T(8,128)(2,1)S(1)} %get-tuple-element.64.old_b), channel_id=1, source_target_pairs={{0,8},{1,9},{2,10},{3,11},{4,12},{5,13},{6,14},{7,15},{8,0},{9,1},... | collective-permute-start | bytes 786440 | tf_op jit(solution)/shard_map/ppermute | solution.py:313
  44.6 5.4 %collective-permute-start.20 = (bf16[4,128,128]{2,1,0:T(8,128)(2,1)S(1)}, bf16[4,128,128]{2,1,0:T(8,128)(2,1)S(1)}, u32[]{:S(2)}, u32[]{:S(2)}) collective-permute-start(bf16[4,128,128]{2,1,0:T(8,128)(2,1)S(1)} %get-tuple-element.70), channel_id=1, source_target_pairs={{0,8},{1,9},{2,10},{3,11},{4,12},{5,13},{6,14},{7,15},{8,0},{9,1},... | collective-permute-start | bytes 393224 | tf_op jit(solution)/shard_map/ppermute | solution.py:313
  44.7 8.6 %collective-permute-start.16 = (bf16[4,128,128]{2,1,0:T(8,128)(2,1)S(1)}, bf16[4,128,128]{2,1,0:T(8,128)(2,1)S(1)}, u32[]{:S(2)}, u32[]{:S(2)}) collective-permute-start(bf16[4,128,128]{2,1,0:T(8,128)(2,1)S(1)} %get-tuple-element.65), channel_id=1, source_target_pairs={{0,8},{1,9},{2,10},{3,11},{4,12},{5,13},{6,14},{7,15},{8,0},{9,1},... | collective-permute-start | bytes 393224 | tf_op jit(solution)/shard_map/ppermute | solution.py:313
  45.9 7.4 %collective-permute-start.17 = (bf16[4,128,128]{2,1,0:T(8,128)(2,1)S(1)}, bf16[4,128,128]{2,1,0:T(8,128)(2,1)S(1)}, u32[]{:S(2)}, u32[]{:S(2)}) collective-permute-start(bf16[4,128,128]{2,1,0:T(8,128)(2,1)S(1)} %get-tuple-element.66), channel_id=1, source_target_pairs={{0,8},{1,9},{2,10},{3,11},{4,12},{5,13},{6,14},{7,15},{8,0},{9,1},... | collective-permute-start | bytes 393224 | tf_op jit(solution)/shard_map/ppermute | solution.py:313

commit v4 on v3

--- a/solution.py
+++ b/solution.py
@@ -48,19 +48,32 @@
     ]
 
 
-def inner_pairs(groups, mate, chain, rows):
+def inner_pairs(groups, mate, chain, rows, idle=None):
     pairs = []
+    paired = [r for r in range(rows) if mate(r, rows) != r]
     for r in range(rows):
-        target = mate(r, rows)
-        if target == r:
+        if r not in paired:
             moves = swap_groups(chain)
         else:
-            pairs += [(g * rows + r, g * rows + target) for g in groups]
-            others = [g for g in range(min(chain, 4)) if g not in groups]
-            moves = dict(zip(others, others[1:] + others[:1]))
-            moves.update(swap_groups(chain, [*range(4), *groups]))
+            pairs += [(g * rows + r, g * rows + mate(r, rows)) for g in groups]
+            if idle is None:
+                others = [g for g in range(min(chain, 4)) if g not in groups]
+                moves = dict(zip(others, others[1:] + others[:1]))
+                moves.update(swap_groups(chain, [*range(4), *groups]))
+            else:
+                alike = [q for q in paired if q % 2 == r % 2]
+                pairs.append((idle * rows + r, idle * rows + alike[(alike.index(r) + 1) % len(alike)]))
+                moves = swap_groups(chain, [idle, *groups])
         pairs += [(a * rows + r, b * rows + r) for a, b in moves.items()]
     return pairs
+
+
+def side_pairs(group, mate, chain, rows):
+    return [
+        (group * rows + r, (group + 1) * rows + mate(r, rows))
+        for r in range(rows)
+        if mate(r, rows) != r
+    ]
 
 
 def dot(a, b):
@@ -127,9 +140,14 @@
     step = pl.program_id(0)
     last = pl.num_programs(0) - 1
     block = lower.shape[-1]
+
+    @pl.when(meta[0] > 0)
+    def _():
+        for half in range(2):
+            premultiply(meta, depend, scale, lower, inverse, wide_a, acc, 0, 2 * step + half, half, keep)
+
     for half in range(2):
-        for level, wide in ((0, wide_a), (1, wide_b)):
-            premultiply(meta, depend, scale, lower, inverse, wide, acc, level, 2 * step + half, half, None if level else keep)
+        premultiply(meta, depend, scale, lower, inverse, wide_b, acc, 1, 2 * step + half, half)
         base[half] = dot(inverse[1, half], right[0, half])
 
     def emit(ref):
@@ -151,8 +169,8 @@
         emit(odd_out)
 
 
-def order_kernel(meta, even_in, odd_in, edges):
-    @pl.when(meta[0] > 1)
+def order_kernel(applies, meta, even_in, odd_in, edges):
+    @pl.when(applies(meta[0]))
     def _():
         odd = meta[1]
         edges[1 - odd] = even_in[...]
@@ -181,12 +199,12 @@
         level_a[put + 2 * p : put + 2 * p + 2] = rows.astype(level_a.dtype).reshape(2, *level_a.shape[1:])
 
 
-def second_of_group(wide_b, base_b, level_a, solved, at, ready=None):
+def second_of_group(wide_b, base_b, level_a, solved, at, done=None):
     for p in range(wide_b.shape[0]):
         rows = dot(wide_b[p], flat(level_a, 2 * p, SPAN + 1)) + flat(base_b, 2 * p, 2, at)
         solved[2 * p : 2 * p + 2] = rows.astype(solved.dtype).reshape(2, *solved.shape[1:])
-        if ready is not None:
-            ready[p].start()
+        if done is not None:
+            done(p)
 
 
 def emit_sends(odd, solved, sends):
@@ -233,8 +251,12 @@
         store(first, old_b, out, slice(None), sems)
 
 
-def later_step(group, chunk, final, meta, centre, even_in, odd_in, edges, first, wide_a, wide_b, base_b, old_a, old_b, out_in, out, solved, solved_a, *rest):
-    *sends, window, level_a, sems = rest
+def later_step(group, chunk, final, meta, centre, even_in, odd_in, edges, first, wide_a, wide_b, base_b, old_a, old_b, *rest):
+    stages = final and chunk == CHUNKS - 1
+    if stages:
+        made_a, made_b, _, out, solved, solved_a, window, level_a, stage, sems = rest
+    else:
+        _, out, solved, solved_a, *sends, window, level_a, sems = rest
     cases = solved.shape[-1]
     at = columns(chunk, cases)
     on_out = pl.ds(chunk * cases, cases)
@@ -247,14 +269,24 @@
         window[halo : halo + count] = centre[...]
         place(window, odd, even_in, odd_in)
         first_of_group(wide_a, first, window.at[pl.ds(REACH, count + halo)], level_a, REACH, at)
-        copy_a, copies_b = None, None
-        if final:
-            copy_a = pltpu.make_async_copy(level_a.at[pl.ds(REACH, count)], out.at[0, :, :, on_out], sems.at[0])
-            copies_b = [
-                pltpu.make_async_copy(solved.at[pl.ds(p, 2)], out.at[1, pl.ds(p, 2), :, on_out], sems.at[1 + p // 2])
-                for p in range(0, count, 2)
+        done, copies = None, []
+        if stages:
+            copies = [
+                pltpu.make_async_copy(stage.at[level, pl.ds(2 * p, 2)], out.at[level, pl.ds(2 * p, 2)], sems.at[level, p])
+                for level in range(2)
+                for p in range(count // 2)
             ]
-            copy_a.start()
+            before = slice(0, chunk * cases)
+            stage[0, :, :, before] = made_a[...]
+            stage[1, :, :, before] = made_b[...]
+            stage[0, :, :, at] = level_a[REACH : REACH + count]
+            for copy in copies[: count // 2]:
+                copy.start()
+
+            def done(p):
+                stage[1, 2 * p : 2 * p + 2, :, at] = solved[2 * p : 2 * p + 2]
+                copies[count // 2 + p].start()
+
         for side in range(2):
             for i in range(REACH):
                 put = side * (count + REACH) + i
@@ -262,18 +294,17 @@
                 blocks = jnp.concatenate([edges[side, i * EDGE + d] for d in range(SPAN)], axis=1)
                 row = dot(blocks, flat(window, put, SPAN)) + base.astype(jnp.float32)
                 level_a[put] = row.astype(level_a.dtype)
-        second_of_group(wide_b, base_b, level_a, solved, at, copies_b)
-        emit_sends(odd, solved, sends)
-        if final:
-            copy_a.wait()
-            for copy in copies_b:
+        second_of_group(wide_b, base_b, level_a, solved, at, done)
+        if stages:
+            for copy in copies:
                 copy.wait()
         else:
+            emit_sends(odd, solved, sends)
             solved_a[...] = level_a[REACH : REACH + count]
 
     @pl.when(meta[0] == group - 1)
     def _():
-        store(old_a.at[:, :, at] if old_a.shape[-1] > cases else old_a, old_b, out, on_out, sems)
+        store(old_a.at[:, :, at] if old_a.shape[-1] > cases else old_a, old_b, out, on_out, *([sems.at[0]] if stages else [sems]))
 
 
 def shaped(shape, dtype=jnp.bfloat16):
@@ -305,13 +336,16 @@
     right_side, lower_blocks, diag_inverse = in_hbm(right_side), in_hbm(lower_blocks), in_hbm(diag_inverse)
     mates = (even_mate, odd_mate)
 
-    def exchange(groups, values):
-        return [lax.ppermute(value, AXES, inner_pairs(groups, mate, chain, rows)) for value, mate in zip(values, mates)]
+    def exchange(groups, values, idle=None):
+        return [
+            lax.ppermute(value, AXES, inner_pairs(groups, mate, chain, rows, idle))
+            for value, mate in zip(values, mates)
+        ]
 
     def travel(group, centre, sides):
-        return [
-            lax.ppermute(value, AXES, hop_pairs(group, mate, chain, rows))
-            for value, mate in zip((centre, *sides), (same_row, *mates))
+        side_table = hop_pairs if group else side_pairs
+        return [lax.ppermute(centre, AXES, hop_pairs(group, same_row, chain, rows))] + [
+            lax.ppermute(value, AXES, side_table(group, mate, chain, rows)) for value, mate in zip(sides, mates)
         ]
 
     def call(kernel, name, in_specs, out_shape, out_specs=None, **more):
@@ -376,8 +410,15 @@
     )(meta, first, *sides, wide_b, base_b)
     arrived = travel(0, solved, sends)
 
-    edge_w = exchange(range(2, chain), after(edge_w, sides))
-    edges, = call(order_kernel, "order", [SMEM, VMEM, VMEM], [shaped((2, *edge_shape.shape))])(meta, *edge_w)
+    def ordered(applies, moved):
+        kernel = functools.partial(order_kernel, applies)
+        return call(kernel, "order", [SMEM, VMEM, VMEM], [shaped((2, *edge_shape.shape))])(meta, *moved)[0]
+
+    early = exchange([2], after(edge_w, sides), 3)
+    edges = [ordered(lambda group: group == 2, early)]
+    if chain > 3:
+        late = exchange(range(3, chain), after(edge_w, early), 2)
+        edges.append(ordered(lambda group: group > 2, late))
 
     out, own, *sides = call(
         functools.partial(level_step, 1),
@@ -387,7 +428,7 @@
         [ANY] + [VMEM] * 3,
         scratch_shapes=[padded, pltpu.SemaphoreType.DMA((2,))],
     )(meta, *arrived, first, wide_a, solved)
-    sides = exchange([1], sides)
+    sides = after(exchange([1], sides), early)
     made_a = [own] * CHUNKS
     sent = []
     for chunk in range(CHUNKS):
@@ -407,19 +448,35 @@
         made = []
         for chunk in range(CHUNKS):
             outs = [half, half] + ([] if final else [half_edge] * 2)
+            stages = final and chunk == CHUNKS - 1
+            extra = [made[0][1], made[0][0][0]] if stages else []
+            sems = (2, pairs) if stages else (2,)
             out, solved, level, *sends = call(
                 functools.partial(later_step, group, chunk, final),
                 f"step_{group}_{chunk}",
-                [SMEM] + [VMEM] * 10 + [ANY],
+                [SMEM] + [VMEM] * (10 + len(extra)) + [ANY],
                 [shaped(right_side.shape), *outs],
                 [ANY] + [VMEM] * len(outs),
                 scratch_shapes=[
                     pltpu.VMEM((count + 2 * halo, block, part), jnp.bfloat16),
                     padded_half,
-                    pltpu.SemaphoreType.DMA((1 + pairs,)),
+                    *([pltpu.VMEM((2, count, block, cases), jnp.bfloat16)] if stages else []),
+                    pltpu.SemaphoreType.DMA(sems),
                 ],
-                input_output_aliases={11: 0},
-            )(meta, *arrived[chunk], edges, first, wide_a, wide_b, base_b, made_a[chunk], sent[chunk][0], out)
+                input_output_aliases={11 + len(extra): 0},
+            )(
+                meta,
+                *arrived[chunk],
+                edges[min(group, 3) - 2],
+                first,
+                wide_a,
+                wide_b,
+                base_b,
+                made_a[chunk],
+                sent[chunk][0],
+                *extra,
+                out,
+            )
             made.append(((solved, *sends), level))
         sent, made_a = [values[0] for values in made], [values[1] for values in made]
     return out

time: 56.8 us -> 61.6 us (1.085)
  waiting for transfers between devices: 11.7 us -> 16.2 us
    ppermute x21 -> x23, waiting for transfers between devices: 11.7 us -> 16.2 us  [the longest x10 8.94 us: travel(): lax.ppermute(value, AXES, side_table(group, mate, chain, rows))]
    pallas_call x4, Pallas kernels: 7.77 us -> 6.65 us  [per_device(): call(functools.partial(later_step, group, chunk, final), f'step_{group}_{...]
    ppermute x21 -> x23, starting transfers between devices: 27.4 us -> 27.5 us  [the longest x8 11.6 us: exchange(): lax.ppermute(value, AXES, inner_pairs(groups, mate, chain, rows, idle))]
  transfers between devices with their start and end apart: 21 -> 23, of which waited for: 6 -> 6; matrix products, arithmetic and copies ran while one was open for 0% -> 0% of each run, Pallas kernels for 20% -> 17%
where the time goes in v4:
time: 61.6 us; the launch traced here: 60.9 us
  starting transfers between devices  27.5 us (45%)
  Pallas kernels  17 us (28%)
  waiting for transfers between devices  16.2 us (26%)
    ppermute x8, starting transfers between devices, exchange(): lax.ppermute(value, AXES, inner_pairs(groups, mate, chain, rows, idle))  11.6 us
    ppermute x5, starting transfers between devices, travel(): lax.ppermute(centre, AXES, hop_pairs(group, same_row, chain, rows))  10.8 us
    ppermute x10, waiting for transfers between devices, travel(): lax.ppermute(value, AXES, side_table(group, mate, chain, rows))  8.94 us
    ppermute x8, waiting for transfers between devices, exchange(): lax.ppermute(value, AXES, inner_pairs(groups, mate, chain, rows, idle))  7.21 us
    pallas_call x4, Pallas kernels, per_device(): call(functools.partial(later_step, group, chunk, final), f'step_{group}_{...  6.65 us
    ppermute x10, starting transfers between devices, travel(): lax.ppermute(value, AXES, side_table(group, mate, chain, rows))  5.04 us
    pallas_call x1, Pallas kernels, per_device(): call(prepare_kernel, 'prepare', [SMEM, SMEM, SMEM, pl.BlockSpec((2, 2, te...  4.9 us
    pallas_call x1, Pallas kernels, per_device(): call(first_kernel, 'first_level', [SMEM, HBM, HBM], [whole, whole_edge, w...  2.04 us
  transfers between devices with their start and end apart: 23, of which 6 were waited for; matrix products, arithmetic and copies ran while one was open for 0% of the time, Pallas kernels for 17%

profile of v4, /device:TPU:11, one launch (start us, length us, event | category | flops | bytes accessed | tf_op | source)
XLA Modules:
  0.0 60.9 jit_solution(15043176409752661762)
XLA Ops:
  0.0 0.1 pad_add_fusion.meta
  0.1 2.0 %first_level.1 = (bf16[8,128,256]{2,1,0:T(8,128)(2,1)S(1)}, bf16[2,128,256]{2,1,0:T(8,128)(2,1)S(1)}, bf16[2,128,256]{2,1,0:T(8,128)(2,1)S(1)}) custom-call(s32[3]{0:T(128)S(1)} %pad_add_fusion.meta, bf16[2,8,128,128]{3,2,1,0:T(8,128)(2,1)} %inverse.1, bf16[2,8,128,256]{3,2,1,0:T(8,128)(2,1)} %right.1), custom_call_target="tpu_custom_call" | custom-call | tf_op jit(solution)/shard_map/first_level/pallas_call | solution.py:365
  2.1 0.3 collective-permute-start
  2.4 1.8 %collective-permute-start.1 = (bf16[2,128,256]{2,1,0:T(8,128)(2,1)S(1)}, bf16[2,128,256]{2,1,0:T(8,128)(2,1)S(1)}, u32[]{:S(2)}, u32[]{:S(2)}) collective-permute-start(bf16[2,128,256]{2,1,0:T(8,128)(2,1)S(1)} %get-tuple-element.48), channel_id=1, source_target_pairs={{0,8},{8,0},{16,24},{24,16},{1,2},{9,17},{17,25},{25,9},{2,1},{10,... | collective-permute-start | bytes 393224 | tf_op jit(solution)/shard_map/ppermute | solution.py:341
  4.2 4.9 %prepare.1 = (bf16[4,256,768]{2,1,0:T(8,128)(2,1)S(1)}, bf16[4,256,768]{2,1,0:T(8,128)(2,1)S(1)}, f32[8,128,256]{2,1,0:T(8,128)S(1)}, bf16[14,128,128]{2,1,0:T(8,128)(2,1)S(1)}, bf16[14,128,128]{2,1,0:T(8,128)(2,1)S(1)}) custom-call(s32[3]{0:T(128)S(1)} %pad_add_fusion.meta, s32[6,2,8]{2,1,0:T(2,128)S(1)} %bitcast.5, f32[6,2,8]{2,1,0:T(2,128)S(1)} %bitcast.6, ...), custom_call_target="tpu_custom_call" | custom-call | tf_op jit(solution)/shard_map/prepare/pallas_call | solution.py:384
  9.2 0.6 step_0.1
  9.7 0.1 collective-permute-start.2
  9.8 1.3 %collective-permute-start.7 = (bf16[14,128,128]{2,1,0:T(8,128)(2,1)S(1)}, bf16[14,128,128]{2,1,0:T(8,128)(2,1)S(1)}, u32[]{:S(2)}, u32[]{:S(2)}) collective-permute-start(bf16[14,128,128]{2,1,0:T(8,128)(2,1)S(1)} %get-tuple-element.75), channel_id=1, source_target_pairs={{16,17},{24,26},{0,8},{8,0},{17,16},{25,27},{1,9},{9,1},{18,19},{2... | collective-permute-start | bytes 1376264 | tf_op jit(solution)/shard_map/ppermute | solution.py:341
  11.1 1.3 %collective-permute-start.8 = (bf16[14,128,128]{2,1,0:T(8,128)(2,1)S(1)}, bf16[14,128,128]{2,1,0:T(8,128)(2,1)S(1)}, u32[]{:S(2)}, u32[]{:S(2)}) collective-permute-start(bf16[14,128,128]{2,1,0:T(8,128)(2,1)S(1)} %get-tuple-element.76), channel_id=1, source_target_pairs={{0,8},{8,0},{16,24},{24,16},{17,18},{25,27},{1,9},{9,1},{18,17},{2... | collective-permute-start | bytes 1376264 | tf_op jit(solution)/shard_map/ppermute | solution.py:341
  12.4 0.7 %collective-permute-start.3 = (bf16[2,128,256]{2,1,0:T(8,128)(2,1)S(1)}, bf16[2,128,256]{2,1,0:T(8,128)(2,1)S(1)}, u32[]{:S(2)}, u32[]{:S(2)}) collective-permute-start(bf16[2,128,256]{2,1,0:T(8,128)(2,1)S(1)} %get-tuple-element.52), channel_id=1, source_target_pairs={{0,9},{1,8},{2,11},{3,10},{4,13},{5,12},{6,15},{7,14}} | collective-permute-start | bytes 393224 | tf_op jit(solution)/shard_map/ppermute | solution.py:348
  13.1 0.7 %collective-permute-start.4 = (bf16[2,128,256]{2,1,0:T(8,128)(2,1)S(1)}, bf16[2,128,256]{2,1,0:T(8,128)(2,1)S(1)}, u32[]{:S(2)}, u32[]{:S(2)}) collective-permute-start(bf16[2,128,256]{2,1,0:T(8,128)(2,1)S(1)} %get-tuple-element.53), channel_id=1, source_target_pairs={{1,10},{2,9},{3,12},{4,11},{5,14},{6,13}} | collective-permute-start | bytes 393224 | tf_op jit(solution)/shard_map/ppermute | solution.py:348
  13.8 0.0 collective-permute-done.4.odd_in
  13.8 0.0 collective-permute-done.2.centre
  13.8 0.6 step_1.1
  14.4 6.2 %collective-permute-start.5 = (bf16[2,128,256]{2,1,0:T(8,128)(2,1)S(1)}, bf16[2,128,256]{2,1,0:T(8,128)(2,1)S(1)}, u32[]{:S(2)}, u32[]{:S(2)}) collective-permute-start(bf16[2,128,256]{2,1,0:T(8,128)(2,1)S(1)} %get-tuple-element.56), channel_id=1, source_target_pairs={{8,9},{0,16},{16,24},{24,0},{9,8},{1,17},{17,25},{25,1},{10,11},{2... | collective-permute-start | bytes 393224 | tf_op jit(solution)/shard_map/ppermute | solution.py:341
  20.6 0.1 collective-permute-start.6
  20.6 0.0 collective-permute-done.7.even_in
  20.6 7.2 %collective-permute-done.8.odd_in = bf16[14,128,128]{2,1,0:T(8,128)(2,1)S(1)} collective-permute-done((bf16[14,128,128]{2,1,0:T(8,128)(2,1)S(1)}, bf16[14,128,128]{2,1,0:T(8,128)(2,1)S(1)}, u32[]{:S(2)}, u32[]{:S(2)}) %collective-permute-start.8) | collective-permute-done | bytes 458784 | tf_op jit(solution)/shard_map/ppermute | solution.py:341
  27.8 0.6 step_1_0.1
  28.4 0.1 collective-permute-start.12
  28.5 0.7 %collective-permute-start.13 = (bf16[4,128,128]{2,1,0:T(8,128)(2,1)S(1)}, bf16[4,128,128]{2,1,0:T(8,128)(2,1)S(1)}, u32[]{:S(2)}, u32[]{:S(2)}) collective-permute-start(bf16[4,128,128]{2,1,0:T(8,128)(2,1)S(1)} %get-tuple-element.68), channel_id=1, source_target_pairs={{8,17},{9,16},{10,19},{11,18},{12,21},{13,20},{14,23},{15,22},{0,8... | collective-permute-start | bytes 393224 | tf_op jit(solution)/shard_map/ppermute | solution.py:348
  29.2 0.6 %collective-permute-start.18 = (bf16[14,128,128]{2,1,0:T(8,128)(2,1)S(1)}, bf16[14,128,128]{2,1,0:T(8,128)(2,1)S(1)}, u32[]{:S(2)}, u32[]{:S(2)}) collective-permute-start(bf16[14,128,128]{2,1,0:T(8,128)(2,1)S(1)} %get-tuple-element.75), channel_id=1, source_target_pairs={{24,25},{16,18},{0,8},{8,0},{25,24},{17,19},{1,9},{9,1},{26,27},{1... | collective-permute-start | bytes 1376264 | tf_op jit(solution)/shard_map/ppermute | solution.py:341
  29.8 1.0 %collective-permute-start.14 = (bf16[4,128,128]{2,1,0:T(8,128)(2,1)S(1)}, bf16[4,128,128]{2,1,0:T(8,128)(2,1)S(1)}, u32[]{:S(2)}, u32[]{:S(2)}) collective-permute-start(bf16[4,128,128]{2,1,0:T(8,128)(2,1)S(1)} %get-tuple-element.69), channel_id=1, source_target_pairs={{8,16},{9,18},{10,17},{11,20},{12,19},{13,22},{14,21},{15,23},{0,8... | collective-permute-start | bytes 393224 | tf_op jit(solution)/shard_map/ppermute | solution.py:348
  30.8 0.5 step_1_1.1
  31.4 1.8 %collective-permute-done.13.even_in = bf16[4,128,128]{2,1,0:T(8,128)(2,1)S(1)} collective-permute-done((bf16[4,128,128]{2,1,0:T(8,128)(2,1)S(1)}, bf16[4,128,128]{2,1,0:T(8,128)(2,1)S(1)}, u32[]{:S(2)}, u32[]{:S(2)}) %collective-permute-start.13) | collective-permute-done | bytes 131104 | tf_op jit(solution)/shard_map/ppermute | solution.py:348
  33.2 2.5 %collective-permute-start.9 = (bf16[8,128,128]{2,1,0:T(8,128)(2,1)S(1)}, bf16[8,128,128]{2,1,0:T(8,128)(2,1)S(1)}, u32[]{:S(2)}, u32[]{:S(2)}) collective-permute-start(bf16[8,128,128]{2,1,0:T(8,128)(2,1)S(1)} %get-tuple-element.64.old_b), channel_id=1, source_target_pairs={{8,16},{9,17},{10,18},{11,19},{12,20},{13,21},{14,22},{15,23},{0,8... | collective-permute-start | bytes 786440 | tf_op jit(solution)/shard_map/ppermute | solution.py:347
  35.7 1.4 %collective-permute-start.10 = (bf16[4,128,128]{2,1,0:T(8,128)(2,1)S(1)}, bf16[4,128,128]{2,1,0:T(8,128)(2,1)S(1)}, u32[]{:S(2)}, u32[]{:S(2)}) collective-permute-start(bf16[4,128,128]{2,1,0:T(8,128)(2,1)S(1)} %get-tuple-element.65), channel_id=1, source_target_pairs={{8,17},{9,16},{10,19},{11,18},{12,21},{13,20},{14,23},{15,22},{0,8... | collective-permute-start | bytes 393224 | tf_op jit(solution)/shard_map/ppermute | solution.py:348
  37.1 0.0 collective-permute-done.12.centre
  37.1 0.4 collective-permute-start.11
  37.5 0.5 order.2.edges
  38.1 0.6 step_2_0.1
  38.6 1.7 %collective-permute-done.10.even_in = bf16[4,128,128]{2,1,0:T(8,128)(2,1)S(1)} collective-permute-done((bf16[4,128,128]{2,1,0:T(8,128)(2,1)S(1)}, bf16[4,128,128]{2,1,0:T(8,128)(2,1)S(1)}, u32[]{:S(2)}, u32[]{:S(2)}) %collective-permute-start.10) | collective-permute-done | bytes 131104 | tf_op jit(solution)/shard_map/ppermute | solution.py:348
  40.4 5.3 %collective-permute-start.20 = (bf16[8,128,128]{2,1,0:T(8,128)(2,1)S(1)}, bf16[8,128,128]{2,1,0:T(8,128)(2,1)S(1)}, u32[]{:S(2)}, u32[]{:S(2)}) collective-permute-start(bf16[8,128,128]{2,1,0:T(8,128)(2,1)S(1)} %get-tuple-element.78.old_b), channel_id=1, source_target_pairs={{0,8},{1,9},{2,10},{3,11},{4,12},{5,13},{6,14},{7,15},{8,0},{9,1},... | collective-permute-start | bytes 786440 | tf_op jit(solution)/shard_map/ppermute | solution.py:347
  45.7 0.0 collective-permute-done.11.odd_in
  45.7 0.0 collective-permute-start.21
  45.7 0.6 step_2_1.1
  46.3 3.0 %collective-permute-start.15 = (bf16[8,128,128]{2,1,0:T(8,128)(2,1)S(1)}, bf16[8,128,128]{2,1,0:T(8,128)(2,1)S(1)}, u32[]{:S(2)}, u32[]{:S(2)}) collective-permute-start(bf16[8,128,128]{2,1,0:T(8,128)(2,1)S(1)} %get-tuple-element.72.old_b), channel_id=1, source_target_pairs={{0,8},{1,9},{2,10},{3,11},{4,12},{5,13},{6,14},{7,15},{8,0},{9,1},... | collective-permute-start | bytes 786440 | tf_op jit(solution)/shard_map/ppermute | solution.py:347
  49.2 0.0 collective-permute-done.18.even_in
  49.2 0.1 collective-permute-start.22
  49.3 0.0 collective-permute-done.19.odd_in
  49.3 0.1 collective-permute-start.16
  49.4 0.7 %collective-permute-done.21.even_in = bf16[4,128,128]{2,1,0:T(8,128)(2,1)S(1)} collective-permute-done((bf16[4,128,128]{2,1,0:T(8,128)(2,1)S(1)}, bf16[4,128,128]{2,1,0:T(8,128)(2,1)S(1)}, u32[]{:S(2)}, u32[]{:S(2)}) %collective-permute-start.21) | collective-permute-done | bytes 131104 | tf_op jit(solution)/shard_map/ppermute | solution.py:348
  50.1 0.0 collective-permute-start.17
  50.1 0.6 %order.3.edges = bf16[2,14,128,128]{3,2,1,0:T(8,128)(2,1)S(1)} custom-call(s32[3]{0:T(128)S(1)} %pad_add_fusion.meta, bf16[14,128,128]{2,1,0:T(8,128)(2,1)S(1)} %collective-permute-done.18.even_in, bf16[14,128,128]{2,1,0:T(8,128)(2,1)S(1)} %collective-permute-done.19.odd_in), custom_call_target="tpu_custom_call" | custom-call | tf_op jit(solution)/shard_map/order/pallas_call | solution.py:415
  50.7 3.8 %collective-permute-done.22.odd_in = bf16[4,128,128]{2,1,0:T(8,128)(2,1)S(1)} collective-permute-done((bf16[4,128,128]{2,1,0:T(8,128)(2,1)S(1)}, bf16[4,128,128]{2,1,0:T(8,128)(2,1)S(1)}, u32[]{:S(2)}, u32[]{:S(2)}) %collective-permute-start.22) | collective-permute-done | bytes 131104 | tf_op jit(solution)/shard_map/ppermute | solution.py:348
  54.5 1.9 %step_3_0.1 = (bf16[2,8,128,256]{3,2,1,0:T(8,128)(2,1)}, bf16[8,128,128]{2,1,0:T(8,128)(2,1)S(1)}, bf16[8,128,128]{2,1,0:T(8,128)(2,1)S(1)}) custom-call(s32[3]{0:T(128)S(1)} %pad_add_fusion.meta, bf16[8,128,128]{2,1,0:T(8,128)(2,1)S(1)} %collective-permute-done.20.centre, ...), custom_call_target="tpu_custom_call", output_to_operand_aliasing={{0}: (11, {})} | custom-call | tf_op jit(solution)/shard_map/step_3_0/pallas_call | solution.py:454
  56.5 0.9 %collective-permute-done.16.even_in = bf16[4,128,128]{2,1,0:T(8,128)(2,1)S(1)} collective-permute-done((bf16[4,128,128]{2,1,0:T(8,128)(2,1)S(1)}, bf16[4,128,128]{2,1,0:T(8,128)(2,1)S(1)}, u32[]{:S(2)}, u32[]{:S(2)}) %collective-permute-start.16) | collective-permute-done | bytes 131104 | tf_op jit(solution)/shard_map/ppermute | solution.py:348
  57.3 3.6 %step_3_1.1 = (bf16[2,8,128,256]{3,2,1,0:T(8,128)(2,1)}, bf16[8,128,128]{2,1,0:T(8,128)(2,1)}, bf16[8,128,128]{2,1,0:T(8,128)(2,1)}) custom-call(s32[3]{0:T(128)S(1)} %pad_add_fusion.meta, bf16[8,128,128]{2,1,0:T(8,128)(2,1)S(1)} %collective-permute-done.15.centre, ...), custom_call_target="tpu_custom_call", output_to_operand_aliasing={{0}: (13, {})} | custom-call | tf_op jit(solution)/shard_map/step_3_1/pallas_call | solution.py:454
  (15 shorter events, 0.0 us)
Async XLA Ops:
  0.0 4.2 %copy-start = (s32[2,8,6]{1,0,2:T(2,128)S(1)}, s32[2,8,6]{1,0,2:T(2,128)}, u32[]{:S(2)}) copy-start(s32[2,8,6]{1,0,2:T(2,128)} %param.9) | copy-start | bytes 1156
  0.0 4.2 %copy-start.1 = (f32[2,8,6]{1,0,2:T(2,128)S(1)}, f32[2,8,6]{1,0,2:T(2,128)}, u32[]{:S(2)}) copy-start(f32[2,8,6]{1,0,2:T(2,128)} %param.7) | copy-start | bytes 1156
  2.1 7.0 %collective-permute-start = (bf16[2,128,256]{2,1,0:T(8,128)(2,1)S(1)}, bf16[2,128,256]{2,1,0:T(8,128)(2,1)S(1)}, u32[]{:S(2)}, u32[]{:S(2)}) collective-permute-start(bf16[2,128,256]{2,1,0:T(8,128)(2,1)S(1)} %get-tuple-element.47), channel_id=1, source_target_pairs={{0,1},{8,16},{16,24},{24,8},{1,0},{9,17},{17,25},{25,9},{2,3},{10,... | collective-permute-start | bytes 393224 | tf_op jit(solution)/shard_map/ppermute | solution.py:341
  2.4 6.7 %collective-permute-start.1 = (bf16[2,128,256]{2,1,0:T(8,128)(2,1)S(1)}, bf16[2,128,256]{2,1,0:T(8,128)(2,1)S(1)}, u32[]{:S(2)}, u32[]{:S(2)}) collective-permute-start(bf16[2,128,256]{2,1,0:T(8,128)(2,1)S(1)} %get-tuple-element.48), channel_id=1, source_target_pairs={{0,8},{8,0},{16,24},{24,16},{1,2},{9,17},{17,25},{25,9},{2,1},{10,... | collective-permute-start | bytes 393224 | tf_op jit(solution)/shard_map/ppermute | solution.py:341
  9.7 4.1 %collective-permute-start.2 = (bf16[8,128,256]{2,1,0:T(8,128)(2,1)S(1)}, bf16[8,128,256]{2,1,0:T(8,128)(2,1)S(1)}, u32[]{:S(2)}, u32[]{:S(2)}) collective-permute-start(bf16[8,128,256]{2,1,0:T(8,128)(2,1)S(1)} %get-tuple-element.51.old_b), channel_id=1, source_target_pairs={{0,8},{1,9},{2,10},{3,11},{4,12},{5,13},{6,14},{7,15},{8,0},{9,1},... | collective-permute-start | bytes 1572872 | tf_op jit(solution)/shard_map/ppermute | solution.py:347
  9.8 10.8 %collective-permute-start.7 = (bf16[14,128,128]{2,1,0:T(8,128)(2,1)S(1)}, bf16[14,128,128]{2,1,0:T(8,128)(2,1)S(1)}, u32[]{:S(2)}, u32[]{:S(2)}) collective-permute-start(bf16[14,128,128]{2,1,0:T(8,128)(2,1)S(1)} %get-tuple-element.75), channel_id=1, source_target_pairs={{16,17},{24,26},{0,8},{8,0},{17,16},{25,27},{1,9},{9,1},{18,19},{2... | collective-permute-start | bytes 1376264 | tf_op jit(solution)/shard_map/ppermute | solution.py:341
  11.1 16.7 %collective-permute-start.8 = (bf16[14,128,128]{2,1,0:T(8,128)(2,1)S(1)}, bf16[14,128,128]{2,1,0:T(8,128)(2,1)S(1)}, u32[]{:S(2)}, u32[]{:S(2)}) collective-permute-start(bf16[14,128,128]{2,1,0:T(8,128)(2,1)S(1)} %get-tuple-element.76), channel_id=1, source_target_pairs={{0,8},{8,0},{16,24},{24,16},{17,18},{25,27},{1,9},{9,1},{18,17},{2... | collective-permute-start | bytes 1376264 | tf_op jit(solution)/shard_map/ppermute | solution.py:341
  12.4 1.3 %collective-permute-start.3 = (bf16[2,128,256]{2,1,0:T(8,128)(2,1)S(1)}, bf16[2,128,256]{2,1,0:T(8,128)(2,1)S(1)}, u32[]{:S(2)}, u32[]{:S(2)}) collective-permute-start(bf16[2,128,256]{2,1,0:T(8,128)(2,1)S(1)} %get-tuple-element.52), channel_id=1, source_target_pairs={{0,9},{1,8},{2,11},{3,10},{4,13},{5,12},{6,15},{7,14}} | collective-permute-start | bytes 393224 | tf_op jit(solution)/shard_map/ppermute | solution.py:348
  13.1 0.7 %collective-permute-start.4 = (bf16[2,128,256]{2,1,0:T(8,128)(2,1)S(1)}, bf16[2,128,256]{2,1,0:T(8,128)(2,1)S(1)}, u32[]{:S(2)}, u32[]{:S(2)}) collective-permute-start(bf16[2,128,256]{2,1,0:T(8,128)(2,1)S(1)} %get-tuple-element.53), channel_id=1, source_target_pairs={{1,10},{2,9},{3,12},{4,11},{5,14},{6,13}} | collective-permute-start | bytes 393224 | tf_op jit(solution)/shard_map/ppermute | solution.py:348
  14.4 13.5 %collective-permute-start.5 = (bf16[2,128,256]{2,1,0:T(8,128)(2,1)S(1)}, bf16[2,128,256]{2,1,0:T(8,128)(2,1)S(1)}, u32[]{:S(2)}, u32[]{:S(2)}) collective-permute-start(bf16[2,128,256]{2,1,0:T(8,128)(2,1)S(1)} %get-tuple-element.56), channel_id=1, source_target_pairs={{8,9},{0,16},{16,24},{24,0},{9,8},{1,17},{17,25},{25,1},{10,11},{2... | collective-permute-start | bytes 393224 | tf_op jit(solution)/shard_map/ppermute | solution.py:341
  20.6 7.3 %collective-permute-start.6 = (bf16[2,128,256]{2,1,0:T(8,128)(2,1)S(1)}, bf16[2,128,256]{2,1,0:T(8,128)(2,1)S(1)}, u32[]{:S(2)}, u32[]{:S(2)}) collective-permute-start(bf16[2,128,256]{2,1,0:T(8,128)(2,1)S(1)} %get-tuple-element.57), channel_id=1, source_target_pairs={{0,8},{8,0},{16,24},{24,16},{9,10},{1,17},{17,25},{25,1},{10,9},{2... | collective-permute-start | bytes 393224 | tf_op jit(solution)/shard_map/ppermute | solution.py:341
  28.4 8.7 %collective-permute-start.12 = (bf16[8,128,128]{2,1,0:T(8,128)(2,1)S(1)}, bf16[8,128,128]{2,1,0:T(8,128)(2,1)S(1)}, u32[]{:S(2)}, u32[]{:S(2)}) collective-permute-start(bf16[8,128,128]{2,1,0:T(8,128)(2,1)S(1)} %get-tuple-element.67.old_b), channel_id=1, source_target_pairs={{8,16},{9,17},{10,18},{11,19},{12,20},{13,21},{14,22},{15,23},{0,8... | collective-permute-start | bytes 786440 | tf_op jit(solution)/shard_map/ppermute | solution.py:347
  28.5 4.7 %collective-permute-start.13 = (bf16[4,128,128]{2,1,0:T(8,128)(2,1)S(1)}, bf16[4,128,128]{2,1,0:T(8,128)(2,1)S(1)}, u32[]{:S(2)}, u32[]{:S(2)}) collective-permute-start(bf16[4,128,128]{2,1,0:T(8,128)(2,1)S(1)} %get-tuple-element.68), channel_id=1, source_target_pairs={{8,17},{9,16},{10,19},{11,18},{12,21},{13,20},{14,23},{15,22},{0,8... | collective-permute-start | bytes 393224 | tf_op jit(solution)/shard_map/ppermute | solution.py:348
  29.2 20.1 %collective-permute-start.18 = (bf16[14,128,128]{2,1,0:T(8,128)(2,1)S(1)}, bf16[14,128,128]{2,1,0:T(8,128)(2,1)S(1)}, u32[]{:S(2)}, u32[]{:S(2)}) collective-permute-start(bf16[14,128,128]{2,1,0:T(8,128)(2,1)S(1)} %get-tuple-element.75), channel_id=1, source_target_pairs={{24,25},{16,18},{0,8},{8,0},{25,24},{17,19},{1,9},{9,1},{26,27},{1... | collective-permute-start | bytes 1376264 | tf_op jit(solution)/shard_map/ppermute | solution.py:341
  29.8 19.5 %collective-permute-start.19 = (bf16[14,128,128]{2,1,0:T(8,128)(2,1)S(1)}, bf16[14,128,128]{2,1,0:T(8,128)(2,1)S(1)}, u32[]{:S(2)}, u32[]{:S(2)}) collective-permute-start(bf16[14,128,128]{2,1,0:T(8,128)(2,1)S(1)} %get-tuple-element.76), channel_id=1, source_target_pairs={{0,8},{8,0},{16,24},{24,16},{25,26},{17,19},{1,9},{9,1},{26,25},{1... | collective-permute-start | bytes 1376264 | tf_op jit(solution)/shard_map/ppermute | solution.py:341
  29.8 5.9 %collective-permute-start.14 = (bf16[4,128,128]{2,1,0:T(8,128)(2,1)S(1)}, bf16[4,128,128]{2,1,0:T(8,128)(2,1)S(1)}, u32[]{:S(2)}, u32[]{:S(2)}) collective-permute-start(bf16[4,128,128]{2,1,0:T(8,128)(2,1)S(1)} %get-tuple-element.69), channel_id=1, source_target_pairs={{8,16},{9,18},{10,17},{11,20},{12,19},{13,22},{14,21},{15,23},{0,8... | collective-permute-start | bytes 393224 | tf_op jit(solution)/shard_map/ppermute | solution.py:348
  33.2 12.5 %collective-permute-start.9 = (bf16[8,128,128]{2,1,0:T(8,128)(2,1)S(1)}, bf16[8,128,128]{2,1,0:T(8,128)(2,1)S(1)}, u32[]{:S(2)}, u32[]{:S(2)}) collective-permute-start(bf16[8,128,128]{2,1,0:T(8,128)(2,1)S(1)} %get-tuple-element.64.old_b), channel_id=1, source_target_pairs={{8,16},{9,17},{10,18},{11,19},{12,20},{13,21},{14,22},{15,23},{0,8... | collective-permute-start | bytes 786440 | tf_op jit(solution)/shard_map/ppermute | solution.py:347
  35.7 4.7 %collective-permute-start.10 = (bf16[4,128,128]{2,1,0:T(8,128)(2,1)S(1)}, bf16[4,128,128]{2,1,0:T(8,128)(2,1)S(1)}, u32[]{:S(2)}, u32[]{:S(2)}) collective-permute-start(bf16[4,128,128]{2,1,0:T(8,128)(2,1)S(1)} %get-tuple-element.65), channel_id=1, source_target_pairs={{8,17},{9,16},{10,19},{11,18},{12,21},{13,20},{14,23},{15,22},{0,8... | collective-permute-start | bytes 393224 | tf_op jit(solution)/shard_map/ppermute | solution.py:348
  37.1 8.6 %collective-permute-start.11 = (bf16[4,128,128]{2,1,0:T(8,128)(2,1)S(1)}, bf16[4,128,128]{2,1,0:T(8,128)(2,1)S(1)}, u32[]{:S(2)}, u32[]{:S(2)}) collective-permute-start(bf16[4,128,128]{2,1,0:T(8,128)(2,1)S(1)} %get-tuple-element.66), channel_id=1, source_target_pairs={{8,16},{9,18},{10,17},{11,20},{12,19},{13,22},{14,21},{15,23},{0,8... | collective-permute-start | bytes 393224 | tf_op jit(solution)/shard_map/ppermute | solution.py:348
  40.4 14.1 %collective-permute-start.20 = (bf16[8,128,128]{2,1,0:T(8,128)(2,1)S(1)}, bf16[8,128,128]{2,1,0:T(8,128)(2,1)S(1)}, u32[]{:S(2)}, u32[]{:S(2)}) collective-permute-start(bf16[8,128,128]{2,1,0:T(8,128)(2,1)S(1)} %get-tuple-element.78.old_b), channel_id=1, source_target_pairs={{0,8},{1,9},{2,10},{3,11},{4,12},{5,13},{6,14},{7,15},{8,0},{9,1},... | collective-permute-start | bytes 786440 | tf_op jit(solution)/shard_map/ppermute | solution.py:347
  45.7 4.4 %collective-permute-start.21 = (bf16[4,128,128]{2,1,0:T(8,128)(2,1)S(1)}, bf16[4,128,128]{2,1,0:T(8,128)(2,1)S(1)}, u32[]{:S(2)}, u32[]{:S(2)}) collective-permute-start(bf16[4,128,128]{2,1,0:T(8,128)(2,1)S(1)} %get-tuple-element.79), channel_id=1, source_target_pairs={{0,8},{1,9},{2,10},{3,11},{4,12},{5,13},{6,14},{7,15},{8,0},{9,1},... | collective-permute-start | bytes 393224 | tf_op jit(solution)/shard_map/ppermute | solution.py:348
  46.3 11.1 %collective-permute-start.15 = (bf16[8,128,128]{2,1,0:T(8,128)(2,1)S(1)}, bf16[8,128,128]{2,1,0:T(8,128)(2,1)S(1)}, u32[]{:S(2)}, u32[]{:S(2)}) collective-permute-start(bf16[8,128,128]{2,1,0:T(8,128)(2,1)S(1)} %get-tuple-element.72.old_b), channel_id=1, source_target_pairs={{0,8},{1,9},{2,10},{3,11},{4,12},{5,13},{6,14},{7,15},{8,0},{9,1},... | collective-permute-start | bytes 786440 | tf_op jit(solution)/shard_map/ppermute | solution.py:347
  49.2 5.3 %collective-permute-start.22 = (bf16[4,128,128]{2,1,0:T(8,128)(2,1)S(1)}, bf16[4,128,128]{2,1,0:T(8,128)(2,1)S(1)}, u32[]{:S(2)}, u32[]{:S(2)}) collective-permute-start(bf16[4,128,128]{2,1,0:T(8,128)(2,1)S(1)} %get-tuple-element.80), channel_id=1, source_target_pairs={{0,8},{1,9},{2,10},{3,11},{4,12},{5,13},{6,14},{7,15},{8,0},{9,1},... | collective-permute-start | bytes 393224 | tf_op jit(solution)/shard_map/ppermute | solution.py:348
  49.3 8.0 %collective-permute-start.16 = (bf16[4,128,128]{2,1,0:T(8,128)(2,1)S(1)}, bf16[4,128,128]{2,1,0:T(8,128)(2,1)S(1)}, u32[]{:S(2)}, u32[]{:S(2)}) collective-permute-start(bf16[4,128,128]{2,1,0:T(8,128)(2,1)S(1)} %get-tuple-element.73), channel_id=1, source_target_pairs={{0,8},{1,9},{2,10},{3,11},{4,12},{5,13},{6,14},{7,15},{8,0},{9,1},... | collective-permute-start | bytes 393224 | tf_op jit(solution)/shard_map/ppermute | solution.py:348
  50.1 7.3 %collective-permute-start.17 = (bf16[4,128,128]{2,1,0:T(8,128)(2,1)S(1)}, bf16[4,128,128]{2,1,0:T(8,128)(2,1)S(1)}, u32[]{:S(2)}, u32[]{:S(2)}) collective-permute-start(bf16[4,128,128]{2,1,0:T(8,128)(2,1)S(1)} %get-tuple-element.74), channel_id=1, source_target_pairs={{0,8},{1,9},{2,10},{3,11},{4,12},{5,13},{6,14},{7,15},{8,0},{9,1},... | collective-permute-start | bytes 393224 | tf_op jit(solution)/shard_map/ppermute | solution.py:348

commit v5 on v3

v5 whole, which is shorter than its diff:
```python
import functools

import jax
import jax.numpy as jnp
from jax import lax
from jax.experimental import pallas as pl
from jax.experimental.pallas import tpu as pltpu
from jax.sharding import PartitionSpec as P

REACH = 2
SPAN = 2 * REACH + 1
AXES = ("chain", "rows")
VMEM = pl.BlockSpec(memory_space=pltpu.VMEM)
SMEM = pl.BlockSpec(memory_space=pltpu.SMEM)
ANY = pl.BlockSpec(memory_space=pl.ANY)
HBM = pl.BlockSpec(memory_space=pltpu.HBM)


def even_mate(row, rows):
    return row ^ 1


def odd_mate(row, rows):
    mate = row + 1 if row % 2 else row - 1
    return mate if 0 <= mate < rows else row


def same_row(row, rows):
    return row


def swap_groups(chain, taken=()):
    return {g: g ^ 1 for g in range(chain) if g not in taken}


def hop_pairs(group, mate, chain, rows):
    if group % 2 == 0:
        moves = swap_groups(chain)
    else:
        moves = swap_groups(chain, range(group - 1, group + 3))
        moves.update({group: group + 1, group - 1: group, group + 1: group + 2, group + 2: group - 1})
    return [
        (source * rows + r, target * rows + (mate(r, rows) if source == group else r))
        for source, target in moves.items()
        for r in range(rows)
    ]


def inner_pairs(groups, mate, chain, rows):
    pairs = []
    for r in range(rows):
        target = mate(r, rows)
        if target == r:
            moves = swap_groups(chain)
        else:
            pairs += [(g * rows + r, g * rows + target) for g in groups]
            others = [g for g in range(min(chain, 4)) if g not in groups]
            moves = dict(zip(others, others[1:] + others[:1]))
            moves.update(swap_groups(chain, [*range(4), *groups]))
        pairs += [(a * rows + r, b * rows + r) for a, b in moves.items()]
    return pairs


def dot(a, b):
    return jnp.dot(a, b, preferred_element_type=jnp.float32)


def by_parity(odd, low_value, high_value, even_ref, odd_ref):
    @pl.when(odd == 0)
    def _():
        even_ref[...] = high_value()
        odd_ref[...] = low_value()

    @pl.when(odd == 1)
    def _():
        even_ref[...] = low_value()
        odd_ref[...] = high_value()


def first_kernel(meta, inverse_hbm, right_hbm, solved, *rest):
    *sends, inverse, right, sems = rest
    count = inverse.shape[0]
    parts = 2
    size = count // parts
    loads = []
    for part in range(parts):
        rows = pl.ds(part * size, size)
        loads.append(
            (
                pltpu.make_async_copy(inverse_hbm.at[0, rows], inverse.at[rows], sems.at[0, part]),
                pltpu.make_async_copy(right_hbm.at[0, rows], right.at[rows], sems.at[1, part]),
            )
        )
    for pair in loads:
        for load in pair:
            load.start()
    for part in range(parts):
        for load in loads[part]:
            load.wait()
        for q in range(part * size, (part + 1) * size):
            solved[q] = dot(inverse[q], right[q]).astype(solved.dtype)
    by_parity(meta[1], lambda: solved[:REACH], lambda: solved[count - REACH :], *sends)


def premultiply(meta, depend, scale, lower, inverse, wide, acc, level, q, half, keep=None):
    block = lower.shape[-1]
    terms = lower.shape[2]
    acc[...] = jnp.zeros_like(acc)
    beside = jnp.concatenate([lower[0, half, k] for k in range(terms)], axis=1)
    products = dot(inverse[0, half], beside)
    for k in range(terms):
        column = jnp.clip(depend[k, level, q] - (meta[2] + q) + REACH, 0, SPAN - 1)
        acc[column] += scale[k, level, q] * products[:, k * block : (k + 1) * block]
    at = slice(half * block, (half + 1) * block)
    for d in range(SPAN):
        value = (-acc[d]).astype(wide.dtype)
        wide[0, at, (d + half) * block : (d + half + 1) * block] = value
        if keep is not None:
            keep[half, d] = value
    other = 0 if half else SPAN
    wide[0, at, other * block : (other + 1) * block] = jnp.zeros((block, block), wide.dtype)


def prepare_kernel(meta, depend, scale, lower, inverse, right, first, wide_b, wide_a, base, even_out, odd_out, acc, keep):
    step = pl.program_id(0)
    pairs = pl.num_programs(0) // 2
    block = lower.shape[-1]

    @pl.when(step < pairs)
    def _():
        for half in range(2):
            premultiply(meta, depend, scale, lower, inverse, wide_b, acc, 1, 2 * step + half, half)
            base[half] = dot(inverse[0, half], right[0, half])

    @pl.when((step >= pairs) & (meta[0] > 0))
    def _():
        for half in range(2):
            premultiply(meta, depend, scale, lower, inverse, wide_a, acc, 0, 2 * (step - pairs) + half, half, keep)

    def emit(ref):
        parts = first.shape[2] // block
        size = SPAN + parts
        for half in range(2):
            for d in range(SPAN):
                ref[half * size + d] = keep[half, d]
            for part in range(parts):
                ref[half * size + SPAN + part] = first[half, :, part * block : (part + 1) * block]

    odd = meta[1]
    at_low, at_high = step == pairs, step == 2 * pairs - 1

    @pl.when((meta[0] > 1) & ((at_low & (odd == 1)) | (at_high & (odd == 0))))
    def _():
        emit(even_out)

    @pl.when((meta[0] > 1) & ((at_low & (odd == 0)) | (at_high & (odd == 1))))
    def _():
        emit(odd_out)


def order_kernel(meta, even_in, odd_in, edges):
    @pl.when(meta[0] > 1)
    def _():
        odd = meta[1]
        size = edges.shape[1]
        edges[1 - odd] = even_in[:size]
        edges[odd] = odd_in[:size]


def flat(ref, start, count):
    block = ref[start : start + count]
    return block.reshape(count * block.shape[1], block.shape[2])


def place(window, odd, even_in, odd_in):
    halo = even_in.shape[0]
    low, high = 0, window.shape[0] - halo
    window[pl.ds(jnp.where(odd == 1, low, high), halo)] = even_in[...]
    window[pl.ds(jnp.where(odd == 1, high, low), halo)] = odd_in[...]


def level(wide, base, window, solved, put, done=None):
    for p in range(wide.shape[0]):
        rows = dot(wide[p], flat(window, 2 * p, SPAN + 1)) + flat(base, 2 * p, 2).astype(jnp.float32)
        solved[put + 2 * p : put + 2 * p + 2] = rows.astype(solved.dtype).reshape(2, *solved.shape[1:])
        if done is not None:
            done(p)


def emit_sends(odd, solved, sends):
    if sends:
        size = sends[0].shape[0]
        count = solved.shape[0]
        by_parity(odd, lambda: solved[:size], lambda: solved[count - size :], *sends)


def store(level_a, solved, out, sems):
    copies = [
        pltpu.make_async_copy(source, out.at[at], sems.at[at]) for at, source in ((0, level_a), (1, solved))
    ]
    for copy in copies:
        copy.start()
    for copy in copies:
        copy.wait()


def exchanged_step(group, meta, own, even_in, odd_in, wide_b, base_b, solved, even_out, odd_out, level_a):
    @pl.when(meta[0] == group)
    def _():
        level_a[REACH : REACH + own.shape[0]] = own[...]
        place(level_a, meta[1], even_in, odd_in)
        level(wide_b, base_b, level_a, solved, 0)
        emit_sends(meta[1], solved, (even_out, odd_out))


def level_step(group, meta, centre, even_in, odd_in, first, wide_a, old_b, out, solved, even_out, odd_out, window, sems):
    @pl.when(meta[0] == group)
    def _():
        window[REACH : REACH + first.shape[0]] = centre[...]
        place(window, meta[1], even_in, odd_in)
        level(wide_a, first, window, solved, 0)
        emit_sends(meta[1], solved, (even_out, odd_out))

    @pl.when(meta[0] == group - 1)
    def _():
        store(first, old_b, out, sems)


def later_step(group, final, meta, centre, even_in, odd_in, edges, first, wide_a, wide_b, base_b, old_a, old_b, _, out, solved, solved_a, *rest):
    *sends, window, level_a, sems = rest
    count, block, cases = first.shape

    @pl.when(meta[0] == group)
    def _():
        odd = meta[1]
        halo = 2 * REACH
        window[halo : halo + count] = centre[...]
        place(window, odd, even_in, odd_in)
        level(wide_a, first, window.at[pl.ds(REACH, count + halo)], level_a, REACH)
        done, copies = None, []
        if final:
            copies = [pltpu.make_async_copy(level_a.at[pl.ds(REACH, count)], out.at[0], sems.at[0])]
            copies += [
                pltpu.make_async_copy(solved.at[pl.ds(2 * p, 2)], out.at[1, pl.ds(2 * p, 2)], sems.at[1 + p])
                for p in range(count // 2)
            ]
            copies[0].start()

            def done(p):
                copies[1 + p].start()

        parts = cases // block
        size = SPAN + parts
        for side in range(2):
            for i in range(REACH):
                put = side * (count + REACH) + i
                base = jnp.concatenate([edges[side, i * size + SPAN + part] for part in range(parts)], axis=1)
                blocks = jnp.concatenate([edges[side, i * size + d] for d in range(SPAN)], axis=1)
                row = dot(blocks, flat(window, put, SPAN)) + base.astype(jnp.float32)
                level_a[put] = row.astype(level_a.dtype)
        level(wide_b, base_b, level_a, solved, 0, done)
        if final:
            for copy in copies:
                copy.wait()
        else:
            emit_sends(odd, solved, sends)
            solved_a[...] = level_a[REACH : REACH + count]

    @pl.when(meta[0] == group - 1)
    def _():
        store(old_a, old_b, out, sems)


def shaped(shape, dtype=jnp.bfloat16):
    return jax.ShapeDtypeStruct(shape, dtype)


def params(**more):
    return pltpu.CompilerParams(vmem_limit_bytes=24 * 1024 * 1024, **more)


def in_hbm(value):
    return pltpu.with_memory_space_constraint(value, pltpu.HBM)


def after(values, *earlier):
    return lax.optimization_barrier((values, earlier))[0]


def per_device(chain, rows, right_side, lower_blocks, block_scale, diag_inverse, depend_rows):
    _, count, block, cases = right_side.shape
    terms = lower_blocks.shape[2]
    width = SPAN * block
    halo = 2 * REACH
    row = lax.axis_index("rows")
    meta = jnp.stack([lax.axis_index("chain"), row % 2, row * count]).astype(jnp.int32)
    depend = depend_rows.transpose(2, 0, 1)
    scale = block_scale.transpose(2, 0, 1)
    right_side, lower_blocks, diag_inverse = in_hbm(right_side), in_hbm(lower_blocks), in_hbm(diag_inverse)
    mates = (even_mate, odd_mate)

    def exchange(groups, values):
        return [lax.ppermute(value, AXES, inner_pairs(groups, mate, chain, rows)) for value, mate in zip(values, mates)]

    def travel(group, centre, sides):
        return [
            lax.ppermute(value, AXES, hop_pairs(group, mate, chain, rows))
            for value, mate in zip((centre, *sides), (same_row, *mates))
        ]

    def call(kernel, name, in_specs, out_shape, out_specs=None, **more):
        return pl.pallas_call(
            kernel,
            in_specs=in_specs,
            out_specs=out_specs or [VMEM] * len(out_shape),
            out_shape=out_shape,
            compiler_params=params(),
            name=name,
            **more,
        )

    whole, edge, wide_edge = (shaped((size, block, cases)) for size in (count, REACH, halo))

    first, *sides = call(
        first_kernel,
        "first_level",
        [SMEM, HBM, HBM],
        [whole, edge, edge],
        scratch_shapes=[
            pltpu.VMEM((count, block, block), jnp.bfloat16),
            pltpu.VMEM(whole.shape, jnp.bfloat16),
            pltpu.SemaphoreType.DMA((2, 2)),
        ],
    )(meta, diag_inverse, right_side)
    sides = exchange([0], sides)

    pairs = count // 2
    wide_shape = shaped((pairs, 2 * block, width + block))
    parts = REACH * (SPAN + cases // block)
    even_shape = shaped((parts, block, block))
    odd_shape = shaped((max(parts, count * cases // block + 1), block, block))

    def stage(i, meta):
        stays = (meta[0] == 0) | (i < pairs)
        return jnp.where(stays, 1, 0), jnp.where(stays, jnp.minimum(i, pairs - 1), i - pairs)

    def early(i):
        return jnp.minimum(i, pairs - 1)

    def late(i):
        return jnp.maximum(i - pairs, 0)

    wide_b, wide_a, base_b, *edge_w = pl.pallas_call(
        prepare_kernel,
        grid_spec=pltpu.PrefetchScalarGridSpec(
            num_scalar_prefetch=1,
            grid=(2 * pairs,),
            in_specs=[
                SMEM,
                SMEM,
                pl.BlockSpec((1, 2, terms, block, block), lambda i, meta: (*stage(i, meta), 0, 0, 0)),
                pl.BlockSpec((1, 2, block, block), lambda i, meta: (*stage(i, meta), 0, 0)),
                pl.BlockSpec((1, 2, block, cases), lambda i, meta: (1, early(i), 0, 0)),
                pl.BlockSpec((2, block, cases), lambda i, meta: (late(i), 0, 0)),
            ],
            out_specs=[
                pl.BlockSpec((1, 2 * block, width + block), lambda i, meta: (early(i), 0, 0)),
                pl.BlockSpec((1, 2 * block, width + block), lambda i, meta: (late(i), 0, 0)),
                pl.BlockSpec((2, block, cases), lambda i, meta: (early(i), 0, 0)),
                pl.BlockSpec(even_shape.shape, lambda i, meta: (0, 0, 0)),
                pl.BlockSpec(odd_shape.shape, lambda i, meta: (0, 0, 0)),
            ],
            scratch_shapes=[
                pltpu.VMEM((SPAN, block, block), jnp.float32),
                pltpu.VMEM((2, SPAN, block, block), jnp.bfloat16),
            ],
        ),
        out_shape=[wide_shape, wide_shape, shaped(whole.shape, jnp.float32), even_shape, odd_shape],
        compiler_params=params(),
        name="prepare",
    )(meta, depend, scale, lower_blocks, diag_inverse, right_side, first)

    padded = pltpu.VMEM((count + halo, block, cases), jnp.bfloat16)
    solved, *sends = call(
        functools.partial(exchanged_step, 0),
        "step_0",
        [SMEM] + [VMEM] * 5,
        [whole, edge, edge],
        scratch_shapes=[padded],
    )(meta, first, *sides, wide_b, base_b)
    arrived = travel(0, solved, sends)

    even_w, odd_w = edge_w
    even_w = lax.ppermute(after(even_w, sides), AXES, inner_pairs(range(2, chain), even_mate, chain, rows))
    odd_w = lax.ppermute(after(odd_w, even_w), AXES, inner_pairs(range(2, chain), odd_mate, chain, rows))
    arrived = after(arrived, even_w)
    edges = call(
        order_kernel,
        "order",
        [SMEM, VMEM, VMEM],
        [shaped((2, *even_shape.shape))],
    )(meta, even_w, odd_w)[0]

    out, made_a, *sides = call(
        functools.partial(level_step, 1),
        "step_1_a",
        [SMEM] + [VMEM] * 6,
        [shaped(right_side.shape), whole, edge, edge],
        [ANY] + [VMEM] * 3,
        scratch_shapes=[padded, pltpu.SemaphoreType.DMA((2,))],
    )(meta, *arrived, first, wide_a, solved)
    solved, *sends = call(
        functools.partial(exchanged_step, 1),
        "step_1_b",
        [SMEM] + [VMEM] * 5,
        [whole, wide_edge, wide_edge],
        scratch_shapes=[padded],
    )(meta, made_a, *exchange([1], sides), wide_b, base_b)

    for group in range(2, chain):
        final = group == chain - 1
        outs = [whole, whole] + ([] if final else [wide_edge] * 2)
        out, *now = call(
            functools.partial(later_step, group, final),
            f"step_{group}",
            [SMEM] + [VMEM] * 10 + [ANY],
            [shaped(right_side.shape), *outs],
            [ANY] + [VMEM] * len(outs),
            scratch_shapes=[
                pltpu.VMEM((count + 2 * halo, block, cases), jnp.bfloat16),
                padded,
                pltpu.SemaphoreType.DMA((1 + pairs,)),
            ],
            input_output_aliases={11: 0},
        )(meta, *travel(group - 1, solved, sends), edges, first, wide_a, wide_b, base_b, made_a, solved, out)
        solved, made_a, *sends = now
    return out


def solution(mesh):
    placed = (
        P("chain", "rows", None, None),
        P("chain", "rows", None, None, None),
        P("chain", "rows", None),
        P("chain", "rows", None, None),
        P("chain", "rows", None),
    )
    return jax.shard_map(
        functools.partial(per_device, mesh.shape["chain"], mesh.shape["rows"]),
        mesh=mesh,
        in_specs=placed,
        out_specs=P("chain", "rows", None, None),
        check_vma=False,
    )
```

time: 56.8 us -> 63.2 us (1.11); the launches traced: 56.6 us -> 62 us
  waiting for transfers between devices: 11.7 us -> 27.4 us
  starting transfers between devices: 27.4 us -> 18.8 us
  Pallas kernels: 17.2 us -> 15.6 us
    ppermute x0 -> x2, waiting for transfers between devices: none -> 18.3 us  [the longest x1 9.94 us: per_device(): lax.ppermute(after(odd_w, even_w), AXES, inner_pairs(range(2, chain), odd...]
    ppermute x15 -> x9, starting transfers between devices: 17.8 us -> 11.3 us  [travel(): lax.ppermute(value, AXES, hop_pairs(group, mate, chain, rows))]
    ppermute x6 -> x4, waiting for transfers between devices: 6.42 us -> 0.82 us  [exchange(): lax.ppermute(value, AXES, inner_pairs(groups, mate, chain, rows))]
    ppermute x6 -> x4, starting transfers between devices: 9.63 us -> 5.04 us  [exchange(): lax.ppermute(value, AXES, inner_pairs(groups, mate, chain, rows))]
    ppermute x15 -> x9, waiting for transfers between devices: 5.31 us -> 8.32 us  [travel(): lax.ppermute(value, AXES, hop_pairs(group, mate, chain, rows))]
    ppermute x0 -> x2, starting transfers between devices: none -> 2.45 us  [the longest x1 1.31 us: per_device(): lax.ppermute(after(even_w, sides), AXES, inner_pairs(range(2, chain), eve...]
    pallas_call x11 -> x8, Pallas kernels: 17.2 us -> 15.6 us  [the longest x1 7.11 us: per_device(): pl.pallas_call(prepare_kernel, grid_spec=pltpu.PrefetchScalarGridSpec(num...]
  transfers between devices with their start and end apart: 21 -> 15, of which waited for: 6 -> 6; matrix products, arithmetic and copies ran while one was open for 0% -> 0% of each run, Pallas kernels for 20% -> 13%
where the time goes in v5:
time: 63.2 us; the launch traced here: 62 us
  waiting for transfers between devices  27.4 us (43%)
  starting transfers between devices  18.8 us (30%)
  Pallas kernels  15.6 us (25%)
    ppermute x9, starting transfers between devices, travel(): lax.ppermute(value, AXES, hop_pairs(group, mate, chain, rows))  11.3 us
    ppermute x1, waiting for transfers between devices, per_device(): lax.ppermute(after(odd_w, even_w), AXES, inner_pairs(range(2, chain), odd...  9.94 us
    ppermute x1, waiting for transfers between devices, per_device(): lax.ppermute(after(even_w, sides), AXES, inner_pairs(range(2, chain), eve...  8.35 us
    ppermute x9, waiting for transfers between devices, travel(): lax.ppermute(value, AXES, hop_pairs(group, mate, chain, rows))  8.32 us
    pallas_call x1, Pallas kernels, per_device(): pl.pallas_call(prepare_kernel, grid_spec=pltpu.PrefetchScalarGridSpec(num...  7.11 us
    ppermute x4, starting transfers between devices, exchange(): lax.ppermute(value, AXES, inner_pairs(groups, mate, chain, rows))  5.04 us
    pallas_call x2, Pallas kernels, per_device(): call(functools.partial(later_step, group, final), f'step_{group}', [SMEM]...  4.18 us
    pallas_call x1, Pallas kernels, per_device(): call(first_kernel, 'first_level', [SMEM, HBM, HBM], [whole, edge, edge],...  2.04 us
  transfers between devices with their start and end apart: 15, of which 6 were waited for; matrix products, arithmetic and copies ran while one was open for 0% of the time, Pallas kernels for 13%

profile of v5, /device:TPU:11, one launch (start us, length us, event | category | flops | bytes accessed | tf_op | source)
XLA Modules:
  0.0 62.0 jit_solution(10523291929397940297)
XLA Ops:
  0.0 0.0 copy-start
  0.0 0.0 copy-start.1
  0.0 0.1 pad_add_fusion.meta
  0.1 2.0 %first_level.1 = (bf16[8,128,256]{2,1,0:T(8,128)(2,1)S(1)}, bf16[2,128,256]{2,1,0:T(8,128)(2,1)S(1)}, bf16[2,128,256]{2,1,0:T(8,128)(2,1)S(1)}) custom-call(s32[3]{0:T(128)S(1)} %pad_add_fusion.meta, bf16[2,8,128,128]{3,2,1,0:T(8,128)(2,1)} %inverse.1, bf16[2,8,128,256]{3,2,1,0:T(8,128)(2,1)} %right.1), custom_call_target="tpu_custom_call" | custom-call | tf_op jit(solution)/shard_map/first_level/pallas_call | solution.py:324
  2.1 0.3 collective-permute-start
  2.4 1.8 %collective-permute-start.1 = (bf16[2,128,256]{2,1,0:T(8,128)(2,1)S(1)}, bf16[2,128,256]{2,1,0:T(8,128)(2,1)S(1)}, u32[]{:S(2)}, u32[]{:S(2)}) collective-permute-start(bf16[2,128,256]{2,1,0:T(8,128)(2,1)S(1)} %get-tuple-element.36), channel_id=1, source_target_pairs={{0,8},{8,0},{16,24},{24,16},{1,2},{9,17},{17,25},{25,9},{2,1},{10,... | collective-permute-start | bytes 393224 | tf_op jit(solution)/shard_map/ppermute | solution.py:303
  4.2 0.0 copy-done
  4.2 0.0 copy-done.1
  4.2 7.1 %prepare.1 = (bf16[4,256,768]{2,1,0:T(8,128)(2,1)S(1)}, bf16[4,256,768]{2,1,0:T(8,128)(2,1)S(1)}, f32[8,128,256]{2,1,0:T(8,128)S(1)}, bf16[14,128,128]{2,1,0:T(8,128)(2,1)S(1)}, bf16[17,128,128]{2,1,0:T(8,128)(2,1)S(1)}) custom-call(s32[3]{0:T(128)S(1)} %pad_add_fusion.meta, s32[6,2,8]{2,1,0:T(2,128)S(1)} %bitcast.5, f32[6,2,8]{2,1,0:T(2,128)S(1)} %bitcast.6, ...), custom_call_target="tpu_custom_call" | custom-call | tf_op jit(solution)/shard_map/prepare/pallas_call | solution.py:353
  11.3 0.0 collective-permute-done.even_in
  11.3 0.0 collective-permute-done.1.odd_in
  11.4 0.6 step_0.1
  11.9 0.1 collective-permute-start.2
  12.0 1.3 %collective-permute-start.5 = (bf16[14,128,128]{2,1,0:T(8,128)(2,1)S(1)}, bf16[14,128,128]{2,1,0:T(8,128)(2,1)S(1)}, u32[]{:S(2)}, u32[]{:S(2)}) collective-permute-start(bf16[14,128,128]{2,1,0:T(8,128)(2,1)S(1)} %get-tuple-element.43), channel_id=1, source_target_pairs={{16,17},{24,25},{0,8},{8,0},{17,16},{25,24},{1,9},{9,1},{18,19},{2... | collective-permute-start | bytes 1376264 | tf_op jit(solution)/shard_map/ppermute | solution.py:394
  13.3 0.7 %collective-permute-start.3 = (bf16[2,128,256]{2,1,0:T(8,128)(2,1)S(1)}, bf16[2,128,256]{2,1,0:T(8,128)(2,1)S(1)}, u32[]{:S(2)}, u32[]{:S(2)}) collective-permute-start(bf16[2,128,256]{2,1,0:T(8,128)(2,1)S(1)} %get-tuple-element.40), channel_id=1, source_target_pairs={{0,9},{1,8},{2,11},{3,10},{4,13},{5,12},{6,15},{7,14},{8,0},{9,1},... | collective-permute-start | bytes 393224 | tf_op jit(solution)/shard_map/ppermute | solution.py:307
  14.0 0.0 collective-permute-start.4
  14.0 1.0 %collective-permute-done.3.even_in = bf16[2,128,256]{2,1,0:T(8,128)(2,1)S(1)} collective-permute-done((bf16[2,128,256]{2,1,0:T(8,128)(2,1)S(1)}, bf16[2,128,256]{2,1,0:T(8,128)(2,1)S(1)}, u32[]{:S(2)}, u32[]{:S(2)}) %collective-permute-start.3) | collective-permute-done | bytes 131104 | tf_op jit(solution)/shard_map/ppermute | solution.py:307
  15.0 0.4 collective-permute-done.4.odd_in
  15.4 8.4 %collective-permute-done.5.even_in = bf16[14,128,128]{2,1,0:T(8,128)(2,1)S(1)} collective-permute-done((bf16[14,128,128]{2,1,0:T(8,128)(2,1)S(1)}, bf16[14,128,128]{2,1,0:T(8,128)(2,1)S(1)}, u32[]{:S(2)}, u32[]{:S(2)}) %collective-permute-start.5) | collective-permute-done | bytes 458784 | tf_op jit(solution)/shard_map/ppermute | solution.py:394
  23.7 0.0 collective-permute-done.2.centre
  23.7 0.6 step_1_a.1
  24.3 0.1 collective-permute-start.6
  24.4 2.9 %collective-permute-start.7 = (bf16[2,128,256]{2,1,0:T(8,128)(2,1)S(1)}, bf16[2,128,256]{2,1,0:T(8,128)(2,1)S(1)}, u32[]{:S(2)}, u32[]{:S(2)}) collective-permute-start(bf16[2,128,256]{2,1,0:T(8,128)(2,1)S(1)} %get-tuple-element.50), channel_id=1, source_target_pairs={{0,8},{8,0},{16,24},{24,16},{9,10},{1,17},{17,25},{25,1},{10,9},{2... | collective-permute-start | bytes 393224 | tf_op jit(solution)/shard_map/ppermute | solution.py:303
  27.3 1.1 %collective-permute-start.11 = (bf16[17,128,128]{2,1,0:T(8,128)(2,1)S(1)}, bf16[17,128,128]{2,1,0:T(8,128)(2,1)S(1)}, u32[]{:S(2)}, u32[]{:S(2)}) collective-permute-start(bf16[17,128,128]{2,1,0:T(8,128)(2,1)S(1)} %get-tuple-element.55), channel_id=1, source_target_pairs={{0,8},{8,0},{16,24},{24,16},{17,18},{25,26},{1,9},{9,1},{18,17},{2... | collective-permute-start | bytes 1671176 | tf_op jit(solution)/shard_map/ppermute | solution.py:395
  28.4 0.0 collective-permute-done.6.even_in
  28.4 0.8 %collective-permute-done.7.odd_in = bf16[2,128,256]{2,1,0:T(8,128)(2,1)S(1)} collective-permute-done((bf16[2,128,256]{2,1,0:T(8,128)(2,1)S(1)}, bf16[2,128,256]{2,1,0:T(8,128)(2,1)S(1)}, u32[]{:S(2)}, u32[]{:S(2)}) %collective-permute-start.7) | collective-permute-done | bytes 131104 | tf_op jit(solution)/shard_map/ppermute | solution.py:303
  29.2 0.5 step_1_b.1
  29.8 2.5 %collective-permute-start.8 = (bf16[8,128,256]{2,1,0:T(8,128)(2,1)S(1)}, bf16[8,128,256]{2,1,0:T(8,128)(2,1)S(1)}, u32[]{:S(2)}, u32[]{:S(2)}) collective-permute-start(bf16[8,128,256]{2,1,0:T(8,128)(2,1)S(1)} %get-tuple-element.51.old_b), channel_id=1, source_target_pairs={{8,16},{9,17},{10,18},{11,19},{12,20},{13,21},{14,22},{15,23},{0,8... | collective-permute-start | bytes 1572872 | tf_op jit(solution)/shard_map/ppermute | solution.py:307
  32.3 0.1 collective-permute-start.9
  32.3 2.0 %collective-permute-start.10 = (bf16[4,128,256]{2,1,0:T(8,128)(2,1)S(1)}, bf16[4,128,256]{2,1,0:T(8,128)(2,1)S(1)}, u32[]{:S(2)}, u32[]{:S(2)}) collective-permute-start(bf16[4,128,256]{2,1,0:T(8,128)(2,1)S(1)} %get-tuple-element.53), channel_id=1, source_target_pairs={{8,16},{9,18},{10,17},{11,20},{12,19},{13,22},{14,21},{15,23},{0,8... | collective-permute-start | bytes 786440 | tf_op jit(solution)/shard_map/ppermute | solution.py:307
  34.4 9.9 %collective-permute-done.11.odd_in = bf16[17,128,128]{2,1,0:T(8,128)(2,1)S(1)} collective-permute-done((bf16[17,128,128]{2,1,0:T(8,128)(2,1)S(1)}, bf16[17,128,128]{2,1,0:T(8,128)(2,1)S(1)}, u32[]{:S(2)}, u32[]{:S(2)}) %collective-permute-start.11) | collective-permute-done | bytes 557088 | tf_op jit(solution)/shard_map/ppermute | solution.py:395
  44.3 0.6 order.1.edges
  44.9 0.0 collective-permute-done.9.even_in
  44.9 0.0 collective-permute-done.10.odd_in
  44.9 0.0 collective-permute-done.8.centre
  45.0 0.6 step_2.1
  45.6 4.3 %collective-permute-start.12 = (bf16[8,128,256]{2,1,0:T(8,128)(2,1)S(1)}, bf16[8,128,256]{2,1,0:T(8,128)(2,1)S(1)}, u32[]{:S(2)}, u32[]{:S(2)}) collective-permute-start(bf16[8,128,256]{2,1,0:T(8,128)(2,1)S(1)} %get-tuple-element.57.old_b), channel_id=1, source_target_pairs={{0,8},{1,9},{2,10},{3,11},{4,12},{5,13},{6,14},{7,15},{8,0},{9,1},... | collective-permute-start | bytes 1572872 | tf_op jit(solution)/shard_map/ppermute | solution.py:307
  49.8 0.1 collective-permute-start.13
  49.9 1.6 %collective-permute-start.14 = (bf16[4,128,256]{2,1,0:T(8,128)(2,1)S(1)}, bf16[4,128,256]{2,1,0:T(8,128)(2,1)S(1)}, u32[]{:S(2)}, u32[]{:S(2)}) collective-permute-start(bf16[4,128,256]{2,1,0:T(8,128)(2,1)S(1)} %get-tuple-element.59), channel_id=1, source_target_pairs={{0,8},{1,9},{2,10},{3,11},{4,12},{5,13},{6,14},{7,15},{8,0},{9,1},... | collective-permute-start | bytes 786440 | tf_op jit(solution)/shard_map/ppermute | solution.py:307
  51.5 7.0 %collective-permute-done.13.even_in = bf16[4,128,256]{2,1,0:T(8,128)(2,1)S(1)} collective-permute-done((bf16[4,128,256]{2,1,0:T(8,128)(2,1)S(1)}, bf16[4,128,256]{2,1,0:T(8,128)(2,1)S(1)}, u32[]{:S(2)}, u32[]{:S(2)}) %collective-permute-start.13) | collective-permute-done | bytes 262176 | tf_op jit(solution)/shard_map/ppermute | solution.py:307
  58.4 0.0 collective-permute-done.14.odd_in
  58.4 0.0 collective-permute-done.12.centre
  58.4 3.6 %step_3.1 = (bf16[2,8,128,256]{3,2,1,0:T(8,128)(2,1)}, bf16[8,128,256]{2,1,0:T(8,128)(2,1)}, bf16[8,128,256]{2,1,0:T(8,128)(2,1)}) custom-call(s32[3]{0:T(128)S(1)} %pad_add_fusion.meta, bf16[8,128,256]{2,1,0:T(8,128)(2,1)S(1)} %collective-permute-done.12.centre, ...), custom_call_target="tpu_custom_call", output_to_operand_aliasing={{0}: (11, {})} | custom-call | tf_op jit(solution)/shard_map/step_3/pallas_call | solution.py:423
Async XLA Ops:
  0.0 4.2 %copy-start = (s32[2,8,6]{1,0,2:T(2,128)S(1)}, s32[2,8,6]{1,0,2:T(2,128)}, u32[]{:S(2)}) copy-start(s32[2,8,6]{1,0,2:T(2,128)} %param.9) | copy-start | bytes 1156
  0.0 4.2 %copy-start.1 = (f32[2,8,6]{1,0,2:T(2,128)S(1)}, f32[2,8,6]{1,0,2:T(2,128)}, u32[]{:S(2)}) copy-start(f32[2,8,6]{1,0,2:T(2,128)} %param.7) | copy-start | bytes 1156
  2.1 9.2 %collective-permute-start = (bf16[2,128,256]{2,1,0:T(8,128)(2,1)S(1)}, bf16[2,128,256]{2,1,0:T(8,128)(2,1)S(1)}, u32[]{:S(2)}, u32[]{:S(2)}) collective-permute-start(bf16[2,128,256]{2,1,0:T(8,128)(2,1)S(1)} %get-tuple-element.35), channel_id=1, source_target_pairs={{0,1},{8,16},{16,24},{24,8},{1,0},{9,17},{17,25},{25,9},{2,3},{10,... | collective-permute-start | bytes 393224 | tf_op jit(solution)/shard_map/ppermute | solution.py:303
  2.4 8.9 %collective-permute-start.1 = (bf16[2,128,256]{2,1,0:T(8,128)(2,1)S(1)}, bf16[2,128,256]{2,1,0:T(8,128)(2,1)S(1)}, u32[]{:S(2)}, u32[]{:S(2)}) collective-permute-start(bf16[2,128,256]{2,1,0:T(8,128)(2,1)S(1)} %get-tuple-element.36), channel_id=1, source_target_pairs={{0,8},{8,0},{16,24},{24,16},{1,2},{9,17},{17,25},{25,9},{2,1},{10,... | collective-permute-start | bytes 393224 | tf_op jit(solution)/shard_map/ppermute | solution.py:303
  11.9 11.8 %collective-permute-start.2 = (bf16[8,128,256]{2,1,0:T(8,128)(2,1)S(1)}, bf16[8,128,256]{2,1,0:T(8,128)(2,1)S(1)}, u32[]{:S(2)}, u32[]{:S(2)}) collective-permute-start(bf16[8,128,256]{2,1,0:T(8,128)(2,1)S(1)} %get-tuple-element.39.old_b), channel_id=1, source_target_pairs={{0,8},{1,9},{2,10},{3,11},{4,12},{5,13},{6,14},{7,15},{8,0},{9,1},... | collective-permute-start | bytes 1572872 | tf_op jit(solution)/shard_map/ppermute | solution.py:307
  12.0 11.7 %collective-permute-start.5 = (bf16[14,128,128]{2,1,0:T(8,128)(2,1)S(1)}, bf16[14,128,128]{2,1,0:T(8,128)(2,1)S(1)}, u32[]{:S(2)}, u32[]{:S(2)}) collective-permute-start(bf16[14,128,128]{2,1,0:T(8,128)(2,1)S(1)} %get-tuple-element.43), channel_id=1, source_target_pairs={{16,17},{24,25},{0,8},{8,0},{17,16},{25,24},{1,9},{9,1},{18,19},{2... | collective-permute-start | bytes 1376264 | tf_op jit(solution)/shard_map/ppermute | solution.py:394
  13.3 1.7 %collective-permute-start.3 = (bf16[2,128,256]{2,1,0:T(8,128)(2,1)S(1)}, bf16[2,128,256]{2,1,0:T(8,128)(2,1)S(1)}, u32[]{:S(2)}, u32[]{:S(2)}) collective-permute-start(bf16[2,128,256]{2,1,0:T(8,128)(2,1)S(1)} %get-tuple-element.40), channel_id=1, source_target_pairs={{0,9},{1,8},{2,11},{3,10},{4,13},{5,12},{6,15},{7,14},{8,0},{9,1},... | collective-permute-start | bytes 393224 | tf_op jit(solution)/shard_map/ppermute | solution.py:307
  14.0 1.3 %collective-permute-start.4 = (bf16[2,128,256]{2,1,0:T(8,128)(2,1)S(1)}, bf16[2,128,256]{2,1,0:T(8,128)(2,1)S(1)}, u32[]{:S(2)}, u32[]{:S(2)}) collective-permute-start(bf16[2,128,256]{2,1,0:T(8,128)(2,1)S(1)} %get-tuple-element.41), channel_id=1, source_target_pairs={{0,8},{1,10},{2,9},{3,12},{4,11},{5,14},{6,13},{7,15},{8,0},{9,1},... | collective-permute-start | bytes 393224 | tf_op jit(solution)/shard_map/ppermute | solution.py:307
  24.3 4.1 %collective-permute-start.6 = (bf16[2,128,256]{2,1,0:T(8,128)(2,1)S(1)}, bf16[2,128,256]{2,1,0:T(8,128)(2,1)S(1)}, u32[]{:S(2)}, u32[]{:S(2)}) collective-permute-start(bf16[2,128,256]{2,1,0:T(8,128)(2,1)S(1)} %get-tuple-element.49), channel_id=1, source_target_pairs={{8,9},{0,16},{16,24},{24,0},{9,8},{1,17},{17,25},{25,1},{10,11},{2... | collective-permute-start | bytes 393224 | tf_op jit(solution)/shard_map/ppermute | solution.py:303
  24.4 4.8 %collective-permute-start.7 = (bf16[2,128,256]{2,1,0:T(8,128)(2,1)S(1)}, bf16[2,128,256]{2,1,0:T(8,128)(2,1)S(1)}, u32[]{:S(2)}, u32[]{:S(2)}) collective-permute-start(bf16[2,128,256]{2,1,0:T(8,128)(2,1)S(1)} %get-tuple-element.50), channel_id=1, source_target_pairs={{0,8},{8,0},{16,24},{24,16},{9,10},{1,17},{17,25},{25,1},{10,9},{2... | collective-permute-start | bytes 393224 | tf_op jit(solution)/shard_map/ppermute | solution.py:303
  27.3 17.0 %collective-permute-start.11 = (bf16[17,128,128]{2,1,0:T(8,128)(2,1)S(1)}, bf16[17,128,128]{2,1,0:T(8,128)(2,1)S(1)}, u32[]{:S(2)}, u32[]{:S(2)}) collective-permute-start(bf16[17,128,128]{2,1,0:T(8,128)(2,1)S(1)} %get-tuple-element.55), channel_id=1, source_target_pairs={{0,8},{8,0},{16,24},{24,16},{17,18},{25,26},{1,9},{9,1},{18,17},{2... | collective-permute-start | bytes 1671176 | tf_op jit(solution)/shard_map/ppermute | solution.py:395
  29.8 15.2 %collective-permute-start.8 = (bf16[8,128,256]{2,1,0:T(8,128)(2,1)S(1)}, bf16[8,128,256]{2,1,0:T(8,128)(2,1)S(1)}, u32[]{:S(2)}, u32[]{:S(2)}) collective-permute-start(bf16[8,128,256]{2,1,0:T(8,128)(2,1)S(1)} %get-tuple-element.51.old_b), channel_id=1, source_target_pairs={{8,16},{9,17},{10,18},{11,19},{12,20},{13,21},{14,22},{15,23},{0,8... | collective-permute-start | bytes 1572872 | tf_op jit(solution)/shard_map/ppermute | solution.py:307
  32.3 12.7 %collective-permute-start.9 = (bf16[4,128,256]{2,1,0:T(8,128)(2,1)S(1)}, bf16[4,128,256]{2,1,0:T(8,128)(2,1)S(1)}, u32[]{:S(2)}, u32[]{:S(2)}) collective-permute-start(bf16[4,128,256]{2,1,0:T(8,128)(2,1)S(1)} %get-tuple-element.52), channel_id=1, source_target_pairs={{8,17},{9,16},{10,19},{11,18},{12,21},{13,20},{14,23},{15,22},{0,8... | collective-permute-start | bytes 786440 | tf_op jit(solution)/shard_map/ppermute | solution.py:307
  32.3 12.6 %collective-permute-start.10 = (bf16[4,128,256]{2,1,0:T(8,128)(2,1)S(1)}, bf16[4,128,256]{2,1,0:T(8,128)(2,1)S(1)}, u32[]{:S(2)}, u32[]{:S(2)}) collective-permute-start(bf16[4,128,256]{2,1,0:T(8,128)(2,1)S(1)} %get-tuple-element.53), channel_id=1, source_target_pairs={{8,16},{9,18},{10,17},{11,20},{12,19},{13,22},{14,21},{15,23},{0,8... | collective-permute-start | bytes 786440 | tf_op jit(solution)/shard_map/ppermute | solution.py:307
  45.6 12.9 %collective-permute-start.12 = (bf16[8,128,256]{2,1,0:T(8,128)(2,1)S(1)}, bf16[8,128,256]{2,1,0:T(8,128)(2,1)S(1)}, u32[]{:S(2)}, u32[]{:S(2)}) collective-permute-start(bf16[8,128,256]{2,1,0:T(8,128)(2,1)S(1)} %get-tuple-element.57.old_b), channel_id=1, source_target_pairs={{0,8},{1,9},{2,10},{3,11},{4,12},{5,13},{6,14},{7,15},{8,0},{9,1},... | collective-permute-start | bytes 1572872 | tf_op jit(solution)/shard_map/ppermute | solution.py:307
  49.8 8.6 %collective-permute-start.13 = (bf16[4,128,256]{2,1,0:T(8,128)(2,1)S(1)}, bf16[4,128,256]{2,1,0:T(8,128)(2,1)S(1)}, u32[]{:S(2)}, u32[]{:S(2)}) collective-permute-start(bf16[4,128,256]{2,1,0:T(8,128)(2,1)S(1)} %get-tuple-element.58), channel_id=1, source_target_pairs={{0,8},{1,9},{2,10},{3,11},{4,12},{5,13},{6,14},{7,15},{8,0},{9,1},... | collective-permute-start | bytes 786440 | tf_op jit(solution)/shard_map/ppermute | solution.py:307
  49.9 8.5 %collective-permute-start.14 = (bf16[4,128,256]{2,1,0:T(8,128)(2,1)S(1)}, bf16[4,128,256]{2,1,0:T(8,128)(2,1)S(1)}, u32[]{:S(2)}, u32[]{:S(2)}) collective-permute-start(bf16[4,128,256]{2,1,0:T(8,128)(2,1)S(1)} %get-tuple-element.59), channel_id=1, source_target_pairs={{0,8},{1,9},{2,10},{3,11},{4,12},{5,13},{6,14},{7,15},{8,0},{9,1},... | collective-permute-start | bytes 786440 | tf_op jit(solution)/shard_map/ppermute | solution.py:307

commit v6 on v5

--- a/solution.py
+++ b/solution.py
@@ -46,17 +46,18 @@
     ]
 
 
-def inner_pairs(groups, mate, chain, rows):
+def inner_pairs(groups, mate, chain, rows, idle=None):
     pairs = []
+    paired = [r for r in range(rows) if mate(r, rows) != r]
     for r in range(rows):
-        target = mate(r, rows)
-        if target == r:
+        if r not in paired:
             moves = swap_groups(chain)
         else:
-            pairs += [(g * rows + r, g * rows + target) for g in groups]
-            others = [g for g in range(min(chain, 4)) if g not in groups]
-            moves = dict(zip(others, others[1:] + others[:1]))
-            moves.update(swap_groups(chain, [*range(4), *groups]))
+            moves = swap_groups(chain, [*groups, idle])
+            pairs += [(g * rows + r, g * rows + mate(r, rows)) for g in groups]
+            if idle is not None:
+                alike = [q for q in paired if q % 2 == r % 2]
+                pairs.append((idle * rows + r, idle * rows + alike[(alike.index(r) + 1) % len(alike)]))
         pairs += [(a * rows + r, b * rows + r) for a, b in moves.items()]
     return pairs
 
@@ -102,60 +103,84 @@
     by_parity(meta[1], lambda: solved[:REACH], lambda: solved[count - REACH :], *sends)
 
 
-def premultiply(meta, depend, scale, lower, inverse, wide, acc, level, q, half, keep=None):
+def premultiply(meta, depend, scale, lower, inverse, wide, acc, level, p, half):
     block = lower.shape[-1]
     terms = lower.shape[2]
+    q = 2 * p + half
     acc[...] = jnp.zeros_like(acc)
-    beside = jnp.concatenate([lower[0, half, k] for k in range(terms)], axis=1)
-    products = dot(inverse[0, half], beside)
+    beside = jnp.concatenate([lower[level, q, k] for k in range(terms)], axis=1)
+    products = dot(inverse[level, q], beside)
     for k in range(terms):
         column = jnp.clip(depend[k, level, q] - (meta[2] + q) + REACH, 0, SPAN - 1)
         acc[column] += scale[k, level, q] * products[:, k * block : (k + 1) * block]
     at = slice(half * block, (half + 1) * block)
     for d in range(SPAN):
-        value = (-acc[d]).astype(wide.dtype)
-        wide[0, at, (d + half) * block : (d + half + 1) * block] = value
-        if keep is not None:
-            keep[half, d] = value
+        wide[p, at, (d + half) * block : (d + half + 1) * block] = (-acc[d]).astype(wide.dtype)
     other = 0 if half else SPAN
-    wide[0, at, other * block : (other + 1) * block] = jnp.zeros((block, block), wide.dtype)
-
-
-def prepare_kernel(meta, depend, scale, lower, inverse, right, first, wide_b, wide_a, base, even_out, odd_out, acc, keep):
-    step = pl.program_id(0)
-    pairs = pl.num_programs(0) // 2
+    wide[p, at, other * block : (other + 1) * block] = jnp.zeros((block, block), wide.dtype)
+
+
+def prepare_kernel(meta, depend, scale, lower_hbm, inverse_hbm, right_hbm, first, wide_b, wide_a, base, even_out, odd_out, lower, inverse, right, acc, sems):
+    pairs = wide_a.shape[0]
     block = lower.shape[-1]
 
-    @pl.when(step < pairs)
-    def _():
+    def loads(level, p):
+        rows = pl.ds(2 * p, 2)
+        copies = [
+            pltpu.make_async_copy(lower_hbm.at[level, rows], lower.at[level, rows], sems.at[level, 0, p]),
+            pltpu.make_async_copy(inverse_hbm.at[level, rows], inverse.at[level, rows], sems.at[level, 1, p]),
+        ]
+        if level:
+            copies.append(pltpu.make_async_copy(right_hbm.at[1, rows], right.at[rows], sems.at[level, 2, p]))
+        return copies
+
+    def start(level):
+        for p in range(pairs):
+            for copy in loads(level, p):
+                copy.start()
+
+    start(1)
+
+    @pl.when(meta[0] > 0)
+    def _():
+        start(0)
+
+    @pl.loop(0, pairs)
+    def _(p):
+        for copy in loads(1, p):
+            copy.wait()
         for half in range(2):
-            premultiply(meta, depend, scale, lower, inverse, wide_b, acc, 1, 2 * step + half, half)
-            base[half] = dot(inverse[0, half], right[0, half])
-
-    @pl.when((step >= pairs) & (meta[0] > 0))
-    def _():
-        for half in range(2):
-            premultiply(meta, depend, scale, lower, inverse, wide_a, acc, 0, 2 * (step - pairs) + half, half, keep)
-
-    def emit(ref):
+            premultiply(meta, depend, scale, lower, inverse, wide_b, acc.at[half], 1, p, half)
+            base[2 * p + half] = dot(inverse[1, 2 * p + half], right[2 * p + half])
+
+    @pl.when(meta[0] > 0)
+    def _():
+        @pl.loop(0, pairs)
+        def _(p):
+            for copy in loads(0, p):
+                copy.wait()
+            for half in range(2):
+                premultiply(meta, depend, scale, lower, inverse, wide_a, acc.at[half], 0, p, half)
+
+    def emit(ref, p):
         parts = first.shape[2] // block
         size = SPAN + parts
         for half in range(2):
             for d in range(SPAN):
-                ref[half * size + d] = keep[half, d]
+                column = (d + half) * block
+                ref[half * size + d] = wide_a[p, half * block : (half + 1) * block, column : column + block]
             for part in range(parts):
-                ref[half * size + SPAN + part] = first[half, :, part * block : (part + 1) * block]
-
-    odd = meta[1]
-    at_low, at_high = step == pairs, step == 2 * pairs - 1
-
-    @pl.when((meta[0] > 1) & ((at_low & (odd == 1)) | (at_high & (odd == 0))))
-    def _():
-        emit(even_out)
-
-    @pl.when((meta[0] > 1) & ((at_low & (odd == 0)) | (at_high & (odd == 1))))
-    def _():
-        emit(odd_out)
+                ref[half * size + SPAN + part] = first[2 * p + half, :, part * block : (part + 1) * block]
+
+    @pl.when((meta[0] > 1) & (meta[1] == 1))
+    def _():
+        emit(even_out, 0)
+        emit(odd_out, pairs - 1)
+
+    @pl.when((meta[0] > 1) & (meta[1] == 0))
+    def _():
+        emit(odd_out, 0)
+        emit(even_out, pairs - 1)
 
 
 def order_kernel(meta, even_in, odd_in, edges):
@@ -289,7 +314,6 @@
 
 def per_device(chain, rows, right_side, lower_blocks, block_scale, diag_inverse, depend_rows):
     _, count, block, cases = right_side.shape
-    terms = lower_blocks.shape[2]
     width = SPAN * block
     halo = 2 * REACH
     row = lax.axis_index("rows")
@@ -299,8 +323,11 @@
     right_side, lower_blocks, diag_inverse = in_hbm(right_side), in_hbm(lower_blocks), in_hbm(diag_inverse)
     mates = (even_mate, odd_mate)
 
-    def exchange(groups, values):
-        return [lax.ppermute(value, AXES, inner_pairs(groups, mate, chain, rows)) for value, mate in zip(values, mates)]
+    def exchange(groups, values, idle):
+        return [
+            lax.ppermute(value, AXES, inner_pairs(groups, mate, chain, rows, idle))
+            for value, mate in zip(values, mates)
+        ]
 
     def travel(group, centre, sides):
         return [
@@ -332,7 +359,7 @@
             pltpu.SemaphoreType.DMA((2, 2)),
         ],
     )(meta, diag_inverse, right_side)
-    sides = exchange([0], sides)
+    sides = exchange([0], sides, 1)
 
     pairs = count // 2
     wide_shape = shaped((pairs, 2 * block, width + block))
@@ -340,44 +367,18 @@
     even_shape = shaped((parts, block, block))
     odd_shape = shaped((max(parts, count * cases // block + 1), block, block))
 
-    def stage(i, meta):
-        stays = (meta[0] == 0) | (i < pairs)
-        return jnp.where(stays, 1, 0), jnp.where(stays, jnp.minimum(i, pairs - 1), i - pairs)
-
-    def early(i):
-        return jnp.minimum(i, pairs - 1)
-
-    def late(i):
-        return jnp.maximum(i - pairs, 0)
-
-    wide_b, wide_a, base_b, *edge_w = pl.pallas_call(
+    wide_b, wide_a, base_b, *edge_w = call(
         prepare_kernel,
-        grid_spec=pltpu.PrefetchScalarGridSpec(
-            num_scalar_prefetch=1,
-            grid=(2 * pairs,),
-            in_specs=[
-                SMEM,
-                SMEM,
-                pl.BlockSpec((1, 2, terms, block, block), lambda i, meta: (*stage(i, meta), 0, 0, 0)),
-                pl.BlockSpec((1, 2, block, block), lambda i, meta: (*stage(i, meta), 0, 0)),
-                pl.BlockSpec((1, 2, block, cases), lambda i, meta: (1, early(i), 0, 0)),
-                pl.BlockSpec((2, block, cases), lambda i, meta: (late(i), 0, 0)),
-            ],
-            out_specs=[
-                pl.BlockSpec((1, 2 * block, width + block), lambda i, meta: (early(i), 0, 0)),
-                pl.BlockSpec((1, 2 * block, width + block), lambda i, meta: (late(i), 0, 0)),
-                pl.BlockSpec((2, block, cases), lambda i, meta: (early(i), 0, 0)),
-                pl.BlockSpec(even_shape.shape, lambda i, meta: (0, 0, 0)),
-                pl.BlockSpec(odd_shape.shape, lambda i, meta: (0, 0, 0)),
-            ],
-            scratch_shapes=[
-                pltpu.VMEM((SPAN, block, block), jnp.float32),
-                pltpu.VMEM((2, SPAN, block, block), jnp.bfloat16),
-            ],
-        ),
-        out_shape=[wide_shape, wide_shape, shaped(whole.shape, jnp.float32), even_shape, odd_shape],
-        compiler_params=params(),
-        name="prepare",
+        "prepare",
+        [SMEM, SMEM, SMEM, HBM, HBM, HBM, VMEM],
+        [wide_shape, wide_shape, shaped(whole.shape, jnp.float32), even_shape, odd_shape],
+        scratch_shapes=[
+            pltpu.VMEM(lower_blocks.shape, jnp.bfloat16),
+            pltpu.VMEM(diag_inverse.shape, jnp.bfloat16),
+            pltpu.VMEM(whole.shape, jnp.bfloat16),
+            pltpu.VMEM((2, SPAN, block, block), jnp.float32),
+            pltpu.SemaphoreType.DMA((2, 3, pairs)),
+        ],
     )(meta, depend, scale, lower_blocks, diag_inverse, right_side, first)
 
     padded = pltpu.VMEM((count + halo, block, cases), jnp.bfloat16)
@@ -415,7 +416,7 @@
         [SMEM] + [VMEM] * 5,
         [whole, wide_edge, wide_edge],
         scratch_shapes=[padded],
-    )(meta, made_a, *exchange([1], sides), wide_b, base_b)
+    )(meta, made_a, *exchange([1], sides, 0), wide_b, base_b)
 
     for group in range(2, chain):
         final = group == chain - 1

time: 63.2 us -> 59.4 us (0.940); the launches traced: 62 us -> 59.2 us
  starting transfers between devices: 18.8 us -> 13.2 us
  waiting for transfers between devices: 27.4 us -> 32.2 us
  Pallas kernels: 15.6 us -> 13.6 us
    ppermute x1, waiting for transfers between devices: 9.94 us -> 14.8 us  [per_device(): lax.ppermute(after(odd_w, even_w), AXES, inner_pairs(range(2, chain), odd...]
    ppermute x4, starting transfers between devices: 5.04 us -> 1.75 us  [exchange(): lax.ppermute(value, AXES, inner_pairs(groups, mate, chain, rows, idle))]
    ppermute x9, starting transfers between devices: 11.3 us -> 9.03 us  [travel(): lax.ppermute(value, AXES, hop_pairs(group, mate, chain, rows))]
    pallas_call x1, Pallas kernels: 7.11 us -> 5.1 us  [per_device(): call(prepare_kernel, 'prepare', [SMEM, SMEM, SMEM, HBM, HBM, HBM, VMEM],...]
    ppermute x1, waiting for transfers between devices: 8.35 us -> 9.14 us  [per_device(): lax.ppermute(after(even_w, sides), AXES, inner_pairs(range(2, chain), eve...]
    ppermute x4, waiting for transfers between devices: 0.82 us -> 0.16 us  [exchange(): lax.ppermute(value, AXES, inner_pairs(groups, mate, chain, rows, idle))]
  transfers between devices with their start and end apart: 15 -> 15, of which waited for: 6 -> 6; matrix products, arithmetic and copies ran while one was open for 0% -> 0% of each run, Pallas kernels for 13% -> 11%
where the time goes in v6:
time: 59.4 us; the launch traced here: 59.2 us
  waiting for transfers between devices  32.2 us (54%)
  Pallas kernels  13.6 us (23%)
  starting transfers between devices  13.2 us (22%)
    ppermute x1, waiting for transfers between devices, per_device(): lax.ppermute(after(odd_w, even_w), AXES, inner_pairs(range(2, chain), odd...  14.8 us
    ppermute x1, waiting for transfers between devices, per_device(): lax.ppermute(after(even_w, sides), AXES, inner_pairs(range(2, chain), eve...  9.14 us
    ppermute x9, starting transfers between devices, travel(): lax.ppermute(value, AXES, hop_pairs(group, mate, chain, rows))  9.03 us
    ppermute x9, waiting for transfers between devices, travel(): lax.ppermute(value, AXES, hop_pairs(group, mate, chain, rows))  8.16 us
    pallas_call x1, Pallas kernels, per_device(): call(prepare_kernel, 'prepare', [SMEM, SMEM, SMEM, HBM, HBM, HBM, VMEM],...  5.1 us
    pallas_call x2, Pallas kernels, per_device(): call(functools.partial(later_step, group, final), f'step_{group}', [SMEM]...  4.18 us
    pallas_call x1, Pallas kernels, per_device(): call(first_kernel, 'first_level', [SMEM, HBM, HBM], [whole, edge, edge],...  2.04 us
    ppermute x4, starting transfers between devices, exchange(): lax.ppermute(value, AXES, inner_pairs(groups, mate, chain, rows, idle))  1.75 us
  transfers between devices with their start and end apart: 15, of which 6 were waited for; matrix products, arithmetic and copies ran while one was open for 0% of the time, Pallas kernels for 11%

profile of v6, /device:TPU:11, one launch (start us, length us, event | category | flops | bytes accessed | tf_op | source)
XLA Modules:
  0.0 59.2 jit_solution(3498390748371595804)
XLA Ops:
  0.0 0.0 copy-start
  0.0 0.0 copy-start.1
  0.0 0.1 pad_add_fusion.meta
  0.1 2.0 %first_level.1 = (bf16[8,128,256]{2,1,0:T(8,128)(2,1)S(1)}, bf16[2,128,256]{2,1,0:T(8,128)(2,1)S(1)}, bf16[2,128,256]{2,1,0:T(8,128)(2,1)S(1)}) custom-call(s32[3]{0:T(128)S(1)} %pad_add_fusion.meta, bf16[2,8,128,128]{3,2,1,0:T(8,128)(2,1)} %inverse_hbm.3, bf16[2,8,128,256]{3,2,1,0:T(8,128)(2,1)} %right_hbm.3), custom_call_target="tpu_custom_call" | custom-call | tf_op jit(solution)/shard_map/first_level/pallas_call | solution.py:351
  2.1 0.7 %collective-permute-start = (bf16[2,128,256]{2,1,0:T(8,128)(2,1)S(1)}, bf16[2,128,256]{2,1,0:T(8,128)(2,1)S(1)}, u32[]{:S(2)}, u32[]{:S(2)}) collective-permute-start(bf16[2,128,256]{2,1,0:T(8,128)(2,1)S(1)} %get-tuple-element.35), channel_id=1, source_target_pairs={{0,1},{8,10},{16,24},{24,16},{1,0},{9,11},{17,25},{25,17},{2,3},{1... | collective-permute-start | bytes 393224 | tf_op jit(solution)/shard_map/ppermute | solution.py:328
  2.9 0.1 collective-permute-start.1
  2.9 0.0 copy-done
  2.9 0.0 copy-done.1
  2.9 5.1 %prepare.1 = (bf16[4,256,768]{2,1,0:T(8,128)(2,1)S(1)}, bf16[4,256,768]{2,1,0:T(8,128)(2,1)S(1)}, f32[8,128,256]{2,1,0:T(8,128)S(1)}, bf16[14,128,128]{2,1,0:T(8,128)(2,1)S(1)}, bf16[17,128,128]{2,1,0:T(8,128)(2,1)S(1)}) custom-call(s32[3]{0:T(128)S(1)} %pad_add_fusion.meta, s32[6,2,8]{2,1,0:T(2,128)S(1)} %bitcast.5, f32[6,2,8]{2,1,0:T(2,128)S(1)} %bitcast.6, ...), custom_call_target="tpu_custom_call" | custom-call | tf_op jit(solution)/shard_map/prepare/pallas_call | solution.py:370
  8.0 0.0 collective-permute-done.even_in
  8.0 0.0 collective-permute-done.1.odd_in
  8.1 0.6 step_0.1
  8.6 0.5 collective-permute-start.2
  9.1 1.3 %collective-permute-start.5 = (bf16[14,128,128]{2,1,0:T(8,128)(2,1)S(1)}, bf16[14,128,128]{2,1,0:T(8,128)(2,1)S(1)}, u32[]{:S(2)}, u32[]{:S(2)}) collective-permute-start(bf16[14,128,128]{2,1,0:T(8,128)(2,1)S(1)} %get-tuple-element.43), channel_id=1, source_target_pairs={{16,17},{24,25},{0,8},{8,0},{17,16},{25,24},{1,9},{9,1},{18,19},{2... | collective-permute-start | bytes 1376264 | tf_op jit(solution)/shard_map/ppermute | solution.py:395
  10.4 0.3 collective-permute-start.3
  10.7 0.2 collective-permute-start.4
  10.9 0.8 %collective-permute-done.3.even_in = bf16[2,128,256]{2,1,0:T(8,128)(2,1)S(1)} collective-permute-done((bf16[2,128,256]{2,1,0:T(8,128)(2,1)S(1)}, bf16[2,128,256]{2,1,0:T(8,128)(2,1)S(1)}, u32[]{:S(2)}, u32[]{:S(2)}) %collective-permute-start.3) | collective-permute-done | bytes 131104 | tf_op jit(solution)/shard_map/ppermute | solution.py:334
  11.7 0.3 collective-permute-done.4.odd_in
  12.1 9.1 %collective-permute-done.5.even_in = bf16[14,128,128]{2,1,0:T(8,128)(2,1)S(1)} collective-permute-done((bf16[14,128,128]{2,1,0:T(8,128)(2,1)S(1)}, bf16[14,128,128]{2,1,0:T(8,128)(2,1)S(1)}, u32[]{:S(2)}, u32[]{:S(2)}) %collective-permute-start.5) | collective-permute-done | bytes 458784 | tf_op jit(solution)/shard_map/ppermute | solution.py:395
  21.2 0.0 collective-permute-done.2.centre
  21.2 0.6 step_1_a.1
  21.8 0.9 %collective-permute-start.6 = (bf16[2,128,256]{2,1,0:T(8,128)(2,1)S(1)}, bf16[2,128,256]{2,1,0:T(8,128)(2,1)S(1)}, u32[]{:S(2)}, u32[]{:S(2)}) collective-permute-start(bf16[2,128,256]{2,1,0:T(8,128)(2,1)S(1)} %get-tuple-element.49), channel_id=1, source_target_pairs={{8,9},{0,2},{16,24},{24,16},{9,8},{1,3},{17,25},{25,17},{10,11},{2... | collective-permute-start | bytes 393224 | tf_op jit(solution)/shard_map/ppermute | solution.py:328
  22.7 0.1 collective-permute-start.7
  22.8 1.1 %collective-permute-start.11 = (bf16[17,128,128]{2,1,0:T(8,128)(2,1)S(1)}, bf16[17,128,128]{2,1,0:T(8,128)(2,1)S(1)}, u32[]{:S(2)}, u32[]{:S(2)}) collective-permute-start(bf16[17,128,128]{2,1,0:T(8,128)(2,1)S(1)} %get-tuple-element.55), channel_id=1, source_target_pairs={{0,8},{8,0},{16,24},{24,16},{17,18},{25,26},{1,9},{9,1},{18,17},{2... | collective-permute-start | bytes 1671176 | tf_op jit(solution)/shard_map/ppermute | solution.py:396
  23.9 0.0 collective-permute-done.6.even_in
  23.9 0.2 collective-permute-done.7.odd_in
  24.1 0.5 step_1_b.1
  24.6 2.4 %collective-permute-start.8 = (bf16[8,128,256]{2,1,0:T(8,128)(2,1)S(1)}, bf16[8,128,256]{2,1,0:T(8,128)(2,1)S(1)}, u32[]{:S(2)}, u32[]{:S(2)}) collective-permute-start(bf16[8,128,256]{2,1,0:T(8,128)(2,1)S(1)} %get-tuple-element.51.old_b), channel_id=1, source_target_pairs={{8,16},{9,17},{10,18},{11,19},{12,20},{13,21},{14,22},{15,23},{0,8... | collective-permute-start | bytes 1572872 | tf_op jit(solution)/shard_map/ppermute | solution.py:334
  27.0 0.9 %collective-permute-start.9 = (bf16[4,128,256]{2,1,0:T(8,128)(2,1)S(1)}, bf16[4,128,256]{2,1,0:T(8,128)(2,1)S(1)}, u32[]{:S(2)}, u32[]{:S(2)}) collective-permute-start(bf16[4,128,256]{2,1,0:T(8,128)(2,1)S(1)} %get-tuple-element.52), channel_id=1, source_target_pairs={{8,17},{9,16},{10,19},{11,18},{12,21},{13,20},{14,23},{15,22},{0,8... | collective-permute-start | bytes 786440 | tf_op jit(solution)/shard_map/ppermute | solution.py:334
  27.9 0.1 collective-permute-start.10
  28.0 14.8 %collective-permute-done.11.odd_in = bf16[17,128,128]{2,1,0:T(8,128)(2,1)S(1)} collective-permute-done((bf16[17,128,128]{2,1,0:T(8,128)(2,1)S(1)}, bf16[17,128,128]{2,1,0:T(8,128)(2,1)S(1)}, u32[]{:S(2)}, u32[]{:S(2)}) %collective-permute-start.11) | collective-permute-done | bytes 557088 | tf_op jit(solution)/shard_map/ppermute | solution.py:396
  42.7 0.6 %order.1.edges = bf16[2,14,128,128]{3,2,1,0:T(8,128)(2,1)S(1)} custom-call(s32[3]{0:T(128)S(1)} %pad_add_fusion.meta, bf16[14,128,128]{2,1,0:T(8,128)(2,1)S(1)} %collective-permute-done.5.even_in, bf16[17,128,128]{2,1,0:T(8,128)(2,1)S(1)} %collective-permute-done.11.odd_in), custom_call_target="tpu_custom_call" | custom-call | tf_op jit(solution)/shard_map/order/pallas_call | solution.py:398
  43.4 0.0 collective-permute-done.9.even_in
  43.4 0.0 collective-permute-done.10.odd_in
  43.4 0.0 collective-permute-done.8.centre
  43.4 0.6 %step_2.1 = (bf16[2,8,128,256]{3,2,1,0:T(8,128)(2,1)}, bf16[8,128,256]{2,1,0:T(8,128)(2,1)S(1)}, bf16[8,128,256]{2,1,0:T(8,128)(2,1)S(1)}, bf16[4,128,256]{2,1,0:T(8,128)(2,1)S(1)}, bf16[4,128,256]{2,1,0:T(8,128)(2,1)S(1)}) custom-call(s32[3]{0:T(128)S(1)} %pad_add_fusion.meta, ...), custom_call_target="tpu_custom_call", output_to_operand_aliasing={{0}: (11, {})} | custom-call | tf_op jit(solution)/shard_map/step_2/pallas_call | solution.py:424
  44.0 3.0 %collective-permute-start.12 = (bf16[8,128,256]{2,1,0:T(8,128)(2,1)S(1)}, bf16[8,128,256]{2,1,0:T(8,128)(2,1)S(1)}, u32[]{:S(2)}, u32[]{:S(2)}) collective-permute-start(bf16[8,128,256]{2,1,0:T(8,128)(2,1)S(1)} %get-tuple-element.57.old_b), channel_id=1, source_target_pairs={{0,8},{1,9},{2,10},{3,11},{4,12},{5,13},{6,14},{7,15},{8,0},{9,1},... | collective-permute-start | bytes 1572872 | tf_op jit(solution)/shard_map/ppermute | solution.py:334
  47.0 0.1 collective-permute-start.13
  47.1 1.6 %collective-permute-start.14 = (bf16[4,128,256]{2,1,0:T(8,128)(2,1)S(1)}, bf16[4,128,256]{2,1,0:T(8,128)(2,1)S(1)}, u32[]{:S(2)}, u32[]{:S(2)}) collective-permute-start(bf16[4,128,256]{2,1,0:T(8,128)(2,1)S(1)} %get-tuple-element.59), channel_id=1, source_target_pairs={{0,8},{1,9},{2,10},{3,11},{4,12},{5,13},{6,14},{7,15},{8,0},{9,1},... | collective-permute-start | bytes 786440 | tf_op jit(solution)/shard_map/ppermute | solution.py:334
  48.7 7.0 %collective-permute-done.13.even_in = bf16[4,128,256]{2,1,0:T(8,128)(2,1)S(1)} collective-permute-done((bf16[4,128,256]{2,1,0:T(8,128)(2,1)S(1)}, bf16[4,128,256]{2,1,0:T(8,128)(2,1)S(1)}, u32[]{:S(2)}, u32[]{:S(2)}) %collective-permute-start.13) | collective-permute-done | bytes 262176 | tf_op jit(solution)/shard_map/ppermute | solution.py:334
  55.6 0.0 collective-permute-done.14.odd_in
  55.6 0.0 collective-permute-done.12.centre
  55.6 3.6 %step_3.1 = (bf16[2,8,128,256]{3,2,1,0:T(8,128)(2,1)}, bf16[8,128,256]{2,1,0:T(8,128)(2,1)}, bf16[8,128,256]{2,1,0:T(8,128)(2,1)}) custom-call(s32[3]{0:T(128)S(1)} %pad_add_fusion.meta, bf16[8,128,256]{2,1,0:T(8,128)(2,1)S(1)} %collective-permute-done.12.centre, ...), custom_call_target="tpu_custom_call", output_to_operand_aliasing={{0}: (11, {})} | custom-call | tf_op jit(solution)/shard_map/step_3/pallas_call | solution.py:424
Async XLA Ops:
  0.0 2.9 %copy-start = (s32[2,8,6]{1,0,2:T(2,128)S(1)}, s32[2,8,6]{1,0,2:T(2,128)}, u32[]{:S(2)}) copy-start(s32[2,8,6]{1,0,2:T(2,128)} %param.9) | copy-start | bytes 1156
  0.0 2.9 %copy-start.1 = (f32[2,8,6]{1,0,2:T(2,128)S(1)}, f32[2,8,6]{1,0,2:T(2,128)}, u32[]{:S(2)}) copy-start(f32[2,8,6]{1,0,2:T(2,128)} %param.7) | copy-start | bytes 1156
  2.1 5.9 %collective-permute-start = (bf16[2,128,256]{2,1,0:T(8,128)(2,1)S(1)}, bf16[2,128,256]{2,1,0:T(8,128)(2,1)S(1)}, u32[]{:S(2)}, u32[]{:S(2)}) collective-permute-start(bf16[2,128,256]{2,1,0:T(8,128)(2,1)S(1)} %get-tuple-element.35), channel_id=1, source_target_pairs={{0,1},{8,10},{16,24},{24,16},{1,0},{9,11},{17,25},{25,17},{2,3},{1... | collective-permute-start | bytes 393224 | tf_op jit(solution)/shard_map/ppermute | solution.py:328
  2.9 5.2 %collective-permute-start.1 = (bf16[2,128,256]{2,1,0:T(8,128)(2,1)S(1)}, bf16[2,128,256]{2,1,0:T(8,128)(2,1)S(1)}, u32[]{:S(2)}, u32[]{:S(2)}) collective-permute-start(bf16[2,128,256]{2,1,0:T(8,128)(2,1)S(1)} %get-tuple-element.36), channel_id=1, source_target_pairs={{0,8},{8,0},{16,24},{24,16},{1,2},{9,11},{17,25},{25,17},{2,1},{10... | collective-permute-start | bytes 393224 | tf_op jit(solution)/shard_map/ppermute | solution.py:328
  8.6 12.6 %collective-permute-start.2 = (bf16[8,128,256]{2,1,0:T(8,128)(2,1)S(1)}, bf16[8,128,256]{2,1,0:T(8,128)(2,1)S(1)}, u32[]{:S(2)}, u32[]{:S(2)}) collective-permute-start(bf16[8,128,256]{2,1,0:T(8,128)(2,1)S(1)} %get-tuple-element.39.old_b), channel_id=1, source_target_pairs={{0,8},{1,9},{2,10},{3,11},{4,12},{5,13},{6,14},{7,15},{8,0},{9,1},... | collective-permute-start | bytes 1572872 | tf_op jit(solution)/shard_map/ppermute | solution.py:334
  9.1 12.1 %collective-permute-start.5 = (bf16[14,128,128]{2,1,0:T(8,128)(2,1)S(1)}, bf16[14,128,128]{2,1,0:T(8,128)(2,1)S(1)}, u32[]{:S(2)}, u32[]{:S(2)}) collective-permute-start(bf16[14,128,128]{2,1,0:T(8,128)(2,1)S(1)} %get-tuple-element.43), channel_id=1, source_target_pairs={{16,17},{24,25},{0,8},{8,0},{17,16},{25,24},{1,9},{9,1},{18,19},{2... | collective-permute-start | bytes 1376264 | tf_op jit(solution)/shard_map/ppermute | solution.py:395
  10.4 1.3 %collective-permute-start.3 = (bf16[2,128,256]{2,1,0:T(8,128)(2,1)S(1)}, bf16[2,128,256]{2,1,0:T(8,128)(2,1)S(1)}, u32[]{:S(2)}, u32[]{:S(2)}) collective-permute-start(bf16[2,128,256]{2,1,0:T(8,128)(2,1)S(1)} %get-tuple-element.40), channel_id=1, source_target_pairs={{0,9},{1,8},{2,11},{3,10},{4,13},{5,12},{6,15},{7,14},{8,0},{9,1},... | collective-permute-start | bytes 393224 | tf_op jit(solution)/shard_map/ppermute | solution.py:334
  10.7 1.3 %collective-permute-start.4 = (bf16[2,128,256]{2,1,0:T(8,128)(2,1)S(1)}, bf16[2,128,256]{2,1,0:T(8,128)(2,1)S(1)}, u32[]{:S(2)}, u32[]{:S(2)}) collective-permute-start(bf16[2,128,256]{2,1,0:T(8,128)(2,1)S(1)} %get-tuple-element.41), channel_id=1, source_target_pairs={{0,8},{1,10},{2,9},{3,12},{4,11},{5,14},{6,13},{7,15},{8,0},{9,1},... | collective-permute-start | bytes 393224 | tf_op jit(solution)/shard_map/ppermute | solution.py:334
  21.8 2.1 %collective-permute-start.6 = (bf16[2,128,256]{2,1,0:T(8,128)(2,1)S(1)}, bf16[2,128,256]{2,1,0:T(8,128)(2,1)S(1)}, u32[]{:S(2)}, u32[]{:S(2)}) collective-permute-start(bf16[2,128,256]{2,1,0:T(8,128)(2,1)S(1)} %get-tuple-element.49), channel_id=1, source_target_pairs={{8,9},{0,2},{16,24},{24,16},{9,8},{1,3},{17,25},{25,17},{10,11},{2... | collective-permute-start | bytes 393224 | tf_op jit(solution)/shard_map/ppermute | solution.py:328
  22.7 1.3 %collective-permute-start.7 = (bf16[2,128,256]{2,1,0:T(8,128)(2,1)S(1)}, bf16[2,128,256]{2,1,0:T(8,128)(2,1)S(1)}, u32[]{:S(2)}, u32[]{:S(2)}) collective-permute-start(bf16[2,128,256]{2,1,0:T(8,128)(2,1)S(1)} %get-tuple-element.50), channel_id=1, source_target_pairs={{0,8},{8,0},{16,24},{24,16},{9,10},{1,3},{17,25},{25,17},{10,9},{2... | collective-permute-start | bytes 393224 | tf_op jit(solution)/shard_map/ppermute | solution.py:328
  22.8 20.0 %collective-permute-start.11 = (bf16[17,128,128]{2,1,0:T(8,128)(2,1)S(1)}, bf16[17,128,128]{2,1,0:T(8,128)(2,1)S(1)}, u32[]{:S(2)}, u32[]{:S(2)}) collective-permute-start(bf16[17,128,128]{2,1,0:T(8,128)(2,1)S(1)} %get-tuple-element.55), channel_id=1, source_target_pairs={{0,8},{8,0},{16,24},{24,16},{17,18},{25,26},{1,9},{9,1},{18,17},{2... | collective-permute-start | bytes 1671176 | tf_op jit(solution)/shard_map/ppermute | solution.py:396
  24.6 18.8 %collective-permute-start.8 = (bf16[8,128,256]{2,1,0:T(8,128)(2,1)S(1)}, bf16[8,128,256]{2,1,0:T(8,128)(2,1)S(1)}, u32[]{:S(2)}, u32[]{:S(2)}) collective-permute-start(bf16[8,128,256]{2,1,0:T(8,128)(2,1)S(1)} %get-tuple-element.51.old_b), channel_id=1, source_target_pairs={{8,16},{9,17},{10,18},{11,19},{12,20},{13,21},{14,22},{15,23},{0,8... | collective-permute-start | bytes 1572872 | tf_op jit(solution)/shard_map/ppermute | solution.py:334
  27.0 16.4 %collective-permute-start.9 = (bf16[4,128,256]{2,1,0:T(8,128)(2,1)S(1)}, bf16[4,128,256]{2,1,0:T(8,128)(2,1)S(1)}, u32[]{:S(2)}, u32[]{:S(2)}) collective-permute-start(bf16[4,128,256]{2,1,0:T(8,128)(2,1)S(1)} %get-tuple-element.52), channel_id=1, source_target_pairs={{8,17},{9,16},{10,19},{11,18},{12,21},{13,20},{14,23},{15,22},{0,8... | collective-permute-start | bytes 786440 | tf_op jit(solution)/shard_map/ppermute | solution.py:334
  27.9 15.5 %collective-permute-start.10 = (bf16[4,128,256]{2,1,0:T(8,128)(2,1)S(1)}, bf16[4,128,256]{2,1,0:T(8,128)(2,1)S(1)}, u32[]{:S(2)}, u32[]{:S(2)}) collective-permute-start(bf16[4,128,256]{2,1,0:T(8,128)(2,1)S(1)} %get-tuple-element.53), channel_id=1, source_target_pairs={{8,16},{9,18},{10,17},{11,20},{12,19},{13,22},{14,21},{15,23},{0,8... | collective-permute-start | bytes 786440 | tf_op jit(solution)/shard_map/ppermute | solution.py:334
  44.0 11.6 %collective-permute-start.12 = (bf16[8,128,256]{2,1,0:T(8,128)(2,1)S(1)}, bf16[8,128,256]{2,1,0:T(8,128)(2,1)S(1)}, u32[]{:S(2)}, u32[]{:S(2)}) collective-permute-start(bf16[8,128,256]{2,1,0:T(8,128)(2,1)S(1)} %get-tuple-element.57.old_b), channel_id=1, source_target_pairs={{0,8},{1,9},{2,10},{3,11},{4,12},{5,13},{6,14},{7,15},{8,0},{9,1},... | collective-permute-start | bytes 1572872 | tf_op jit(solution)/shard_map/ppermute | solution.py:334
  47.0 8.6 %collective-permute-start.13 = (bf16[4,128,256]{2,1,0:T(8,128)(2,1)S(1)}, bf16[4,128,256]{2,1,0:T(8,128)(2,1)S(1)}, u32[]{:S(2)}, u32[]{:S(2)}) collective-permute-start(bf16[4,128,256]{2,1,0:T(8,128)(2,1)S(1)} %get-tuple-element.58), channel_id=1, source_target_pairs={{0,8},{1,9},{2,10},{3,11},{4,12},{5,13},{6,14},{7,15},{8,0},{9,1},... | collective-permute-start | bytes 786440 | tf_op jit(solution)/shard_map/ppermute | solution.py:334
  47.1 8.5 %collective-permute-start.14 = (bf16[4,128,256]{2,1,0:T(8,128)(2,1)S(1)}, bf16[4,128,256]{2,1,0:T(8,128)(2,1)S(1)}, u32[]{:S(2)}, u32[]{:S(2)}) collective-permute-start(bf16[4,128,256]{2,1,0:T(8,128)(2,1)S(1)} %get-tuple-element.59), channel_id=1, source_target_pairs={{0,8},{1,9},{2,10},{3,11},{4,12},{5,13},{6,14},{7,15},{8,0},{9,1},... | collective-permute-start | bytes 786440 | tf_op jit(solution)/shard_map/ppermute | solution.py:334

commit v7 on v6

--- a/solution.py
+++ b/solution.py
@@ -108,11 +108,9 @@
     terms = lower.shape[2]
     q = 2 * p + half
     acc[...] = jnp.zeros_like(acc)
-    beside = jnp.concatenate([lower[level, q, k] for k in range(terms)], axis=1)
-    products = dot(inverse[level, q], beside)
     for k in range(terms):
         column = jnp.clip(depend[k, level, q] - (meta[2] + q) + REACH, 0, SPAN - 1)
-        acc[column] += scale[k, level, q] * products[:, k * block : (k + 1) * block]
+        acc[column] += scale[k, level, q] * dot(inverse[level, q], lower[level, q, k])
     at = slice(half * block, (half + 1) * block)
     for d in range(SPAN):
         wide[p, at, (d + half) * block : (d + half + 1) * block] = (-acc[d]).astype(wide.dtype)
@@ -187,9 +185,8 @@
     @pl.when(meta[0] > 1)
     def _():
         odd = meta[1]
-        size = edges.shape[1]
-        edges[1 - odd] = even_in[:size]
-        edges[odd] = odd_in[:size]
+        edges[1 - odd] = even_in[...]
+        edges[odd] = odd_in[...]
 
 
 def flat(ref, start, count):
@@ -229,16 +226,39 @@
         copy.wait()
 
 
-def exchanged_step(group, meta, own, even_in, odd_in, wide_b, base_b, solved, even_out, odd_out, level_a):
+def exchanged_step(group, final, meta, own, even_in, odd_in, wide_b, base_b, *rest):
+    if final:
+        _, out, solved, level_a, sems = rest
+    else:
+        solved, even_out, odd_out, level_a = rest
+
     @pl.when(meta[0] == group)
     def _():
+        done, copies = None, []
+        if final:
+            copies = [pltpu.make_async_copy(own, out.at[0], sems.at[0])]
+            copies += [
+                pltpu.make_async_copy(solved.at[pl.ds(2 * p, 2)], out.at[1, pl.ds(2 * p, 2)], sems.at[1 + p])
+                for p in range(wide_b.shape[0])
+            ]
+            copies[0].start()
+
+            def done(p):
+                copies[1 + p].start()
+
         level_a[REACH : REACH + own.shape[0]] = own[...]
         place(level_a, meta[1], even_in, odd_in)
-        level(wide_b, base_b, level_a, solved, 0)
-        emit_sends(meta[1], solved, (even_out, odd_out))
-
-
-def level_step(group, meta, centre, even_in, odd_in, first, wide_a, old_b, out, solved, even_out, odd_out, window, sems):
+        level(wide_b, base_b, level_a, solved, 0, done)
+        if final:
+            for copy in copies:
+                copy.wait()
+        else:
+            emit_sends(meta[1], solved, (even_out, odd_out))
+
+
+def level_step(group, meta, centre, even_in, odd_in, first, wide_a, old_a, old_b, *rest):
+    out, solved, even_out, odd_out, window, sems = rest[-6:]
+
     @pl.when(meta[0] == group)
     def _():
         window[REACH : REACH + first.shape[0]] = centre[...]
@@ -248,10 +268,10 @@
 
     @pl.when(meta[0] == group - 1)
     def _():
-        store(first, old_b, out, sems)
-
-
-def later_step(group, final, meta, centre, even_in, odd_in, edges, first, wide_a, wide_b, base_b, old_a, old_b, _, out, solved, solved_a, *rest):
+        store(old_a, old_b, out, sems)
+
+
+def later_step(group, meta, centre, even_in, odd_in, edges, first, wide_a, wide_b, base_b, old_a, old_b, _, out, solved, solved_a, *rest):
     *sends, window, level_a, sems = rest
     count, block, cases = first.shape
 
@@ -262,18 +282,6 @@
         window[halo : halo + count] = centre[...]
         place(window, odd, even_in, odd_in)
         level(wide_a, first, window.at[pl.ds(REACH, count + halo)], level_a, REACH)
-        done, copies = None, []
-        if final:
-            copies = [pltpu.make_async_copy(level_a.at[pl.ds(REACH, count)], out.at[0], sems.at[0])]
-            copies += [
-                pltpu.make_async_copy(solved.at[pl.ds(2 * p, 2)], out.at[1, pl.ds(2 * p, 2)], sems.at[1 + p])
-                for p in range(count // 2)
-            ]
-            copies[0].start()
-
-            def done(p):
-                copies[1 + p].start()
-
         parts = cases // block
         size = SPAN + parts
         for side in range(2):
@@ -283,13 +291,9 @@
                 blocks = jnp.concatenate([edges[side, i * size + d] for d in range(SPAN)], axis=1)
                 row = dot(blocks, flat(window, put, SPAN)) + base.astype(jnp.float32)
                 level_a[put] = row.astype(level_a.dtype)
-        level(wide_b, base_b, level_a, solved, 0, done)
-        if final:
-            for copy in copies:
-                copy.wait()
-        else:
-            emit_sends(odd, solved, sends)
-            solved_a[...] = level_a[REACH : REACH + count]
+        level(wide_b, base_b, level_a, solved, 0)
+        emit_sends(odd, solved, sends)
+        solved_a[...] = level_a[REACH : REACH + count]
 
     @pl.when(meta[0] == group - 1)
     def _():
@@ -363,15 +367,13 @@
 
     pairs = count // 2
     wide_shape = shaped((pairs, 2 * block, width + block))
-    parts = REACH * (SPAN + cases // block)
-    even_shape = shaped((parts, block, block))
-    odd_shape = shaped((max(parts, count * cases // block + 1), block, block))
+    weight_edge = shaped((REACH * (SPAN + cases // block), block, block))
 
     wide_b, wide_a, base_b, *edge_w = call(
         prepare_kernel,
         "prepare",
         [SMEM, SMEM, SMEM, HBM, HBM, HBM, VMEM],
-        [wide_shape, wide_shape, shaped(whole.shape, jnp.float32), even_shape, odd_shape],
+        [wide_shape, wide_shape, shaped(whole.shape, jnp.float32), weight_edge, weight_edge],
         scratch_shapes=[
             pltpu.VMEM(lower_blocks.shape, jnp.bfloat16),
             pltpu.VMEM(diag_inverse.shape, jnp.bfloat16),
@@ -382,60 +384,63 @@
     )(meta, depend, scale, lower_blocks, diag_inverse, right_side, first)
 
     padded = pltpu.VMEM((count + halo, block, cases), jnp.bfloat16)
-    solved, *sends = call(
-        functools.partial(exchanged_step, 0),
-        "step_0",
-        [SMEM] + [VMEM] * 5,
-        [whole, edge, edge],
-        scratch_shapes=[padded],
-    )(meta, first, *sides, wide_b, base_b)
+    def own_exchange(group, values, sides, final=False):
+        sems = pltpu.SemaphoreType.DMA((1 + pairs,))
+        sizes = [] if final else [edge if group in (0, chain - 2) else wide_edge] * 2
+        return call(
+            functools.partial(exchanged_step, group, final),
+            f"step_{group}_b",
+            [SMEM] + [VMEM] * 5 + [ANY] * final,
+            [shaped(right_side.shape)] * final + [whole, *sizes],
+            [ANY] * final + [VMEM] * (1 + len(sizes)),
+            scratch_shapes=[padded] + [sems] * final,
+            input_output_aliases={6: 0} if final else {},
+        )(meta, values, *sides, wide_b, base_b, *([out] * final))
+
+    def own_level(group, arrived, made_a, solved, out):
+        aliased = out is not None
+        return call(
+            functools.partial(level_step, group),
+            f"step_{group}_a",
+            [SMEM] + [VMEM] * 7 + [ANY] * aliased,
+            [shaped(right_side.shape), whole, edge, edge],
+            [ANY] + [VMEM] * 3,
+            scratch_shapes=[padded, pltpu.SemaphoreType.DMA((2,))],
+            input_output_aliases={8: 0} if aliased else {},
+        )(meta, *arrived, first, wide_a, made_a, solved, *([out] * aliased))
+
+    out = None
+    solved, *sends = own_exchange(0, first, sides)
     arrived = travel(0, solved, sends)
 
-    even_w, odd_w = edge_w
-    even_w = lax.ppermute(after(even_w, sides), AXES, inner_pairs(range(2, chain), even_mate, chain, rows))
-    odd_w = lax.ppermute(after(odd_w, even_w), AXES, inner_pairs(range(2, chain), odd_mate, chain, rows))
-    arrived = after(arrived, even_w)
-    edges = call(
-        order_kernel,
-        "order",
-        [SMEM, VMEM, VMEM],
-        [shaped((2, *even_shape.shape))],
-    )(meta, even_w, odd_w)[0]
-
-    out, made_a, *sides = call(
-        functools.partial(level_step, 1),
-        "step_1_a",
-        [SMEM] + [VMEM] * 6,
-        [shaped(right_side.shape), whole, edge, edge],
-        [ANY] + [VMEM] * 3,
-        scratch_shapes=[padded, pltpu.SemaphoreType.DMA((2,))],
-    )(meta, *arrived, first, wide_a, solved)
-    solved, *sends = call(
-        functools.partial(exchanged_step, 1),
-        "step_1_b",
-        [SMEM] + [VMEM] * 5,
-        [whole, wide_edge, wide_edge],
-        scratch_shapes=[padded],
-    )(meta, made_a, *exchange([1], sides, 0), wide_b, base_b)
-
-    for group in range(2, chain):
-        final = group == chain - 1
-        outs = [whole, whole] + ([] if final else [wide_edge] * 2)
+    between = range(2, chain - 1)
+    moved = [
+        lax.ppermute(after(value, sides), AXES, inner_pairs(between, mate, chain, rows, chain - 1))
+        for value, mate in zip(edge_w, mates)
+    ]
+    edges = call(order_kernel, "order", [SMEM, VMEM, VMEM], [shaped((2, *weight_edge.shape))])(meta, *moved)[0]
+
+    out, made_a, *sides = own_level(1, after(arrived, moved), first, solved, out)
+    solved, *sends = own_exchange(1, made_a, exchange([1], sides, 0))
+    for group in between:
+        size = edge if group == chain - 2 else wide_edge
         out, *now = call(
-            functools.partial(later_step, group, final),
+            functools.partial(later_step, group),
             f"step_{group}",
             [SMEM] + [VMEM] * 10 + [ANY],
-            [shaped(right_side.shape), *outs],
-            [ANY] + [VMEM] * len(outs),
+            [shaped(right_side.shape), whole, whole, size, size],
+            [ANY] + [VMEM] * 4,
             scratch_shapes=[
                 pltpu.VMEM((count + 2 * halo, block, cases), jnp.bfloat16),
                 padded,
-                pltpu.SemaphoreType.DMA((1 + pairs,)),
+                pltpu.SemaphoreType.DMA((2,)),
             ],
             input_output_aliases={11: 0},
         )(meta, *travel(group - 1, solved, sends), edges, first, wide_a, wide_b, base_b, made_a, solved, out)
         solved, made_a, *sends = now
-    return out
+    last = chain - 1
+    out, made_a, *sides = own_level(last, travel(last - 1, solved, sends), made_a, solved, out)
+    return own_exchange(last, made_a, exchange([last], sides, last - 1), True)[0]
 
 
 def solution(mesh):

time: 59.4 us -> 66.2 us (1.11)
  the two profiles are of different devices: /device:TPU:11 before, /device:TPU:15 now
where the time goes in v7:
time: 66.2 us; the launch traced here: 66 us
  waiting for transfers between devices  36.3 us (55%)
  starting transfers between devices  15.8 us (24%)
  Pallas kernels  13.8 us (21%)
    ppermute x9, waiting for transfers between devices, travel(): lax.ppermute(value, AXES, hop_pairs(group, mate, chain, rows))  14 us
    ppermute x2, waiting for transfers between devices, per_device(): lax.ppermute(after(value, sides), AXES, inner_pairs(between, mate, chain,...  13.8 us
    ppermute x9, starting transfers between devices, travel(): lax.ppermute(value, AXES, hop_pairs(group, mate, chain, rows))  9.01 us
    ppermute x6, waiting for transfers between devices, exchange(): lax.ppermute(value, AXES, inner_pairs(groups, mate, chain, rows, idle))  8.44 us
    ppermute x6, starting transfers between devices, exchange(): lax.ppermute(value, AXES, inner_pairs(groups, mate, chain, rows, idle))  5.41 us
    pallas_call x1, Pallas kernels, per_device(): call(prepare_kernel, 'prepare', [SMEM, SMEM, SMEM, HBM, HBM, HBM, VMEM],...  4.97 us
    pallas_call x3, Pallas kernels, own_exchange(): call(functools.partial(exchanged_step, group, final), f'step_{group}_b',...  3.8 us
    pallas_call x1, Pallas kernels, per_device(): call(first_kernel, 'first_level', [SMEM, HBM, HBM], [whole, edge, edge],...  2.04 us
  transfers between devices with their start and end apart: 17, of which 11 were waited for; matrix products, arithmetic and copies ran while one was open for 0% of the time, Pallas kernels for 8%

profile of v7, /device:TPU:15, one launch (start us, length us, event | category | flops | bytes accessed | tf_op | source)
XLA Modules:
  0.0 66.0 jit_solution(15259044773377869533)
XLA Ops:
  0.0 0.0 copy-start
  0.0 0.0 copy-start.1
  0.0 0.1 pad_add_fusion.meta
  0.1 2.0 %first_level.1 = (bf16[8,128,256]{2,1,0:T(8,128)(2,1)S(1)}, bf16[2,128,256]{2,1,0:T(8,128)(2,1)S(1)}, bf16[2,128,256]{2,1,0:T(8,128)(2,1)S(1)}) custom-call(s32[3]{0:T(128)S(1)} %pad_add_fusion.meta, bf16[2,8,128,128]{3,2,1,0:T(8,128)(2,1)} %inverse_hbm.3, bf16[2,8,128,256]{3,2,1,0:T(8,128)(2,1)} %right_hbm.3), custom_call_target="tpu_custom_call" | custom-call | tf_op jit(solution)/shard_map/first_level/pallas_call | solution.py:355
  2.1 0.7 %collective-permute-start = (bf16[2,128,256]{2,1,0:T(8,128)(2,1)S(1)}, bf16[2,128,256]{2,1,0:T(8,128)(2,1)S(1)}, u32[]{:S(2)}, u32[]{:S(2)}) collective-permute-start(bf16[2,128,256]{2,1,0:T(8,128)(2,1)S(1)} %get-tuple-element.39), channel_id=1, source_target_pairs={{0,1},{8,10},{16,24},{24,16},{1,0},{9,11},{17,25},{25,17},{2,3},{1... | collective-permute-start | bytes 393224 | tf_op jit(solution)/shard_map/ppermute | solution.py:332
  2.9 0.1 collective-permute-start.1
  2.9 0.0 copy-done
  2.9 0.0 copy-done.1
  2.9 5.0 %prepare.1 = (bf16[4,256,768]{2,1,0:T(8,128)(2,1)S(1)}, bf16[4,256,768]{2,1,0:T(8,128)(2,1)S(1)}, f32[8,128,256]{2,1,0:T(8,128)S(1)}, bf16[14,128,128]{2,1,0:T(8,128)(2,1)S(1)}, bf16[14,128,128]{2,1,0:T(8,128)(2,1)S(1)}) custom-call(s32[3]{0:T(128)S(1)} %pad_add_fusion.meta, s32[6,2,8]{2,1,0:T(2,128)S(1)} %bitcast.5, f32[6,2,8]{2,1,0:T(2,128)S(1)} %bitcast.6, ...), custom_call_target="tpu_custom_call" | custom-call | tf_op jit(solution)/shard_map/prepare/pallas_call | solution.py:372
  7.9 0.0 collective-permute-done.even_in
  7.9 0.0 collective-permute-done.1.odd_in
  7.9 0.6 step_0_b.1
  8.5 0.5 collective-permute-start.2
  9.0 1.3 %collective-permute-start.6 = (bf16[14,128,128]{2,1,0:T(8,128)(2,1)S(1)}, bf16[14,128,128]{2,1,0:T(8,128)(2,1)S(1)}, u32[]{:S(2)}, u32[]{:S(2)}) collective-permute-start(bf16[14,128,128]{2,1,0:T(8,128)(2,1)S(1)} %get-tuple-element.49), channel_id=1, source_target_pairs={{0,8},{8,0},{16,24},{24,16},{17,18},{25,27},{1,9},{9,1},{18,17},{2... | collective-permute-start | bytes 1376264 | tf_op jit(solution)/shard_map/ppermute | solution.py:418
  10.3 0.1 collective-permute-start.5
  10.4 0.6 collective-permute-start.3
  11.0 0.0 collective-permute-start.4
  11.0 1.0 %collective-permute-done.3.even_in = bf16[2,128,256]{2,1,0:T(8,128)(2,1)S(1)} collective-permute-done((bf16[2,128,256]{2,1,0:T(8,128)(2,1)S(1)}, bf16[2,128,256]{2,1,0:T(8,128)(2,1)S(1)}, u32[]{:S(2)}, u32[]{:S(2)}) %collective-permute-start.3) | collective-permute-done | bytes 131104 | tf_op jit(solution)/shard_map/ppermute | solution.py:338
  12.0 0.4 collective-permute-done.4.odd_in
  12.3 8.8 %collective-permute-done.6.odd_in = bf16[14,128,128]{2,1,0:T(8,128)(2,1)S(1)} collective-permute-done((bf16[14,128,128]{2,1,0:T(8,128)(2,1)S(1)}, bf16[14,128,128]{2,1,0:T(8,128)(2,1)S(1)}, u32[]{:S(2)}, u32[]{:S(2)}) %collective-permute-start.6) | collective-permute-done | bytes 458784 | tf_op jit(solution)/shard_map/ppermute | solution.py:418
  21.2 5.0 %collective-permute-done.5.even_in = bf16[14,128,128]{2,1,0:T(8,128)(2,1)S(1)} collective-permute-done((bf16[14,128,128]{2,1,0:T(8,128)(2,1)S(1)}, bf16[14,128,128]{2,1,0:T(8,128)(2,1)S(1)}, u32[]{:S(2)}, u32[]{:S(2)}) %collective-permute-start.5) | collective-permute-done | bytes 458784 | tf_op jit(solution)/shard_map/ppermute | solution.py:418
  26.2 0.0 collective-permute-done.2.centre
  26.2 0.6 step_1_a.1
  26.7 0.1 collective-permute-start.7
  26.8 0.5 collective-permute-start.8
  27.3 0.8 %collective-permute-done.7.even_in = bf16[2,128,256]{2,1,0:T(8,128)(2,1)S(1)} collective-permute-done((bf16[2,128,256]{2,1,0:T(8,128)(2,1)S(1)}, bf16[2,128,256]{2,1,0:T(8,128)(2,1)S(1)}, u32[]{:S(2)}, u32[]{:S(2)}) %collective-permute-start.7) | collective-permute-done | bytes 131104 | tf_op jit(solution)/shard_map/ppermute | solution.py:332
  28.1 0.2 collective-permute-done.8.odd_in
  28.3 0.5 step_1_b.1
  28.9 0.1 collective-permute-start.9
  29.0 0.1 collective-permute-start.10
  29.0 2.0 %collective-permute-start.11 = (bf16[4,128,256]{2,1,0:T(8,128)(2,1)S(1)}, bf16[4,128,256]{2,1,0:T(8,128)(2,1)S(1)}, u32[]{:S(2)}, u32[]{:S(2)}) collective-permute-start(bf16[4,128,256]{2,1,0:T(8,128)(2,1)S(1)} %get-tuple-element.59), channel_id=1, source_target_pairs={{8,16},{9,18},{10,17},{11,20},{12,19},{13,22},{14,21},{15,23},{0,8... | collective-permute-start | bytes 786440 | tf_op jit(solution)/shard_map/ppermute | solution.py:338
  31.0 0.6 order.1.edges
  31.6 6.3 %collective-permute-done.10.even_in = bf16[4,128,256]{2,1,0:T(8,128)(2,1)S(1)} collective-permute-done((bf16[4,128,256]{2,1,0:T(8,128)(2,1)S(1)}, bf16[4,128,256]{2,1,0:T(8,128)(2,1)S(1)}, u32[]{:S(2)}, u32[]{:S(2)}) %collective-permute-start.10) | collective-permute-done | bytes 262176 | tf_op jit(solution)/shard_map/ppermute | solution.py:338
  37.9 2.8 %collective-permute-done.11.odd_in = bf16[4,128,256]{2,1,0:T(8,128)(2,1)S(1)} collective-permute-done((bf16[4,128,256]{2,1,0:T(8,128)(2,1)S(1)}, bf16[4,128,256]{2,1,0:T(8,128)(2,1)S(1)}, u32[]{:S(2)}, u32[]{:S(2)}) %collective-permute-start.11) | collective-permute-done | bytes 262176 | tf_op jit(solution)/shard_map/ppermute | solution.py:338
  40.7 0.0 collective-permute-done.9.centre
  40.7 0.6 step_2.1
  41.3 1.6 %collective-permute-start.12 = (bf16[8,128,256]{2,1,0:T(8,128)(2,1)S(1)}, bf16[8,128,256]{2,1,0:T(8,128)(2,1)S(1)}, u32[]{:S(2)}, u32[]{:S(2)}) collective-permute-start(bf16[8,128,256]{2,1,0:T(8,128)(2,1)S(1)} %get-tuple-element.61.old_b), channel_id=1, source_target_pairs={{0,8},{1,9},{2,10},{3,11},{4,12},{5,13},{6,14},{7,15},{8,0},{9,1},... | collective-permute-start | bytes 1572872 | tf_op jit(solution)/shard_map/ppermute | solution.py:338
  42.8 0.1 collective-permute-start.13
  42.9 4.1 %collective-permute-start.14 = (bf16[2,128,256]{2,1,0:T(8,128)(2,1)S(1)}, bf16[2,128,256]{2,1,0:T(8,128)(2,1)S(1)}, u32[]{:S(2)}, u32[]{:S(2)}) collective-permute-start(bf16[2,128,256]{2,1,0:T(8,128)(2,1)S(1)} %get-tuple-element.63), channel_id=1, source_target_pairs={{0,8},{1,9},{2,10},{3,11},{4,12},{5,13},{6,14},{7,15},{8,0},{9,1},... | collective-permute-start | bytes 393224 | tf_op jit(solution)/shard_map/ppermute | solution.py:338
  47.0 3.6 %collective-permute-done.13.even_in = bf16[2,128,256]{2,1,0:T(8,128)(2,1)S(1)} collective-permute-done((bf16[2,128,256]{2,1,0:T(8,128)(2,1)S(1)}, bf16[2,128,256]{2,1,0:T(8,128)(2,1)S(1)}, u32[]{:S(2)}, u32[]{:S(2)}) %collective-permute-start.13) | collective-permute-done | bytes 131104 | tf_op jit(solution)/shard_map/ppermute | solution.py:338
  50.7 0.0 collective-permute-done.14.odd_in
  50.7 0.0 collective-permute-done.12.centre
  50.7 1.2 %step_3_a.1 = (bf16[2,8,128,256]{3,2,1,0:T(8,128)(2,1)}, bf16[8,128,256]{2,1,0:T(8,128)(2,1)S(1)}, bf16[2,128,256]{2,1,0:T(8,128)(2,1)S(1)}, bf16[2,128,256]{2,1,0:T(8,128)(2,1)S(1)}) custom-call(s32[3]{0:T(128)S(1)} %pad_add_fusion.meta, bf16[8,128,256]{2,1,0:T(8,128)(2,1)S(1)} %collective-permute-done.12.centre, ...), custom_call_target="tpu_custom_call", output_to_operand_aliasing={{0}: (8, {})} | custom-call | tf_op jit(solution)/shard_map/step_3_a/pallas_call | solution.py:402
  51.9 4.1 %collective-permute-start.15 = (bf16[2,128,256]{2,1,0:T(8,128)(2,1)S(1)}, bf16[2,128,256]{2,1,0:T(8,128)(2,1)S(1)}, u32[]{:S(2)}, u32[]{:S(2)}) collective-permute-start(bf16[2,128,256]{2,1,0:T(8,128)(2,1)S(1)} %get-tuple-element.67), channel_id=1, source_target_pairs={{24,25},{16,18},{0,8},{8,0},{25,24},{17,19},{1,9},{9,1},{26,27},{1... | collective-permute-start | bytes 393224 | tf_op jit(solution)/shard_map/ppermute | solution.py:332
  55.9 0.0 collective-permute-start.16
  55.9 2.6 %collective-permute-done.15.even_in = bf16[2,128,256]{2,1,0:T(8,128)(2,1)S(1)} collective-permute-done((bf16[2,128,256]{2,1,0:T(8,128)(2,1)S(1)}, bf16[2,128,256]{2,1,0:T(8,128)(2,1)S(1)}, u32[]{:S(2)}, u32[]{:S(2)}) %collective-permute-start.15) | collective-permute-done | bytes 131104 | tf_op jit(solution)/shard_map/ppermute | solution.py:332
  58.6 4.8 %collective-permute-done.16.odd_in = bf16[2,128,256]{2,1,0:T(8,128)(2,1)S(1)} collective-permute-done((bf16[2,128,256]{2,1,0:T(8,128)(2,1)S(1)}, bf16[2,128,256]{2,1,0:T(8,128)(2,1)S(1)}, u32[]{:S(2)}, u32[]{:S(2)}) %collective-permute-start.16) | collective-permute-done | bytes 131104 | tf_op jit(solution)/shard_map/ppermute | solution.py:332
  63.3 2.7 %step_3_b.1 = (bf16[2,8,128,256]{3,2,1,0:T(8,128)(2,1)}, bf16[8,128,256]{2,1,0:T(8,128)(2,1)}) custom-call(s32[3]{0:T(128)S(1)} %pad_add_fusion.meta, bf16[8,128,256]{2,1,0:T(8,128)(2,1)S(1)} %get-tuple-element.66.own, bf16[2,128,256]{2,1,0:T(8,128)(2,1)S(1)} %collective-permute-done.15.even_in, ...), custom_call_target="tpu_custom_call", output_to_operand_aliasing={{0}: (6, {})} | custom-call | tf_op jit(solution)/shard_map/step_3_b/pallas_call | solution.py:390
Async XLA Ops:
  0.0 2.9 %copy-start = (s32[2,8,6]{1,0,2:T(2,128)S(1)}, s32[2,8,6]{1,0,2:T(2,128)}, u32[]{:S(2)}) copy-start(s32[2,8,6]{1,0,2:T(2,128)} %param.9) | copy-start | bytes 1156
  0.0 2.9 %copy-start.1 = (f32[2,8,6]{1,0,2:T(2,128)S(1)}, f32[2,8,6]{1,0,2:T(2,128)}, u32[]{:S(2)}) copy-start(f32[2,8,6]{1,0,2:T(2,128)} %param.7) | copy-start | bytes 1156
  2.1 5.8 %collective-permute-start = (bf16[2,128,256]{2,1,0:T(8,128)(2,1)S(1)}, bf16[2,128,256]{2,1,0:T(8,128)(2,1)S(1)}, u32[]{:S(2)}, u32[]{:S(2)}) collective-permute-start(bf16[2,128,256]{2,1,0:T(8,128)(2,1)S(1)} %get-tuple-element.39), channel_id=1, source_target_pairs={{0,1},{8,10},{16,24},{24,16},{1,0},{9,11},{17,25},{25,17},{2,3},{1... | collective-permute-start | bytes 393224 | tf_op jit(solution)/shard_map/ppermute | solution.py:332
  2.9 5.1 %collective-permute-start.1 = (bf16[2,128,256]{2,1,0:T(8,128)(2,1)S(1)}, bf16[2,128,256]{2,1,0:T(8,128)(2,1)S(1)}, u32[]{:S(2)}, u32[]{:S(2)}) collective-permute-start(bf16[2,128,256]{2,1,0:T(8,128)(2,1)S(1)} %get-tuple-element.40), channel_id=1, source_target_pairs={{0,8},{8,0},{16,24},{24,16},{1,2},{9,11},{17,25},{25,17},{2,1},{10... | collective-permute-start | bytes 393224 | tf_op jit(solution)/shard_map/ppermute | solution.py:332
  8.5 17.7 %collective-permute-start.2 = (bf16[8,128,256]{2,1,0:T(8,128)(2,1)S(1)}, bf16[8,128,256]{2,1,0:T(8,128)(2,1)S(1)}, u32[]{:S(2)}, u32[]{:S(2)}) collective-permute-start(bf16[8,128,256]{2,1,0:T(8,128)(2,1)S(1)} %get-tuple-element.43.old_b), channel_id=1, source_target_pairs={{0,8},{1,9},{2,10},{3,11},{4,12},{5,13},{6,14},{7,15},{8,0},{9,1},... | collective-permute-start | bytes 1572872 | tf_op jit(solution)/shard_map/ppermute | solution.py:338
  9.0 12.2 %collective-permute-start.6 = (bf16[14,128,128]{2,1,0:T(8,128)(2,1)S(1)}, bf16[14,128,128]{2,1,0:T(8,128)(2,1)S(1)}, u32[]{:S(2)}, u32[]{:S(2)}) collective-permute-start(bf16[14,128,128]{2,1,0:T(8,128)(2,1)S(1)} %get-tuple-element.49), channel_id=1, source_target_pairs={{0,8},{8,0},{16,24},{24,16},{17,18},{25,27},{1,9},{9,1},{18,17},{2... | collective-permute-start | bytes 1376264 | tf_op jit(solution)/shard_map/ppermute | solution.py:418
  10.3 15.9 %collective-permute-start.5 = (bf16[14,128,128]{2,1,0:T(8,128)(2,1)S(1)}, bf16[14,128,128]{2,1,0:T(8,128)(2,1)S(1)}, u32[]{:S(2)}, u32[]{:S(2)}) collective-permute-start(bf16[14,128,128]{2,1,0:T(8,128)(2,1)S(1)} %get-tuple-element.47), channel_id=1, source_target_pairs={{16,17},{24,26},{0,8},{8,0},{17,16},{25,27},{1,9},{9,1},{18,19},{2... | collective-permute-start | bytes 1376264 | tf_op jit(solution)/shard_map/ppermute | solution.py:418
  10.4 1.6 %collective-permute-start.3 = (bf16[2,128,256]{2,1,0:T(8,128)(2,1)S(1)}, bf16[2,128,256]{2,1,0:T(8,128)(2,1)S(1)}, u32[]{:S(2)}, u32[]{:S(2)}) collective-permute-start(bf16[2,128,256]{2,1,0:T(8,128)(2,1)S(1)} %get-tuple-element.44), channel_id=1, source_target_pairs={{0,9},{1,8},{2,11},{3,10},{4,13},{5,12},{6,15},{7,14},{8,0},{9,1},... | collective-permute-start | bytes 393224 | tf_op jit(solution)/shard_map/ppermute | solution.py:338
  11.0 1.3 %collective-permute-start.4 = (bf16[2,128,256]{2,1,0:T(8,128)(2,1)S(1)}, bf16[2,128,256]{2,1,0:T(8,128)(2,1)S(1)}, u32[]{:S(2)}, u32[]{:S(2)}) collective-permute-start(bf16[2,128,256]{2,1,0:T(8,128)(2,1)S(1)} %get-tuple-element.45), channel_id=1, source_target_pairs={{0,8},{1,10},{2,9},{3,12},{4,11},{5,14},{6,13},{7,15},{8,0},{9,1},... | collective-permute-start | bytes 393224 | tf_op jit(solution)/shard_map/ppermute | solution.py:338
  26.7 1.4 %collective-permute-start.7 = (bf16[2,128,256]{2,1,0:T(8,128)(2,1)S(1)}, bf16[2,128,256]{2,1,0:T(8,128)(2,1)S(1)}, u32[]{:S(2)}, u32[]{:S(2)}) collective-permute-start(bf16[2,128,256]{2,1,0:T(8,128)(2,1)S(1)} %get-tuple-element.55), channel_id=1, source_target_pairs={{8,9},{0,2},{16,24},{24,16},{9,8},{1,3},{17,25},{25,17},{10,11},{2... | collective-permute-start | bytes 393224 | tf_op jit(solution)/shard_map/ppermute | solution.py:332
  26.8 1.5 %collective-permute-start.8 = (bf16[2,128,256]{2,1,0:T(8,128)(2,1)S(1)}, bf16[2,128,256]{2,1,0:T(8,128)(2,1)S(1)}, u32[]{:S(2)}, u32[]{:S(2)}) collective-permute-start(bf16[2,128,256]{2,1,0:T(8,128)(2,1)S(1)} %get-tuple-element.56), channel_id=1, source_target_pairs={{0,8},{8,0},{16,24},{24,16},{9,10},{1,3},{17,25},{25,17},{10,9},{2... | collective-permute-start | bytes 393224 | tf_op jit(solution)/shard_map/ppermute | solution.py:332
  28.9 11.8 %collective-permute-start.9 = (bf16[8,128,256]{2,1,0:T(8,128)(2,1)S(1)}, bf16[8,128,256]{2,1,0:T(8,128)(2,1)S(1)}, u32[]{:S(2)}, u32[]{:S(2)}) collective-permute-start(bf16[8,128,256]{2,1,0:T(8,128)(2,1)S(1)} %get-tuple-element.57.old_b), channel_id=1, source_target_pairs={{8,16},{9,17},{10,18},{11,19},{12,20},{13,21},{14,22},{15,23},{0,8... | collective-permute-start | bytes 1572872 | tf_op jit(solution)/shard_map/ppermute | solution.py:338
  29.0 8.9 %collective-permute-start.10 = (bf16[4,128,256]{2,1,0:T(8,128)(2,1)S(1)}, bf16[4,128,256]{2,1,0:T(8,128)(2,1)S(1)}, u32[]{:S(2)}, u32[]{:S(2)}) collective-permute-start(bf16[4,128,256]{2,1,0:T(8,128)(2,1)S(1)} %get-tuple-element.58), channel_id=1, source_target_pairs={{8,17},{9,16},{10,19},{11,18},{12,21},{13,20},{14,23},{15,22},{0,8... | collective-permute-start | bytes 786440 | tf_op jit(solution)/shard_map/ppermute | solution.py:338
  29.0 11.7 %collective-permute-start.11 = (bf16[4,128,256]{2,1,0:T(8,128)(2,1)S(1)}, bf16[4,128,256]{2,1,0:T(8,128)(2,1)S(1)}, u32[]{:S(2)}, u32[]{:S(2)}) collective-permute-start(bf16[4,128,256]{2,1,0:T(8,128)(2,1)S(1)} %get-tuple-element.59), channel_id=1, source_target_pairs={{8,16},{9,18},{10,17},{11,20},{12,19},{13,22},{14,21},{15,23},{0,8... | collective-permute-start | bytes 786440 | tf_op jit(solution)/shard_map/ppermute | solution.py:338
  41.3 9.4 %collective-permute-start.12 = (bf16[8,128,256]{2,1,0:T(8,128)(2,1)S(1)}, bf16[8,128,256]{2,1,0:T(8,128)(2,1)S(1)}, u32[]{:S(2)}, u32[]{:S(2)}) collective-permute-start(bf16[8,128,256]{2,1,0:T(8,128)(2,1)S(1)} %get-tuple-element.61.old_b), channel_id=1, source_target_pairs={{0,8},{1,9},{2,10},{3,11},{4,12},{5,13},{6,14},{7,15},{8,0},{9,1},... | collective-permute-start | bytes 1572872 | tf_op jit(solution)/shard_map/ppermute | solution.py:338
  42.8 7.8 %collective-permute-start.13 = (bf16[2,128,256]{2,1,0:T(8,128)(2,1)S(1)}, bf16[2,128,256]{2,1,0:T(8,128)(2,1)S(1)}, u32[]{:S(2)}, u32[]{:S(2)}) collective-permute-start(bf16[2,128,256]{2,1,0:T(8,128)(2,1)S(1)} %get-tuple-element.62), channel_id=1, source_target_pairs={{0,8},{1,9},{2,10},{3,11},{4,12},{5,13},{6,14},{7,15},{8,0},{9,1},... | collective-permute-start | bytes 393224 | tf_op jit(solution)/shard_map/ppermute | solution.py:338
  42.9 7.7 %collective-permute-start.14 = (bf16[2,128,256]{2,1,0:T(8,128)(2,1)S(1)}, bf16[2,128,256]{2,1,0:T(8,128)(2,1)S(1)}, u32[]{:S(2)}, u32[]{:S(2)}) collective-permute-start(bf16[2,128,256]{2,1,0:T(8,128)(2,1)S(1)} %get-tuple-element.63), channel_id=1, source_target_pairs={{0,8},{1,9},{2,10},{3,11},{4,12},{5,13},{6,14},{7,15},{8,0},{9,1},... | collective-permute-start | bytes 393224 | tf_op jit(solution)/shard_map/ppermute | solution.py:338
  51.9 6.7 %collective-permute-start.15 = (bf16[2,128,256]{2,1,0:T(8,128)(2,1)S(1)}, bf16[2,128,256]{2,1,0:T(8,128)(2,1)S(1)}, u32[]{:S(2)}, u32[]{:S(2)}) collective-permute-start(bf16[2,128,256]{2,1,0:T(8,128)(2,1)S(1)} %get-tuple-element.67), channel_id=1, source_target_pairs={{24,25},{16,18},{0,8},{8,0},{25,24},{17,19},{1,9},{9,1},{26,27},{1... | collective-permute-start | bytes 393224 | tf_op jit(solution)/shard_map/ppermute | solution.py:332
  55.9 7.4 %collective-permute-start.16 = (bf16[2,128,256]{2,1,0:T(8,128)(2,1)S(1)}, bf16[2,128,256]{2,1,0:T(8,128)(2,1)S(1)}, u32[]{:S(2)}, u32[]{:S(2)}) collective-permute-start(bf16[2,128,256]{2,1,0:T(8,128)(2,1)S(1)} %get-tuple-element.68), channel_id=1, source_target_pairs={{0,8},{8,0},{16,24},{24,16},{25,26},{17,19},{1,9},{9,1},{26,25},{1... | collective-permute-start | bytes 393224 | tf_op jit(solution)/shard_map/ppermute | solution.py:332

commit v8 on v4

--- a/solution.py
+++ b/solution.py
@@ -55,27 +55,15 @@
         if r not in paired:
             moves = swap_groups(chain)
         else:
+            moves = swap_groups(chain, [*groups, idle])
             pairs += [(g * rows + r, g * rows + mate(r, rows)) for g in groups]
-            if idle is None:
-                others = [g for g in range(min(chain, 4)) if g not in groups]
-                moves = dict(zip(others, others[1:] + others[:1]))
-                moves.update(swap_groups(chain, [*range(4), *groups]))
-            else:
+            if idle is not None:
                 alike = [q for q in paired if q % 2 == r % 2]
                 pairs.append((idle * rows + r, idle * rows + alike[(alike.index(r) + 1) % len(alike)]))
-                moves = swap_groups(chain, [idle, *groups])
         pairs += [(a * rows + r, b * rows + r) for a, b in moves.items()]
     return pairs
 
 
-def side_pairs(group, mate, chain, rows):
-    return [
-        (group * rows + r, (group + 1) * rows + mate(r, rows))
-        for r in range(rows)
-        if mate(r, rows) != r
-    ]
-
-
 def dot(a, b):
     return jnp.dot(a, b, preferred_element_type=jnp.float32)
 
@@ -92,89 +80,140 @@
         odd_ref[...] = high_value()
 
 
-def first_kernel(meta, inverse_hbm, right_hbm, solved, *rest):
-    *sends, inverse, right, sems = rest
+def premultiplied(meta, depend, scale, lower, inverse, acc, level, q):
+    acc[...] = jnp.zeros_like(acc)
+    for k in range(len(lower)):
+        column = jnp.clip(depend[k, level, q] - (meta[2] + q) + REACH, 0, SPAN - 1)
+        acc[column] += scale[k, level, q] * dot(inverse, lower[k])
+
+
+def first_kernel(meta, depend, scale, lower_hbm, inverse_hbm, right_hbm, solved, even_a, odd_a, even_b, odd_b, inverse, right, lower, acc, edges, sems):
     count = inverse.shape[0]
-    parts = 2
-    size = count // parts
+    block = inverse.shape[1]
+    parts = right.shape[2] // block
+    steps = 4
+    size = count // steps
     loads = []
-    for part in range(parts):
-        rows = pl.ds(part * size, size)
+    for step in range(steps):
+        rows = pl.ds(step * size, size)
         loads.append(
             (
-                pltpu.make_async_copy(inverse_hbm.at[0, rows], inverse.at[rows], sems.at[0, part]),
-                pltpu.make_async_copy(right_hbm.at[0, rows], right.at[rows], sems.at[1, part]),
+                pltpu.make_async_copy(inverse_hbm.at[0, rows], inverse.at[rows], sems.at[0, step]),
+                pltpu.make_async_copy(right_hbm.at[0, rows], right.at[rows], sems.at[1, step]),
             )
         )
+    ends = (0, count - REACH)
+
+    def edge_load(side):
+        rows = pl.ds(ends[side], REACH)
+        return pltpu.make_async_copy(lower_hbm.at[0, rows], lower.at[side], sems.at[2, side])
+
     for pair in loads:
         for load in pair:
             load.start()
-    for part in range(parts):
-        for load in loads[part]:
+
+    @pl.when(meta[0] > 1)
+    def _():
+        for side in range(2):
+            edge_load(side).start()
+
+    for step in range(steps):
+        for load in loads[step]:
             load.wait()
-        for q in range(part * size, (part + 1) * size):
+        for q in range(step * size, (step + 1) * size):
             solved[q] = dot(inverse[q], right[q]).astype(solved.dtype)
-    by_parity(meta[1], lambda: solved[:REACH], lambda: solved[count - REACH :], *sends)
-
-
-def premultiply(meta, depend, scale, lower, inverse, wide, acc, level, q, half, keep=None):
+
+    def row_parts(q):
+        return [solved[q, :, part * block : (part + 1) * block] for part in range(parts)]
+
+    @pl.when(meta[0] < 2)
+    def _():
+        for side in range(2):
+            for i in range(REACH):
+                for part, value in enumerate(row_parts(ends[side] + i)):
+                    edges[side, i * parts + part] = value
+
+    @pl.when(meta[0] > 1)
+    def _():
+        for side in range(2):
+            edge_load(side).wait()
+            for i in range(REACH):
+                q = ends[side] + i
+                blocks = [lower[side, i, k] for k in range(lower.shape[2])]
+                premultiplied(meta, depend, scale, blocks, inverse[q], acc.at[i], 0, q)
+                for d in range(SPAN):
+                    edges[side, i * EDGE + d] = (-acc[i, d]).astype(edges.dtype)
+                for part, value in enumerate(row_parts(q)):
+                    edges[side, i * EDGE + SPAN + part] = value
+
+    soon = even_a.shape[0]
+    by_parity(meta[1], lambda: edges[0, :soon], lambda: edges[1, :soon], even_a, odd_a)
+
+    @pl.when(meta[0] > 1)
+    def _():
+        by_parity(meta[1], lambda: edges[0, soon:], lambda: edges[1, soon:], even_b, odd_b)
+
+
+def prepare_kernel(meta, depend, scale, lower_hbm, inverse_hbm, right_hbm, wide_b, wide_a, base, lower, inverse, right, acc, sems):
+    pairs = wide_a.shape[0]
     block = lower.shape[-1]
-    terms = lower.shape[2]
-    acc[...] = jnp.zeros_like(acc)
-    beside = jnp.concatenate([lower[level, half, k] for k in range(terms)], axis=1)
-    products = dot(inverse[level, half], beside)
-    for k in range(terms):
-        column = jnp.clip(depend[k, level, q] - (meta[2] + q) + REACH, 0, SPAN - 1)
-        acc[column] += scale[k, level, q] * products[:, k * block : (k + 1) * block]
-    at = slice(half * block, (half + 1) * block)
-    for d in range(SPAN):
-        value = (-acc[d]).astype(wide.dtype)
-        wide[0, at, (d + half) * block : (d + half + 1) * block] = value
-        if keep is not None:
-            keep[half, d] = value
-    other = 0 if half else SPAN
-    wide[0, at, other * block : (other + 1) * block] = jnp.zeros((block, block), wide.dtype)
-
-
-def prepare_kernel(meta, depend, scale, lower, inverse, right, first, wide_a, wide_b, base, even_out, odd_out, acc, keep):
-    step = pl.program_id(0)
-    last = pl.num_programs(0) - 1
-    block = lower.shape[-1]
+
+    def loads(level, p):
+        rows = pl.ds(2 * p, 2)
+        copies = [
+            pltpu.make_async_copy(lower_hbm.at[level, rows], lower.at[level, rows], sems.at[level, 0, p]),
+            pltpu.make_async_copy(inverse_hbm.at[level, rows], inverse.at[level, rows], sems.at[level, 1, p]),
+        ]
+        if level:
+            copies.append(pltpu.make_async_copy(right_hbm.at[1, rows], right.at[rows], sems.at[level, 2, p]))
+        return copies
+
+    def start(level):
+        for p in range(pairs):
+            for copy in loads(level, p):
+                copy.start()
+
+    def pair(level, p, wide):
+        for copy in loads(level, p):
+            copy.wait()
+        for half in range(2):
+            q = 2 * p + half
+            blocks = [lower[level, q, k] for k in range(lower.shape[2])]
+            premultiplied(meta, depend, scale, blocks, inverse[level, q], acc.at[half], level, q)
+            at = slice(half * block, (half + 1) * block)
+            for d in range(SPAN):
+                wide[p, at, (d + half) * block : (d + half + 1) * block] = (-acc[half, d]).astype(wide.dtype)
+            other = 0 if half else SPAN
+            wide[p, at, other * block : (other + 1) * block] = jnp.zeros((block, block), wide.dtype)
+
+    start(1)
 
     @pl.when(meta[0] > 0)
     def _():
+        start(0)
+
+    @pl.loop(0, pairs)
+    def _(p):
+        pair(1, p, wide_b)
         for half in range(2):
-            premultiply(meta, depend, scale, lower, inverse, wide_a, acc, 0, 2 * step + half, half, keep)
-
-    for half in range(2):
-        premultiply(meta, depend, scale, lower, inverse, wide_b, acc, 1, 2 * step + half, half)
-        base[half] = dot(inverse[1, half], right[0, half])
-
-    def emit(ref):
-        for half in range(2):
-            for d in range(SPAN):
-                ref[half * EDGE + d] = keep[half, d]
-            for chunk in range(CHUNKS):
-                ref[half * EDGE + SPAN + chunk] = first[half, :, chunk * block : (chunk + 1) * block]
-
-    odd = meta[1]
-    at_low, at_high = step == 0, step == last
-
-    @pl.when((at_low & (odd == 1)) | (at_high & (odd == 0)))
-    def _():
-        emit(even_out)
-
-    @pl.when((at_low & (odd == 0)) | (at_high & (odd == 1)))
-    def _():
-        emit(odd_out)
-
-
-def order_kernel(applies, meta, even_in, odd_in, edges):
-    @pl.when(applies(meta[0]))
+            base[2 * p + half] = dot(inverse[1, 2 * p + half], right[2 * p + half])
+
+    @pl.when(meta[0] > 0)
+    def _():
+        @pl.loop(0, pairs)
+        def _(p):
+            pair(0, p, wide_a)
+
+
+def order_kernel(meta, even_a, odd_a, even_b, odd_b, edges):
+    @pl.when(meta[0] > 1)
     def _():
         odd = meta[1]
-        edges[1 - odd] = even_in[...]
-        edges[odd] = odd_in[...]
+        soon = even_a.shape[0]
+        edges[1 - odd, :soon] = even_a[...]
+        edges[1 - odd, soon:] = even_b[...]
+        edges[odd, :soon] = odd_a[...]
+        edges[odd, soon:] = odd_b[...]
 
 
 def flat(ref, start, count, at=slice(None)):
@@ -229,9 +268,18 @@
     @pl.when(meta[0] == group)
     def _():
         at = columns(chunk, solved.shape[-1])
-        count = own.shape[0]
+        count, block = own.shape[0], own.shape[1]
         level_a[REACH : REACH + count] = own[:, :, at]
-        place(level_a, meta[1], even_in, odd_in, at)
+        if even_in.shape[0] == REACH:
+            place(level_a, meta[1], even_in, odd_in, at)
+        else:
+            parts = even_in.shape[0] // REACH
+            low, high = 0, count + REACH
+            for i in range(REACH):
+                for part in range(parts):
+                    cols = slice(part * block, (part + 1) * block)
+                    level_a[i + jnp.where(meta[1] == 1, low, high), :, cols] = even_in[i * parts + part]
+                    level_a[i + jnp.where(meta[1] == 1, high, low), :, cols] = odd_in[i * parts + part]
         second_of_group(wide_b, base_b, level_a, solved, at)
         emit_sends(meta[1], solved, (even_out, odd_out))
 
@@ -343,9 +391,8 @@
         ]
 
     def travel(group, centre, sides):
-        side_table = hop_pairs if group else side_pairs
         return [lax.ppermute(centre, AXES, hop_pairs(group, same_row, chain, rows))] + [
-            lax.ppermute(value, AXES, side_table(group, mate, chain, rows)) for value, mate in zip(sides, mates)
+            lax.ppermute(value, AXES, hop_pairs(group, mate, chain, rows)) for value, mate in zip(sides, mates)
         ]
 
     def call(kernel, name, in_specs, out_shape, out_specs=None, **more):
@@ -362,42 +409,40 @@
     whole, half = shaped((count, block, cases)), shaped((count, block, part))
     whole_edge, half_edge = shaped((REACH, block, cases)), shaped((halo, block, part))
 
-    first, *sides = call(
+    total = REACH * EDGE
+    soon = REACH * cases // block
+    edge_shapes = [shaped((size, block, block)) for size in (soon, total - soon)]
+    first, *edge_w = call(
         first_kernel,
         "first_level",
-        [SMEM, HBM, HBM],
-        [whole, whole_edge, whole_edge],
+        [SMEM, SMEM, SMEM, HBM, HBM, HBM],
+        [whole, *(shape for shape in edge_shapes for _ in range(2))],
         scratch_shapes=[
             pltpu.VMEM((count, block, block), jnp.bfloat16),
             pltpu.VMEM(whole.shape, jnp.bfloat16),
-            pltpu.SemaphoreType.DMA((2, 2)),
+            pltpu.VMEM((2, REACH, terms, block, block), jnp.bfloat16),
+            pltpu.VMEM((REACH, SPAN, block, block), jnp.float32),
+            pltpu.VMEM((2, total, block, block), jnp.bfloat16),
+            pltpu.SemaphoreType.DMA((3, 4)),
         ],
-    )(meta, diag_inverse, right_side)
-    sides = exchange([0], sides)
+    )(meta, depend, scale, lower_blocks, diag_inverse, right_side)
+    sides = exchange([0, *range(2, chain)], edge_w[:2], 1)
 
     pairs = count // 2
     wide_shape = shaped((pairs, 2 * block, width + block))
-    wide_spec = pl.BlockSpec((1, 2 * block, width + block), lambda i: (i, 0, 0))
-    edge_shape = shaped((REACH * EDGE, block, block))
-    edge_spec = pl.BlockSpec(edge_shape.shape, lambda i: (0, 0, 0))
-
-    wide_a, wide_b, base_b, *edge_w = call(
+    wide_b, wide_a, base_b = call(
         prepare_kernel,
         "prepare",
-        [
-            SMEM,
-            SMEM,
-            SMEM,
-            pl.BlockSpec((2, 2, terms, block, block), lambda i: (0, i, 0, 0, 0)),
-            pl.BlockSpec((2, 2, block, block), lambda i: (0, i, 0, 0)),
-            pl.BlockSpec((1, 2, block, cases), lambda i: (1, i, 0, 0)),
-            pl.BlockSpec((2, block, cases), lambda i: (i, 0, 0)),
+        [SMEM, SMEM, SMEM, HBM, HBM, HBM],
+        [wide_shape, wide_shape, shaped(whole.shape, jnp.float32)],
+        scratch_shapes=[
+            pltpu.VMEM(lower_blocks.shape, jnp.bfloat16),
+            pltpu.VMEM(diag_inverse.shape, jnp.bfloat16),
+            pltpu.VMEM(whole.shape, jnp.bfloat16),
+            pltpu.VMEM((2, SPAN, block, block), jnp.float32),
+            pltpu.SemaphoreType.DMA((2, 3, pairs)),
         ],
-        [wide_shape, wide_shape, shaped((count, block, cases), jnp.float32), edge_shape, edge_shape],
-        [wide_spec, wide_spec, pl.BlockSpec((2, block, cases), lambda i: (i, 0, 0)), edge_spec, edge_spec],
-        grid=(pairs,),
-        scratch_shapes=[pltpu.VMEM((SPAN, block, block), jnp.float32), pltpu.VMEM((2, SPAN, block, block), jnp.bfloat16)],
-    )(meta, depend, scale, lower_blocks, diag_inverse, right_side, first)
+    )(meta, depend, scale, lower_blocks, diag_inverse, right_side)
 
     padded = pltpu.VMEM((count + halo, block, cases), jnp.bfloat16)
     padded_half = pltpu.VMEM((count + halo, block, part), jnp.bfloat16)
@@ -410,15 +455,10 @@
     )(meta, first, *sides, wide_b, base_b)
     arrived = travel(0, solved, sends)
 
-    def ordered(applies, moved):
-        kernel = functools.partial(order_kernel, applies)
-        return call(kernel, "order", [SMEM, VMEM, VMEM], [shaped((2, *edge_shape.shape))])(meta, *moved)[0]
-
-    early = exchange([2], after(edge_w, sides), 3)
-    edges = [ordered(lambda group: group == 2, early)]
-    if chain > 3:
-        late = exchange(range(3, chain), after(edge_w, early), 2)
-        edges.append(ordered(lambda group: group > 2, late))
+    later_w = exchange(range(2, chain), after(edge_w[2:], sides))
+    edges, = call(
+        order_kernel, "order", [SMEM] + [VMEM] * 4, [shaped((2, total, block, block))]
+    )(meta, *sides, *later_w)
 
     out, own, *sides = call(
         functools.partial(level_step, 1),
@@ -428,7 +468,7 @@
         [ANY] + [VMEM] * 3,
         scratch_shapes=[padded, pltpu.SemaphoreType.DMA((2,))],
     )(meta, *arrived, first, wide_a, solved)
-    sides = after(exchange([1], sides), early)
+    sides = exchange([1], sides, 0)
     made_a = [own] * CHUNKS
     sent = []
     for chunk in range(CHUNKS):
@@ -467,7 +507,7 @@
             )(
                 meta,
                 *arrived[chunk],
-                edges[min(group, 3) - 2],
+                edges,
                 first,
                 wide_a,
                 wide_b,

time: 61.6 us -> 55.8 us (0.906)
  waiting for transfers between devices: 16.2 us -> 9.54 us
  local copies, waits for them, and re-layouts: 0.01 us -> 1.38 us
  starting transfers between devices: 27.5 us -> 26.7 us
    ppermute x8 -> x6, starting transfers between devices: 11.6 us -> 3.2 us  [exchange(): lax.ppermute(value, AXES, inner_pairs(groups, mate, chain, rows, idle))]
    ppermute x8 -> x6, waiting for transfers between devices: 7.21 us -> 1.63 us  [exchange(): lax.ppermute(value, AXES, inner_pairs(groups, mate, chain, rows, idle))]
    ppermute x5, starting transfers between devices: 10.8 us -> 15.2 us  [travel(): lax.ppermute(centre, AXES, hop_pairs(group, same_row, chain, rows))]
    ppermute x10, starting transfers between devices: 5.04 us -> 8.31 us  [travel(): lax.ppermute(value, AXES, hop_pairs(group, mate, chain, rows))]
    unnamed x4, local copies, waits for them, and re-layouts: 0.01 us -> 1.38 us
    ppermute x10, waiting for transfers between devices: 8.94 us -> 7.9 us  [travel(): lax.ppermute(value, AXES, hop_pairs(group, mate, chain, rows))]
    pallas_call x4 -> x3, Pallas kernels: 8.1 us -> 8.64 us  [the longest x1 4.82 us: per_device(): call(prepare_kernel, 'prepare', [SMEM, SMEM, SMEM, HBM, HBM, HBM], [wide_...]
  transfers between devices with their start and end apart: 23 -> 21, of which waited for: 6 -> 9; matrix products, arithmetic and copies ran while one was open for 0% -> 0% of each run, Pallas kernels for 17% -> 18%
where the time goes in v8:
time: 55.8 us; the launch traced here: 55.4 us
  starting transfers between devices  26.7 us (48%)
  Pallas kernels  17.5 us (31%)
  waiting for transfers between devices  9.54 us (17%)
  local copies, waits for them, and re-layouts  1.38 us (2%)
    ppermute x5, starting transfers between devices, travel(): lax.ppermute(centre, AXES, hop_pairs(group, same_row, chain, rows))  15.2 us
    ppermute x10, starting transfers between devices, travel(): lax.ppermute(value, AXES, hop_pairs(group, mate, chain, rows))  8.31 us
    ppermute x10, waiting for transfers between devices, travel(): lax.ppermute(value, AXES, hop_pairs(group, mate, chain, rows))  7.9 us
    pallas_call x4, Pallas kernels, per_device(): call(functools.partial(later_step, group, chunk, final), f'step_{group}_{...  6.64 us
    pallas_call x1, Pallas kernels, per_device(): call(prepare_kernel, 'prepare', [SMEM, SMEM, SMEM, HBM, HBM, HBM], [wide_...  4.82 us
    pallas_call x1, Pallas kernels, per_device(): call(first_kernel, 'first_level', [SMEM, SMEM, SMEM, HBM, HBM, HBM], [who...  3.22 us
    ppermute x6, starting transfers between devices, exchange(): lax.ppermute(value, AXES, inner_pairs(groups, mate, chain, rows, idle))  3.2 us
    ppermute x6, waiting for transfers between devices, exchange(): lax.ppermute(value, AXES, inner_pairs(groups, mate, chain, rows, idle))  1.63 us
  transfers between devices with their start and end apart: 21, of which 9 were waited for; matrix products, arithmetic and copies ran while one was open for 0% of the time, Pallas kernels for 18%

profile of v8, /device:TPU:11, one launch (start us, length us, event | category | flops | bytes accessed | tf_op | source)
XLA Modules:
  0.0 55.4 jit_solution(7702159938628010883)
XLA Ops:
  0.0 0.1 pad_add_fusion.meta
  0.1 0.7 %copy-done = s32[2,8,6]{1,0,2:T(2,128)S(1)} copy-done((s32[2,8,6]{1,0,2:T(2,128)S(1)}, s32[2,8,6]{1,0,2:T(2,128)}, u32[]{:S(2)}) %copy-start) | copy-done | bytes 408
  0.8 0.7 %copy-done.1 = f32[2,8,6]{1,0,2:T(2,128)S(1)} copy-done((f32[2,8,6]{1,0,2:T(2,128)S(1)}, f32[2,8,6]{1,0,2:T(2,128)}, u32[]{:S(2)}) %copy-start.1) | copy-done | bytes 408
  1.5 3.2 %first_level.1 = (bf16[8,128,256]{2,1,0:T(8,128)(2,1)S(1)}, bf16[4,128,128]{2,1,0:T(8,128)(2,1)S(1)}, bf16[4,128,128]{2,1,0:T(8,128)(2,1)S(1)}, bf16[10,128,128]...) custom-call(s32[3]{0:T(128)S(1)} %pad_add_fusion.meta, s32[6,2,8]{2,1,0:T(2,128)S(1)} %bitcast.5, f32[6,2,8]{2,1,0:T(2,128)S(1)} %bitcast.7, ...), custom_call_target="tpu_custom_call" | custom-call | tf_op jit(solution)/shard_map/first_level/pallas_call | solution.py:415
  4.7 1.3 %collective-permute-start = (bf16[4,128,128]{2,1,0:T(8,128)(2,1)S(1)}, bf16[4,128,128]{2,1,0:T(8,128)(2,1)S(1)}, u32[]{:S(2)}, u32[]{:S(2)}) collective-permute-start(bf16[4,128,128]{2,1,0:T(8,128)(2,1)S(1)} %get-tuple-element.43), channel_id=1, source_target_pairs={{0,1},{16,17},{24,25},{8,10},{1,0},{17,16},{25,24},{9,11},{2,3},{1... | collective-permute-start | bytes 393224 | tf_op jit(solution)/shard_map/ppermute | solution.py:389
  6.0 0.1 collective-permute-start.1
  6.1 4.8 %prepare.1 = (bf16[4,256,768]{2,1,0:T(8,128)(2,1)S(1)}, bf16[4,256,768]{2,1,0:T(8,128)(2,1)S(1)}, f32[8,128,256]{2,1,0:T(8,128)S(1)}) custom-call(s32[3]{0:T(128)S(1)} %pad_add_fusion.meta, s32[6,2,8]{2,1,0:T(2,128)S(1)} %bitcast.6, f32[6,2,8]{2,1,0:T(2,128)S(1)} %bitcast.8, bf16[2,8,6,128,128]{4,3,2,1,0:T(8,128)(2,1)} %lower_hbm.3, ...), custom_call_target="tpu_custom_call" | custom-call | tf_op jit(solution)/shard_map/prepare/pallas_call | solution.py:433
  10.9 0.0 collective-permute-done.even_in.even_a
  10.9 0.0 collective-permute-done.1.odd_in.odd_a
  10.9 0.6 step_0.1
  11.5 2.6 %collective-permute-start.2 = (bf16[8,128,256]{2,1,0:T(8,128)(2,1)S(1)}, bf16[8,128,256]{2,1,0:T(8,128)(2,1)S(1)}, u32[]{:S(2)}, u32[]{:S(2)}) collective-permute-start(bf16[8,128,256]{2,1,0:T(8,128)(2,1)S(1)} %get-tuple-element.47.old_b), channel_id=1, source_target_pairs={{0,8},{1,9},{2,10},{3,11},{4,12},{5,13},{6,14},{7,15},{8,0},{9,1},... | collective-permute-start | bytes 1572872 | tf_op jit(solution)/shard_map/ppermute | solution.py:394
  14.1 0.1 collective-permute-start.3
  14.2 0.4 collective-permute-start.4
  14.6 1.2 %collective-permute-start.10 = (bf16[10,128,128]{2,1,0:T(8,128)(2,1)S(1)}, bf16[10,128,128]{2,1,0:T(8,128)(2,1)S(1)}, u32[]{:S(2)}, u32[]{:S(2)}) collective-permute-start(bf16[10,128,128]{2,1,0:T(8,128)(2,1)S(1)} %get-tuple-element.59), channel_id=1, source_target_pairs={{16,17},{24,25},{0,8},{8,0},{17,16},{25,24},{1,9},{9,1},{18,19},{2... | collective-permute-start | bytes 983048 | tf_op jit(solution)/shard_map/ppermute | solution.py:389
  15.8 0.0 collective-permute-start.11
  15.8 0.2 collective-permute-done.4.odd_in
  16.0 0.0 collective-permute-done.2.centre
  16.0 0.6 %step_1.1 = (bf16[2,8,128,256]{3,2,1,0:T(8,128)(2,1)}, bf16[8,128,256]{2,1,0:T(8,128)(2,1)S(1)}, bf16[2,128,256]{2,1,0:T(8,128)(2,1)S(1)}, bf16[2,128,256]{2,1,0:T(8,128)(2,1)S(1)}) custom-call(s32[3]{0:T(128)S(1)} %pad_add_fusion.meta, bf16[8,128,256]{2,1,0:T(8,128)(2,1)S(1)} %collective-permute-done.2.centre, ...), custom_call_target="tpu_custom_call" | custom-call | tf_op jit(solution)/shard_map/step_1/pallas_call | solution.py:463
  16.6 0.4 collective-permute-start.5
  17.0 0.1 collective-permute-start.6
  17.1 0.8 %collective-permute-done.5.even_in = bf16[2,128,256]{2,1,0:T(8,128)(2,1)S(1)} collective-permute-done((bf16[2,128,256]{2,1,0:T(8,128)(2,1)S(1)}, bf16[2,128,256]{2,1,0:T(8,128)(2,1)S(1)}, u32[]{:S(2)}, u32[]{:S(2)}) %collective-permute-start.5) | collective-permute-done | bytes 131104 | tf_op jit(solution)/shard_map/ppermute | solution.py:389
  18.0 0.4 collective-permute-done.6.odd_in
  18.4 0.5 step_1_0.1
  18.9 10.2 %collective-permute-start.12 = (bf16[8,128,128]{2,1,0:T(8,128)(2,1)S(1)}, bf16[8,128,128]{2,1,0:T(8,128)(2,1)S(1)}, u32[]{:S(2)}, u32[]{:S(2)}) collective-permute-start(bf16[8,128,128]{2,1,0:T(8,128)(2,1)S(1)} %get-tuple-element.61.old_b), channel_id=1, source_target_pairs={{8,16},{9,17},{10,18},{11,19},{12,20},{13,21},{14,22},{15,23},{0,8... | collective-permute-start | bytes 786440 | tf_op jit(solution)/shard_map/ppermute | solution.py:394
  29.1 0.7 %collective-permute-start.13 = (bf16[4,128,128]{2,1,0:T(8,128)(2,1)S(1)}, bf16[4,128,128]{2,1,0:T(8,128)(2,1)S(1)}, u32[]{:S(2)}, u32[]{:S(2)}) collective-permute-start(bf16[4,128,128]{2,1,0:T(8,128)(2,1)S(1)} %get-tuple-element.62), channel_id=1, source_target_pairs={{8,17},{9,16},{10,19},{11,18},{12,21},{13,20},{14,23},{15,22},{0,8... | collective-permute-start | bytes 393224 | tf_op jit(solution)/shard_map/ppermute | solution.py:395
  29.8 0.5 step_1_1.1
  30.4 0.1 collective-permute-start.7
  30.5 0.4 collective-permute-done.10.even_b
  30.9 0.2 collective-permute-start.14
  31.1 0.8 %collective-permute-start.8 = (bf16[4,128,128]{2,1,0:T(8,128)(2,1)S(1)}, bf16[4,128,128]{2,1,0:T(8,128)(2,1)S(1)}, u32[]{:S(2)}, u32[]{:S(2)}) collective-permute-start(bf16[4,128,128]{2,1,0:T(8,128)(2,1)S(1)} %get-tuple-element.55), channel_id=1, source_target_pairs={{8,17},{9,16},{10,19},{11,18},{12,21},{13,20},{14,23},{15,22},{0,8... | collective-permute-start | bytes 393224 | tf_op jit(solution)/shard_map/ppermute | solution.py:395
  31.9 1.8 %collective-permute-done.13.even_in = bf16[4,128,128]{2,1,0:T(8,128)(2,1)S(1)} collective-permute-done((bf16[4,128,128]{2,1,0:T(8,128)(2,1)S(1)}, bf16[4,128,128]{2,1,0:T(8,128)(2,1)S(1)}, u32[]{:S(2)}, u32[]{:S(2)}) %collective-permute-start.13) | collective-permute-done | bytes 131104 | tf_op jit(solution)/shard_map/ppermute | solution.py:395
  33.8 2.5 %collective-permute-start.9 = (bf16[4,128,128]{2,1,0:T(8,128)(2,1)S(1)}, bf16[4,128,128]{2,1,0:T(8,128)(2,1)S(1)}, u32[]{:S(2)}, u32[]{:S(2)}) collective-permute-start(bf16[4,128,128]{2,1,0:T(8,128)(2,1)S(1)} %get-tuple-element.56), channel_id=1, source_target_pairs={{8,16},{9,18},{10,17},{11,20},{12,19},{13,22},{14,21},{15,23},{0,8... | collective-permute-start | bytes 393224 | tf_op jit(solution)/shard_map/ppermute | solution.py:395
  36.3 0.6 %order.1.edges = bf16[2,14,128,128]{3,2,1,0:T(8,128)(2,1)S(1)} custom-call(s32[3]{0:T(128)S(1)} %pad_add_fusion.meta, bf16[4,128,128]{2,1,0:T(8,128)(2,1)S(1)} %collective-permute-done.even_in.even_a, bf16[4,128,128]{2,1,0:T(8,128)(2,1)S(1)} %collective-permute-done.1.odd_in.odd_a, bf16[10,128,128]{2,1,0:T(8,128)(2,1)S(1)} %collective-permute-done.10.even_b, ...), custom_call_target="tpu_custom_call" | custom-call | tf_op jit(solution)/shard_map/order/pallas_call | solution.py:459
  36.9 1.1 %collective-permute-done.14.odd_in = bf16[4,128,128]{2,1,0:T(8,128)(2,1)S(1)} collective-permute-done((bf16[4,128,128]{2,1,0:T(8,128)(2,1)S(1)}, bf16[4,128,128]{2,1,0:T(8,128)(2,1)S(1)}, u32[]{:S(2)}, u32[]{:S(2)}) %collective-permute-start.14) | collective-permute-done | bytes 131104 | tf_op jit(solution)/shard_map/ppermute | solution.py:395
  38.0 0.0 collective-permute-done.12.centre
  38.0 0.6 %step_2_0.1 = (bf16[2,8,128,256]{3,2,1,0:T(8,128)(2,1)}, bf16[8,128,128]{2,1,0:T(8,128)(2,1)S(1)}, bf16[8,128,128]{2,1,0:T(8,128)(2,1)S(1)}, bf16[4,128,128]{2,1,0:T(8,128)(2,1)S(1)}, bf16[4,128,128]{2,1,0:T(8,128)(2,1)S(1)}) custom-call(s32[3]{0:T(128)S(1)} %pad_add_fusion.meta, ...), custom_call_target="tpu_custom_call", output_to_operand_aliasing={{0}: (11, {})} | custom-call | tf_op jit(solution)/shard_map/step_2_0/pallas_call | solution.py:494
  38.6 1.3 %collective-permute-start.19 = (bf16[4,128,128]{2,1,0:T(8,128)(2,1)S(1)}, bf16[4,128,128]{2,1,0:T(8,128)(2,1)S(1)}, u32[]{:S(2)}, u32[]{:S(2)}) collective-permute-start(bf16[4,128,128]{2,1,0:T(8,128)(2,1)S(1)} %get-tuple-element.71), channel_id=1, source_target_pairs={{0,8},{1,9},{2,10},{3,11},{4,12},{5,13},{6,14},{7,15},{8,0},{9,1},... | collective-permute-start | bytes 393224 | tf_op jit(solution)/shard_map/ppermute | solution.py:395
  39.9 0.1 collective-permute-start.18
  40.0 0.8 %collective-permute-done.9.odd_in = bf16[4,128,128]{2,1,0:T(8,128)(2,1)S(1)} collective-permute-done((bf16[4,128,128]{2,1,0:T(8,128)(2,1)S(1)}, bf16[4,128,128]{2,1,0:T(8,128)(2,1)S(1)}, u32[]{:S(2)}, u32[]{:S(2)}) %collective-permute-start.9) | collective-permute-done | bytes 131104 | tf_op jit(solution)/shard_map/ppermute | solution.py:395
  40.8 0.6 %step_2_1.1 = (bf16[2,8,128,256]{3,2,1,0:T(8,128)(2,1)}, bf16[8,128,128]{2,1,0:T(8,128)(2,1)S(1)}, bf16[8,128,128]{2,1,0:T(8,128)(2,1)S(1)}, bf16[4,128,128]{2,1,0:T(8,128)(2,1)S(1)}, bf16[4,128,128]{2,1,0:T(8,128)(2,1)S(1)}) custom-call(s32[3]{0:T(128)S(1)} %pad_add_fusion.meta, ...), custom_call_target="tpu_custom_call", output_to_operand_aliasing={{0}: (11, {})} | custom-call | tf_op jit(solution)/shard_map/step_2_1/pallas_call | solution.py:494
  41.4 2.3 %collective-permute-start.15 = (bf16[8,128,128]{2,1,0:T(8,128)(2,1)S(1)}, bf16[8,128,128]{2,1,0:T(8,128)(2,1)S(1)}, u32[]{:S(2)}, u32[]{:S(2)}) collective-permute-start(bf16[8,128,128]{2,1,0:T(8,128)(2,1)S(1)} %get-tuple-element.66.old_b), channel_id=1, source_target_pairs={{0,8},{1,9},{2,10},{3,11},{4,12},{5,13},{6,14},{7,15},{8,0},{9,1},... | collective-permute-start | bytes 786440 | tf_op jit(solution)/shard_map/ppermute | solution.py:394
  43.7 0.1 collective-permute-start.20
  43.8 1.6 %collective-permute-start.16 = (bf16[4,128,128]{2,1,0:T(8,128)(2,1)S(1)}, bf16[4,128,128]{2,1,0:T(8,128)(2,1)S(1)}, u32[]{:S(2)}, u32[]{:S(2)}) collective-permute-start(bf16[4,128,128]{2,1,0:T(8,128)(2,1)S(1)} %get-tuple-element.67), channel_id=1, source_target_pairs={{0,8},{1,9},{2,10},{3,11},{4,12},{5,13},{6,14},{7,15},{8,0},{9,1},... | collective-permute-start | bytes 393224 | tf_op jit(solution)/shard_map/ppermute | solution.py:395
  45.3 0.6 %collective-permute-start.17 = (bf16[4,128,128]{2,1,0:T(8,128)(2,1)S(1)}, bf16[4,128,128]{2,1,0:T(8,128)(2,1)S(1)}, u32[]{:S(2)}, u32[]{:S(2)}) collective-permute-start(bf16[4,128,128]{2,1,0:T(8,128)(2,1)S(1)} %get-tuple-element.68), channel_id=1, source_target_pairs={{0,8},{1,9},{2,10},{3,11},{4,12},{5,13},{6,14},{7,15},{8,0},{9,1},... | collective-permute-start | bytes 393224 | tf_op jit(solution)/shard_map/ppermute | solution.py:395
  45.9 3.2 %collective-permute-done.20.odd_in = bf16[4,128,128]{2,1,0:T(8,128)(2,1)S(1)} collective-permute-done((bf16[4,128,128]{2,1,0:T(8,128)(2,1)S(1)}, bf16[4,128,128]{2,1,0:T(8,128)(2,1)S(1)}, u32[]{:S(2)}, u32[]{:S(2)}) %collective-permute-start.20) | collective-permute-done | bytes 131104 | tf_op jit(solution)/shard_map/ppermute | solution.py:395
  49.1 1.9 %step_3_0.1 = (bf16[2,8,128,256]{3,2,1,0:T(8,128)(2,1)}, bf16[8,128,128]{2,1,0:T(8,128)(2,1)S(1)}, bf16[8,128,128]{2,1,0:T(8,128)(2,1)S(1)}) custom-call(s32[3]{0:T(128)S(1)} %pad_add_fusion.meta, bf16[8,128,128]{2,1,0:T(8,128)(2,1)S(1)} %collective-permute-done.18.centre, ...), custom_call_target="tpu_custom_call", output_to_operand_aliasing={{0}: (11, {})} | custom-call | tf_op jit(solution)/shard_map/step_3_0/pallas_call | solution.py:494
  51.0 0.8 %collective-permute-done.16.even_in = bf16[4,128,128]{2,1,0:T(8,128)(2,1)S(1)} collective-permute-done((bf16[4,128,128]{2,1,0:T(8,128)(2,1)S(1)}, bf16[4,128,128]{2,1,0:T(8,128)(2,1)S(1)}, u32[]{:S(2)}, u32[]{:S(2)}) %collective-permute-start.16) | collective-permute-done | bytes 131104 | tf_op jit(solution)/shard_map/ppermute | solution.py:395
  51.8 3.6 %step_3_1.1 = (bf16[2,8,128,256]{3,2,1,0:T(8,128)(2,1)}, bf16[8,128,128]{2,1,0:T(8,128)(2,1)}, bf16[8,128,128]{2,1,0:T(8,128)(2,1)}) custom-call(s32[3]{0:T(128)S(1)} %pad_add_fusion.meta, bf16[8,128,128]{2,1,0:T(8,128)(2,1)S(1)} %collective-permute-done.15.centre, ...), custom_call_target="tpu_custom_call", output_to_operand_aliasing={{0}: (13, {})} | custom-call | tf_op jit(solution)/shard_map/step_3_1/pallas_call | solution.py:494
  (10 shorter events, 0.0 us)
Async XLA Ops:
  0.1 0.7 %copy-start = (s32[2,8,6]{1,0,2:T(2,128)S(1)}, s32[2,8,6]{1,0,2:T(2,128)}, u32[]{:S(2)}) copy-start(s32[2,8,6]{1,0,2:T(2,128)} %param.9) | copy-start | bytes 1156
  0.8 0.7 %copy-start.1 = (f32[2,8,6]{1,0,2:T(2,128)S(1)}, f32[2,8,6]{1,0,2:T(2,128)}, u32[]{:S(2)}) copy-start(f32[2,8,6]{1,0,2:T(2,128)} %param.7) | copy-start | bytes 1156
  4.7 6.2 %collective-permute-start = (bf16[4,128,128]{2,1,0:T(8,128)(2,1)S(1)}, bf16[4,128,128]{2,1,0:T(8,128)(2,1)S(1)}, u32[]{:S(2)}, u32[]{:S(2)}) collective-permute-start(bf16[4,128,128]{2,1,0:T(8,128)(2,1)S(1)} %get-tuple-element.43), channel_id=1, source_target_pairs={{0,1},{16,17},{24,25},{8,10},{1,0},{17,16},{25,24},{9,11},{2,3},{1... | collective-permute-start | bytes 393224 | tf_op jit(solution)/shard_map/ppermute | solution.py:389
  6.0 5.0 %collective-permute-start.1 = (bf16[4,128,128]{2,1,0:T(8,128)(2,1)S(1)}, bf16[4,128,128]{2,1,0:T(8,128)(2,1)S(1)}, u32[]{:S(2)}, u32[]{:S(2)}) collective-permute-start(bf16[4,128,128]{2,1,0:T(8,128)(2,1)S(1)} %get-tuple-element.44), channel_id=1, source_target_pairs={{0,8},{8,0},{16,24},{24,16},{1,2},{17,18},{25,26},{9,11},{2,1},{18... | collective-permute-start | bytes 393224 | tf_op jit(solution)/shard_map/ppermute | solution.py:389
  11.5 4.5 %collective-permute-start.2 = (bf16[8,128,256]{2,1,0:T(8,128)(2,1)S(1)}, bf16[8,128,256]{2,1,0:T(8,128)(2,1)S(1)}, u32[]{:S(2)}, u32[]{:S(2)}) collective-permute-start(bf16[8,128,256]{2,1,0:T(8,128)(2,1)S(1)} %get-tuple-element.47.old_b), channel_id=1, source_target_pairs={{0,8},{1,9},{2,10},{3,11},{4,12},{5,13},{6,14},{7,15},{8,0},{9,1},... | collective-permute-start | bytes 1572872 | tf_op jit(solution)/shard_map/ppermute | solution.py:394
  14.1 1.8 %collective-permute-start.3 = (bf16[2,128,256]{2,1,0:T(8,128)(2,1)S(1)}, bf16[2,128,256]{2,1,0:T(8,128)(2,1)S(1)}, u32[]{:S(2)}, u32[]{:S(2)}) collective-permute-start(bf16[2,128,256]{2,1,0:T(8,128)(2,1)S(1)} %get-tuple-element.48), channel_id=1, source_target_pairs={{0,9},{1,8},{2,11},{3,10},{4,13},{5,12},{6,15},{7,14},{8,0},{9,1},... | collective-permute-start | bytes 393224 | tf_op jit(solution)/shard_map/ppermute | solution.py:395
  14.2 1.8 %collective-permute-start.4 = (bf16[2,128,256]{2,1,0:T(8,128)(2,1)S(1)}, bf16[2,128,256]{2,1,0:T(8,128)(2,1)S(1)}, u32[]{:S(2)}, u32[]{:S(2)}) collective-permute-start(bf16[2,128,256]{2,1,0:T(8,128)(2,1)S(1)} %get-tuple-element.49), channel_id=1, source_target_pairs={{0,8},{1,10},{2,9},{3,12},{4,11},{5,14},{6,13},{7,15},{8,0},{9,1},... | collective-permute-start | bytes 393224 | tf_op jit(solution)/shard_map/ppermute | solution.py:395
  14.6 16.3 %collective-permute-start.10 = (bf16[10,128,128]{2,1,0:T(8,128)(2,1)S(1)}, bf16[10,128,128]{2,1,0:T(8,128)(2,1)S(1)}, u32[]{:S(2)}, u32[]{:S(2)}) collective-permute-start(bf16[10,128,128]{2,1,0:T(8,128)(2,1)S(1)} %get-tuple-element.59), channel_id=1, source_target_pairs={{16,17},{24,25},{0,8},{8,0},{17,16},{25,24},{1,9},{9,1},{18,19},{2... | collective-permute-start | bytes 983048 | tf_op jit(solution)/shard_map/ppermute | solution.py:389
  15.8 15.3 %collective-permute-start.11 = (bf16[10,128,128]{2,1,0:T(8,128)(2,1)S(1)}, bf16[10,128,128]{2,1,0:T(8,128)(2,1)S(1)}, u32[]{:S(2)}, u32[]{:S(2)}) collective-permute-start(bf16[10,128,128]{2,1,0:T(8,128)(2,1)S(1)} %get-tuple-element.60), channel_id=1, source_target_pairs={{0,8},{8,0},{16,24},{24,16},{17,18},{25,26},{1,9},{9,1},{18,17},{2... | collective-permute-start | bytes 983048 | tf_op jit(solution)/shard_map/ppermute | solution.py:389
  16.6 1.4 %collective-permute-start.5 = (bf16[2,128,256]{2,1,0:T(8,128)(2,1)S(1)}, bf16[2,128,256]{2,1,0:T(8,128)(2,1)S(1)}, u32[]{:S(2)}, u32[]{:S(2)}) collective-permute-start(bf16[2,128,256]{2,1,0:T(8,128)(2,1)S(1)} %get-tuple-element.52), channel_id=1, source_target_pairs={{8,9},{0,2},{16,24},{24,16},{9,8},{1,3},{17,25},{25,17},{10,11},{2... | collective-permute-start | bytes 393224 | tf_op jit(solution)/shard_map/ppermute | solution.py:389
  17.0 1.3 %collective-permute-start.6 = (bf16[2,128,256]{2,1,0:T(8,128)(2,1)S(1)}, bf16[2,128,256]{2,1,0:T(8,128)(2,1)S(1)}, u32[]{:S(2)}, u32[]{:S(2)}) collective-permute-start(bf16[2,128,256]{2,1,0:T(8,128)(2,1)S(1)} %get-tuple-element.53), channel_id=1, source_target_pairs={{0,8},{8,0},{16,24},{24,16},{9,10},{1,3},{17,25},{25,17},{10,9},{2... | collective-permute-start | bytes 393224 | tf_op jit(solution)/shard_map/ppermute | solution.py:389
  18.9 19.1 %collective-permute-start.12 = (bf16[8,128,128]{2,1,0:T(8,128)(2,1)S(1)}, bf16[8,128,128]{2,1,0:T(8,128)(2,1)S(1)}, u32[]{:S(2)}, u32[]{:S(2)}) collective-permute-start(bf16[8,128,128]{2,1,0:T(8,128)(2,1)S(1)} %get-tuple-element.61.old_b), channel_id=1, source_target_pairs={{8,16},{9,17},{10,18},{11,19},{12,20},{13,21},{14,22},{15,23},{0,8... | collective-permute-start | bytes 786440 | tf_op jit(solution)/shard_map/ppermute | solution.py:394
  29.1 4.7 %collective-permute-start.13 = (bf16[4,128,128]{2,1,0:T(8,128)(2,1)S(1)}, bf16[4,128,128]{2,1,0:T(8,128)(2,1)S(1)}, u32[]{:S(2)}, u32[]{:S(2)}) collective-permute-start(bf16[4,128,128]{2,1,0:T(8,128)(2,1)S(1)} %get-tuple-element.62), channel_id=1, source_target_pairs={{8,17},{9,16},{10,19},{11,18},{12,21},{13,20},{14,23},{15,22},{0,8... | collective-permute-start | bytes 393224 | tf_op jit(solution)/shard_map/ppermute | solution.py:395
  30.4 10.4 %collective-permute-start.7 = (bf16[8,128,128]{2,1,0:T(8,128)(2,1)S(1)}, bf16[8,128,128]{2,1,0:T(8,128)(2,1)S(1)}, u32[]{:S(2)}, u32[]{:S(2)}) collective-permute-start(bf16[8,128,128]{2,1,0:T(8,128)(2,1)S(1)} %get-tuple-element.54.old_b), channel_id=1, source_target_pairs={{8,16},{9,17},{10,18},{11,19},{12,20},{13,21},{14,22},{15,23},{0,8... | collective-permute-start | bytes 786440 | tf_op jit(solution)/shard_map/ppermute | solution.py:394
  30.9 7.1 %collective-permute-start.14 = (bf16[4,128,128]{2,1,0:T(8,128)(2,1)S(1)}, bf16[4,128,128]{2,1,0:T(8,128)(2,1)S(1)}, u32[]{:S(2)}, u32[]{:S(2)}) collective-permute-start(bf16[4,128,128]{2,1,0:T(8,128)(2,1)S(1)} %get-tuple-element.63), channel_id=1, source_target_pairs={{8,16},{9,18},{10,17},{11,20},{12,19},{13,22},{14,21},{15,23},{0,8... | collective-permute-start | bytes 393224 | tf_op jit(solution)/shard_map/ppermute | solution.py:395
  31.1 8.9 %collective-permute-start.8 = (bf16[4,128,128]{2,1,0:T(8,128)(2,1)S(1)}, bf16[4,128,128]{2,1,0:T(8,128)(2,1)S(1)}, u32[]{:S(2)}, u32[]{:S(2)}) collective-permute-start(bf16[4,128,128]{2,1,0:T(8,128)(2,1)S(1)} %get-tuple-element.55), channel_id=1, source_target_pairs={{8,17},{9,16},{10,19},{11,18},{12,21},{13,20},{14,23},{15,22},{0,8... | collective-permute-start | bytes 393224 | tf_op jit(solution)/shard_map/ppermute | solution.py:395
  33.8 7.0 %collective-permute-start.9 = (bf16[4,128,128]{2,1,0:T(8,128)(2,1)S(1)}, bf16[4,128,128]{2,1,0:T(8,128)(2,1)S(1)}, u32[]{:S(2)}, u32[]{:S(2)}) collective-permute-start(bf16[4,128,128]{2,1,0:T(8,128)(2,1)S(1)} %get-tuple-element.56), channel_id=1, source_target_pairs={{8,16},{9,18},{10,17},{11,20},{12,19},{13,22},{14,21},{15,23},{0,8... | collective-permute-start | bytes 393224 | tf_op jit(solution)/shard_map/ppermute | solution.py:395
  38.6 6.7 %collective-permute-start.19 = (bf16[4,128,128]{2,1,0:T(8,128)(2,1)S(1)}, bf16[4,128,128]{2,1,0:T(8,128)(2,1)S(1)}, u32[]{:S(2)}, u32[]{:S(2)}) collective-permute-start(bf16[4,128,128]{2,1,0:T(8,128)(2,1)S(1)} %get-tuple-element.71), channel_id=1, source_target_pairs={{0,8},{1,9},{2,10},{3,11},{4,12},{5,13},{6,14},{7,15},{8,0},{9,1},... | collective-permute-start | bytes 393224 | tf_op jit(solution)/shard_map/ppermute | solution.py:395
  39.9 9.2 %collective-permute-start.18 = (bf16[8,128,128]{2,1,0:T(8,128)(2,1)S(1)}, bf16[8,128,128]{2,1,0:T(8,128)(2,1)S(1)}, u32[]{:S(2)}, u32[]{:S(2)}) collective-permute-start(bf16[8,128,128]{2,1,0:T(8,128)(2,1)S(1)} %get-tuple-element.70.old_b), channel_id=1, source_target_pairs={{0,8},{1,9},{2,10},{3,11},{4,12},{5,13},{6,14},{7,15},{8,0},{9,1},... | collective-permute-start | bytes 786440 | tf_op jit(solution)/shard_map/ppermute | solution.py:394
  41.4 10.4 %collective-permute-start.15 = (bf16[8,128,128]{2,1,0:T(8,128)(2,1)S(1)}, bf16[8,128,128]{2,1,0:T(8,128)(2,1)S(1)}, u32[]{:S(2)}, u32[]{:S(2)}) collective-permute-start(bf16[8,128,128]{2,1,0:T(8,128)(2,1)S(1)} %get-tuple-element.66.old_b), channel_id=1, source_target_pairs={{0,8},{1,9},{2,10},{3,11},{4,12},{5,13},{6,14},{7,15},{8,0},{9,1},... | collective-permute-start | bytes 786440 | tf_op jit(solution)/shard_map/ppermute | solution.py:394
  43.7 5.4 %collective-permute-start.20 = (bf16[4,128,128]{2,1,0:T(8,128)(2,1)S(1)}, bf16[4,128,128]{2,1,0:T(8,128)(2,1)S(1)}, u32[]{:S(2)}, u32[]{:S(2)}) collective-permute-start(bf16[4,128,128]{2,1,0:T(8,128)(2,1)S(1)} %get-tuple-element.72), channel_id=1, source_target_pairs={{0,8},{1,9},{2,10},{3,11},{4,12},{5,13},{6,14},{7,15},{8,0},{9,1},... | collective-permute-start | bytes 393224 | tf_op jit(solution)/shard_map/ppermute | solution.py:395
  43.8 8.0 %collective-permute-start.16 = (bf16[4,128,128]{2,1,0:T(8,128)(2,1)S(1)}, bf16[4,128,128]{2,1,0:T(8,128)(2,1)S(1)}, u32[]{:S(2)}, u32[]{:S(2)}) collective-permute-start(bf16[4,128,128]{2,1,0:T(8,128)(2,1)S(1)} %get-tuple-element.67), channel_id=1, source_target_pairs={{0,8},{1,9},{2,10},{3,11},{4,12},{5,13},{6,14},{7,15},{8,0},{9,1},... | collective-permute-start | bytes 393224 | tf_op jit(solution)/shard_map/ppermute | solution.py:395
  45.3 6.5 %collective-permute-start.17 = (bf16[4,128,128]{2,1,0:T(8,128)(2,1)S(1)}, bf16[4,128,128]{2,1,0:T(8,128)(2,1)S(1)}, u32[]{:S(2)}, u32[]{:S(2)}) collective-permute-start(bf16[4,128,128]{2,1,0:T(8,128)(2,1)S(1)} %get-tuple-element.68), channel_id=1, source_target_pairs={{0,8},{1,9},{2,10},{3,11},{4,12},{5,13},{6,14},{7,15},{8,0},{9,1},... | collective-permute-start | bytes 393224 | tf_op jit(solution)/shard_map/ppermute | solution.py:395

commit v9 on v8

--- a/solution.py
+++ b/solution.py
@@ -87,7 +87,7 @@
         acc[column] += scale[k, level, q] * dot(inverse, lower[k])
 
 
-def first_kernel(meta, depend, scale, lower_hbm, inverse_hbm, right_hbm, solved, even_a, odd_a, even_b, odd_b, inverse, right, lower, acc, edges, sems):
+def first_kernel(meta, depend_hbm, scale_hbm, lower_hbm, inverse_hbm, right_hbm, solved, even_a, odd_a, even_b, odd_b, inverse, right, lower, depend, scale, acc, edges, sems):
     count = inverse.shape[0]
     block = inverse.shape[1]
     parts = right.shape[2] // block
@@ -108,14 +108,19 @@
         rows = pl.ds(ends[side], REACH)
         return pltpu.make_async_copy(lower_hbm.at[0, rows], lower.at[side], sems.at[2, side])
 
+    tables = [
+        pltpu.make_async_copy(source, target, sems.at[2, 2 + i])
+        for i, (source, target) in enumerate(((depend_hbm, depend), (scale_hbm, scale)))
+    ]
+
     for pair in loads:
         for load in pair:
             load.start()
 
     @pl.when(meta[0] > 1)
     def _():
-        for side in range(2):
-            edge_load(side).start()
+        for load in (edge_load(0), edge_load(1), *tables):
+            load.start()
 
     for step in range(steps):
         for load in loads[step]:
@@ -135,6 +140,8 @@
 
     @pl.when(meta[0] > 1)
     def _():
+        for table in tables:
+            table.wait()
         for side in range(2):
             edge_load(side).wait()
             for i in range(REACH):
@@ -154,55 +161,46 @@
         by_parity(meta[1], lambda: edges[0, soon:], lambda: edges[1, soon:], even_b, odd_b)
 
 
-def prepare_kernel(meta, depend, scale, lower_hbm, inverse_hbm, right_hbm, wide_b, wide_a, base, lower, inverse, right, acc, sems):
-    pairs = wide_a.shape[0]
+def prepare_kernel(turn, meta, depend_hbm, scale_hbm, lower_hbm, inverse_hbm, right_hbm, wide, base, lower, inverse, right, depend, scale, acc, sems):
+    pairs = wide.shape[0]
     block = lower.shape[-1]
-
-    def loads(level, p):
+    level = jnp.where(meta[0] == 0, 1, turn)
+
+    def loads(p):
         rows = pl.ds(2 * p, 2)
-        copies = [
-            pltpu.make_async_copy(lower_hbm.at[level, rows], lower.at[level, rows], sems.at[level, 0, p]),
-            pltpu.make_async_copy(inverse_hbm.at[level, rows], inverse.at[level, rows], sems.at[level, 1, p]),
+        return [
+            pltpu.make_async_copy(source.at[level, rows], target.at[rows], sems.at[i, p])
+            for i, (source, target) in enumerate(((lower_hbm, lower), (inverse_hbm, inverse), (right_hbm, right)))
         ]
-        if level:
-            copies.append(pltpu.make_async_copy(right_hbm.at[1, rows], right.at[rows], sems.at[level, 2, p]))
-        return copies
-
-    def start(level):
+
+    @pl.when((meta[0] > 0) | (turn == 0))
+    def _():
+        tables = [
+            pltpu.make_async_copy(source, target, sems.at[3, i])
+            for i, (source, target) in enumerate(((depend_hbm, depend), (scale_hbm, scale)))
+        ]
+        for table in tables:
+            table.start()
         for p in range(pairs):
-            for copy in loads(level, p):
-                copy.start()
-
-    def pair(level, p, wide):
-        for copy in loads(level, p):
-            copy.wait()
-        for half in range(2):
-            q = 2 * p + half
-            blocks = [lower[level, q, k] for k in range(lower.shape[2])]
-            premultiplied(meta, depend, scale, blocks, inverse[level, q], acc.at[half], level, q)
-            at = slice(half * block, (half + 1) * block)
-            for d in range(SPAN):
-                wide[p, at, (d + half) * block : (d + half + 1) * block] = (-acc[half, d]).astype(wide.dtype)
-            other = 0 if half else SPAN
-            wide[p, at, other * block : (other + 1) * block] = jnp.zeros((block, block), wide.dtype)
-
-    start(1)
-
-    @pl.when(meta[0] > 0)
-    def _():
-        start(0)
-
-    @pl.loop(0, pairs)
-    def _(p):
-        pair(1, p, wide_b)
-        for half in range(2):
-            base[2 * p + half] = dot(inverse[1, 2 * p + half], right[2 * p + half])
-
-    @pl.when(meta[0] > 0)
-    def _():
+            for load in loads(p):
+                load.start()
+        for table in tables:
+            table.wait()
+
         @pl.loop(0, pairs)
         def _(p):
-            pair(0, p, wide_a)
+            for load in loads(p):
+                load.wait()
+            for half in range(2):
+                q = 2 * p + half
+                blocks = [lower[q, k] for k in range(lower.shape[1])]
+                premultiplied(meta, depend, scale, blocks, inverse[q], acc.at[half], level, q)
+                at = slice(half * block, (half + 1) * block)
+                for d in range(SPAN):
+                    wide[p, at, (d + half) * block : (d + half + 1) * block] = (-acc[half, d]).astype(wide.dtype)
+                other = 0 if half else SPAN
+                wide[p, at, other * block : (other + 1) * block] = jnp.zeros((block, block), wide.dtype)
+                base[q] = dot(inverse[q], right[q])
 
 
 def order_kernel(meta, even_a, odd_a, even_b, odd_b, edges):
@@ -302,7 +300,7 @@
 def later_step(group, chunk, final, meta, centre, even_in, odd_in, edges, first, wide_a, wide_b, base_b, old_a, old_b, *rest):
     stages = final and chunk == CHUNKS - 1
     if stages:
-        made_a, made_b, _, out, solved, solved_a, window, level_a, stage, sems = rest
+        made_a, made_b, _, out, window, level_a, solved, stage, sems = rest
     else:
         _, out, solved, solved_a, *sends, window, level_a, sems = rest
     cases = solved.shape[-1]
@@ -379,8 +377,9 @@
     halo = 2 * REACH
     row = lax.axis_index("rows")
     meta = jnp.stack([lax.axis_index("chain"), row % 2, row * count]).astype(jnp.int32)
-    depend = depend_rows.transpose(2, 0, 1)
-    scale = block_scale.transpose(2, 0, 1)
+    depend = in_hbm(depend_rows.transpose(2, 0, 1))
+    scale = in_hbm(block_scale.transpose(2, 0, 1))
+    tables = [pltpu.SMEM(depend.shape, jnp.int32), pltpu.SMEM(scale.shape, jnp.float32)]
     right_side, lower_blocks, diag_inverse = in_hbm(right_side), in_hbm(lower_blocks), in_hbm(diag_inverse)
     mates = (even_mate, odd_mate)
 
@@ -415,12 +414,13 @@
     first, *edge_w = call(
         first_kernel,
         "first_level",
-        [SMEM, SMEM, SMEM, HBM, HBM, HBM],
+        [SMEM] + [HBM] * 5,
         [whole, *(shape for shape in edge_shapes for _ in range(2))],
         scratch_shapes=[
             pltpu.VMEM((count, block, block), jnp.bfloat16),
             pltpu.VMEM(whole.shape, jnp.bfloat16),
             pltpu.VMEM((2, REACH, terms, block, block), jnp.bfloat16),
+            *tables,
             pltpu.VMEM((REACH, SPAN, block, block), jnp.float32),
             pltpu.VMEM((2, total, block, block), jnp.bfloat16),
             pltpu.SemaphoreType.DMA((3, 4)),
@@ -430,19 +430,24 @@
 
     pairs = count // 2
     wide_shape = shaped((pairs, 2 * block, width + block))
-    wide_b, wide_a, base_b = call(
-        prepare_kernel,
-        "prepare",
-        [SMEM, SMEM, SMEM, HBM, HBM, HBM],
-        [wide_shape, wide_shape, shaped(whole.shape, jnp.float32)],
-        scratch_shapes=[
-            pltpu.VMEM(lower_blocks.shape, jnp.bfloat16),
-            pltpu.VMEM(diag_inverse.shape, jnp.bfloat16),
-            pltpu.VMEM(whole.shape, jnp.bfloat16),
-            pltpu.VMEM((2, SPAN, block, block), jnp.float32),
-            pltpu.SemaphoreType.DMA((2, 3, pairs)),
-        ],
-    )(meta, depend, scale, lower_blocks, diag_inverse, right_side)
+
+    def prepare(turn, meta):
+        return call(
+            functools.partial(prepare_kernel, turn),
+            f"prepare_{turn}",
+            [SMEM] + [HBM] * 5,
+            [wide_shape, shaped(whole.shape, jnp.float32)],
+            scratch_shapes=[
+                pltpu.VMEM(lower_blocks.shape[1:], jnp.bfloat16),
+                pltpu.VMEM(diag_inverse.shape[1:], jnp.bfloat16),
+                pltpu.VMEM(whole.shape, jnp.bfloat16),
+                *tables,
+                pltpu.VMEM((2, SPAN, block, block), jnp.float32),
+                pltpu.SemaphoreType.DMA((4, pairs)),
+            ],
+        )(meta, depend, scale, lower_blocks, diag_inverse, right_side)
+
+    wide_a, base_0 = prepare(0, meta)
 
     padded = pltpu.VMEM((count + halo, block, cases), jnp.bfloat16)
     padded_half = pltpu.VMEM((count + halo, block, part), jnp.bfloat16)
@@ -452,7 +457,8 @@
         [SMEM] + [VMEM] * 5,
         [whole, whole_edge, whole_edge],
         scratch_shapes=[padded],
-    )(meta, first, *sides, wide_b, base_b)
+    )(meta, first, *sides, wide_a, base_0)
+    wide_b, base_b = prepare(1, after(meta, solved))
     arrived = travel(0, solved, sends)
 
     later_w = exchange(range(2, chain), after(edge_w[2:], sides))
@@ -487,11 +493,11 @@
         arrived = [travel(group - 1, solved, sends) for solved, *sends in sent]
         made = []
         for chunk in range(CHUNKS):
-            outs = [half, half] + ([] if final else [half_edge] * 2)
             stages = final and chunk == CHUNKS - 1
+            outs = [] if stages else [half, half] + ([] if final else [half_edge] * 2)
             extra = [made[0][1], made[0][0][0]] if stages else []
             sems = (2, pairs) if stages else (2,)
-            out, solved, level, *sends = call(
+            out, *now = call(
                 functools.partial(later_step, group, chunk, final),
                 f"step_{group}_{chunk}",
                 [SMEM] + [VMEM] * (10 + len(extra)) + [ANY],
@@ -500,7 +506,7 @@
                 scratch_shapes=[
                     pltpu.VMEM((count + 2 * halo, block, part), jnp.bfloat16),
                     padded_half,
-                    *([pltpu.VMEM((2, count, block, cases), jnp.bfloat16)] if stages else []),
+                    *([pltpu.VMEM(shape, jnp.bfloat16) for shape in (half.shape, (2, *whole.shape))] if stages else []),
                     pltpu.SemaphoreType.DMA(sems),
                 ],
                 input_output_aliases={11 + len(extra): 0},
@@ -517,7 +523,9 @@
                 *extra,
                 out,
             )
-            made.append(((solved, *sends), level))
+            if now:
+                solved, level, *sends = now
+                made.append(((solved, *sends), level))
         sent, made_a = [values[0] for values in made], [values[1] for values in made]
     return out
 

time: 55.8 us -> 53.4 us (0.957)
  starting transfers between devices: 26.7 us -> 24.7 us
  local copies, waits for them, and re-layouts: 1.38 us -> 0 us
  waiting for transfers between devices: 9.54 us -> 10.2 us
    ppermute x5, starting transfers between devices: 15.2 us -> 13.5 us  [travel(): lax.ppermute(centre, AXES, hop_pairs(group, same_row, chain, rows))]
    unnamed x4 -> x0, local copies, waits for them, and re-layouts: 1.38 us -> none
    pallas_call x2 -> x3, Pallas kernels: 8.03 us -> 9.37 us  [the longest x2 6.33 us: prepare(): call(functools.partial(prepare_kernel, turn), f'prepare_{turn}', [SMEM] +...]
    pallas_call x4, Pallas kernels: 6.64 us -> 5.83 us  [per_device(): call(functools.partial(later_step, group, chunk, final), f'step_{group}_{...]
  transfers between devices with their start and end apart: 21 -> 21, of which waited for: 9 -> 8; matrix products, arithmetic and copies ran while one was open for 0% -> 0% of each run, Pallas kernels for 18% -> 22%
where the time goes in v9:
time: 53.4 us; the launch traced here: 53.2 us
  starting transfers between devices  24.7 us (46%)
  Pallas kernels  18 us (34%)
  waiting for transfers between devices  10.2 us (19%)
    ppermute x5, starting transfers between devices, travel(): lax.ppermute(centre, AXES, hop_pairs(group, same_row, chain, rows))  13.5 us
    ppermute x10, waiting for transfers between devices, travel(): lax.ppermute(value, AXES, hop_pairs(group, mate, chain, rows))  8.04 us
    ppermute x10, starting transfers between devices, travel(): lax.ppermute(value, AXES, hop_pairs(group, mate, chain, rows))  8.01 us
    pallas_call x2, Pallas kernels, prepare(): call(functools.partial(prepare_kernel, turn), f'prepare_{turn}', [SMEM] +...  6.33 us
    pallas_call x4, Pallas kernels, per_device(): call(functools.partial(later_step, group, chunk, final), f'step_{group}_{...  5.83 us
    ppermute x6, starting transfers between devices, exchange(): lax.ppermute(value, AXES, inner_pairs(groups, mate, chain, rows, idle))  3.2 us
    pallas_call x1, Pallas kernels, per_device(): call(first_kernel, 'first_level', [SMEM] + [HBM] * 5, [whole, *(shape for...  3.04 us
    ppermute x6, waiting for transfers between devices, exchange(): lax.ppermute(value, AXES, inner_pairs(groups, mate, chain, rows, idle))  2.13 us
  transfers between devices with their start and end apart: 21, of which 8 were waited for; matrix products, arithmetic and copies ran while one was open for 0% of the time, Pallas kernels for 22%

profile of v9, /device:TPU:11, one launch (start us, length us, event | category | flops | bytes accessed | tf_op | source)
XLA Modules:
  0.0 53.2 jit_solution(13964370353428499982)
XLA Ops:
  0.0 0.1 pad_add_fusion.meta
  0.1 3.0 %first_level.1 = (bf16[8,128,256]{2,1,0:T(8,128)(2,1)S(1)}, bf16[4,128,128]{2,1,0:T(8,128)(2,1)S(1)}, bf16[4,128,128]{2,1,0:T(8,128)(2,1)S(1)}, bf16[10,128,128]...) custom-call(s32[3]{0:T(128)S(1)} %pad_add_fusion.meta, s32[6,2,8]{2,1,0:T(2,128)} %bitcast.5, f32[6,2,8]{2,1,0:T(2,128)} %bitcast.8, ...), custom_call_target="tpu_custom_call" | custom-call | tf_op jit(solution)/shard_map/first_level/pallas_call | solution.py:414
  3.1 1.3 %collective-permute-start = (bf16[4,128,128]{2,1,0:T(8,128)(2,1)S(1)}, bf16[4,128,128]{2,1,0:T(8,128)(2,1)S(1)}, u32[]{:S(2)}, u32[]{:S(2)}) collective-permute-start(bf16[4,128,128]{2,1,0:T(8,128)(2,1)S(1)} %get-tuple-element.44), channel_id=1, source_target_pairs={{0,1},{16,17},{24,25},{8,10},{1,0},{17,16},{25,24},{9,11},{2,3},{1... | collective-permute-start | bytes 393224 | tf_op jit(solution)/shard_map/ppermute | solution.py:388
  4.4 0.1 collective-permute-start.1
  4.5 3.2 %prepare_0.1 = (bf16[4,256,768]{2,1,0:T(8,128)(2,1)S(1)}, f32[8,128,256]{2,1,0:T(8,128)S(1)}) custom-call(s32[3]{0:T(128)S(1)} %pad_add_fusion.meta, s32[6,2,8]{2,1,0:T(2,128)} %bitcast.6, f32[6,2,8]{2,1,0:T(2,128)} %bitcast.9, bf16[2,8,6,128,128]{4,3,2,1,0:T(8,128)(2,1)} %lower_hbm.5, bf16[2,8,128,128]{3,2,1,0:T(8,128)(2,1)} %inverse_hbm.5, ...), custom_call_target="tpu_custom_call" | custom-call | tf_op jit(solution)/shard_map/prepare_0/pallas_call | solution.py:435
  7.7 1.6 %collective-permute-done.even_in.even_a = bf16[4,128,128]{2,1,0:T(8,128)(2,1)S(1)} collective-permute-done((bf16[4,128,128]{2,1,0:T(8,128)(2,1)S(1)}, bf16[4,128,128]{2,1,0:T(8,128)(2,1)S(1)}, u32[]{:S(2)}, u32[]{:S(2)}) %collective-permute-start) | collective-permute-done | bytes 131104 | tf_op jit(solution)/shard_map/ppermute | solution.py:388
  9.2 0.0 collective-permute-done.1.odd_in.odd_a
  9.2 0.5 %step_0.1 = (bf16[8,128,256]{2,1,0:T(8,128)(2,1)S(1)}, bf16[2,128,256]{2,1,0:T(8,128)(2,1)S(1)}, bf16[2,128,256]{2,1,0:T(8,128)(2,1)S(1)}) custom-call(s32[3]{0:T(128)S(1)} %pad_add_fusion.meta, bf16[8,128,256]{2,1,0:T(8,128)(2,1)S(1)} %get-tuple-element.43.own.first, bf16[4,128,128]{2,1,0:T(8,128)(2,1)S(1)} %collective-permute-done.even_in.even_a, ...), custom_call_target="tpu_custom_call" | custom-call | tf_op jit(solution)/shard_map/step_0/pallas_call | solution.py:454
  9.8 2.7 %collective-permute-start.2 = (bf16[8,128,256]{2,1,0:T(8,128)(2,1)S(1)}, bf16[8,128,256]{2,1,0:T(8,128)(2,1)S(1)}, u32[]{:S(2)}, u32[]{:S(2)}) collective-permute-start(bf16[8,128,256]{2,1,0:T(8,128)(2,1)S(1)} %get-tuple-element.48.old_b), channel_id=1, source_target_pairs={{0,8},{1,9},{2,10},{3,11},{4,12},{5,13},{6,14},{7,15},{8,0},{9,1},... | collective-permute-start | bytes 1572872 | tf_op jit(solution)/shard_map/ppermute | solution.py:393
  12.5 0.1 collective-permute-start.3
  12.6 0.4 collective-permute-start.4
  13.0 1.2 %collective-permute-start.10 = (bf16[10,128,128]{2,1,0:T(8,128)(2,1)S(1)}, bf16[10,128,128]{2,1,0:T(8,128)(2,1)S(1)}, u32[]{:S(2)}, u32[]{:S(2)}) collective-permute-start(bf16[10,128,128]{2,1,0:T(8,128)(2,1)S(1)} %get-tuple-element.62), channel_id=1, source_target_pairs={{16,17},{24,25},{0,8},{8,0},{17,16},{25,24},{1,9},{9,1},{18,19},{2... | collective-permute-start | bytes 983048 | tf_op jit(solution)/shard_map/ppermute | solution.py:388
  14.3 0.0 collective-permute-start.11
  14.3 0.0 collective-permute-done.3.even_in
  14.3 0.2 collective-permute-done.4.odd_in
  14.4 0.0 collective-permute-done.2.centre
  14.4 0.6 %step_1.1 = (bf16[2,8,128,256]{3,2,1,0:T(8,128)(2,1)}, bf16[8,128,256]{2,1,0:T(8,128)(2,1)S(1)}, bf16[2,128,256]{2,1,0:T(8,128)(2,1)S(1)}, bf16[2,128,256]{2,1,0:T(8,128)(2,1)S(1)}) custom-call(s32[3]{0:T(128)S(1)} %pad_add_fusion.meta, bf16[8,128,256]{2,1,0:T(8,128)(2,1)S(1)} %collective-permute-done.2.centre, ...), custom_call_target="tpu_custom_call" | custom-call | tf_op jit(solution)/shard_map/step_1/pallas_call | solution.py:469
  15.0 0.4 collective-permute-start.5
  15.4 0.1 collective-permute-start.6
  15.6 3.2 %prepare_1.1 = (bf16[4,256,768]{2,1,0:T(8,128)(2,1)S(1)}, f32[8,128,256]{2,1,0:T(8,128)S(1)}) custom-call(s32[3]{0:T(128)S(1)} %pad_add_fusion.meta, s32[6,2,8]{2,1,0:T(2,128)} %bitcast.7, f32[6,2,8]{2,1,0:T(2,128)} %bitcast.10, bf16[2,8,6,128,128]{4,3,2,1,0:T(8,128)(2,1)} %lower_hbm.5, bf16[2,8,128,128]{3,2,1,0:T(8,128)(2,1)} %inverse_hbm.5, ...), custom_call_target="tpu_custom_call" | custom-call | tf_op jit(solution)/shard_map/prepare_1/pallas_call | solution.py:435
  18.8 0.0 collective-permute-done.6.odd_in
  18.8 0.6 %step_1_0.1 = (bf16[8,128,128]{2,1,0:T(8,128)(2,1)S(1)}, bf16[4,128,128]{2,1,0:T(8,128)(2,1)S(1)}, bf16[4,128,128]{2,1,0:T(8,128)(2,1)S(1)}) custom-call(s32[3]{0:T(128)S(1)} %pad_add_fusion.meta, bf16[8,128,256]{2,1,0:T(8,128)(2,1)S(1)} %get-tuple-element.51.own.old_a, bf16[2,128,256]{2,1,0:T(8,128)(2,1)S(1)} %collective-permute-done.5.even_in, ...), custom_call_target="tpu_custom_call" | custom-call | tf_op jit(solution)/shard_map/step_1_0/pallas_call | solution.py:482
  19.3 8.0 %collective-permute-start.12 = (bf16[8,128,128]{2,1,0:T(8,128)(2,1)S(1)}, bf16[8,128,128]{2,1,0:T(8,128)(2,1)S(1)}, u32[]{:S(2)}, u32[]{:S(2)}) collective-permute-start(bf16[8,128,128]{2,1,0:T(8,128)(2,1)S(1)} %get-tuple-element.64.old_b), channel_id=1, source_target_pairs={{8,16},{9,17},{10,18},{11,19},{12,20},{13,21},{14,22},{15,23},{0,8... | collective-permute-start | bytes 786440 | tf_op jit(solution)/shard_map/ppermute | solution.py:393
  27.3 0.8 %collective-permute-start.13 = (bf16[4,128,128]{2,1,0:T(8,128)(2,1)S(1)}, bf16[4,128,128]{2,1,0:T(8,128)(2,1)S(1)}, u32[]{:S(2)}, u32[]{:S(2)}) collective-permute-start(bf16[4,128,128]{2,1,0:T(8,128)(2,1)S(1)} %get-tuple-element.65), channel_id=1, source_target_pairs={{8,17},{9,16},{10,19},{11,18},{12,21},{13,20},{14,23},{15,22},{0,8... | collective-permute-start | bytes 393224 | tf_op jit(solution)/shard_map/ppermute | solution.py:394
  28.1 0.5 %step_1_1.1 = (bf16[8,128,128]{2,1,0:T(8,128)(2,1)S(1)}, bf16[4,128,128]{2,1,0:T(8,128)(2,1)S(1)}, bf16[4,128,128]{2,1,0:T(8,128)(2,1)S(1)}) custom-call(s32[3]{0:T(128)S(1)} %pad_add_fusion.meta, bf16[8,128,256]{2,1,0:T(8,128)(2,1)S(1)} %get-tuple-element.51.own.old_a, bf16[2,128,256]{2,1,0:T(8,128)(2,1)S(1)} %collective-permute-done.5.even_in, ...), custom_call_target="tpu_custom_call" | custom-call | tf_op jit(solution)/shard_map/step_1_1/pallas_call | solution.py:482
  28.6 0.1 collective-permute-start.7
  28.8 0.6 %collective-permute-done.10.even_b = bf16[10,128,128]{2,1,0:T(8,128)(2,1)S(1)} collective-permute-done((bf16[10,128,128]{2,1,0:T(8,128)(2,1)S(1)}, bf16[10,128,128]{2,1,0:T(8,128)(2,1)S(1)}, u32[]{:S(2)}, u32[]{:S(2)}) %collective-permute-start.10) | collective-permute-done | bytes 327712 | tf_op jit(solution)/shard_map/ppermute | solution.py:388
  29.3 0.1 collective-permute-start.14
  29.4 0.0 collective-permute-done.11.odd_b
  29.4 0.8 %collective-permute-start.8 = (bf16[4,128,128]{2,1,0:T(8,128)(2,1)S(1)}, bf16[4,128,128]{2,1,0:T(8,128)(2,1)S(1)}, u32[]{:S(2)}, u32[]{:S(2)}) collective-permute-start(bf16[4,128,128]{2,1,0:T(8,128)(2,1)S(1)} %get-tuple-element.58), channel_id=1, source_target_pairs={{8,17},{9,16},{10,19},{11,18},{12,21},{13,20},{14,23},{15,22},{0,8... | collective-permute-start | bytes 393224 | tf_op jit(solution)/shard_map/ppermute | solution.py:394
  30.2 1.8 %collective-permute-done.13.even_in = bf16[4,128,128]{2,1,0:T(8,128)(2,1)S(1)} collective-permute-done((bf16[4,128,128]{2,1,0:T(8,128)(2,1)S(1)}, bf16[4,128,128]{2,1,0:T(8,128)(2,1)S(1)}, u32[]{:S(2)}, u32[]{:S(2)}) %collective-permute-start.13) | collective-permute-done | bytes 131104 | tf_op jit(solution)/shard_map/ppermute | solution.py:394
  32.0 2.5 %collective-permute-start.9 = (bf16[4,128,128]{2,1,0:T(8,128)(2,1)S(1)}, bf16[4,128,128]{2,1,0:T(8,128)(2,1)S(1)}, u32[]{:S(2)}, u32[]{:S(2)}) collective-permute-start(bf16[4,128,128]{2,1,0:T(8,128)(2,1)S(1)} %get-tuple-element.59), channel_id=1, source_target_pairs={{8,16},{9,18},{10,17},{11,20},{12,19},{13,22},{14,21},{15,23},{0,8... | collective-permute-start | bytes 393224 | tf_op jit(solution)/shard_map/ppermute | solution.py:394
  34.5 0.6 %order.1.edges = bf16[2,14,128,128]{3,2,1,0:T(8,128)(2,1)S(1)} custom-call(s32[3]{0:T(128)S(1)} %pad_add_fusion.meta, bf16[4,128,128]{2,1,0:T(8,128)(2,1)S(1)} %collective-permute-done.even_in.even_a, bf16[4,128,128]{2,1,0:T(8,128)(2,1)S(1)} %collective-permute-done.1.odd_in.odd_a, bf16[10,128,128]{2,1,0:T(8,128)(2,1)S(1)} %collective-permute-done.10.even_b, ...), custom_call_target="tpu_custom_call" | custom-call | tf_op jit(solution)/shard_map/order/pallas_call | solution.py:465
  35.1 1.1 %collective-permute-done.14.odd_in = bf16[4,128,128]{2,1,0:T(8,128)(2,1)S(1)} collective-permute-done((bf16[4,128,128]{2,1,0:T(8,128)(2,1)S(1)}, bf16[4,128,128]{2,1,0:T(8,128)(2,1)S(1)}, u32[]{:S(2)}, u32[]{:S(2)}) %collective-permute-start.14) | collective-permute-done | bytes 131104 | tf_op jit(solution)/shard_map/ppermute | solution.py:394
  36.2 0.0 collective-permute-done.12.centre
  36.2 0.6 %step_2_0.1 = (bf16[2,8,128,256]{3,2,1,0:T(8,128)(2,1)}, bf16[8,128,128]{2,1,0:T(8,128)(2,1)S(1)}, bf16[8,128,128]{2,1,0:T(8,128)(2,1)S(1)}, bf16[4,128,128]{2,1,0:T(8,128)(2,1)S(1)}, bf16[4,128,128]{2,1,0:T(8,128)(2,1)S(1)}) custom-call(s32[3]{0:T(128)S(1)} %pad_add_fusion.meta, ...), custom_call_target="tpu_custom_call", output_to_operand_aliasing={{0}: (11, {})} | custom-call | tf_op jit(solution)/shard_map/step_2_0/pallas_call | solution.py:500
  36.8 1.5 %collective-permute-start.19 = (bf16[4,128,128]{2,1,0:T(8,128)(2,1)S(1)}, bf16[4,128,128]{2,1,0:T(8,128)(2,1)S(1)}, u32[]{:S(2)}, u32[]{:S(2)}) collective-permute-start(bf16[4,128,128]{2,1,0:T(8,128)(2,1)S(1)} %get-tuple-element.74), channel_id=1, source_target_pairs={{0,8},{1,9},{2,10},{3,11},{4,12},{5,13},{6,14},{7,15},{8,0},{9,1},... | collective-permute-start | bytes 393224 | tf_op jit(solution)/shard_map/ppermute | solution.py:394
  38.4 0.1 collective-permute-start.18
  38.5 0.6 %collective-permute-done.9.odd_in = bf16[4,128,128]{2,1,0:T(8,128)(2,1)S(1)} collective-permute-done((bf16[4,128,128]{2,1,0:T(8,128)(2,1)S(1)}, bf16[4,128,128]{2,1,0:T(8,128)(2,1)S(1)}, u32[]{:S(2)}, u32[]{:S(2)}) %collective-permute-start.9) | collective-permute-done | bytes 131104 | tf_op jit(solution)/shard_map/ppermute | solution.py:394
  39.1 0.6 %step_2_1.1 = (bf16[2,8,128,256]{3,2,1,0:T(8,128)(2,1)}, bf16[8,128,128]{2,1,0:T(8,128)(2,1)S(1)}, bf16[8,128,128]{2,1,0:T(8,128)(2,1)S(1)}, bf16[4,128,128]{2,1,0:T(8,128)(2,1)S(1)}, bf16[4,128,128]{2,1,0:T(8,128)(2,1)S(1)}) custom-call(s32[3]{0:T(128)S(1)} %pad_add_fusion.meta, ...), custom_call_target="tpu_custom_call", output_to_operand_aliasing={{0}: (11, {})} | custom-call | tf_op jit(solution)/shard_map/step_2_1/pallas_call | solution.py:500
  39.6 2.7 %collective-permute-start.15 = (bf16[8,128,128]{2,1,0:T(8,128)(2,1)S(1)}, bf16[8,128,128]{2,1,0:T(8,128)(2,1)S(1)}, u32[]{:S(2)}, u32[]{:S(2)}) collective-permute-start(bf16[8,128,128]{2,1,0:T(8,128)(2,1)S(1)} %get-tuple-element.69.old_b), channel_id=1, source_target_pairs={{0,8},{1,9},{2,10},{3,11},{4,12},{5,13},{6,14},{7,15},{8,0},{9,1},... | collective-permute-start | bytes 786440 | tf_op jit(solution)/shard_map/ppermute | solution.py:393
  42.3 0.1 collective-permute-start.20
  42.4 1.4 %collective-permute-start.16 = (bf16[4,128,128]{2,1,0:T(8,128)(2,1)S(1)}, bf16[4,128,128]{2,1,0:T(8,128)(2,1)S(1)}, u32[]{:S(2)}, u32[]{:S(2)}) collective-permute-start(bf16[4,128,128]{2,1,0:T(8,128)(2,1)S(1)} %get-tuple-element.70), channel_id=1, source_target_pairs={{0,8},{1,9},{2,10},{3,11},{4,12},{5,13},{6,14},{7,15},{8,0},{9,1},... | collective-permute-start | bytes 393224 | tf_op jit(solution)/shard_map/ppermute | solution.py:394
  43.8 0.4 collective-permute-start.17
  44.1 3.5 %collective-permute-done.20.odd_in = bf16[4,128,128]{2,1,0:T(8,128)(2,1)S(1)} collective-permute-done((bf16[4,128,128]{2,1,0:T(8,128)(2,1)S(1)}, bf16[4,128,128]{2,1,0:T(8,128)(2,1)S(1)}, u32[]{:S(2)}, u32[]{:S(2)}) %collective-permute-start.20) | collective-permute-done | bytes 131104 | tf_op jit(solution)/shard_map/ppermute | solution.py:394
  47.7 1.9 %step_3_0.1 = (bf16[2,8,128,256]{3,2,1,0:T(8,128)(2,1)}, bf16[8,128,128]{2,1,0:T(8,128)(2,1)S(1)}, bf16[8,128,128]{2,1,0:T(8,128)(2,1)S(1)}) custom-call(s32[3]{0:T(128)S(1)} %pad_add_fusion.meta, bf16[8,128,128]{2,1,0:T(8,128)(2,1)S(1)} %collective-permute-done.18.centre, ...), custom_call_target="tpu_custom_call", output_to_operand_aliasing={{0}: (11, {})} | custom-call | tf_op jit(solution)/shard_map/step_3_0/pallas_call | solution.py:500
  49.6 0.8 %collective-permute-done.16.even_in = bf16[4,128,128]{2,1,0:T(8,128)(2,1)S(1)} collective-permute-done((bf16[4,128,128]{2,1,0:T(8,128)(2,1)S(1)}, bf16[4,128,128]{2,1,0:T(8,128)(2,1)S(1)}, u32[]{:S(2)}, u32[]{:S(2)}) %collective-permute-start.16) | collective-permute-done | bytes 131104 | tf_op jit(solution)/shard_map/ppermute | solution.py:394
  50.4 2.8 %step_3_1.1 = bf16[2,8,128,256]{3,2,1,0:T(8,128)(2,1)} custom-call(s32[3]{0:T(128)S(1)} %pad_add_fusion.meta, bf16[8,128,128]{2,1,0:T(8,128)(2,1)S(1)} %collective-permute-done.15.centre, bf16[4,128,128]{2,1,0:T(8,128)(2,1)S(1)} %collective-permute-done.16.even_in, ...), custom_call_target="tpu_custom_call", output_to_operand_aliasing={{}: (13, {})} | custom-call | tf_op jit(solution)/shard_map/step_3_1/pallas_call | solution.py:500
  (7 shorter events, 0.0 us)
Async XLA Ops:
  3.1 6.1 %collective-permute-start = (bf16[4,128,128]{2,1,0:T(8,128)(2,1)S(1)}, bf16[4,128,128]{2,1,0:T(8,128)(2,1)S(1)}, u32[]{:S(2)}, u32[]{:S(2)}) collective-permute-start(bf16[4,128,128]{2,1,0:T(8,128)(2,1)S(1)} %get-tuple-element.44), channel_id=1, source_target_pairs={{0,1},{16,17},{24,25},{8,10},{1,0},{17,16},{25,24},{9,11},{2,3},{1... | collective-permute-start | bytes 393224 | tf_op jit(solution)/shard_map/ppermute | solution.py:388
  4.4 4.8 %collective-permute-start.1 = (bf16[4,128,128]{2,1,0:T(8,128)(2,1)S(1)}, bf16[4,128,128]{2,1,0:T(8,128)(2,1)S(1)}, u32[]{:S(2)}, u32[]{:S(2)}) collective-permute-start(bf16[4,128,128]{2,1,0:T(8,128)(2,1)S(1)} %get-tuple-element.45), channel_id=1, source_target_pairs={{0,8},{8,0},{16,24},{24,16},{1,2},{17,18},{25,26},{9,11},{2,1},{18... | collective-permute-start | bytes 393224 | tf_op jit(solution)/shard_map/ppermute | solution.py:388
  9.8 4.6 %collective-permute-start.2 = (bf16[8,128,256]{2,1,0:T(8,128)(2,1)S(1)}, bf16[8,128,256]{2,1,0:T(8,128)(2,1)S(1)}, u32[]{:S(2)}, u32[]{:S(2)}) collective-permute-start(bf16[8,128,256]{2,1,0:T(8,128)(2,1)S(1)} %get-tuple-element.48.old_b), channel_id=1, source_target_pairs={{0,8},{1,9},{2,10},{3,11},{4,12},{5,13},{6,14},{7,15},{8,0},{9,1},... | collective-permute-start | bytes 1572872 | tf_op jit(solution)/shard_map/ppermute | solution.py:393
  12.5 1.8 %collective-permute-start.3 = (bf16[2,128,256]{2,1,0:T(8,128)(2,1)S(1)}, bf16[2,128,256]{2,1,0:T(8,128)(2,1)S(1)}, u32[]{:S(2)}, u32[]{:S(2)}) collective-permute-start(bf16[2,128,256]{2,1,0:T(8,128)(2,1)S(1)} %get-tuple-element.49), channel_id=1, source_target_pairs={{0,9},{1,8},{2,11},{3,10},{4,13},{5,12},{6,15},{7,14},{8,0},{9,1},... | collective-permute-start | bytes 393224 | tf_op jit(solution)/shard_map/ppermute | solution.py:394
  12.6 1.8 %collective-permute-start.4 = (bf16[2,128,256]{2,1,0:T(8,128)(2,1)S(1)}, bf16[2,128,256]{2,1,0:T(8,128)(2,1)S(1)}, u32[]{:S(2)}, u32[]{:S(2)}) collective-permute-start(bf16[2,128,256]{2,1,0:T(8,128)(2,1)S(1)} %get-tuple-element.50), channel_id=1, source_target_pairs={{0,8},{1,10},{2,9},{3,12},{4,11},{5,14},{6,13},{7,15},{8,0},{9,1},... | collective-permute-start | bytes 393224 | tf_op jit(solution)/shard_map/ppermute | solution.py:394
  13.0 16.3 %collective-permute-start.10 = (bf16[10,128,128]{2,1,0:T(8,128)(2,1)S(1)}, bf16[10,128,128]{2,1,0:T(8,128)(2,1)S(1)}, u32[]{:S(2)}, u32[]{:S(2)}) collective-permute-start(bf16[10,128,128]{2,1,0:T(8,128)(2,1)S(1)} %get-tuple-element.62), channel_id=1, source_target_pairs={{16,17},{24,25},{0,8},{8,0},{17,16},{25,24},{1,9},{9,1},{18,19},{2... | collective-permute-start | bytes 983048 | tf_op jit(solution)/shard_map/ppermute | solution.py:388
  14.3 15.1 %collective-permute-start.11 = (bf16[10,128,128]{2,1,0:T(8,128)(2,1)S(1)}, bf16[10,128,128]{2,1,0:T(8,128)(2,1)S(1)}, u32[]{:S(2)}, u32[]{:S(2)}) collective-permute-start(bf16[10,128,128]{2,1,0:T(8,128)(2,1)S(1)} %get-tuple-element.63), channel_id=1, source_target_pairs={{0,8},{8,0},{16,24},{24,16},{17,18},{25,26},{1,9},{9,1},{18,17},{2... | collective-permute-start | bytes 983048 | tf_op jit(solution)/shard_map/ppermute | solution.py:388
  15.0 3.7 %collective-permute-start.5 = (bf16[2,128,256]{2,1,0:T(8,128)(2,1)S(1)}, bf16[2,128,256]{2,1,0:T(8,128)(2,1)S(1)}, u32[]{:S(2)}, u32[]{:S(2)}) collective-permute-start(bf16[2,128,256]{2,1,0:T(8,128)(2,1)S(1)} %get-tuple-element.52), channel_id=1, source_target_pairs={{8,9},{0,2},{16,24},{24,16},{9,8},{1,3},{17,25},{25,17},{10,11},{2... | collective-permute-start | bytes 393224 | tf_op jit(solution)/shard_map/ppermute | solution.py:388
  15.4 3.3 %collective-permute-start.6 = (bf16[2,128,256]{2,1,0:T(8,128)(2,1)S(1)}, bf16[2,128,256]{2,1,0:T(8,128)(2,1)S(1)}, u32[]{:S(2)}, u32[]{:S(2)}) collective-permute-start(bf16[2,128,256]{2,1,0:T(8,128)(2,1)S(1)} %get-tuple-element.53), channel_id=1, source_target_pairs={{0,8},{8,0},{16,24},{24,16},{9,10},{1,3},{17,25},{25,17},{10,9},{2... | collective-permute-start | bytes 393224 | tf_op jit(solution)/shard_map/ppermute | solution.py:388
  19.3 16.9 %collective-permute-start.12 = (bf16[8,128,128]{2,1,0:T(8,128)(2,1)S(1)}, bf16[8,128,128]{2,1,0:T(8,128)(2,1)S(1)}, u32[]{:S(2)}, u32[]{:S(2)}) collective-permute-start(bf16[8,128,128]{2,1,0:T(8,128)(2,1)S(1)} %get-tuple-element.64.old_b), channel_id=1, source_target_pairs={{8,16},{9,17},{10,18},{11,19},{12,20},{13,21},{14,22},{15,23},{0,8... | collective-permute-start | bytes 786440 | tf_op jit(solution)/shard_map/ppermute | solution.py:393
  27.3 4.7 %collective-permute-start.13 = (bf16[4,128,128]{2,1,0:T(8,128)(2,1)S(1)}, bf16[4,128,128]{2,1,0:T(8,128)(2,1)S(1)}, u32[]{:S(2)}, u32[]{:S(2)}) collective-permute-start(bf16[4,128,128]{2,1,0:T(8,128)(2,1)S(1)} %get-tuple-element.65), channel_id=1, source_target_pairs={{8,17},{9,16},{10,19},{11,18},{12,21},{13,20},{14,23},{15,22},{0,8... | collective-permute-start | bytes 393224 | tf_op jit(solution)/shard_map/ppermute | solution.py:394
  28.6 10.4 %collective-permute-start.7 = (bf16[8,128,128]{2,1,0:T(8,128)(2,1)S(1)}, bf16[8,128,128]{2,1,0:T(8,128)(2,1)S(1)}, u32[]{:S(2)}, u32[]{:S(2)}) collective-permute-start(bf16[8,128,128]{2,1,0:T(8,128)(2,1)S(1)} %get-tuple-element.57.old_b), channel_id=1, source_target_pairs={{8,16},{9,17},{10,18},{11,19},{12,20},{13,21},{14,22},{15,23},{0,8... | collective-permute-start | bytes 786440 | tf_op jit(solution)/shard_map/ppermute | solution.py:393
  29.3 6.9 %collective-permute-start.14 = (bf16[4,128,128]{2,1,0:T(8,128)(2,1)S(1)}, bf16[4,128,128]{2,1,0:T(8,128)(2,1)S(1)}, u32[]{:S(2)}, u32[]{:S(2)}) collective-permute-start(bf16[4,128,128]{2,1,0:T(8,128)(2,1)S(1)} %get-tuple-element.66), channel_id=1, source_target_pairs={{8,16},{9,18},{10,17},{11,20},{12,19},{13,22},{14,21},{15,23},{0,8... | collective-permute-start | bytes 393224 | tf_op jit(solution)/shard_map/ppermute | solution.py:394
  29.4 9.0 %collective-permute-start.8 = (bf16[4,128,128]{2,1,0:T(8,128)(2,1)S(1)}, bf16[4,128,128]{2,1,0:T(8,128)(2,1)S(1)}, u32[]{:S(2)}, u32[]{:S(2)}) collective-permute-start(bf16[4,128,128]{2,1,0:T(8,128)(2,1)S(1)} %get-tuple-element.58), channel_id=1, source_target_pairs={{8,17},{9,16},{10,19},{11,18},{12,21},{13,20},{14,23},{15,22},{0,8... | collective-permute-start | bytes 393224 | tf_op jit(solution)/shard_map/ppermute | solution.py:394
  32.0 7.0 %collective-permute-start.9 = (bf16[4,128,128]{2,1,0:T(8,128)(2,1)S(1)}, bf16[4,128,128]{2,1,0:T(8,128)(2,1)S(1)}, u32[]{:S(2)}, u32[]{:S(2)}) collective-permute-start(bf16[4,128,128]{2,1,0:T(8,128)(2,1)S(1)} %get-tuple-element.59), channel_id=1, source_target_pairs={{8,16},{9,18},{10,17},{11,20},{12,19},{13,22},{14,21},{15,23},{0,8... | collective-permute-start | bytes 393224 | tf_op jit(solution)/shard_map/ppermute | solution.py:394
  36.8 6.9 %collective-permute-start.19 = (bf16[4,128,128]{2,1,0:T(8,128)(2,1)S(1)}, bf16[4,128,128]{2,1,0:T(8,128)(2,1)S(1)}, u32[]{:S(2)}, u32[]{:S(2)}) collective-permute-start(bf16[4,128,128]{2,1,0:T(8,128)(2,1)S(1)} %get-tuple-element.74), channel_id=1, source_target_pairs={{0,8},{1,9},{2,10},{3,11},{4,12},{5,13},{6,14},{7,15},{8,0},{9,1},... | collective-permute-start | bytes 393224 | tf_op jit(solution)/shard_map/ppermute | solution.py:394
  38.4 9.3 %collective-permute-start.18 = (bf16[8,128,128]{2,1,0:T(8,128)(2,1)S(1)}, bf16[8,128,128]{2,1,0:T(8,128)(2,1)S(1)}, u32[]{:S(2)}, u32[]{:S(2)}) collective-permute-start(bf16[8,128,128]{2,1,0:T(8,128)(2,1)S(1)} %get-tuple-element.73.old_b), channel_id=1, source_target_pairs={{0,8},{1,9},{2,10},{3,11},{4,12},{5,13},{6,14},{7,15},{8,0},{9,1},... | collective-permute-start | bytes 786440 | tf_op jit(solution)/shard_map/ppermute | solution.py:393
  39.6 10.8 %collective-permute-start.15 = (bf16[8,128,128]{2,1,0:T(8,128)(2,1)S(1)}, bf16[8,128,128]{2,1,0:T(8,128)(2,1)S(1)}, u32[]{:S(2)}, u32[]{:S(2)}) collective-permute-start(bf16[8,128,128]{2,1,0:T(8,128)(2,1)S(1)} %get-tuple-element.69.old_b), channel_id=1, source_target_pairs={{0,8},{1,9},{2,10},{3,11},{4,12},{5,13},{6,14},{7,15},{8,0},{9,1},... | collective-permute-start | bytes 786440 | tf_op jit(solution)/shard_map/ppermute | solution.py:393
  42.3 5.4 %collective-permute-start.20 = (bf16[4,128,128]{2,1,0:T(8,128)(2,1)S(1)}, bf16[4,128,128]{2,1,0:T(8,128)(2,1)S(1)}, u32[]{:S(2)}, u32[]{:S(2)}) collective-permute-start(bf16[4,128,128]{2,1,0:T(8,128)(2,1)S(1)} %get-tuple-element.75), channel_id=1, source_target_pairs={{0,8},{1,9},{2,10},{3,11},{4,12},{5,13},{6,14},{7,15},{8,0},{9,1},... | collective-permute-start | bytes 393224 | tf_op jit(solution)/shard_map/ppermute | solution.py:394
  42.4 8.0 %collective-permute-start.16 = (bf16[4,128,128]{2,1,0:T(8,128)(2,1)S(1)}, bf16[4,128,128]{2,1,0:T(8,128)(2,1)S(1)}, u32[]{:S(2)}, u32[]{:S(2)}) collective-permute-start(bf16[4,128,128]{2,1,0:T(8,128)(2,1)S(1)} %get-tuple-element.70), channel_id=1, source_target_pairs={{0,8},{1,9},{2,10},{3,11},{4,12},{5,13},{6,14},{7,15},{8,0},{9,1},... | collective-permute-start | bytes 393224 | tf_op jit(solution)/shard_map/ppermute | solution.py:394
  43.8 6.6 %collective-permute-start.17 = (bf16[4,128,128]{2,1,0:T(8,128)(2,1)S(1)}, bf16[4,128,128]{2,1,0:T(8,128)(2,1)S(1)}, u32[]{:S(2)}, u32[]{:S(2)}) collective-permute-start(bf16[4,128,128]{2,1,0:T(8,128)(2,1)S(1)} %get-tuple-element.71), channel_id=1, source_target_pairs={{0,8},{1,9},{2,10},{3,11},{4,12},{5,13},{6,14},{7,15},{8,0},{9,1},... | collective-permute-start | bytes 393224 | tf_op jit(solution)/shard_map/ppermute | solution.py:394

commit v10 on v9

--- a/solution.py
+++ b/solution.py
@@ -262,14 +262,15 @@
         copy.wait()
 
 
-def exchanged_step(group, chunk, meta, own, even_in, odd_in, wide_b, base_b, solved, even_out, odd_out, level_a):
+def exchanged_step(group, meta, own, even_in, odd_in, wide_b, base_b, *rest):
+    *parts_out, even_out, odd_out, level_a, solved = rest
+
     @pl.when(meta[0] == group)
     def _():
-        at = columns(chunk, solved.shape[-1])
         count, block = own.shape[0], own.shape[1]
-        level_a[REACH : REACH + count] = own[:, :, at]
+        level_a[REACH : REACH + count] = own[...]
         if even_in.shape[0] == REACH:
-            place(level_a, meta[1], even_in, odd_in, at)
+            place(level_a, meta[1], even_in, odd_in)
         else:
             parts = even_in.shape[0] // REACH
             low, high = 0, count + REACH
@@ -278,8 +279,10 @@
                     cols = slice(part * block, (part + 1) * block)
                     level_a[i + jnp.where(meta[1] == 1, low, high), :, cols] = even_in[i * parts + part]
                     level_a[i + jnp.where(meta[1] == 1, high, low), :, cols] = odd_in[i * parts + part]
-        second_of_group(wide_b, base_b, level_a, solved, at)
+        second_of_group(wide_b, base_b, level_a, solved, slice(None))
         emit_sends(meta[1], solved, (even_out, odd_out))
+        for i, part in enumerate(parts_out):
+            part[...] = solved[:, :, columns(i, part.shape[-1])]
 
 
 def level_step(group, meta, centre, even_in, odd_in, first, wide_a, old_b, out, solved, even_out, odd_out, window, sems):
@@ -298,9 +301,12 @@
 
 
 def later_step(group, chunk, final, meta, centre, even_in, odd_in, edges, first, wide_a, wide_b, base_b, old_a, old_b, *rest):
-    stages = final and chunk == CHUNKS - 1
+    ends = chunk == CHUNKS - 1
+    stages = final and ends
     if stages:
         made_a, made_b, _, out, window, level_a, solved, stage, sems = rest
+    elif ends:
+        made_b, _, out, joined, solved, solved_a, *sends, window, level_a, sems = rest
     else:
         _, out, solved, solved_a, *sends, window, level_a, sems = rest
     cases = solved.shape[-1]
@@ -312,8 +318,8 @@
     def _():
         odd = meta[1]
         halo = 2 * REACH
-        window[halo : halo + count] = centre[...]
-        place(window, odd, even_in, odd_in)
+        window[halo : halo + count] = centre[:, :, at if centre.shape[-1] > cases else slice(None)]
+        place(window, odd, even_in, odd_in, at if even_in.shape[-1] > cases else slice(None))
         first_of_group(wide_a, first, window.at[pl.ds(REACH, count + halo)], level_a, REACH, at)
         done, copies = None, []
         if stages:
@@ -347,6 +353,9 @@
         else:
             emit_sends(odd, solved, sends)
             solved_a[...] = level_a[REACH : REACH + count]
+            if ends:
+                joined[:, :, : chunk * cases] = made_b[...]
+                joined[:, :, at] = solved[...]
 
     @pl.when(meta[0] == group - 1)
     def _():
@@ -389,10 +398,11 @@
             for value, mate in zip(values, mates)
         ]
 
-    def travel(group, centre, sides):
-        return [lax.ppermute(centre, AXES, hop_pairs(group, same_row, chain, rows))] + [
-            lax.ppermute(value, AXES, hop_pairs(group, mate, chain, rows)) for value, mate in zip(sides, mates)
-        ]
+    def travel_centre(group, value):
+        return lax.ppermute(value, AXES, hop_pairs(group, same_row, chain, rows))
+
+    def travel_sides(group, values):
+        return [lax.ppermute(value, AXES, hop_pairs(group, mate, chain, rows)) for value, mate in zip(values, mates)]
 
     def call(kernel, name, in_specs, out_shape, out_specs=None, **more):
         return pl.pallas_call(
@@ -452,14 +462,14 @@
     padded = pltpu.VMEM((count + halo, block, cases), jnp.bfloat16)
     padded_half = pltpu.VMEM((count + halo, block, part), jnp.bfloat16)
     solved, *sends = call(
-        functools.partial(exchanged_step, 0, None),
+        functools.partial(exchanged_step, 0),
         "step_0",
         [SMEM] + [VMEM] * 5,
         [whole, whole_edge, whole_edge],
-        scratch_shapes=[padded],
+        scratch_shapes=[padded, pltpu.VMEM(whole.shape, jnp.bfloat16)],
     )(meta, first, *sides, wide_a, base_0)
     wide_b, base_b = prepare(1, after(meta, solved))
-    arrived = travel(0, solved, sends)
+    arrived = [travel_centre(0, solved), *travel_sides(0, sends)]
 
     later_w = exchange(range(2, chain), after(edge_w[2:], sides))
     edges, = call(
@@ -476,27 +486,27 @@
     )(meta, *arrived, first, wide_a, solved)
     sides = exchange([1], sides, 0)
     made_a = [own] * CHUNKS
-    sent = []
-    for chunk in range(CHUNKS):
-        sent.append(
-            call(
-                functools.partial(exchanged_step, 1, chunk),
-                f"step_1_{chunk}",
-                [SMEM] + [VMEM] * 5,
-                [half, half_edge, half_edge],
-                scratch_shapes=[padded_half],
-            )(meta, own, *sides, wide_b, base_b)
-        )
+    wide_side = shaped((halo, block, cases))
+    *sent, even_side, odd_side = call(
+        functools.partial(exchanged_step, 1),
+        "step_1_b",
+        [SMEM] + [VMEM] * 5,
+        [half] * CHUNKS + [wide_side] * 2,
+        scratch_shapes=[padded, pltpu.VMEM(whole.shape, jnp.bfloat16)],
+    )(meta, own, *sides, wide_b, base_b)
+    sides = travel_sides(1, (even_side, odd_side))
+    arrived = [
+        [travel_centre(1, after(value, later_w) if chunk else value), *sides] for chunk, value in enumerate(sent)
+    ]
 
     for group in range(2, chain):
         final = group == chain - 1
-        arrived = [travel(group - 1, solved, sends) for solved, *sends in sent]
-        made = []
+        made, sides = [], []
         for chunk in range(CHUNKS):
-            stages = final and chunk == CHUNKS - 1
-            outs = [] if stages else [half, half] + ([] if final else [half_edge] * 2)
-            extra = [made[0][1], made[0][0][0]] if stages else []
-            sems = (2, pairs) if stages else (2,)
+            ends = chunk == CHUNKS - 1
+            stages = final and ends
+            extra = [level for _, level in made] * stages + [value for value, _ in made] * ends
+            outs = [whole] * (ends and not final) + [half, half] * (not stages) + [half_edge] * (2 * (not final))
             out, *now = call(
                 functools.partial(later_step, group, chunk, final),
                 f"step_{group}_{chunk}",
@@ -507,7 +517,7 @@
                     pltpu.VMEM((count + 2 * halo, block, part), jnp.bfloat16),
                     padded_half,
                     *([pltpu.VMEM(shape, jnp.bfloat16) for shape in (half.shape, (2, *whole.shape))] if stages else []),
-                    pltpu.SemaphoreType.DMA(sems),
+                    pltpu.SemaphoreType.DMA((2, pairs) if stages else (2,)),
                 ],
                 input_output_aliases={11 + len(extra): 0},
             )(
@@ -519,14 +529,20 @@
                 wide_b,
                 base_b,
                 made_a[chunk],
-                sent[chunk][0],
+                sent[chunk],
                 *extra,
                 out,
             )
-            if now:
-                solved, level, *sends = now
-                made.append(((solved, *sends), level))
-        sent, made_a = [values[0] for values in made], [values[1] for values in made]
+            if not final:
+                *joined, solved, level, even_side, odd_side = now
+                made.append((solved, level))
+                sides.append(travel_sides(group, (even_side, odd_side)))
+            elif now:
+                made.append(now)
+        if not final:
+            centre = travel_centre(group, joined[0])
+            arrived = [[centre, *pair] for pair in sides]
+            sent, made_a = [value for value, _ in made], [level for _, level in made]
     return out
 
 

time: 53.4 us -> 55.4 us (1.037)
  waiting for transfers between devices: 10.2 us -> 17.3 us
  starting transfers between devices: 24.7 us -> 20.2 us
    ppermute x15 -> x12, waiting for transfers between devices: 8.06 us -> 15.7 us  [the longest x8 10.6 us: travel_sides(): lax.ppermute(value, AXES, hop_pairs(group, mate, chain, rows))]
    ppermute x15 -> x12, starting transfers between devices: 21.5 us -> 17 us  [the longest x8 11.1 us: travel_sides(): lax.ppermute(value, AXES, hop_pairs(group, mate, chain, rows))]
    pallas_call x3 -> x2, Pallas kernels: 1.65 us -> 1.1 us  [the longest x1 0.55 us: per_device(): call(functools.partial(exchanged_step, 1), 'step_1_b', [SMEM] + [VMEM] *...]
  transfers between devices with their start and end apart: 21 -> 18, of which waited for: 8 -> 8; matrix products, arithmetic and copies ran while one was open for 0% -> 0% of each run, Pallas kernels for 22% -> 19%
where the time goes in v10:
time: 55.4 us; the launch traced here: 55.2 us
  starting transfers between devices  20.2 us (36%)
  Pallas kernels  17.5 us (32%)
  waiting for transfers between devices  17.3 us (31%)
    ppermute x8, starting transfers between devices, travel_sides(): lax.ppermute(value, AXES, hop_pairs(group, mate, chain, rows))  11.1 us
    ppermute x8, waiting for transfers between devices, travel_sides(): lax.ppermute(value, AXES, hop_pairs(group, mate, chain, rows))  10.6 us
    pallas_call x2, Pallas kernels, prepare(): call(functools.partial(prepare_kernel, turn), f'prepare_{turn}', [SMEM] +...  6.32 us
    ppermute x4, starting transfers between devices, travel_centre(): return lax.ppermute(value, AXES, hop_pairs(group, same_row, chain, rows))  5.89 us
    pallas_call x4, Pallas kernels, per_device(): call(functools.partial(later_step, group, chunk, final), f'step_{group}_{...  5.87 us
    ppermute x4, waiting for transfers between devices, travel_centre(): return lax.ppermute(value, AXES, hop_pairs(group, same_row, chain, rows))  5.04 us
    ppermute x6, starting transfers between devices, exchange(): lax.ppermute(value, AXES, inner_pairs(groups, mate, chain, rows, idle))  3.22 us
    pallas_call x1, Pallas kernels, per_device(): call(first_kernel, 'first_level', [SMEM] + [HBM] * 5, [whole, *(shape for...  3.04 us
  transfers between devices with their start and end apart: 18, of which 8 were waited for; matrix products, arithmetic and copies ran while one was open for 0% of the time, Pallas kernels for 19%

profile of v10, /device:TPU:11, one launch (start us, length us, event | category | flops | bytes accessed | tf_op | source)
XLA Modules:
  0.0 55.2 jit_solution(10715276652476414790)
XLA Ops:
  0.0 0.1 pad_add_fusion.meta
  0.1 3.0 %first_level.1 = (bf16[8,128,256]{2,1,0:T(8,128)(2,1)S(1)}, bf16[4,128,128]{2,1,0:T(8,128)(2,1)S(1)}, bf16[4,128,128]{2,1,0:T(8,128)(2,1)S(1)}, bf16[10,128,128]...) custom-call(s32[3]{0:T(128)S(1)} %pad_add_fusion.meta, s32[6,2,8]{2,1,0:T(2,128)} %bitcast.5, f32[6,2,8]{2,1,0:T(2,128)} %bitcast.8, ...), custom_call_target="tpu_custom_call" | custom-call | tf_op jit(solution)/shard_map/first_level/pallas_call | solution.py:424
  3.1 1.3 %collective-permute-start = (bf16[4,128,128]{2,1,0:T(8,128)(2,1)S(1)}, bf16[4,128,128]{2,1,0:T(8,128)(2,1)S(1)}, u32[]{:S(2)}, u32[]{:S(2)}) collective-permute-start(bf16[4,128,128]{2,1,0:T(8,128)(2,1)S(1)} %get-tuple-element.44), channel_id=1, source_target_pairs={{0,1},{16,17},{24,25},{8,10},{1,0},{17,16},{25,24},{9,11},{2,3},{1... | collective-permute-start | bytes 393224 | tf_op jit(solution)/shard_map/ppermute | solution.py:397
  4.4 0.1 collective-permute-start.1
  4.5 3.2 %prepare_0.1 = (bf16[4,256,768]{2,1,0:T(8,128)(2,1)S(1)}, f32[8,128,256]{2,1,0:T(8,128)S(1)}) custom-call(s32[3]{0:T(128)S(1)} %pad_add_fusion.meta, s32[6,2,8]{2,1,0:T(2,128)} %bitcast.6, f32[6,2,8]{2,1,0:T(2,128)} %bitcast.9, bf16[2,8,6,128,128]{4,3,2,1,0:T(8,128)(2,1)} %lower_hbm.5, bf16[2,8,128,128]{3,2,1,0:T(8,128)(2,1)} %inverse_hbm.5, ...), custom_call_target="tpu_custom_call" | custom-call | tf_op jit(solution)/shard_map/prepare_0/pallas_call | solution.py:445
  7.7 1.6 %collective-permute-done.even_in.even_a = bf16[4,128,128]{2,1,0:T(8,128)(2,1)S(1)} collective-permute-done((bf16[4,128,128]{2,1,0:T(8,128)(2,1)S(1)}, bf16[4,128,128]{2,1,0:T(8,128)(2,1)S(1)}, u32[]{:S(2)}, u32[]{:S(2)}) %collective-permute-start) | collective-permute-done | bytes 131104 | tf_op jit(solution)/shard_map/ppermute | solution.py:397
  9.3 0.0 collective-permute-done.1.odd_in.odd_a
  9.3 0.5 step_0.1
  9.8 2.7 %collective-permute-start.2 = (bf16[8,128,256]{2,1,0:T(8,128)(2,1)S(1)}, bf16[8,128,256]{2,1,0:T(8,128)(2,1)S(1)}, u32[]{:S(2)}, u32[]{:S(2)}) collective-permute-start(bf16[8,128,256]{2,1,0:T(8,128)(2,1)S(1)} %get-tuple-element.48.old_b), channel_id=1, source_target_pairs={{0,8},{1,9},{2,10},{3,11},{4,12},{5,13},{6,14},{7,15},{8,0},{9,1},... | collective-permute-start | bytes 1572872 | tf_op jit(solution)/shard_map/ppermute | solution.py:402
  12.5 1.3 %collective-permute-start.7 = (bf16[10,128,128]{2,1,0:T(8,128)(2,1)S(1)}, bf16[10,128,128]{2,1,0:T(8,128)(2,1)S(1)}, u32[]{:S(2)}, u32[]{:S(2)}) collective-permute-start(bf16[10,128,128]{2,1,0:T(8,128)(2,1)S(1)} %get-tuple-element.60), channel_id=1, source_target_pairs={{16,17},{24,25},{0,8},{8,0},{17,16},{25,24},{1,9},{9,1},{18,19},{2... | collective-permute-start | bytes 983048 | tf_op jit(solution)/shard_map/ppermute | solution.py:397
  13.8 0.0 collective-permute-start.8
  13.8 0.3 collective-permute-start.3
  14.1 0.2 collective-permute-start.4
  14.3 0.8 %collective-permute-done.3.even_in = bf16[2,128,256]{2,1,0:T(8,128)(2,1)S(1)} collective-permute-done((bf16[2,128,256]{2,1,0:T(8,128)(2,1)S(1)}, bf16[2,128,256]{2,1,0:T(8,128)(2,1)S(1)}, u32[]{:S(2)}, u32[]{:S(2)}) %collective-permute-start.3) | collective-permute-done | bytes 131104 | tf_op jit(solution)/shard_map/ppermute | solution.py:405
  15.1 0.3 collective-permute-done.4.odd_in
  15.5 0.0 collective-permute-done.2.centre
  15.5 0.6 %step_1.1 = (bf16[2,8,128,256]{3,2,1,0:T(8,128)(2,1)}, bf16[8,128,256]{2,1,0:T(8,128)(2,1)S(1)}, bf16[2,128,256]{2,1,0:T(8,128)(2,1)S(1)}, bf16[2,128,256]{2,1,0:T(8,128)(2,1)S(1)}) custom-call(s32[3]{0:T(128)S(1)} %pad_add_fusion.meta, bf16[8,128,256]{2,1,0:T(8,128)(2,1)S(1)} %collective-permute-done.2.centre, ...), custom_call_target="tpu_custom_call" | custom-call | tf_op jit(solution)/shard_map/step_1/pallas_call | solution.py:479
  16.1 0.2 collective-permute-start.5
  16.3 0.3 collective-permute-start.6
  16.6 3.2 %prepare_1.1 = (bf16[4,256,768]{2,1,0:T(8,128)(2,1)S(1)}, f32[8,128,256]{2,1,0:T(8,128)S(1)}) custom-call(s32[3]{0:T(128)S(1)} %pad_add_fusion.meta, s32[6,2,8]{2,1,0:T(2,128)} %bitcast.7, f32[6,2,8]{2,1,0:T(2,128)} %bitcast.10, bf16[2,8,6,128,128]{4,3,2,1,0:T(8,128)(2,1)} %lower_hbm.5, bf16[2,8,128,128]{3,2,1,0:T(8,128)(2,1)} %inverse_hbm.5, ...), custom_call_target="tpu_custom_call" | custom-call | tf_op jit(solution)/shard_map/prepare_1/pallas_call | solution.py:445
  19.8 0.0 collective-permute-done.5.even_in
  19.8 0.0 collective-permute-done.6.odd_in
  19.8 0.6 step_1_b.1
  20.4 7.5 %collective-permute-start.10 = (bf16[4,128,256]{2,1,0:T(8,128)(2,1)S(1)}, bf16[4,128,256]{2,1,0:T(8,128)(2,1)S(1)}, u32[]{:S(2)}, u32[]{:S(2)}) collective-permute-start(bf16[4,128,256]{2,1,0:T(8,128)(2,1)S(1)} %get-tuple-element.63), channel_id=1, source_target_pairs={{8,17},{9,16},{10,19},{11,18},{12,21},{13,20},{14,23},{15,22},{0,8... | collective-permute-start | bytes 786440 | tf_op jit(solution)/shard_map/ppermute | solution.py:405
  27.9 0.9 %collective-permute-start.11 = (bf16[4,128,256]{2,1,0:T(8,128)(2,1)S(1)}, bf16[4,128,256]{2,1,0:T(8,128)(2,1)S(1)}, u32[]{:S(2)}, u32[]{:S(2)}) collective-permute-start(bf16[4,128,256]{2,1,0:T(8,128)(2,1)S(1)} %get-tuple-element.64), channel_id=1, source_target_pairs={{8,16},{9,18},{10,17},{11,20},{12,19},{13,22},{14,21},{15,23},{0,8... | collective-permute-start | bytes 786440 | tf_op jit(solution)/shard_map/ppermute | solution.py:405
  28.7 0.1 collective-permute-start.12
  28.8 0.0 collective-permute-done.7.even_b
  28.8 0.0 collective-permute-done.8.odd_b
  28.8 0.0 collective-permute-start.9
  28.9 0.6 %order.1.edges = bf16[2,14,128,128]{3,2,1,0:T(8,128)(2,1)S(1)} custom-call(s32[3]{0:T(128)S(1)} %pad_add_fusion.meta, bf16[4,128,128]{2,1,0:T(8,128)(2,1)S(1)} %collective-permute-done.even_in.even_a, bf16[4,128,128]{2,1,0:T(8,128)(2,1)S(1)} %collective-permute-done.1.odd_in.odd_a, bf16[10,128,128]{2,1,0:T(8,128)(2,1)S(1)} %collective-permute-done.7.even_b, ...), custom_call_target="tpu_custom_call" | custom-call | tf_op jit(solution)/shard_map/order/pallas_call | solution.py:475
  29.5 1.7 %collective-permute-done.10.even_in = bf16[4,128,256]{2,1,0:T(8,128)(2,1)S(1)} collective-permute-done((bf16[4,128,256]{2,1,0:T(8,128)(2,1)S(1)}, bf16[4,128,256]{2,1,0:T(8,128)(2,1)S(1)}, u32[]{:S(2)}, u32[]{:S(2)}) %collective-permute-start.10) | collective-permute-done | bytes 262176 | tf_op jit(solution)/shard_map/ppermute | solution.py:405
  31.2 2.8 %collective-permute-done.11.odd_in = bf16[4,128,256]{2,1,0:T(8,128)(2,1)S(1)} collective-permute-done((bf16[4,128,256]{2,1,0:T(8,128)(2,1)S(1)}, bf16[4,128,256]{2,1,0:T(8,128)(2,1)S(1)}, u32[]{:S(2)}, u32[]{:S(2)}) %collective-permute-start.11) | collective-permute-done | bytes 262176 | tf_op jit(solution)/shard_map/ppermute | solution.py:405
  34.0 2.8 %collective-permute-done.12.centre = bf16[8,128,128]{2,1,0:T(8,128)(2,1)S(1)} collective-permute-done((bf16[8,128,128]{2,1,0:T(8,128)(2,1)S(1)}, bf16[8,128,128]{2,1,0:T(8,128)(2,1)S(1)}, u32[]{:S(2)}, u32[]{:S(2)}) %collective-permute-start.12) | collective-permute-done | bytes 262176 | tf_op jit(solution)/shard_map/ppermute | solution.py:402
  36.8 0.6 %step_2_0.1 = (bf16[2,8,128,256]{3,2,1,0:T(8,128)(2,1)}, bf16[8,128,128]{2,1,0:T(8,128)(2,1)S(1)}, bf16[8,128,128]{2,1,0:T(8,128)(2,1)S(1)}, bf16[4,128,128]{2,1,0:T(8,128)(2,1)S(1)}, bf16[4,128,128]{2,1,0:T(8,128)(2,1)S(1)}) custom-call(s32[3]{0:T(128)S(1)} %pad_add_fusion.meta, ...), custom_call_target="tpu_custom_call", output_to_operand_aliasing={{0}: (11, {})} | custom-call | tf_op jit(solution)/shard_map/step_2_0/pallas_call | solution.py:510
  37.4 2.2 %collective-permute-done.9.centre = bf16[8,128,128]{2,1,0:T(8,128)(2,1)S(1)} collective-permute-done((bf16[8,128,128]{2,1,0:T(8,128)(2,1)S(1)}, bf16[8,128,128]{2,1,0:T(8,128)(2,1)S(1)}, u32[]{:S(2)}, u32[]{:S(2)}) %collective-permute-start.9) | collective-permute-done | bytes 262176 | tf_op jit(solution)/shard_map/ppermute | solution.py:402
  39.6 0.6 %step_2_1.1 = (bf16[2,8,128,256]{3,2,1,0:T(8,128)(2,1)}, bf16[8,128,256]{2,1,0:T(8,128)(2,1)S(1)}, bf16[8,128,128]{2,1,0:T(8,128)(2,1)S(1)}, bf16[8,128,128]{2,1...) custom-call(s32[3]{0:T(128)S(1)} %pad_add_fusion.meta, ...), custom_call_target="tpu_custom_call", output_to_operand_aliasing={{0}: (12, {})} | custom-call | tf_op jit(solution)/shard_map/step_2_1/pallas_call | solution.py:510
  40.2 3.1 %collective-permute-start.13 = (bf16[8,128,256]{2,1,0:T(8,128)(2,1)S(1)}, bf16[8,128,256]{2,1,0:T(8,128)(2,1)S(1)}, u32[]{:S(2)}, u32[]{:S(2)}) collective-permute-start(bf16[8,128,256]{2,1,0:T(8,128)(2,1)S(1)} %get-tuple-element.69), channel_id=1, source_target_pairs={{0,8},{1,9},{2,10},{3,11},{4,12},{5,13},{6,14},{7,15},{8,0},{9,1},... | collective-permute-start | bytes 1572872 | tf_op jit(solution)/shard_map/ppermute | solution.py:402
  43.3 0.1 collective-permute-start.16
  43.3 0.3 collective-permute-start.17
  43.6 1.1 %collective-permute-start.14 = (bf16[4,128,128]{2,1,0:T(8,128)(2,1)S(1)}, bf16[4,128,128]{2,1,0:T(8,128)(2,1)S(1)}, u32[]{:S(2)}, u32[]{:S(2)}) collective-permute-start(bf16[4,128,128]{2,1,0:T(8,128)(2,1)S(1)} %get-tuple-element.70), channel_id=1, source_target_pairs={{0,8},{1,9},{2,10},{3,11},{4,12},{5,13},{6,14},{7,15},{8,0},{9,1},... | collective-permute-start | bytes 393224 | tf_op jit(solution)/shard_map/ppermute | solution.py:405
  44.7 0.8 %collective-permute-start.15 = (bf16[4,128,128]{2,1,0:T(8,128)(2,1)S(1)}, bf16[4,128,128]{2,1,0:T(8,128)(2,1)S(1)}, u32[]{:S(2)}, u32[]{:S(2)}) collective-permute-start(bf16[4,128,128]{2,1,0:T(8,128)(2,1)S(1)} %get-tuple-element.71), channel_id=1, source_target_pairs={{0,8},{1,9},{2,10},{3,11},{4,12},{5,13},{6,14},{7,15},{8,0},{9,1},... | collective-permute-start | bytes 393224 | tf_op jit(solution)/shard_map/ppermute | solution.py:405
  45.5 4.9 %collective-permute-done.16.even_in = bf16[4,128,128]{2,1,0:T(8,128)(2,1)S(1)} collective-permute-done((bf16[4,128,128]{2,1,0:T(8,128)(2,1)S(1)}, bf16[4,128,128]{2,1,0:T(8,128)(2,1)S(1)}, u32[]{:S(2)}, u32[]{:S(2)}) %collective-permute-start.16) | collective-permute-done | bytes 131104 | tf_op jit(solution)/shard_map/ppermute | solution.py:405
  50.5 0.0 collective-permute-done.17.odd_in
  50.5 0.0 collective-permute-done.13.centre
  50.5 1.9 %step_3_0.1 = (bf16[2,8,128,256]{3,2,1,0:T(8,128)(2,1)}, bf16[8,128,128]{2,1,0:T(8,128)(2,1)S(1)}, bf16[8,128,128]{2,1,0:T(8,128)(2,1)S(1)}) custom-call(s32[3]{0:T(128)S(1)} %pad_add_fusion.meta, bf16[8,128,256]{2,1,0:T(8,128)(2,1)S(1)} %collective-permute-done.13.centre, ...), custom_call_target="tpu_custom_call", output_to_operand_aliasing={{0}: (11, {})} | custom-call | tf_op jit(solution)/shard_map/step_3_0/pallas_call | solution.py:510
  52.4 0.0 collective-permute-done.14.even_in
  52.4 0.0 collective-permute-done.15.odd_in
  52.4 2.8 %step_3_1.1 = bf16[2,8,128,256]{3,2,1,0:T(8,128)(2,1)} custom-call(s32[3]{0:T(128)S(1)} %pad_add_fusion.meta, bf16[8,128,256]{2,1,0:T(8,128)(2,1)S(1)} %collective-permute-done.13.centre, bf16[4,128,128]{2,1,0:T(8,128)(2,1)S(1)} %collective-permute-done.14.even_in, ...), custom_call_target="tpu_custom_call", output_to_operand_aliasing={{}: (13, {})} | custom-call | tf_op jit(solution)/shard_map/step_3_1/pallas_call | solution.py:510
Async XLA Ops:
  3.1 6.1 %collective-permute-start = (bf16[4,128,128]{2,1,0:T(8,128)(2,1)S(1)}, bf16[4,128,128]{2,1,0:T(8,128)(2,1)S(1)}, u32[]{:S(2)}, u32[]{:S(2)}) collective-permute-start(bf16[4,128,128]{2,1,0:T(8,128)(2,1)S(1)} %get-tuple-element.44), channel_id=1, source_target_pairs={{0,1},{16,17},{24,25},{8,10},{1,0},{17,16},{25,24},{9,11},{2,3},{1... | collective-permute-start | bytes 393224 | tf_op jit(solution)/shard_map/ppermute | solution.py:397
  4.4 4.8 %collective-permute-start.1 = (bf16[4,128,128]{2,1,0:T(8,128)(2,1)S(1)}, bf16[4,128,128]{2,1,0:T(8,128)(2,1)S(1)}, u32[]{:S(2)}, u32[]{:S(2)}) collective-permute-start(bf16[4,128,128]{2,1,0:T(8,128)(2,1)S(1)} %get-tuple-element.45), channel_id=1, source_target_pairs={{0,8},{8,0},{16,24},{24,16},{1,2},{17,18},{25,26},{9,11},{2,1},{18... | collective-permute-start | bytes 393224 | tf_op jit(solution)/shard_map/ppermute | solution.py:397
  9.8 5.7 %collective-permute-start.2 = (bf16[8,128,256]{2,1,0:T(8,128)(2,1)S(1)}, bf16[8,128,256]{2,1,0:T(8,128)(2,1)S(1)}, u32[]{:S(2)}, u32[]{:S(2)}) collective-permute-start(bf16[8,128,256]{2,1,0:T(8,128)(2,1)S(1)} %get-tuple-element.48.old_b), channel_id=1, source_target_pairs={{0,8},{1,9},{2,10},{3,11},{4,12},{5,13},{6,14},{7,15},{8,0},{9,1},... | collective-permute-start | bytes 1572872 | tf_op jit(solution)/shard_map/ppermute | solution.py:402
  12.5 16.3 %collective-permute-start.7 = (bf16[10,128,128]{2,1,0:T(8,128)(2,1)S(1)}, bf16[10,128,128]{2,1,0:T(8,128)(2,1)S(1)}, u32[]{:S(2)}, u32[]{:S(2)}) collective-permute-start(bf16[10,128,128]{2,1,0:T(8,128)(2,1)S(1)} %get-tuple-element.60), channel_id=1, source_target_pairs={{16,17},{24,25},{0,8},{8,0},{17,16},{25,24},{1,9},{9,1},{18,19},{2... | collective-permute-start | bytes 983048 | tf_op jit(solution)/shard_map/ppermute | solution.py:397
  13.8 15.1 %collective-permute-start.8 = (bf16[10,128,128]{2,1,0:T(8,128)(2,1)S(1)}, bf16[10,128,128]{2,1,0:T(8,128)(2,1)S(1)}, u32[]{:S(2)}, u32[]{:S(2)}) collective-permute-start(bf16[10,128,128]{2,1,0:T(8,128)(2,1)S(1)} %get-tuple-element.61), channel_id=1, source_target_pairs={{0,8},{8,0},{16,24},{24,16},{17,18},{25,26},{1,9},{9,1},{18,17},{2... | collective-permute-start | bytes 983048 | tf_op jit(solution)/shard_map/ppermute | solution.py:397
  13.8 1.3 %collective-permute-start.3 = (bf16[2,128,256]{2,1,0:T(8,128)(2,1)S(1)}, bf16[2,128,256]{2,1,0:T(8,128)(2,1)S(1)}, u32[]{:S(2)}, u32[]{:S(2)}) collective-permute-start(bf16[2,128,256]{2,1,0:T(8,128)(2,1)S(1)} %get-tuple-element.49), channel_id=1, source_target_pairs={{0,9},{1,8},{2,11},{3,10},{4,13},{5,12},{6,15},{7,14},{8,0},{9,1},... | collective-permute-start | bytes 393224 | tf_op jit(solution)/shard_map/ppermute | solution.py:405
  14.1 1.3 %collective-permute-start.4 = (bf16[2,128,256]{2,1,0:T(8,128)(2,1)S(1)}, bf16[2,128,256]{2,1,0:T(8,128)(2,1)S(1)}, u32[]{:S(2)}, u32[]{:S(2)}) collective-permute-start(bf16[2,128,256]{2,1,0:T(8,128)(2,1)S(1)} %get-tuple-element.50), channel_id=1, source_target_pairs={{0,8},{1,10},{2,9},{3,12},{4,11},{5,14},{6,13},{7,15},{8,0},{9,1},... | collective-permute-start | bytes 393224 | tf_op jit(solution)/shard_map/ppermute | solution.py:405
  16.1 3.7 %collective-permute-start.5 = (bf16[2,128,256]{2,1,0:T(8,128)(2,1)S(1)}, bf16[2,128,256]{2,1,0:T(8,128)(2,1)S(1)}, u32[]{:S(2)}, u32[]{:S(2)}) collective-permute-start(bf16[2,128,256]{2,1,0:T(8,128)(2,1)S(1)} %get-tuple-element.52), channel_id=1, source_target_pairs={{8,9},{0,2},{16,24},{24,16},{9,8},{1,3},{17,25},{25,17},{10,11},{2... | collective-permute-start | bytes 393224 | tf_op jit(solution)/shard_map/ppermute | solution.py:397
  16.3 3.5 %collective-permute-start.6 = (bf16[2,128,256]{2,1,0:T(8,128)(2,1)S(1)}, bf16[2,128,256]{2,1,0:T(8,128)(2,1)S(1)}, u32[]{:S(2)}, u32[]{:S(2)}) collective-permute-start(bf16[2,128,256]{2,1,0:T(8,128)(2,1)S(1)} %get-tuple-element.53), channel_id=1, source_target_pairs={{0,8},{8,0},{16,24},{24,16},{9,10},{1,3},{17,25},{25,17},{10,9},{2... | collective-permute-start | bytes 393224 | tf_op jit(solution)/shard_map/ppermute | solution.py:397
  20.4 10.8 %collective-permute-start.10 = (bf16[4,128,256]{2,1,0:T(8,128)(2,1)S(1)}, bf16[4,128,256]{2,1,0:T(8,128)(2,1)S(1)}, u32[]{:S(2)}, u32[]{:S(2)}) collective-permute-start(bf16[4,128,256]{2,1,0:T(8,128)(2,1)S(1)} %get-tuple-element.63), channel_id=1, source_target_pairs={{8,17},{9,16},{10,19},{11,18},{12,21},{13,20},{14,23},{15,22},{0,8... | collective-permute-start | bytes 786440 | tf_op jit(solution)/shard_map/ppermute | solution.py:405
  27.9 6.1 %collective-permute-start.11 = (bf16[4,128,256]{2,1,0:T(8,128)(2,1)S(1)}, bf16[4,128,256]{2,1,0:T(8,128)(2,1)S(1)}, u32[]{:S(2)}, u32[]{:S(2)}) collective-permute-start(bf16[4,128,256]{2,1,0:T(8,128)(2,1)S(1)} %get-tuple-element.64), channel_id=1, source_target_pairs={{8,16},{9,18},{10,17},{11,20},{12,19},{13,22},{14,21},{15,23},{0,8... | collective-permute-start | bytes 786440 | tf_op jit(solution)/shard_map/ppermute | solution.py:405
  28.7 8.0 %collective-permute-start.12 = (bf16[8,128,128]{2,1,0:T(8,128)(2,1)S(1)}, bf16[8,128,128]{2,1,0:T(8,128)(2,1)S(1)}, u32[]{:S(2)}, u32[]{:S(2)}) collective-permute-start(bf16[8,128,128]{2,1,0:T(8,128)(2,1)S(1)} %get-tuple-element.65.old_b), channel_id=1, source_target_pairs={{8,16},{9,17},{10,18},{11,19},{12,20},{13,21},{14,22},{15,23},{0,8... | collective-permute-start | bytes 786440 | tf_op jit(solution)/shard_map/ppermute | solution.py:402
  28.8 10.8 %collective-permute-start.9 = (bf16[8,128,128]{2,1,0:T(8,128)(2,1)S(1)}, bf16[8,128,128]{2,1,0:T(8,128)(2,1)S(1)}, u32[]{:S(2)}, u32[]{:S(2)}) collective-permute-start(bf16[8,128,128]{2,1,0:T(8,128)(2,1)S(1)} %get-tuple-element.62.old_b), channel_id=1, source_target_pairs={{8,16},{9,17},{10,18},{11,19},{12,20},{13,21},{14,22},{15,23},{0,8... | collective-permute-start | bytes 786440 | tf_op jit(solution)/shard_map/ppermute | solution.py:402
  40.2 10.3 %collective-permute-start.13 = (bf16[8,128,256]{2,1,0:T(8,128)(2,1)S(1)}, bf16[8,128,256]{2,1,0:T(8,128)(2,1)S(1)}, u32[]{:S(2)}, u32[]{:S(2)}) collective-permute-start(bf16[8,128,256]{2,1,0:T(8,128)(2,1)S(1)} %get-tuple-element.69), channel_id=1, source_target_pairs={{0,8},{1,9},{2,10},{3,11},{4,12},{5,13},{6,14},{7,15},{8,0},{9,1},... | collective-permute-start | bytes 1572872 | tf_op jit(solution)/shard_map/ppermute | solution.py:402
  43.3 7.2 %collective-permute-start.16 = (bf16[4,128,128]{2,1,0:T(8,128)(2,1)S(1)}, bf16[4,128,128]{2,1,0:T(8,128)(2,1)S(1)}, u32[]{:S(2)}, u32[]{:S(2)}) collective-permute-start(bf16[4,128,128]{2,1,0:T(8,128)(2,1)S(1)} %get-tuple-element.74), channel_id=1, source_target_pairs={{0,8},{1,9},{2,10},{3,11},{4,12},{5,13},{6,14},{7,15},{8,0},{9,1},... | collective-permute-start | bytes 393224 | tf_op jit(solution)/shard_map/ppermute | solution.py:405
  43.3 7.1 %collective-permute-start.17 = (bf16[4,128,128]{2,1,0:T(8,128)(2,1)S(1)}, bf16[4,128,128]{2,1,0:T(8,128)(2,1)S(1)}, u32[]{:S(2)}, u32[]{:S(2)}) collective-permute-start(bf16[4,128,128]{2,1,0:T(8,128)(2,1)S(1)} %get-tuple-element.75), channel_id=1, source_target_pairs={{0,8},{1,9},{2,10},{3,11},{4,12},{5,13},{6,14},{7,15},{8,0},{9,1},... | collective-permute-start | bytes 393224 | tf_op jit(solution)/shard_map/ppermute | solution.py:405
  43.6 8.8 %collective-permute-start.14 = (bf16[4,128,128]{2,1,0:T(8,128)(2,1)S(1)}, bf16[4,128,128]{2,1,0:T(8,128)(2,1)S(1)}, u32[]{:S(2)}, u32[]{:S(2)}) collective-permute-start(bf16[4,128,128]{2,1,0:T(8,128)(2,1)S(1)} %get-tuple-element.70), channel_id=1, source_target_pairs={{0,8},{1,9},{2,10},{3,11},{4,12},{5,13},{6,14},{7,15},{8,0},{9,1},... | collective-permute-start | bytes 393224 | tf_op jit(solution)/shard_map/ppermute | solution.py:405
  44.7 7.7 %collective-permute-start.15 = (bf16[4,128,128]{2,1,0:T(8,128)(2,1)S(1)}, bf16[4,128,128]{2,1,0:T(8,128)(2,1)S(1)}, u32[]{:S(2)}, u32[]{:S(2)}) collective-permute-start(bf16[4,128,128]{2,1,0:T(8,128)(2,1)S(1)} %get-tuple-element.71), channel_id=1, source_target_pairs={{0,8},{1,9},{2,10},{3,11},{4,12},{5,13},{6,14},{7,15},{8,0},{9,1},... | collective-permute-start | bytes 393224 | tf_op jit(solution)/shard_map/ppermute | solution.py:405

commit v11 on v9

--- a/solution.py
+++ b/solution.py
@@ -226,6 +226,15 @@
     window[pl.ds(jnp.where(odd == 1, high, low), halo)] = odd_in[:, :, at]
 
 
+def clear_beyond(meta, window, halo):
+    for end in range(2):
+        start = end * (window.shape[0] - halo)
+
+        @pl.when(meta[3 + end] == 1)
+        def _():
+            window[start : start + halo] = jnp.zeros((halo, *window.shape[1:]), window.dtype)
+
+
 def columns(chunk, cases):
     return slice(None) if chunk is None else slice(chunk * cases, (chunk + 1) * cases)
 
@@ -278,6 +287,7 @@
                     cols = slice(part * block, (part + 1) * block)
                     level_a[i + jnp.where(meta[1] == 1, low, high), :, cols] = even_in[i * parts + part]
                     level_a[i + jnp.where(meta[1] == 1, high, low), :, cols] = odd_in[i * parts + part]
+        clear_beyond(meta, level_a, REACH)
         second_of_group(wide_b, base_b, level_a, solved, at)
         emit_sends(meta[1], solved, (even_out, odd_out))
 
@@ -289,6 +299,7 @@
     def _():
         window[REACH : REACH + count] = centre[...]
         place(window, meta[1], even_in, odd_in)
+        clear_beyond(meta, window, REACH)
         first_of_group(wide_a, first, window, solved, 0, slice(None))
         emit_sends(meta[1], solved, (even_out, odd_out))
 
@@ -297,8 +308,15 @@
         store(first, old_b, out, slice(None), sems)
 
 
-def later_step(group, chunk, final, meta, centre, even_in, odd_in, edges, first, wide_a, wide_b, base_b, old_a, old_b, *rest):
+def later_step(group, chunk, final, meta, *refs):
     stages = final and chunk == CHUNKS - 1
+    if final and chunk == 0:
+        even_in, odd_in, low, high, *rest = refs
+        centre = [low, high]
+    else:
+        one, even_in, odd_in, *rest = refs
+        centre = [one]
+    edges, first, wide_a, wide_b, base_b, old_a, old_b, *rest = rest
     if stages:
         made_a, made_b, _, out, window, level_a, solved, stage, sems = rest
     else:
@@ -312,8 +330,10 @@
     def _():
         odd = meta[1]
         halo = 2 * REACH
-        window[halo : halo + count] = centre[...]
+        for i, part in enumerate(centre):
+            window[halo + i * part.shape[0] : halo + (i + 1) * part.shape[0]] = part[...]
         place(window, odd, even_in, odd_in)
+        clear_beyond(meta, window, halo)
         first_of_group(wide_a, first, window.at[pl.ds(REACH, count + halo)], level_a, REACH, at)
         done, copies = None, []
         if stages:
@@ -340,12 +360,15 @@
                 blocks = jnp.concatenate([edges[side, i * EDGE + d] for d in range(SPAN)], axis=1)
                 row = dot(blocks, flat(window, put, SPAN)) + base.astype(jnp.float32)
                 level_a[put] = row.astype(level_a.dtype)
+        clear_beyond(meta, level_a, REACH)
         second_of_group(wide_b, base_b, level_a, solved, at, done)
         if stages:
             for copy in copies:
                 copy.wait()
         else:
-            emit_sends(odd, solved, sends)
+            emit_sends(odd, solved, sends[:2])
+            for i, part in enumerate(sends[2:]):
+                part[...] = solved[i * part.shape[0] : (i + 1) * part.shape[0]]
             solved_a[...] = level_a[REACH : REACH + count]
 
     @pl.when(meta[0] == group - 1)
@@ -376,7 +399,8 @@
     part = cases // CHUNKS
     halo = 2 * REACH
     row = lax.axis_index("rows")
-    meta = jnp.stack([lax.axis_index("chain"), row % 2, row * count]).astype(jnp.int32)
+    ends = [row == 0, row == rows - 1]
+    meta = jnp.stack([lax.axis_index("chain"), row % 2, row * count, *ends]).astype(jnp.int32)
     depend = in_hbm(depend_rows.transpose(2, 0, 1))
     scale = in_hbm(block_scale.transpose(2, 0, 1))
     tables = [pltpu.SMEM(depend.shape, jnp.int32), pltpu.SMEM(scale.shape, jnp.float32)]
@@ -390,9 +414,11 @@
         ]
 
     def travel(group, centre, sides):
-        return [lax.ppermute(centre, AXES, hop_pairs(group, same_row, chain, rows))] + [
-            lax.ppermute(value, AXES, hop_pairs(group, mate, chain, rows)) for value, mate in zip(sides, mates)
-        ]
+        *sides, = sides
+        centres = sides[2:] or [centre]
+        kinds = [lax.ppermute(value, AXES, hop_pairs(group, same_row, chain, rows)) for value in centres]
+        kinds += [lax.ppermute(value, AXES, hop_pairs(group, mate, chain, rows)) for value, mate in zip(sides, mates)]
+        return [kinds[i] for i in (2, 3, 0, 1)] if len(kinds) > 3 else kinds
 
     def call(kernel, name, in_specs, out_shape, out_specs=None, **more):
         return pl.pallas_call(
@@ -494,13 +520,14 @@
         made = []
         for chunk in range(CHUNKS):
             stages = final and chunk == CHUNKS - 1
-            outs = [] if stages else [half, half] + ([] if final else [half_edge] * 2)
+            splits = group == chain - 2 and chunk == 0
+            outs = [] if stages else [half, half] + ([] if final else [half_edge] * (4 if splits else 2))
             extra = [made[0][1], made[0][0][0]] if stages else []
             sems = (2, pairs) if stages else (2,)
             out, *now = call(
                 functools.partial(later_step, group, chunk, final),
                 f"step_{group}_{chunk}",
-                [SMEM] + [VMEM] * (10 + len(extra)) + [ANY],
+                [SMEM] + [VMEM] * (7 + len(arrived[chunk]) + len(extra)) + [ANY],
                 [shaped(right_side.shape), *outs],
                 [ANY] + [VMEM] * len(outs),
                 scratch_shapes=[
@@ -509,7 +536,7 @@
                     *([pltpu.VMEM(shape, jnp.bfloat16) for shape in (half.shape, (2, *whole.shape))] if stages else []),
                     pltpu.SemaphoreType.DMA(sems),
                 ],
-                input_output_aliases={11 + len(extra): 0},
+                input_output_aliases={8 + len(arrived[chunk]) + len(extra): 0},
             )(
                 meta,
                 *arrived[chunk],

time: 53.4 us -> 53.6 us (level); the launches traced: 53.2 us -> 52.7 us
  waiting for transfers between devices: 10.2 us -> 8.71 us
  starting transfers between devices: 24.7 us -> 25.6 us
    ppermute x5 -> x6, starting transfers between devices: 13.5 us -> 15.2 us  [travel(): lax.ppermute(value, AXES, hop_pairs(group, same_row, chain, rows))]
    ppermute x10, waiting for transfers between devices: 8.04 us -> 6.5 us  [travel(): lax.ppermute(value, AXES, hop_pairs(group, mate, chain, rows))]
    ppermute x10, starting transfers between devices: 8.01 us -> 7.26 us  [travel(): lax.ppermute(value, AXES, hop_pairs(group, mate, chain, rows))]
  transfers between devices with their start and end apart: 21 -> 22, of which waited for: 8 -> 8; matrix products, arithmetic and copies ran while one was open for 0% -> 0% of each run, Pallas kernels for 22% -> 22%
where the time goes in v11:
time: 53.6 us; the launch traced here: 52.7 us
  starting transfers between devices  25.6 us (48%)
  Pallas kernels  18.1 us (34%)
  waiting for transfers between devices  8.71 us (16%)
    ppermute x6, starting transfers between devices, travel(): lax.ppermute(value, AXES, hop_pairs(group, same_row, chain, rows))  15.2 us
    ppermute x10, starting transfers between devices, travel(): lax.ppermute(value, AXES, hop_pairs(group, mate, chain, rows))  7.26 us
    ppermute x10, waiting for transfers between devices, travel(): lax.ppermute(value, AXES, hop_pairs(group, mate, chain, rows))  6.5 us
    pallas_call x2, Pallas kernels, prepare(): call(functools.partial(prepare_kernel, turn), f'prepare_{turn}', [SMEM] +...  6.33 us
    pallas_call x4, Pallas kernels, per_device(): call(functools.partial(later_step, group, chunk, final), f'step_{group}_{...  5.93 us
    ppermute x6, starting transfers between devices, exchange(): lax.ppermute(value, AXES, inner_pairs(groups, mate, chain, rows, idle))  3.22 us
    pallas_call x1, Pallas kernels, per_device(): call(first_kernel, 'first_level', [SMEM] + [HBM] * 5, [whole, *(shape for...  3.04 us
    ppermute x6, waiting for transfers between devices, exchange(): lax.ppermute(value, AXES, inner_pairs(groups, mate, chain, rows, idle))  2.01 us
  transfers between devices with their start and end apart: 22, of which 8 were waited for; matrix products, arithmetic and copies ran while one was open for 0% of the time, Pallas kernels for 22%

profile of v11, /device:TPU:11, one launch (start us, length us, event | category | flops | bytes accessed | tf_op | source)
XLA Modules:
  0.0 52.7 jit_solution(13796808938099228935)
XLA Ops:
  0.0 0.1 stack.31.meta
  0.1 3.0 %first_level.1 = (bf16[8,128,256]{2,1,0:T(8,128)(2,1)S(1)}, bf16[4,128,128]{2,1,0:T(8,128)(2,1)S(1)}, bf16[4,128,128]{2,1,0:T(8,128)(2,1)S(1)}, bf16[10,128,128]...) custom-call(s32[5]{0:T(128)S(1)} %stack.31.meta, s32[6,2,8]{2,1,0:T(2,128)} %bitcast.7, f32[6,2,8]{2,1,0:T(2,128)} %bitcast.10, ...), custom_call_target="tpu_custom_call" | custom-call | tf_op jit(solution)/shard_map/first_level/pallas_call | solution.py:440
  3.1 1.3 %collective-permute-start = (bf16[4,128,128]{2,1,0:T(8,128)(2,1)S(1)}, bf16[4,128,128]{2,1,0:T(8,128)(2,1)S(1)}, u32[]{:S(2)}, u32[]{:S(2)}) collective-permute-start(bf16[4,128,128]{2,1,0:T(8,128)(2,1)S(1)} %get-tuple-element.46), channel_id=1, source_target_pairs={{0,1},{16,17},{24,25},{8,10},{1,0},{17,16},{25,24},{9,11},{2,3},{1... | collective-permute-start | bytes 393224 | tf_op jit(solution)/shard_map/ppermute | solution.py:412
  4.4 0.1 collective-permute-start.1
  4.5 3.2 %prepare_0.1 = (bf16[4,256,768]{2,1,0:T(8,128)(2,1)S(1)}, f32[8,128,256]{2,1,0:T(8,128)S(1)}) custom-call(s32[5]{0:T(128)S(1)} %stack.31.meta, s32[6,2,8]{2,1,0:T(2,128)} %bitcast.8, f32[6,2,8]{2,1,0:T(2,128)} %bitcast.11, bf16[2,8,6,128,128]{4,3,2,1,0:T(8,128)(2,1)} %lower_hbm.5, bf16[2,8,128,128]{3,2,1,0:T(8,128)(2,1)} %inverse_hbm.5, ...), custom_call_target="tpu_custom_call" | custom-call | tf_op jit(solution)/shard_map/prepare_0/pallas_call | solution.py:461
  7.7 1.6 %collective-permute-done.even_in.even_a = bf16[4,128,128]{2,1,0:T(8,128)(2,1)S(1)} collective-permute-done((bf16[4,128,128]{2,1,0:T(8,128)(2,1)S(1)}, bf16[4,128,128]{2,1,0:T(8,128)(2,1)S(1)}, u32[]{:S(2)}, u32[]{:S(2)}) %collective-permute-start) | collective-permute-done | bytes 131104 | tf_op jit(solution)/shard_map/ppermute | solution.py:412
  9.3 0.0 collective-permute-done.1.odd_in.odd_a
  9.3 0.5 %step_0.1 = (bf16[8,128,256]{2,1,0:T(8,128)(2,1)S(1)}, bf16[2,128,256]{2,1,0:T(8,128)(2,1)S(1)}, bf16[2,128,256]{2,1,0:T(8,128)(2,1)S(1)}) custom-call(s32[5]{0:T(128)S(1)} %stack.31.meta, bf16[8,128,256]{2,1,0:T(8,128)(2,1)S(1)} %get-tuple-element.45.own.first.refs_4_.refs_5_, bf16[4,128,128]{2,1,0:T(8,128)(2,1)S(1)} %collective-permute-done.even_in.even_a, ...), custom_call_target="tpu_custom_call" | custom-call | tf_op jit(solution)/shard_map/step_0/pallas_call | solution.py:480
  9.8 2.7 %collective-permute-start.2 = (bf16[8,128,256]{2,1,0:T(8,128)(2,1)S(1)}, bf16[8,128,256]{2,1,0:T(8,128)(2,1)S(1)}, u32[]{:S(2)}, u32[]{:S(2)}) collective-permute-start(bf16[8,128,256]{2,1,0:T(8,128)(2,1)S(1)} %get-tuple-element.50.old_b), channel_id=1, source_target_pairs={{0,8},{1,9},{2,10},{3,11},{4,12},{5,13},{6,14},{7,15},{8,0},{9,1},... | collective-permute-start | bytes 1572872 | tf_op jit(solution)/shard_map/ppermute | solution.py:419
  12.5 0.1 collective-permute-start.3
  12.6 0.4 collective-permute-start.4
  13.0 1.2 %collective-permute-start.10 = (bf16[10,128,128]{2,1,0:T(8,128)(2,1)S(1)}, bf16[10,128,128]{2,1,0:T(8,128)(2,1)S(1)}, u32[]{:S(2)}, u32[]{:S(2)}) collective-permute-start(bf16[10,128,128]{2,1,0:T(8,128)(2,1)S(1)} %get-tuple-element.64), channel_id=1, source_target_pairs={{16,17},{24,25},{0,8},{8,0},{17,16},{25,24},{1,9},{9,1},{18,19},{2... | collective-permute-start | bytes 983048 | tf_op jit(solution)/shard_map/ppermute | solution.py:412
  14.3 0.0 collective-permute-start.11
  14.3 0.1 collective-permute-done.4.odd_in
  14.4 0.6 %step_1.1 = (bf16[2,8,128,256]{3,2,1,0:T(8,128)(2,1)}, bf16[8,128,256]{2,1,0:T(8,128)(2,1)S(1)}, bf16[2,128,256]{2,1,0:T(8,128)(2,1)S(1)}, bf16[2,128,256]{2,1,0:T(8,128)(2,1)S(1)}) custom-call(s32[5]{0:T(128)S(1)} %stack.31.meta, bf16[8,128,256]{2,1,0:T(8,128)(2,1)S(1)} %collective-permute-done.2.centre, ...), custom_call_target="tpu_custom_call" | custom-call | tf_op jit(solution)/shard_map/step_1/pallas_call | solution.py:495
  15.0 0.4 collective-permute-start.5
  15.5 0.1 collective-permute-start.6
  15.6 3.2 %prepare_1.1 = (bf16[4,256,768]{2,1,0:T(8,128)(2,1)S(1)}, f32[8,128,256]{2,1,0:T(8,128)S(1)}) custom-call(s32[5]{0:T(128)S(1)} %stack.31.meta, s32[6,2,8]{2,1,0:T(2,128)} %bitcast.9, f32[6,2,8]{2,1,0:T(2,128)} %bitcast.12, bf16[2,8,6,128,128]{4,3,2,1,0:T(8,128)(2,1)} %lower_hbm.5, bf16[2,8,128,128]{3,2,1,0:T(8,128)(2,1)} %inverse_hbm.5, ...), custom_call_target="tpu_custom_call" | custom-call | tf_op jit(solution)/shard_map/prepare_1/pallas_call | solution.py:461
  18.8 0.6 %step_1_0.1 = (bf16[8,128,128]{2,1,0:T(8,128)(2,1)S(1)}, bf16[4,128,128]{2,1,0:T(8,128)(2,1)S(1)}, bf16[4,128,128]{2,1,0:T(8,128)(2,1)S(1)}) custom-call(s32[5]{0:T(128)S(1)} %stack.31.meta, bf16[8,128,256]{2,1,0:T(8,128)(2,1)S(1)} %get-tuple-element.53.own.refs_8_, bf16[2,128,256]{2,1,0:T(8,128)(2,1)S(1)} %collective-permute-done.5.even_in, ...), custom_call_target="tpu_custom_call" | custom-call | tf_op jit(solution)/shard_map/step_1_0/pallas_call | solution.py:508
  19.3 8.0 %collective-permute-start.12 = (bf16[8,128,128]{2,1,0:T(8,128)(2,1)S(1)}, bf16[8,128,128]{2,1,0:T(8,128)(2,1)S(1)}, u32[]{:S(2)}, u32[]{:S(2)}) collective-permute-start(bf16[8,128,128]{2,1,0:T(8,128)(2,1)S(1)} %get-tuple-element.66.refs_9_), channel_id=1, source_target_pairs={{8,16},{9,17},{10,18},{11,19},{12,20},{13,21},{14,22},{15,23},{0,8... | collective-permute-start | bytes 786440 | tf_op jit(solution)/shard_map/ppermute | solution.py:419
  27.4 0.8 %collective-permute-start.13 = (bf16[4,128,128]{2,1,0:T(8,128)(2,1)S(1)}, bf16[4,128,128]{2,1,0:T(8,128)(2,1)S(1)}, u32[]{:S(2)}, u32[]{:S(2)}) collective-permute-start(bf16[4,128,128]{2,1,0:T(8,128)(2,1)S(1)} %get-tuple-element.67), channel_id=1, source_target_pairs={{8,17},{9,16},{10,19},{11,18},{12,21},{13,20},{14,23},{15,22},{0,8... | collective-permute-start | bytes 393224 | tf_op jit(solution)/shard_map/ppermute | solution.py:420
  28.2 0.5 %step_1_1.1 = (bf16[8,128,128]{2,1,0:T(8,128)(2,1)S(1)}, bf16[4,128,128]{2,1,0:T(8,128)(2,1)S(1)}, bf16[4,128,128]{2,1,0:T(8,128)(2,1)S(1)}) custom-call(s32[5]{0:T(128)S(1)} %stack.31.meta, bf16[8,128,256]{2,1,0:T(8,128)(2,1)S(1)} %get-tuple-element.53.own.refs_8_, bf16[2,128,256]{2,1,0:T(8,128)(2,1)S(1)} %collective-permute-done.5.even_in, ...), custom_call_target="tpu_custom_call" | custom-call | tf_op jit(solution)/shard_map/step_1_1/pallas_call | solution.py:508
  28.8 0.1 collective-permute-start.7
  28.9 0.4 collective-permute-done.10.even_b
  29.3 0.2 collective-permute-start.14
  29.6 0.0 collective-permute-done.11.odd_b
  29.6 0.7 %collective-permute-start.8 = (bf16[4,128,128]{2,1,0:T(8,128)(2,1)S(1)}, bf16[4,128,128]{2,1,0:T(8,128)(2,1)S(1)}, u32[]{:S(2)}, u32[]{:S(2)}) collective-permute-start(bf16[4,128,128]{2,1,0:T(8,128)(2,1)S(1)} %get-tuple-element.60), channel_id=1, source_target_pairs={{8,17},{9,16},{10,19},{11,18},{12,21},{13,20},{14,23},{15,22},{0,8... | collective-permute-start | bytes 393224 | tf_op jit(solution)/shard_map/ppermute | solution.py:420
  30.3 1.8 %collective-permute-done.13.refs_1_ = bf16[4,128,128]{2,1,0:T(8,128)(2,1)S(1)} collective-permute-done((bf16[4,128,128]{2,1,0:T(8,128)(2,1)S(1)}, bf16[4,128,128]{2,1,0:T(8,128)(2,1)S(1)}, u32[]{:S(2)}, u32[]{:S(2)}) %collective-permute-start.13) | collective-permute-done | bytes 131104 | tf_op jit(solution)/shard_map/ppermute | solution.py:420
  32.1 2.5 %collective-permute-start.9 = (bf16[4,128,128]{2,1,0:T(8,128)(2,1)S(1)}, bf16[4,128,128]{2,1,0:T(8,128)(2,1)S(1)}, u32[]{:S(2)}, u32[]{:S(2)}) collective-permute-start(bf16[4,128,128]{2,1,0:T(8,128)(2,1)S(1)} %get-tuple-element.61), channel_id=1, source_target_pairs={{8,16},{9,18},{10,17},{11,20},{12,19},{13,22},{14,21},{15,23},{0,8... | collective-permute-start | bytes 393224 | tf_op jit(solution)/shard_map/ppermute | solution.py:420
  34.6 0.6 %order.1.refs_3_.refs_4_ = bf16[2,14,128,128]{3,2,1,0:T(8,128)(2,1)S(1)} custom-call(s32[5]{0:T(128)S(1)} %stack.31.meta, bf16[4,128,128]{2,1,0:T(8,128)(2,1)S(1)} %collective-permute-done.even_in.even_a, bf16[4,128,128]{2,1,0:T(8,128)(2,1)S(1)} %collective-permute-done.1.odd_in.odd_a, bf16[10,128,128]{2,1,0:T(8,128)(2,1)S(1)} %collective-permute-done.10.even_b, ...), custom_call_target="tpu_custom_call" | custom-call | tf_op jit(solution)/shard_map/order/pallas_call | solution.py:491
  35.2 1.1 %collective-permute-done.14.refs_2_ = bf16[4,128,128]{2,1,0:T(8,128)(2,1)S(1)} collective-permute-done((bf16[4,128,128]{2,1,0:T(8,128)(2,1)S(1)}, bf16[4,128,128]{2,1,0:T(8,128)(2,1)S(1)}, u32[]{:S(2)}, u32[]{:S(2)}) %collective-permute-start.14) | collective-permute-done | bytes 131104 | tf_op jit(solution)/shard_map/ppermute | solution.py:420
  36.3 0.0 collective-permute-done.12.refs_0_
  36.3 0.6 %step_2_0.1 = (bf16[2,8,128,256]{3,2,1,0:T(8,128)(2,1)}, bf16[8,128,128]{2,1,0:T(8,128)(2,1)S(1)}, bf16[8,128,128]{2,1,0:T(8,128)(2,1)S(1)}, bf16[4,128,128]{2,1...) custom-call(s32[5]{0:T(128)S(1)} %stack.31.meta, ...), custom_call_target="tpu_custom_call", output_to_operand_aliasing={{0}: (11, {})} | custom-call | tf_op jit(solution)/shard_map/step_2_0/pallas_call | solution.py:527
  36.9 1.6 %collective-permute-start.18 = (bf16[4,128,128]{2,1,0:T(8,128)(2,1)S(1)}, bf16[4,128,128]{2,1,0:T(8,128)(2,1)S(1)}, u32[]{:S(2)}, u32[]{:S(2)}) collective-permute-start(bf16[4,128,128]{2,1,0:T(8,128)(2,1)S(1)} %get-tuple-element.75), channel_id=1, source_target_pairs={{0,8},{1,9},{2,10},{3,11},{4,12},{5,13},{6,14},{7,15},{8,0},{9,1},... | collective-permute-start | bytes 393224 | tf_op jit(solution)/shard_map/ppermute | solution.py:420
  38.5 0.1 collective-permute-start.19
  38.6 0.0 collective-permute-done.8.refs_1_
  38.6 0.5 %collective-permute-done.9.refs_2_ = bf16[4,128,128]{2,1,0:T(8,128)(2,1)S(1)} collective-permute-done((bf16[4,128,128]{2,1,0:T(8,128)(2,1)S(1)}, bf16[4,128,128]{2,1,0:T(8,128)(2,1)S(1)}, u32[]{:S(2)}, u32[]{:S(2)}) %collective-permute-start.9) | collective-permute-done | bytes 131104 | tf_op jit(solution)/shard_map/ppermute | solution.py:420
  39.1 0.6 %step_2_1.1 = (bf16[2,8,128,256]{3,2,1,0:T(8,128)(2,1)}, bf16[8,128,128]{2,1,0:T(8,128)(2,1)S(1)}, bf16[8,128,128]{2,1,0:T(8,128)(2,1)S(1)}, bf16[4,128,128]{2,1,0:T(8,128)(2,1)S(1)}, bf16[4,128,128]{2,1,0:T(8,128)(2,1)S(1)}) custom-call(s32[5]{0:T(128)S(1)} %stack.31.meta, ...), custom_call_target="tpu_custom_call", output_to_operand_aliasing={{0}: (11, {})} | custom-call | tf_op jit(solution)/shard_map/step_2_1/pallas_call | solution.py:527
  39.7 3.8 %collective-permute-start.15 = (bf16[8,128,128]{2,1,0:T(8,128)(2,1)S(1)}, bf16[8,128,128]{2,1,0:T(8,128)(2,1)S(1)}, u32[]{:S(2)}, u32[]{:S(2)}) collective-permute-start(bf16[8,128,128]{2,1,0:T(8,128)(2,1)S(1)} %get-tuple-element.71.refs_9_), channel_id=1, source_target_pairs={{0,8},{1,9},{2,10},{3,11},{4,12},{5,13},{6,14},{7,15},{8,0},{9,1},... | collective-permute-start | bytes 786440 | tf_op jit(solution)/shard_map/ppermute | solution.py:419
  43.5 0.1 collective-permute-start.20
  43.6 0.4 collective-permute-start.21
  44.0 0.0 collective-permute-done.18.refs_0_
  44.0 0.1 collective-permute-start.16
  44.1 0.8 %collective-permute-start.17 = (bf16[4,128,128]{2,1,0:T(8,128)(2,1)S(1)}, bf16[4,128,128]{2,1,0:T(8,128)(2,1)S(1)}, u32[]{:S(2)}, u32[]{:S(2)}) collective-permute-start(bf16[4,128,128]{2,1,0:T(8,128)(2,1)S(1)} %get-tuple-element.73), channel_id=1, source_target_pairs={{0,8},{1,9},{2,10},{3,11},{4,12},{5,13},{6,14},{7,15},{8,0},{9,1},... | collective-permute-start | bytes 393224 | tf_op jit(solution)/shard_map/ppermute | solution.py:420
  44.9 0.2 collective-permute-done.21.refs_3_
  45.0 1.9 %step_3_0.1 = (bf16[2,8,128,256]{3,2,1,0:T(8,128)(2,1)}, bf16[8,128,128]{2,1,0:T(8,128)(2,1)S(1)}, bf16[8,128,128]{2,1,0:T(8,128)(2,1)S(1)}) custom-call(s32[5]{0:T(128)S(1)} %stack.31.meta, bf16[4,128,128]{2,1,0:T(8,128)(2,1)S(1)} %collective-permute-done.18.refs_0_, ...), custom_call_target="tpu_custom_call", output_to_operand_aliasing={{0}: (12, {})} | custom-call | tf_op jit(solution)/shard_map/step_3_0/pallas_call | solution.py:527
  47.0 2.8 %collective-permute-done.16.refs_1_ = bf16[4,128,128]{2,1,0:T(8,128)(2,1)S(1)} collective-permute-done((bf16[4,128,128]{2,1,0:T(8,128)(2,1)S(1)}, bf16[4,128,128]{2,1,0:T(8,128)(2,1)S(1)}, u32[]{:S(2)}, u32[]{:S(2)}) %collective-permute-start.16) | collective-permute-done | bytes 131104 | tf_op jit(solution)/shard_map/ppermute | solution.py:420
  49.8 2.9 %step_3_1.1 = bf16[2,8,128,256]{3,2,1,0:T(8,128)(2,1)} custom-call(s32[5]{0:T(128)S(1)} %stack.31.meta, bf16[8,128,128]{2,1,0:T(8,128)(2,1)S(1)} %collective-permute-done.15.refs_0_, bf16[4,128,128]{2,1,0:T(8,128)(2,1)S(1)} %collective-permute-done.16.refs_1_, ...), custom_call_target="tpu_custom_call", output_to_operand_aliasing={{}: (13, {})} | custom-call | tf_op jit(solution)/shard_map/step_3_1/pallas_call | solution.py:527
  (9 shorter events, 0.0 us)
Async XLA Ops:
  3.1 6.1 %collective-permute-start = (bf16[4,128,128]{2,1,0:T(8,128)(2,1)S(1)}, bf16[4,128,128]{2,1,0:T(8,128)(2,1)S(1)}, u32[]{:S(2)}, u32[]{:S(2)}) collective-permute-start(bf16[4,128,128]{2,1,0:T(8,128)(2,1)S(1)} %get-tuple-element.46), channel_id=1, source_target_pairs={{0,1},{16,17},{24,25},{8,10},{1,0},{17,16},{25,24},{9,11},{2,3},{1... | collective-permute-start | bytes 393224 | tf_op jit(solution)/shard_map/ppermute | solution.py:412
  4.4 4.8 %collective-permute-start.1 = (bf16[4,128,128]{2,1,0:T(8,128)(2,1)S(1)}, bf16[4,128,128]{2,1,0:T(8,128)(2,1)S(1)}, u32[]{:S(2)}, u32[]{:S(2)}) collective-permute-start(bf16[4,128,128]{2,1,0:T(8,128)(2,1)S(1)} %get-tuple-element.47), channel_id=1, source_target_pairs={{0,8},{8,0},{16,24},{24,16},{1,2},{17,18},{25,26},{9,11},{2,1},{18... | collective-permute-start | bytes 393224 | tf_op jit(solution)/shard_map/ppermute | solution.py:412
  9.8 4.6 %collective-permute-start.2 = (bf16[8,128,256]{2,1,0:T(8,128)(2,1)S(1)}, bf16[8,128,256]{2,1,0:T(8,128)(2,1)S(1)}, u32[]{:S(2)}, u32[]{:S(2)}) collective-permute-start(bf16[8,128,256]{2,1,0:T(8,128)(2,1)S(1)} %get-tuple-element.50.old_b), channel_id=1, source_target_pairs={{0,8},{1,9},{2,10},{3,11},{4,12},{5,13},{6,14},{7,15},{8,0},{9,1},... | collective-permute-start | bytes 1572872 | tf_op jit(solution)/shard_map/ppermute | solution.py:419
  12.5 1.8 %collective-permute-start.3 = (bf16[2,128,256]{2,1,0:T(8,128)(2,1)S(1)}, bf16[2,128,256]{2,1,0:T(8,128)(2,1)S(1)}, u32[]{:S(2)}, u32[]{:S(2)}) collective-permute-start(bf16[2,128,256]{2,1,0:T(8,128)(2,1)S(1)} %get-tuple-element.51), channel_id=1, source_target_pairs={{0,9},{1,8},{2,11},{3,10},{4,13},{5,12},{6,15},{7,14},{8,0},{9,1},... | collective-permute-start | bytes 393224 | tf_op jit(solution)/shard_map/ppermute | solution.py:420
  12.6 1.8 %collective-permute-start.4 = (bf16[2,128,256]{2,1,0:T(8,128)(2,1)S(1)}, bf16[2,128,256]{2,1,0:T(8,128)(2,1)S(1)}, u32[]{:S(2)}, u32[]{:S(2)}) collective-permute-start(bf16[2,128,256]{2,1,0:T(8,128)(2,1)S(1)} %get-tuple-element.52), channel_id=1, source_target_pairs={{0,8},{1,10},{2,9},{3,12},{4,11},{5,14},{6,13},{7,15},{8,0},{9,1},... | collective-permute-start | bytes 393224 | tf_op jit(solution)/shard_map/ppermute | solution.py:420
  13.0 16.3 %collective-permute-start.10 = (bf16[10,128,128]{2,1,0:T(8,128)(2,1)S(1)}, bf16[10,128,128]{2,1,0:T(8,128)(2,1)S(1)}, u32[]{:S(2)}, u32[]{:S(2)}) collective-permute-start(bf16[10,128,128]{2,1,0:T(8,128)(2,1)S(1)} %get-tuple-element.64), channel_id=1, source_target_pairs={{16,17},{24,25},{0,8},{8,0},{17,16},{25,24},{1,9},{9,1},{18,19},{2... | collective-permute-start | bytes 983048 | tf_op jit(solution)/shard_map/ppermute | solution.py:412
  14.3 15.3 %collective-permute-start.11 = (bf16[10,128,128]{2,1,0:T(8,128)(2,1)S(1)}, bf16[10,128,128]{2,1,0:T(8,128)(2,1)S(1)}, u32[]{:S(2)}, u32[]{:S(2)}) collective-permute-start(bf16[10,128,128]{2,1,0:T(8,128)(2,1)S(1)} %get-tuple-element.65), channel_id=1, source_target_pairs={{0,8},{8,0},{16,24},{24,16},{17,18},{25,26},{1,9},{9,1},{18,17},{2... | collective-permute-start | bytes 983048 | tf_op jit(solution)/shard_map/ppermute | solution.py:412
  15.0 3.7 %collective-permute-start.5 = (bf16[2,128,256]{2,1,0:T(8,128)(2,1)S(1)}, bf16[2,128,256]{2,1,0:T(8,128)(2,1)S(1)}, u32[]{:S(2)}, u32[]{:S(2)}) collective-permute-start(bf16[2,128,256]{2,1,0:T(8,128)(2,1)S(1)} %get-tuple-element.54), channel_id=1, source_target_pairs={{8,9},{0,2},{16,24},{24,16},{9,8},{1,3},{17,25},{25,17},{10,11},{2... | collective-permute-start | bytes 393224 | tf_op jit(solution)/shard_map/ppermute | solution.py:412
  15.5 3.3 %collective-permute-start.6 = (bf16[2,128,256]{2,1,0:T(8,128)(2,1)S(1)}, bf16[2,128,256]{2,1,0:T(8,128)(2,1)S(1)}, u32[]{:S(2)}, u32[]{:S(2)}) collective-permute-start(bf16[2,128,256]{2,1,0:T(8,128)(2,1)S(1)} %get-tuple-element.55), channel_id=1, source_target_pairs={{0,8},{8,0},{16,24},{24,16},{9,10},{1,3},{17,25},{25,17},{10,9},{2... | collective-permute-start | bytes 393224 | tf_op jit(solution)/shard_map/ppermute | solution.py:412
  19.3 17.0 %collective-permute-start.12 = (bf16[8,128,128]{2,1,0:T(8,128)(2,1)S(1)}, bf16[8,128,128]{2,1,0:T(8,128)(2,1)S(1)}, u32[]{:S(2)}, u32[]{:S(2)}) collective-permute-start(bf16[8,128,128]{2,1,0:T(8,128)(2,1)S(1)} %get-tuple-element.66.refs_9_), channel_id=1, source_target_pairs={{8,16},{9,17},{10,18},{11,19},{12,20},{13,21},{14,22},{15,23},{0,8... | collective-permute-start | bytes 786440 | tf_op jit(solution)/shard_map/ppermute | solution.py:419
  27.4 4.7 %collective-permute-start.13 = (bf16[4,128,128]{2,1,0:T(8,128)(2,1)S(1)}, bf16[4,128,128]{2,1,0:T(8,128)(2,1)S(1)}, u32[]{:S(2)}, u32[]{:S(2)}) collective-permute-start(bf16[4,128,128]{2,1,0:T(8,128)(2,1)S(1)} %get-tuple-element.67), channel_id=1, source_target_pairs={{8,17},{9,16},{10,19},{11,18},{12,21},{13,20},{14,23},{15,22},{0,8... | collective-permute-start | bytes 393224 | tf_op jit(solution)/shard_map/ppermute | solution.py:420
  28.8 10.4 %collective-permute-start.7 = (bf16[8,128,128]{2,1,0:T(8,128)(2,1)S(1)}, bf16[8,128,128]{2,1,0:T(8,128)(2,1)S(1)}, u32[]{:S(2)}, u32[]{:S(2)}) collective-permute-start(bf16[8,128,128]{2,1,0:T(8,128)(2,1)S(1)} %get-tuple-element.59.refs_9_), channel_id=1, source_target_pairs={{8,16},{9,17},{10,18},{11,19},{12,20},{13,21},{14,22},{15,23},{0,8... | collective-permute-start | bytes 786440 | tf_op jit(solution)/shard_map/ppermute | solution.py:419
  29.3 7.0 %collective-permute-start.14 = (bf16[4,128,128]{2,1,0:T(8,128)(2,1)S(1)}, bf16[4,128,128]{2,1,0:T(8,128)(2,1)S(1)}, u32[]{:S(2)}, u32[]{:S(2)}) collective-permute-start(bf16[4,128,128]{2,1,0:T(8,128)(2,1)S(1)} %get-tuple-element.68), channel_id=1, source_target_pairs={{8,16},{9,18},{10,17},{11,20},{12,19},{13,22},{14,21},{15,23},{0,8... | collective-permute-start | bytes 393224 | tf_op jit(solution)/shard_map/ppermute | solution.py:420
  29.6 9.0 %collective-permute-start.8 = (bf16[4,128,128]{2,1,0:T(8,128)(2,1)S(1)}, bf16[4,128,128]{2,1,0:T(8,128)(2,1)S(1)}, u32[]{:S(2)}, u32[]{:S(2)}) collective-permute-start(bf16[4,128,128]{2,1,0:T(8,128)(2,1)S(1)} %get-tuple-element.60), channel_id=1, source_target_pairs={{8,17},{9,16},{10,19},{11,18},{12,21},{13,20},{14,23},{15,22},{0,8... | collective-permute-start | bytes 393224 | tf_op jit(solution)/shard_map/ppermute | solution.py:420
  32.1 7.0 %collective-permute-start.9 = (bf16[4,128,128]{2,1,0:T(8,128)(2,1)S(1)}, bf16[4,128,128]{2,1,0:T(8,128)(2,1)S(1)}, u32[]{:S(2)}, u32[]{:S(2)}) collective-permute-start(bf16[4,128,128]{2,1,0:T(8,128)(2,1)S(1)} %get-tuple-element.61), channel_id=1, source_target_pairs={{8,16},{9,18},{10,17},{11,20},{12,19},{13,22},{14,21},{15,23},{0,8... | collective-permute-start | bytes 393224 | tf_op jit(solution)/shard_map/ppermute | solution.py:420
  36.9 7.1 %collective-permute-start.18 = (bf16[4,128,128]{2,1,0:T(8,128)(2,1)S(1)}, bf16[4,128,128]{2,1,0:T(8,128)(2,1)S(1)}, u32[]{:S(2)}, u32[]{:S(2)}) collective-permute-start(bf16[4,128,128]{2,1,0:T(8,128)(2,1)S(1)} %get-tuple-element.75), channel_id=1, source_target_pairs={{0,8},{1,9},{2,10},{3,11},{4,12},{5,13},{6,14},{7,15},{8,0},{9,1},... | collective-permute-start | bytes 393224 | tf_op jit(solution)/shard_map/ppermute | solution.py:420
  38.5 5.6 %collective-permute-start.19 = (bf16[4,128,128]{2,1,0:T(8,128)(2,1)S(1)}, bf16[4,128,128]{2,1,0:T(8,128)(2,1)S(1)}, u32[]{:S(2)}, u32[]{:S(2)}) collective-permute-start(bf16[4,128,128]{2,1,0:T(8,128)(2,1)S(1)} %get-tuple-element.76), channel_id=1, source_target_pairs={{0,8},{1,9},{2,10},{3,11},{4,12},{5,13},{6,14},{7,15},{8,0},{9,1},... | collective-permute-start | bytes 393224 | tf_op jit(solution)/shard_map/ppermute | solution.py:420
  39.7 10.1 %collective-permute-start.15 = (bf16[8,128,128]{2,1,0:T(8,128)(2,1)S(1)}, bf16[8,128,128]{2,1,0:T(8,128)(2,1)S(1)}, u32[]{:S(2)}, u32[]{:S(2)}) collective-permute-start(bf16[8,128,128]{2,1,0:T(8,128)(2,1)S(1)} %get-tuple-element.71.refs_9_), channel_id=1, source_target_pairs={{0,8},{1,9},{2,10},{3,11},{4,12},{5,13},{6,14},{7,15},{8,0},{9,1},... | collective-permute-start | bytes 786440 | tf_op jit(solution)/shard_map/ppermute | solution.py:419
  43.5 1.4 %collective-permute-start.20 = (bf16[4,128,128]{2,1,0:T(8,128)(2,1)S(1)}, bf16[4,128,128]{2,1,0:T(8,128)(2,1)S(1)}, u32[]{:S(2)}, u32[]{:S(2)}) collective-permute-start(bf16[4,128,128]{2,1,0:T(8,128)(2,1)S(1)} %get-tuple-element.77), channel_id=1, source_target_pairs={{0,8},{1,9},{2,10},{3,11},{4,12},{5,13},{6,14},{7,15},{8,0},{9,1},... | collective-permute-start | bytes 393224 | tf_op jit(solution)/shard_map/ppermute | solution.py:419
  43.6 1.5 %collective-permute-start.21 = (bf16[4,128,128]{2,1,0:T(8,128)(2,1)S(1)}, bf16[4,128,128]{2,1,0:T(8,128)(2,1)S(1)}, u32[]{:S(2)}, u32[]{:S(2)}) collective-permute-start(bf16[4,128,128]{2,1,0:T(8,128)(2,1)S(1)} %get-tuple-element.78), channel_id=1, source_target_pairs={{0,8},{1,9},{2,10},{3,11},{4,12},{5,13},{6,14},{7,15},{8,0},{9,1},... | collective-permute-start | bytes 393224 | tf_op jit(solution)/shard_map/ppermute | solution.py:419
  44.0 5.8 %collective-permute-start.16 = (bf16[4,128,128]{2,1,0:T(8,128)(2,1)S(1)}, bf16[4,128,128]{2,1,0:T(8,128)(2,1)S(1)}, u32[]{:S(2)}, u32[]{:S(2)}) collective-permute-start(bf16[4,128,128]{2,1,0:T(8,128)(2,1)S(1)} %get-tuple-element.72), channel_id=1, source_target_pairs={{0,8},{1,9},{2,10},{3,11},{4,12},{5,13},{6,14},{7,15},{8,0},{9,1},... | collective-permute-start | bytes 393224 | tf_op jit(solution)/shard_map/ppermute | solution.py:420
  44.1 5.7 %collective-permute-start.17 = (bf16[4,128,128]{2,1,0:T(8,128)(2,1)S(1)}, bf16[4,128,128]{2,1,0:T(8,128)(2,1)S(1)}, u32[]{:S(2)}, u32[]{:S(2)}) collective-permute-start(bf16[4,128,128]{2,1,0:T(8,128)(2,1)S(1)} %get-tuple-element.73), channel_id=1, source_target_pairs={{0,8},{1,9},{2,10},{3,11},{4,12},{5,13},{6,14},{7,15},{8,0},{9,1},... | collective-permute-start | bytes 393224 | tf_op jit(solution)/shard_map/ppermute | solution.py:420

commit v12 on v11

--- a/solution.py
+++ b/solution.py
@@ -310,13 +310,16 @@
 
 def later_step(group, chunk, final, meta, *refs):
     stages = final and chunk == CHUNKS - 1
-    if final and chunk == 0:
+    if final:
         even_in, odd_in, low, high, *rest = refs
         centre = [low, high]
     else:
         one, even_in, odd_in, *rest = refs
         centre = [one]
     edges, first, wide_a, wide_b, base_b, old_a, old_b, *rest = rest
+    joins = not final and len(rest) > 9
+    if joins:
+        made_b, *rest = rest
     if stages:
         made_a, made_b, _, out, window, level_a, solved, stage, sems = rest
     else:
@@ -331,7 +334,8 @@
         odd = meta[1]
         halo = 2 * REACH
         for i, part in enumerate(centre):
-            window[halo + i * part.shape[0] : halo + (i + 1) * part.shape[0]] = part[...]
+            cut = at if part.shape[-1] > cases else slice(None)
+            window[halo + i * part.shape[0] : halo + (i + 1) * part.shape[0]] = part[:, :, cut]
         place(window, odd, even_in, odd_in)
         clear_beyond(meta, window, halo)
         first_of_group(wide_a, first, window.at[pl.ds(REACH, count + halo)], level_a, REACH, at)
@@ -368,7 +372,9 @@
         else:
             emit_sends(odd, solved, sends[:2])
             for i, part in enumerate(sends[2:]):
-                part[...] = solved[i * part.shape[0] : (i + 1) * part.shape[0]]
+                rows = slice(i * part.shape[0], (i + 1) * part.shape[0])
+                part[:, :, : chunk * cases] = made_b[rows]
+                part[:, :, at] = solved[rows]
             solved_a[...] = level_a[REACH : REACH + count]
 
     @pl.when(meta[0] == group - 1)
@@ -413,12 +419,11 @@
             for value, mate in zip(values, mates)
         ]
 
-    def travel(group, centre, sides):
-        *sides, = sides
-        centres = sides[2:] or [centre]
-        kinds = [lax.ppermute(value, AXES, hop_pairs(group, same_row, chain, rows)) for value in centres]
-        kinds += [lax.ppermute(value, AXES, hop_pairs(group, mate, chain, rows)) for value, mate in zip(sides, mates)]
-        return [kinds[i] for i in (2, 3, 0, 1)] if len(kinds) > 3 else kinds
+    def travel_centre(group, value):
+        return lax.ppermute(value, AXES, hop_pairs(group, same_row, chain, rows))
+
+    def travel_sides(group, values):
+        return [lax.ppermute(value, AXES, hop_pairs(group, mate, chain, rows)) for value, mate in zip(values, mates)]
 
     def call(kernel, name, in_specs, out_shape, out_specs=None, **more):
         return pl.pallas_call(
@@ -485,7 +490,7 @@
         scratch_shapes=[padded],
     )(meta, first, *sides, wide_a, base_0)
     wide_b, base_b = prepare(1, after(meta, solved))
-    arrived = travel(0, solved, sends)
+    arrived = [travel_centre(0, solved), *travel_sides(0, sends)]
 
     later_w = exchange(range(2, chain), after(edge_w[2:], sides))
     edges, = call(
@@ -516,13 +521,18 @@
 
     for group in range(2, chain):
         final = group == chain - 1
-        arrived = [travel(group - 1, solved, sends) for solved, *sends in sent]
+        if final:
+            centres = [travel_centre(group - 1, value) for value in sent[-1][3:]]
+            arrived = [[*travel_sides(group - 1, sends[:2]), *centres] for _, *sends in sent]
+        else:
+            arrived = [[travel_centre(group - 1, solved), *travel_sides(group - 1, sends)] for solved, *sends in sent]
         made = []
         for chunk in range(CHUNKS):
             stages = final and chunk == CHUNKS - 1
-            splits = group == chain - 2 and chunk == 0
-            outs = [] if stages else [half, half] + ([] if final else [half_edge] * (4 if splits else 2))
-            extra = [made[0][1], made[0][0][0]] if stages else []
+            joins = group == chain - 2 and chunk == CHUNKS - 1
+            outs = [] if stages else [half, half] + ([] if final else [half_edge] * 2)
+            outs += [shaped((count // 2, block, cases))] * (2 * joins)
+            extra = [level for _, level in made] * stages + [values[0] for values, _ in made] * (stages or joins)
             sems = (2, pairs) if stages else (2,)
             out, *now = call(
                 functools.partial(later_step, group, chunk, final),

time: 53.6 us -> 56.4 us (1.052)
  waiting for transfers between devices: 8.71 us -> 13.3 us
  starting transfers between devices: 25.6 us -> 23.6 us
    ppermute x16 -> x15, waiting for transfers between devices: 6.7 us -> 11.3 us  [the longest x10 11.3 us: travel_sides(): lax.ppermute(value, AXES, hop_pairs(group, mate, chain, rows))]
    ppermute x16 -> x15, starting transfers between devices: 22.4 us -> 20.4 us  [the longest x5 13.9 us: travel_centre(): return lax.ppermute(value, AXES, hop_pairs(group, same_row, chain, rows))]
  transfers between devices with their start and end apart: 22 -> 21, of which waited for: 8 -> 10; matrix products, arithmetic and copies ran while one was open for 0% -> 0% of each run, Pallas kernels for 22% -> 20%
where the time goes in v12:
time: 56.4 us; the launch traced here: 55.3 us
  starting transfers between devices  23.6 us (42%)
  Pallas kernels  18.2 us (32%)
  waiting for transfers between devices  13.3 us (24%)
    ppermute x5, starting transfers between devices, travel_centre(): return lax.ppermute(value, AXES, hop_pairs(group, same_row, chain, rows))  13.9 us
    ppermute x10, waiting for transfers between devices, travel_sides(): lax.ppermute(value, AXES, hop_pairs(group, mate, chain, rows))  11.3 us
    ppermute x10, starting transfers between devices, travel_sides(): lax.ppermute(value, AXES, hop_pairs(group, mate, chain, rows))  6.53 us
    pallas_call x2, Pallas kernels, prepare(): call(functools.partial(prepare_kernel, turn), f'prepare_{turn}', [SMEM] +...  6.31 us
    pallas_call x4, Pallas kernels, per_device(): call(functools.partial(later_step, group, chunk, final), f'step_{group}_{...  5.97 us
    ppermute x6, starting transfers between devices, exchange(): lax.ppermute(value, AXES, inner_pairs(groups, mate, chain, rows, idle))  3.19 us
    pallas_call x1, Pallas kernels, per_device(): call(first_kernel, 'first_level', [SMEM] + [HBM] * 5, [whole, *(shape for...  3.04 us
    ppermute x6, waiting for transfers between devices, exchange(): lax.ppermute(value, AXES, inner_pairs(groups, mate, chain, rows, idle))  2.01 us
  transfers between devices with their start and end apart: 21, of which 10 were waited for; matrix products, arithmetic and copies ran while one was open for 0% of the time, Pallas kernels for 20%

profile of v12, /device:TPU:11, one launch (start us, length us, event | category | flops | bytes accessed | tf_op | source)
XLA Modules:
  0.0 55.3 jit_solution(11660457826299203684)
XLA Ops:
  0.0 0.1 stack.31.meta
  0.1 3.0 %first_level.1 = (bf16[8,128,256]{2,1,0:T(8,128)(2,1)S(1)}, bf16[4,128,128]{2,1,0:T(8,128)(2,1)S(1)}, bf16[4,128,128]{2,1,0:T(8,128)(2,1)S(1)}, bf16[10,128,128]...) custom-call(s32[5]{0:T(128)S(1)} %stack.31.meta, s32[6,2,8]{2,1,0:T(2,128)} %bitcast.7, f32[6,2,8]{2,1,0:T(2,128)} %bitcast.10, ...), custom_call_target="tpu_custom_call" | custom-call | tf_op jit(solution)/shard_map/first_level/pallas_call | solution.py:445
  3.1 1.3 %collective-permute-start = (bf16[4,128,128]{2,1,0:T(8,128)(2,1)S(1)}, bf16[4,128,128]{2,1,0:T(8,128)(2,1)S(1)}, u32[]{:S(2)}, u32[]{:S(2)}) collective-permute-start(bf16[4,128,128]{2,1,0:T(8,128)(2,1)S(1)} %get-tuple-element.46), channel_id=1, source_target_pairs={{0,1},{16,17},{24,25},{8,10},{1,0},{17,16},{25,24},{9,11},{2,3},{1... | collective-permute-start | bytes 393224 | tf_op jit(solution)/shard_map/ppermute | solution.py:418
  4.4 0.1 collective-permute-start.1
  4.5 3.2 %prepare_0.1 = (bf16[4,256,768]{2,1,0:T(8,128)(2,1)S(1)}, f32[8,128,256]{2,1,0:T(8,128)S(1)}) custom-call(s32[5]{0:T(128)S(1)} %stack.31.meta, s32[6,2,8]{2,1,0:T(2,128)} %bitcast.8, f32[6,2,8]{2,1,0:T(2,128)} %bitcast.11, bf16[2,8,6,128,128]{4,3,2,1,0:T(8,128)(2,1)} %lower_hbm.5, bf16[2,8,128,128]{3,2,1,0:T(8,128)(2,1)} %inverse_hbm.5, ...), custom_call_target="tpu_custom_call" | custom-call | tf_op jit(solution)/shard_map/prepare_0/pallas_call | solution.py:466
  7.7 1.6 %collective-permute-done.even_in.even_a = bf16[4,128,128]{2,1,0:T(8,128)(2,1)S(1)} collective-permute-done((bf16[4,128,128]{2,1,0:T(8,128)(2,1)S(1)}, bf16[4,128,128]{2,1,0:T(8,128)(2,1)S(1)}, u32[]{:S(2)}, u32[]{:S(2)}) %collective-permute-start) | collective-permute-done | bytes 131104 | tf_op jit(solution)/shard_map/ppermute | solution.py:418
  9.3 0.5 step_0.1
  9.8 2.7 %collective-permute-start.2 = (bf16[8,128,256]{2,1,0:T(8,128)(2,1)S(1)}, bf16[8,128,256]{2,1,0:T(8,128)(2,1)S(1)}, u32[]{:S(2)}, u32[]{:S(2)}) collective-permute-start(bf16[8,128,256]{2,1,0:T(8,128)(2,1)S(1)} %get-tuple-element.50.old_b), channel_id=1, source_target_pairs={{0,8},{1,9},{2,10},{3,11},{4,12},{5,13},{6,14},{7,15},{8,0},{9,1},... | collective-permute-start | bytes 1572872 | tf_op jit(solution)/shard_map/ppermute | solution.py:423
  12.5 0.1 collective-permute-start.3
  12.6 0.4 collective-permute-start.4
  13.0 1.2 %collective-permute-start.10 = (bf16[10,128,128]{2,1,0:T(8,128)(2,1)S(1)}, bf16[10,128,128]{2,1,0:T(8,128)(2,1)S(1)}, u32[]{:S(2)}, u32[]{:S(2)}) collective-permute-start(bf16[10,128,128]{2,1,0:T(8,128)(2,1)S(1)} %get-tuple-element.64), channel_id=1, source_target_pairs={{16,17},{24,25},{0,8},{8,0},{17,16},{25,24},{1,9},{9,1},{18,19},{2... | collective-permute-start | bytes 983048 | tf_op jit(solution)/shard_map/ppermute | solution.py:418
  14.3 0.0 collective-permute-start.11
  14.3 0.0 collective-permute-done.3.even_in
  14.3 0.2 collective-permute-done.4.odd_in
  14.4 0.0 collective-permute-done.2.centre
  14.4 0.6 %step_1.1 = (bf16[2,8,128,256]{3,2,1,0:T(8,128)(2,1)}, bf16[8,128,256]{2,1,0:T(8,128)(2,1)S(1)}, bf16[2,128,256]{2,1,0:T(8,128)(2,1)S(1)}, bf16[2,128,256]{2,1,0:T(8,128)(2,1)S(1)}) custom-call(s32[5]{0:T(128)S(1)} %stack.31.meta, bf16[8,128,256]{2,1,0:T(8,128)(2,1)S(1)} %collective-permute-done.2.centre, ...), custom_call_target="tpu_custom_call" | custom-call | tf_op jit(solution)/shard_map/step_1/pallas_call | solution.py:500
  15.0 0.4 collective-permute-start.5
  15.5 0.1 collective-permute-start.6
  15.6 3.2 %prepare_1.1 = (bf16[4,256,768]{2,1,0:T(8,128)(2,1)S(1)}, f32[8,128,256]{2,1,0:T(8,128)S(1)}) custom-call(s32[5]{0:T(128)S(1)} %stack.31.meta, s32[6,2,8]{2,1,0:T(2,128)} %bitcast.9, f32[6,2,8]{2,1,0:T(2,128)} %bitcast.12, bf16[2,8,6,128,128]{4,3,2,1,0:T(8,128)(2,1)} %lower_hbm.5, bf16[2,8,128,128]{3,2,1,0:T(8,128)(2,1)} %inverse_hbm.5, ...), custom_call_target="tpu_custom_call" | custom-call | tf_op jit(solution)/shard_map/prepare_1/pallas_call | solution.py:466
  18.8 0.0 collective-permute-done.6.odd_in
  18.8 0.6 step_1_0.1
  19.3 8.0 %collective-permute-start.12 = (bf16[8,128,128]{2,1,0:T(8,128)(2,1)S(1)}, bf16[8,128,128]{2,1,0:T(8,128)(2,1)S(1)}, u32[]{:S(2)}, u32[]{:S(2)}) collective-permute-start(bf16[8,128,128]{2,1,0:T(8,128)(2,1)S(1)} %get-tuple-element.66.refs_9_), channel_id=1, source_target_pairs={{8,16},{9,17},{10,18},{11,19},{12,20},{13,21},{14,22},{15,23},{0,8... | collective-permute-start | bytes 786440 | tf_op jit(solution)/shard_map/ppermute | solution.py:423
  27.4 0.8 %collective-permute-start.13 = (bf16[4,128,128]{2,1,0:T(8,128)(2,1)S(1)}, bf16[4,128,128]{2,1,0:T(8,128)(2,1)S(1)}, u32[]{:S(2)}, u32[]{:S(2)}) collective-permute-start(bf16[4,128,128]{2,1,0:T(8,128)(2,1)S(1)} %get-tuple-element.67), channel_id=1, source_target_pairs={{8,17},{9,16},{10,19},{11,18},{12,21},{13,20},{14,23},{15,22},{0,8... | collective-permute-start | bytes 393224 | tf_op jit(solution)/shard_map/ppermute | solution.py:426
  28.2 0.5 step_1_1.1
  28.8 0.1 collective-permute-start.7
  28.9 0.4 collective-permute-done.10.even_b
  29.3 0.2 collective-permute-start.14
  29.6 0.0 collective-permute-done.11.odd_b
  29.6 0.7 %collective-permute-start.8 = (bf16[4,128,128]{2,1,0:T(8,128)(2,1)S(1)}, bf16[4,128,128]{2,1,0:T(8,128)(2,1)S(1)}, u32[]{:S(2)}, u32[]{:S(2)}) collective-permute-start(bf16[4,128,128]{2,1,0:T(8,128)(2,1)S(1)} %get-tuple-element.60), channel_id=1, source_target_pairs={{8,17},{9,16},{10,19},{11,18},{12,21},{13,20},{14,23},{15,22},{0,8... | collective-permute-start | bytes 393224 | tf_op jit(solution)/shard_map/ppermute | solution.py:426
  30.3 1.8 %collective-permute-done.13.refs_1_ = bf16[4,128,128]{2,1,0:T(8,128)(2,1)S(1)} collective-permute-done((bf16[4,128,128]{2,1,0:T(8,128)(2,1)S(1)}, bf16[4,128,128]{2,1,0:T(8,128)(2,1)S(1)}, u32[]{:S(2)}, u32[]{:S(2)}) %collective-permute-start.13) | collective-permute-done | bytes 131104 | tf_op jit(solution)/shard_map/ppermute | solution.py:426
  32.1 2.5 %collective-permute-start.9 = (bf16[4,128,128]{2,1,0:T(8,128)(2,1)S(1)}, bf16[4,128,128]{2,1,0:T(8,128)(2,1)S(1)}, u32[]{:S(2)}, u32[]{:S(2)}) collective-permute-start(bf16[4,128,128]{2,1,0:T(8,128)(2,1)S(1)} %get-tuple-element.61), channel_id=1, source_target_pairs={{8,16},{9,18},{10,17},{11,20},{12,19},{13,22},{14,21},{15,23},{0,8... | collective-permute-start | bytes 393224 | tf_op jit(solution)/shard_map/ppermute | solution.py:426
  34.6 0.6 %order.1.refs_3_.refs_4_ = bf16[2,14,128,128]{3,2,1,0:T(8,128)(2,1)S(1)} custom-call(s32[5]{0:T(128)S(1)} %stack.31.meta, bf16[4,128,128]{2,1,0:T(8,128)(2,1)S(1)} %collective-permute-done.even_in.even_a, bf16[4,128,128]{2,1,0:T(8,128)(2,1)S(1)} %collective-permute-done.1.odd_in.odd_a, bf16[10,128,128]{2,1,0:T(8,128)(2,1)S(1)} %collective-permute-done.10.even_b, ...), custom_call_target="tpu_custom_call" | custom-call | tf_op jit(solution)/shard_map/order/pallas_call | solution.py:496
  35.2 1.1 %collective-permute-done.14.refs_2_ = bf16[4,128,128]{2,1,0:T(8,128)(2,1)S(1)} collective-permute-done((bf16[4,128,128]{2,1,0:T(8,128)(2,1)S(1)}, bf16[4,128,128]{2,1,0:T(8,128)(2,1)S(1)}, u32[]{:S(2)}, u32[]{:S(2)}) %collective-permute-start.14) | collective-permute-done | bytes 131104 | tf_op jit(solution)/shard_map/ppermute | solution.py:426
  36.3 0.0 collective-permute-done.12.refs_0_
  36.3 0.6 %step_2_0.1 = (bf16[2,8,128,256]{3,2,1,0:T(8,128)(2,1)}, bf16[8,128,128]{2,1,0:T(8,128)(2,1)S(1)}, bf16[8,128,128]{2,1,0:T(8,128)(2,1)S(1)}, bf16[4,128,128]{2,1,0:T(8,128)(2,1)S(1)}, bf16[4,128,128]{2,1,0:T(8,128)(2,1)S(1)}) custom-call(s32[5]{0:T(128)S(1)} %stack.31.meta, ...), custom_call_target="tpu_custom_call", output_to_operand_aliasing={{0}: (11, {})} | custom-call | tf_op jit(solution)/shard_map/step_2_0/pallas_call | solution.py:537
  36.9 0.8 %collective-permute-done.8.refs_1_ = bf16[4,128,128]{2,1,0:T(8,128)(2,1)S(1)} collective-permute-done((bf16[4,128,128]{2,1,0:T(8,128)(2,1)S(1)}, bf16[4,128,128]{2,1,0:T(8,128)(2,1)S(1)}, u32[]{:S(2)}, u32[]{:S(2)}) %collective-permute-start.8) | collective-permute-done | bytes 131104 | tf_op jit(solution)/shard_map/ppermute | solution.py:426
  37.7 1.4 %collective-permute-done.9.refs_2_ = bf16[4,128,128]{2,1,0:T(8,128)(2,1)S(1)} collective-permute-done((bf16[4,128,128]{2,1,0:T(8,128)(2,1)S(1)}, bf16[4,128,128]{2,1,0:T(8,128)(2,1)S(1)}, u32[]{:S(2)}, u32[]{:S(2)}) %collective-permute-start.9) | collective-permute-done | bytes 131104 | tf_op jit(solution)/shard_map/ppermute | solution.py:426
  39.1 0.6 %step_2_1.1 = (bf16[2,8,128,256]{3,2,1,0:T(8,128)(2,1)}, bf16[8,128,128]{2,1,0:T(8,128)(2,1)S(1)}, bf16[8,128,128]{2,1,0:T(8,128)(2,1)S(1)}, bf16[4,128,128]{2,1...) custom-call(s32[5]{0:T(128)S(1)} %stack.31.meta, ...), custom_call_target="tpu_custom_call", output_to_operand_aliasing={{0}: (12, {})} | custom-call | tf_op jit(solution)/shard_map/step_2_1/pallas_call | solution.py:537
  39.7 2.9 %collective-permute-start.17 = (bf16[4,128,256]{2,1,0:T(8,128)(2,1)S(1)}, bf16[4,128,256]{2,1,0:T(8,128)(2,1)S(1)}, u32[]{:S(2)}, u32[]{:S(2)}) collective-permute-start(bf16[4,128,256]{2,1,0:T(8,128)(2,1)S(1)} %get-tuple-element.74), channel_id=1, source_target_pairs={{0,8},{1,9},{2,10},{3,11},{4,12},{5,13},{6,14},{7,15},{8,0},{9,1},... | collective-permute-start | bytes 786440 | tf_op jit(solution)/shard_map/ppermute | solution.py:423
  42.6 0.1 collective-permute-start.18
  42.7 0.4 collective-permute-start.19
  43.2 1.4 %collective-permute-start.20 = (bf16[4,128,128]{2,1,0:T(8,128)(2,1)S(1)}, bf16[4,128,128]{2,1,0:T(8,128)(2,1)S(1)}, u32[]{:S(2)}, u32[]{:S(2)}) collective-permute-start(bf16[4,128,128]{2,1,0:T(8,128)(2,1)S(1)} %get-tuple-element.79), channel_id=1, source_target_pairs={{0,8},{1,9},{2,10},{3,11},{4,12},{5,13},{6,14},{7,15},{8,0},{9,1},... | collective-permute-start | bytes 393224 | tf_op jit(solution)/shard_map/ppermute | solution.py:426
  44.5 0.0 collective-permute-start.15
  44.5 2.6 %collective-permute-done.19.refs_0_ = bf16[4,128,128]{2,1,0:T(8,128)(2,1)S(1)} collective-permute-done((bf16[4,128,128]{2,1,0:T(8,128)(2,1)S(1)}, bf16[4,128,128]{2,1,0:T(8,128)(2,1)S(1)}, u32[]{:S(2)}, u32[]{:S(2)}) %collective-permute-start.19) | collective-permute-done | bytes 131104 | tf_op jit(solution)/shard_map/ppermute | solution.py:426
  47.1 1.4 %collective-permute-done.20.refs_1_ = bf16[4,128,128]{2,1,0:T(8,128)(2,1)S(1)} collective-permute-done((bf16[4,128,128]{2,1,0:T(8,128)(2,1)S(1)}, bf16[4,128,128]{2,1,0:T(8,128)(2,1)S(1)}, u32[]{:S(2)}, u32[]{:S(2)}) %collective-permute-start.20) | collective-permute-done | bytes 131104 | tf_op jit(solution)/shard_map/ppermute | solution.py:426
  48.6 2.0 %step_3_0.1 = (bf16[2,8,128,256]{3,2,1,0:T(8,128)(2,1)}, bf16[8,128,128]{2,1,0:T(8,128)(2,1)S(1)}, bf16[8,128,128]{2,1,0:T(8,128)(2,1)S(1)}) custom-call(s32[5]{0:T(128)S(1)} %stack.31.meta, bf16[4,128,128]{2,1,0:T(8,128)(2,1)S(1)} %collective-permute-done.19.refs_0_, ...), custom_call_target="tpu_custom_call", output_to_operand_aliasing={{0}: (12, {})} | custom-call | tf_op jit(solution)/shard_map/step_3_0/pallas_call | solution.py:537
  50.5 1.9 %collective-permute-done.16.refs_1_ = bf16[4,128,128]{2,1,0:T(8,128)(2,1)S(1)} collective-permute-done((bf16[4,128,128]{2,1,0:T(8,128)(2,1)S(1)}, bf16[4,128,128]{2,1,0:T(8,128)(2,1)S(1)}, u32[]{:S(2)}, u32[]{:S(2)}) %collective-permute-start.16) | collective-permute-done | bytes 131104 | tf_op jit(solution)/shard_map/ppermute | solution.py:426
  52.4 2.9 %step_3_1.1 = bf16[2,8,128,256]{3,2,1,0:T(8,128)(2,1)} custom-call(s32[5]{0:T(128)S(1)} %stack.31.meta, bf16[4,128,128]{2,1,0:T(8,128)(2,1)S(1)} %collective-permute-done.15.refs_0_, bf16[4,128,128]{2,1,0:T(8,128)(2,1)S(1)} %collective-permute-done.16.refs_1_, ...), custom_call_target="tpu_custom_call", output_to_operand_aliasing={{}: (14, {})} | custom-call | tf_op jit(solution)/shard_map/step_3_1/pallas_call | solution.py:537
  (7 shorter events, 0.0 us)
Async XLA Ops:
  3.1 6.1 %collective-permute-start = (bf16[4,128,128]{2,1,0:T(8,128)(2,1)S(1)}, bf16[4,128,128]{2,1,0:T(8,128)(2,1)S(1)}, u32[]{:S(2)}, u32[]{:S(2)}) collective-permute-start(bf16[4,128,128]{2,1,0:T(8,128)(2,1)S(1)} %get-tuple-element.46), channel_id=1, source_target_pairs={{0,1},{16,17},{24,25},{8,10},{1,0},{17,16},{25,24},{9,11},{2,3},{1... | collective-permute-start | bytes 393224 | tf_op jit(solution)/shard_map/ppermute | solution.py:418
  4.4 4.8 %collective-permute-start.1 = (bf16[4,128,128]{2,1,0:T(8,128)(2,1)S(1)}, bf16[4,128,128]{2,1,0:T(8,128)(2,1)S(1)}, u32[]{:S(2)}, u32[]{:S(2)}) collective-permute-start(bf16[4,128,128]{2,1,0:T(8,128)(2,1)S(1)} %get-tuple-element.47), channel_id=1, source_target_pairs={{0,8},{8,0},{16,24},{24,16},{1,2},{17,18},{25,26},{9,11},{2,1},{18... | collective-permute-start | bytes 393224 | tf_op jit(solution)/shard_map/ppermute | solution.py:418
  9.8 4.6 %collective-permute-start.2 = (bf16[8,128,256]{2,1,0:T(8,128)(2,1)S(1)}, bf16[8,128,256]{2,1,0:T(8,128)(2,1)S(1)}, u32[]{:S(2)}, u32[]{:S(2)}) collective-permute-start(bf16[8,128,256]{2,1,0:T(8,128)(2,1)S(1)} %get-tuple-element.50.old_b), channel_id=1, source_target_pairs={{0,8},{1,9},{2,10},{3,11},{4,12},{5,13},{6,14},{7,15},{8,0},{9,1},... | collective-permute-start | bytes 1572872 | tf_op jit(solution)/shard_map/ppermute | solution.py:423
  12.5 1.7 %collective-permute-start.3 = (bf16[2,128,256]{2,1,0:T(8,128)(2,1)S(1)}, bf16[2,128,256]{2,1,0:T(8,128)(2,1)S(1)}, u32[]{:S(2)}, u32[]{:S(2)}) collective-permute-start(bf16[2,128,256]{2,1,0:T(8,128)(2,1)S(1)} %get-tuple-element.51), channel_id=1, source_target_pairs={{0,9},{1,8},{2,11},{3,10},{4,13},{5,12},{6,15},{7,14},{8,0},{9,1},... | collective-permute-start | bytes 393224 | tf_op jit(solution)/shard_map/ppermute | solution.py:426
  12.6 1.8 %collective-permute-start.4 = (bf16[2,128,256]{2,1,0:T(8,128)(2,1)S(1)}, bf16[2,128,256]{2,1,0:T(8,128)(2,1)S(1)}, u32[]{:S(2)}, u32[]{:S(2)}) collective-permute-start(bf16[2,128,256]{2,1,0:T(8,128)(2,1)S(1)} %get-tuple-element.52), channel_id=1, source_target_pairs={{0,8},{1,10},{2,9},{3,12},{4,11},{5,14},{6,13},{7,15},{8,0},{9,1},... | collective-permute-start | bytes 393224 | tf_op jit(solution)/shard_map/ppermute | solution.py:426
  13.0 16.3 %collective-permute-start.10 = (bf16[10,128,128]{2,1,0:T(8,128)(2,1)S(1)}, bf16[10,128,128]{2,1,0:T(8,128)(2,1)S(1)}, u32[]{:S(2)}, u32[]{:S(2)}) collective-permute-start(bf16[10,128,128]{2,1,0:T(8,128)(2,1)S(1)} %get-tuple-element.64), channel_id=1, source_target_pairs={{16,17},{24,25},{0,8},{8,0},{17,16},{25,24},{1,9},{9,1},{18,19},{2... | collective-permute-start | bytes 983048 | tf_op jit(solution)/shard_map/ppermute | solution.py:418
  14.3 15.3 %collective-permute-start.11 = (bf16[10,128,128]{2,1,0:T(8,128)(2,1)S(1)}, bf16[10,128,128]{2,1,0:T(8,128)(2,1)S(1)}, u32[]{:S(2)}, u32[]{:S(2)}) collective-permute-start(bf16[10,128,128]{2,1,0:T(8,128)(2,1)S(1)} %get-tuple-element.65), channel_id=1, source_target_pairs={{0,8},{8,0},{16,24},{24,16},{17,18},{25,26},{1,9},{9,1},{18,17},{2... | collective-permute-start | bytes 983048 | tf_op jit(solution)/shard_map/ppermute | solution.py:418
  15.0 3.7 %collective-permute-start.5 = (bf16[2,128,256]{2,1,0:T(8,128)(2,1)S(1)}, bf16[2,128,256]{2,1,0:T(8,128)(2,1)S(1)}, u32[]{:S(2)}, u32[]{:S(2)}) collective-permute-start(bf16[2,128,256]{2,1,0:T(8,128)(2,1)S(1)} %get-tuple-element.54), channel_id=1, source_target_pairs={{8,9},{0,2},{16,24},{24,16},{9,8},{1,3},{17,25},{25,17},{10,11},{2... | collective-permute-start | bytes 393224 | tf_op jit(solution)/shard_map/ppermute | solution.py:418
  15.5 3.3 %collective-permute-start.6 = (bf16[2,128,256]{2,1,0:T(8,128)(2,1)S(1)}, bf16[2,128,256]{2,1,0:T(8,128)(2,1)S(1)}, u32[]{:S(2)}, u32[]{:S(2)}) collective-permute-start(bf16[2,128,256]{2,1,0:T(8,128)(2,1)S(1)} %get-tuple-element.55), channel_id=1, source_target_pairs={{0,8},{8,0},{16,24},{24,16},{9,10},{1,3},{17,25},{25,17},{10,9},{2... | collective-permute-start | bytes 393224 | tf_op jit(solution)/shard_map/ppermute | solution.py:418
  19.3 17.0 %collective-permute-start.12 = (bf16[8,128,128]{2,1,0:T(8,128)(2,1)S(1)}, bf16[8,128,128]{2,1,0:T(8,128)(2,1)S(1)}, u32[]{:S(2)}, u32[]{:S(2)}) collective-permute-start(bf16[8,128,128]{2,1,0:T(8,128)(2,1)S(1)} %get-tuple-element.66.refs_9_), channel_id=1, source_target_pairs={{8,16},{9,17},{10,18},{11,19},{12,20},{13,21},{14,22},{15,23},{0,8... | collective-permute-start | bytes 786440 | tf_op jit(solution)/shard_map/ppermute | solution.py:423
  27.4 4.7 %collective-permute-start.13 = (bf16[4,128,128]{2,1,0:T(8,128)(2,1)S(1)}, bf16[4,128,128]{2,1,0:T(8,128)(2,1)S(1)}, u32[]{:S(2)}, u32[]{:S(2)}) collective-permute-start(bf16[4,128,128]{2,1,0:T(8,128)(2,1)S(1)} %get-tuple-element.67), channel_id=1, source_target_pairs={{8,17},{9,16},{10,19},{11,18},{12,21},{13,20},{14,23},{15,22},{0,8... | collective-permute-start | bytes 393224 | tf_op jit(solution)/shard_map/ppermute | solution.py:426
  28.8 10.4 %collective-permute-start.7 = (bf16[8,128,128]{2,1,0:T(8,128)(2,1)S(1)}, bf16[8,128,128]{2,1,0:T(8,128)(2,1)S(1)}, u32[]{:S(2)}, u32[]{:S(2)}) collective-permute-start(bf16[8,128,128]{2,1,0:T(8,128)(2,1)S(1)} %get-tuple-element.59.refs_9_), channel_id=1, source_target_pairs={{8,16},{9,17},{10,18},{11,19},{12,20},{13,21},{14,22},{15,23},{0,8... | collective-permute-start | bytes 786440 | tf_op jit(solution)/shard_map/ppermute | solution.py:423
  29.3 7.0 %collective-permute-start.14 = (bf16[4,128,128]{2,1,0:T(8,128)(2,1)S(1)}, bf16[4,128,128]{2,1,0:T(8,128)(2,1)S(1)}, u32[]{:S(2)}, u32[]{:S(2)}) collective-permute-start(bf16[4,128,128]{2,1,0:T(8,128)(2,1)S(1)} %get-tuple-element.68), channel_id=1, source_target_pairs={{8,16},{9,18},{10,17},{11,20},{12,19},{13,22},{14,21},{15,23},{0,8... | collective-permute-start | bytes 393224 | tf_op jit(solution)/shard_map/ppermute | solution.py:426
  29.6 8.2 %collective-permute-start.8 = (bf16[4,128,128]{2,1,0:T(8,128)(2,1)S(1)}, bf16[4,128,128]{2,1,0:T(8,128)(2,1)S(1)}, u32[]{:S(2)}, u32[]{:S(2)}) collective-permute-start(bf16[4,128,128]{2,1,0:T(8,128)(2,1)S(1)} %get-tuple-element.60), channel_id=1, source_target_pairs={{8,17},{9,16},{10,19},{11,18},{12,21},{13,20},{14,23},{15,22},{0,8... | collective-permute-start | bytes 393224 | tf_op jit(solution)/shard_map/ppermute | solution.py:426
  32.1 7.0 %collective-permute-start.9 = (bf16[4,128,128]{2,1,0:T(8,128)(2,1)S(1)}, bf16[4,128,128]{2,1,0:T(8,128)(2,1)S(1)}, u32[]{:S(2)}, u32[]{:S(2)}) collective-permute-start(bf16[4,128,128]{2,1,0:T(8,128)(2,1)S(1)} %get-tuple-element.61), channel_id=1, source_target_pairs={{8,16},{9,18},{10,17},{11,20},{12,19},{13,22},{14,21},{15,23},{0,8... | collective-permute-start | bytes 393224 | tf_op jit(solution)/shard_map/ppermute | solution.py:426
  39.7 8.8 %collective-permute-start.17 = (bf16[4,128,256]{2,1,0:T(8,128)(2,1)S(1)}, bf16[4,128,256]{2,1,0:T(8,128)(2,1)S(1)}, u32[]{:S(2)}, u32[]{:S(2)}) collective-permute-start(bf16[4,128,256]{2,1,0:T(8,128)(2,1)S(1)} %get-tuple-element.74), channel_id=1, source_target_pairs={{0,8},{1,9},{2,10},{3,11},{4,12},{5,13},{6,14},{7,15},{8,0},{9,1},... | collective-permute-start | bytes 786440 | tf_op jit(solution)/shard_map/ppermute | solution.py:423
  42.6 5.9 %collective-permute-start.18 = (bf16[4,128,256]{2,1,0:T(8,128)(2,1)S(1)}, bf16[4,128,256]{2,1,0:T(8,128)(2,1)S(1)}, u32[]{:S(2)}, u32[]{:S(2)}) collective-permute-start(bf16[4,128,256]{2,1,0:T(8,128)(2,1)S(1)} %get-tuple-element.75), channel_id=1, source_target_pairs={{0,8},{1,9},{2,10},{3,11},{4,12},{5,13},{6,14},{7,15},{8,0},{9,1},... | collective-permute-start | bytes 786440 | tf_op jit(solution)/shard_map/ppermute | solution.py:423
  42.7 4.4 %collective-permute-start.19 = (bf16[4,128,128]{2,1,0:T(8,128)(2,1)S(1)}, bf16[4,128,128]{2,1,0:T(8,128)(2,1)S(1)}, u32[]{:S(2)}, u32[]{:S(2)}) collective-permute-start(bf16[4,128,128]{2,1,0:T(8,128)(2,1)S(1)} %get-tuple-element.78), channel_id=1, source_target_pairs={{0,8},{1,9},{2,10},{3,11},{4,12},{5,13},{6,14},{7,15},{8,0},{9,1},... | collective-permute-start | bytes 393224 | tf_op jit(solution)/shard_map/ppermute | solution.py:426
  43.2 5.4 %collective-permute-start.20 = (bf16[4,128,128]{2,1,0:T(8,128)(2,1)S(1)}, bf16[4,128,128]{2,1,0:T(8,128)(2,1)S(1)}, u32[]{:S(2)}, u32[]{:S(2)}) collective-permute-start(bf16[4,128,128]{2,1,0:T(8,128)(2,1)S(1)} %get-tuple-element.79), channel_id=1, source_target_pairs={{0,8},{1,9},{2,10},{3,11},{4,12},{5,13},{6,14},{7,15},{8,0},{9,1},... | collective-permute-start | bytes 393224 | tf_op jit(solution)/shard_map/ppermute | solution.py:426
  44.5 6.0 %collective-permute-start.15 = (bf16[4,128,128]{2,1,0:T(8,128)(2,1)S(1)}, bf16[4,128,128]{2,1,0:T(8,128)(2,1)S(1)}, u32[]{:S(2)}, u32[]{:S(2)}) collective-permute-start(bf16[4,128,128]{2,1,0:T(8,128)(2,1)S(1)} %get-tuple-element.72), channel_id=1, source_target_pairs={{0,8},{1,9},{2,10},{3,11},{4,12},{5,13},{6,14},{7,15},{8,0},{9,1},... | collective-permute-start | bytes 393224 | tf_op jit(solution)/shard_map/ppermute | solution.py:426
  47.1 5.3 %collective-permute-start.16 = (bf16[4,128,128]{2,1,0:T(8,128)(2,1)S(1)}, bf16[4,128,128]{2,1,0:T(8,128)(2,1)S(1)}, u32[]{:S(2)}, u32[]{:S(2)}) collective-permute-start(bf16[4,128,128]{2,1,0:T(8,128)(2,1)S(1)} %get-tuple-element.73), channel_id=1, source_target_pairs={{0,8},{1,9},{2,10},{3,11},{4,12},{5,13},{6,14},{7,15},{8,0},{9,1},... | collective-permute-start | bytes 393224 | tf_op jit(solution)/shard_map/ppermute | solution.py:426

commit v13 on v11

--- a/solution.py
+++ b/solution.py
@@ -310,7 +310,7 @@
 
 def later_step(group, chunk, final, meta, *refs):
     stages = final and chunk == CHUNKS - 1
-    if final and chunk == 0:
+    if final:
         even_in, odd_in, low, high, *rest = refs
         centre = [low, high]
     else:
@@ -520,7 +520,7 @@
         made = []
         for chunk in range(CHUNKS):
             stages = final and chunk == CHUNKS - 1
-            splits = group == chain - 2 and chunk == 0
+            splits = group == chain - 2
             outs = [] if stages else [half, half] + ([] if final else [half_edge] * (4 if splits else 2))
             extra = [made[0][1], made[0][0][0]] if stages else []
             sems = (2, pairs) if stages else (2,)

time: 53.6 us -> 52.2 us (0.974)
  waiting for transfers between devices: 8.71 us -> 7.57 us
    ppermute x10, waiting for transfers between devices: 6.5 us -> 5.22 us  [travel(): lax.ppermute(value, AXES, hop_pairs(group, mate, chain, rows))]
    ppermute x10, starting transfers between devices: 7.26 us -> 8.33 us  [travel(): lax.ppermute(value, AXES, hop_pairs(group, mate, chain, rows))]
    ppermute x6 -> x7, starting transfers between devices: 15.2 us -> 14.3 us  [travel(): lax.ppermute(value, AXES, hop_pairs(group, same_row, chain, rows))]
  transfers between devices with their start and end apart: 22 -> 23, of which waited for: 8 -> 7; matrix products, arithmetic and copies ran while one was open for 0% -> 0% of each run, Pallas kernels for 22% -> 23%
where the time goes in v13:
time: 52.2 us; the launch traced here: 51.8 us
  starting transfers between devices  25.8 us (49%)
  Pallas kernels  18.1 us (35%)
  waiting for transfers between devices  7.57 us (15%)
    ppermute x7, starting transfers between devices, travel(): lax.ppermute(value, AXES, hop_pairs(group, same_row, chain, rows))  14.3 us
    ppermute x10, starting transfers between devices, travel(): lax.ppermute(value, AXES, hop_pairs(group, mate, chain, rows))  8.33 us
    pallas_call x2, Pallas kernels, prepare(): call(functools.partial(prepare_kernel, turn), f'prepare_{turn}', [SMEM] +...  6.32 us
    pallas_call x4, Pallas kernels, per_device(): call(functools.partial(later_step, group, chunk, final), f'step_{group}_{...  5.93 us
    ppermute x10, waiting for transfers between devices, travel(): lax.ppermute(value, AXES, hop_pairs(group, mate, chain, rows))  5.22 us
    ppermute x6, starting transfers between devices, exchange(): lax.ppermute(value, AXES, inner_pairs(groups, mate, chain, rows, idle))  3.2 us
    pallas_call x1, Pallas kernels, per_device(): call(first_kernel, 'first_level', [SMEM] + [HBM] * 5, [whole, *(shape for...  3.04 us
    ppermute x6, waiting for transfers between devices, exchange(): lax.ppermute(value, AXES, inner_pairs(groups, mate, chain, rows, idle))  2.02 us
  transfers between devices with their start and end apart: 23, of which 7 were waited for; matrix products, arithmetic and copies ran while one was open for 0% of the time, Pallas kernels for 23%

profile of v13, /device:TPU:11, one launch (start us, length us, event | category | flops | bytes accessed | tf_op | source)
XLA Modules:
  0.0 51.8 jit_solution(1110107237128317850)
XLA Ops:
  0.0 0.1 stack.31.meta
  0.1 3.0 %first_level.1 = (bf16[8,128,256]{2,1,0:T(8,128)(2,1)S(1)}, bf16[4,128,128]{2,1,0:T(8,128)(2,1)S(1)}, bf16[4,128,128]{2,1,0:T(8,128)(2,1)S(1)}, bf16[10,128,128]...) custom-call(s32[5]{0:T(128)S(1)} %stack.31.meta, s32[6,2,8]{2,1,0:T(2,128)} %bitcast.7, f32[6,2,8]{2,1,0:T(2,128)} %bitcast.10, ...), custom_call_target="tpu_custom_call" | custom-call | tf_op jit(solution)/shard_map/first_level/pallas_call | solution.py:440
  3.1 1.3 %collective-permute-start = (bf16[4,128,128]{2,1,0:T(8,128)(2,1)S(1)}, bf16[4,128,128]{2,1,0:T(8,128)(2,1)S(1)}, u32[]{:S(2)}, u32[]{:S(2)}) collective-permute-start(bf16[4,128,128]{2,1,0:T(8,128)(2,1)S(1)} %get-tuple-element.48), channel_id=1, source_target_pairs={{0,1},{16,17},{24,25},{8,10},{1,0},{17,16},{25,24},{9,11},{2,3},{1... | collective-permute-start | bytes 393224 | tf_op jit(solution)/shard_map/ppermute | solution.py:412
  4.4 0.1 collective-permute-start.1
  4.5 3.2 %prepare_0.1 = (bf16[4,256,768]{2,1,0:T(8,128)(2,1)S(1)}, f32[8,128,256]{2,1,0:T(8,128)S(1)}) custom-call(s32[5]{0:T(128)S(1)} %stack.31.meta, s32[6,2,8]{2,1,0:T(2,128)} %bitcast.8, f32[6,2,8]{2,1,0:T(2,128)} %bitcast.11, bf16[2,8,6,128,128]{4,3,2,1,0:T(8,128)(2,1)} %lower_hbm.5, bf16[2,8,128,128]{3,2,1,0:T(8,128)(2,1)} %inverse_hbm.5, ...), custom_call_target="tpu_custom_call" | custom-call | tf_op jit(solution)/shard_map/prepare_0/pallas_call | solution.py:461
  7.7 1.6 %collective-permute-done.even_in.even_a = bf16[4,128,128]{2,1,0:T(8,128)(2,1)S(1)} collective-permute-done((bf16[4,128,128]{2,1,0:T(8,128)(2,1)S(1)}, bf16[4,128,128]{2,1,0:T(8,128)(2,1)S(1)}, u32[]{:S(2)}, u32[]{:S(2)}) %collective-permute-start) | collective-permute-done | bytes 131104 | tf_op jit(solution)/shard_map/ppermute | solution.py:412
  9.3 0.0 collective-permute-done.1.odd_in.odd_a
  9.3 0.5 %step_0.1 = (bf16[8,128,256]{2,1,0:T(8,128)(2,1)S(1)}, bf16[2,128,256]{2,1,0:T(8,128)(2,1)S(1)}, bf16[2,128,256]{2,1,0:T(8,128)(2,1)S(1)}) custom-call(s32[5]{0:T(128)S(1)} %stack.31.meta, bf16[8,128,256]{2,1,0:T(8,128)(2,1)S(1)} %get-tuple-element.47.own.first.refs_4_.refs_5_, bf16[4,128,128]{2,1,0:T(8,128)(2,1)S(1)} %collective-permute-done.even_in.even_a, ...), custom_call_target="tpu_custom_call" | custom-call | tf_op jit(solution)/shard_map/step_0/pallas_call | solution.py:480
  9.8 2.7 %collective-permute-start.2 = (bf16[8,128,256]{2,1,0:T(8,128)(2,1)S(1)}, bf16[8,128,256]{2,1,0:T(8,128)(2,1)S(1)}, u32[]{:S(2)}, u32[]{:S(2)}) collective-permute-start(bf16[8,128,256]{2,1,0:T(8,128)(2,1)S(1)} %get-tuple-element.52.old_b), channel_id=1, source_target_pairs={{0,8},{1,9},{2,10},{3,11},{4,12},{5,13},{6,14},{7,15},{8,0},{9,1},... | collective-permute-start | bytes 1572872 | tf_op jit(solution)/shard_map/ppermute | solution.py:419
  12.5 0.1 collective-permute-start.3
  12.6 0.4 collective-permute-start.4
  13.0 1.2 %collective-permute-start.10 = (bf16[10,128,128]{2,1,0:T(8,128)(2,1)S(1)}, bf16[10,128,128]{2,1,0:T(8,128)(2,1)S(1)}, u32[]{:S(2)}, u32[]{:S(2)}) collective-permute-start(bf16[10,128,128]{2,1,0:T(8,128)(2,1)S(1)} %get-tuple-element.66), channel_id=1, source_target_pairs={{16,17},{24,25},{0,8},{8,0},{17,16},{25,24},{1,9},{9,1},{18,19},{2... | collective-permute-start | bytes 983048 | tf_op jit(solution)/shard_map/ppermute | solution.py:412
  14.3 0.2 collective-permute-done.4.odd_in
  14.4 0.0 collective-permute-done.2.centre
  14.4 0.6 %step_1.1 = (bf16[2,8,128,256]{3,2,1,0:T(8,128)(2,1)}, bf16[8,128,256]{2,1,0:T(8,128)(2,1)S(1)}, bf16[2,128,256]{2,1,0:T(8,128)(2,1)S(1)}, bf16[2,128,256]{2,1,0:T(8,128)(2,1)S(1)}) custom-call(s32[5]{0:T(128)S(1)} %stack.31.meta, bf16[8,128,256]{2,1,0:T(8,128)(2,1)S(1)} %collective-permute-done.2.centre, ...), custom_call_target="tpu_custom_call" | custom-call | tf_op jit(solution)/shard_map/step_1/pallas_call | solution.py:495
  15.0 0.4 collective-permute-start.5
  15.5 0.1 collective-permute-start.6
  15.6 3.2 %prepare_1.1 = (bf16[4,256,768]{2,1,0:T(8,128)(2,1)S(1)}, f32[8,128,256]{2,1,0:T(8,128)S(1)}) custom-call(s32[5]{0:T(128)S(1)} %stack.31.meta, s32[6,2,8]{2,1,0:T(2,128)} %bitcast.9, f32[6,2,8]{2,1,0:T(2,128)} %bitcast.12, bf16[2,8,6,128,128]{4,3,2,1,0:T(8,128)(2,1)} %lower_hbm.5, bf16[2,8,128,128]{3,2,1,0:T(8,128)(2,1)} %inverse_hbm.5, ...), custom_call_target="tpu_custom_call" | custom-call | tf_op jit(solution)/shard_map/prepare_1/pallas_call | solution.py:461
  18.8 0.0 collective-permute-done.5.even_in
  18.8 0.0 collective-permute-done.6.odd_in
  18.8 0.6 %step_1_0.1 = (bf16[8,128,128]{2,1,0:T(8,128)(2,1)S(1)}, bf16[4,128,128]{2,1,0:T(8,128)(2,1)S(1)}, bf16[4,128,128]{2,1,0:T(8,128)(2,1)S(1)}) custom-call(s32[5]{0:T(128)S(1)} %stack.31.meta, bf16[8,128,256]{2,1,0:T(8,128)(2,1)S(1)} %get-tuple-element.55.own.refs_8_, bf16[2,128,256]{2,1,0:T(8,128)(2,1)S(1)} %collective-permute-done.5.even_in, ...), custom_call_target="tpu_custom_call" | custom-call | tf_op jit(solution)/shard_map/step_1_0/pallas_call | solution.py:508
  19.3 8.0 %collective-permute-start.12 = (bf16[8,128,128]{2,1,0:T(8,128)(2,1)S(1)}, bf16[8,128,128]{2,1,0:T(8,128)(2,1)S(1)}, u32[]{:S(2)}, u32[]{:S(2)}) collective-permute-start(bf16[8,128,128]{2,1,0:T(8,128)(2,1)S(1)} %get-tuple-element.68.refs_9_), channel_id=1, source_target_pairs={{8,16},{9,17},{10,18},{11,19},{12,20},{13,21},{14,22},{15,23},{0,8... | collective-permute-start | bytes 786440 | tf_op jit(solution)/shard_map/ppermute | solution.py:419
  27.4 0.8 %collective-permute-start.13 = (bf16[4,128,128]{2,1,0:T(8,128)(2,1)S(1)}, bf16[4,128,128]{2,1,0:T(8,128)(2,1)S(1)}, u32[]{:S(2)}, u32[]{:S(2)}) collective-permute-start(bf16[4,128,128]{2,1,0:T(8,128)(2,1)S(1)} %get-tuple-element.69), channel_id=1, source_target_pairs={{8,17},{9,16},{10,19},{11,18},{12,21},{13,20},{14,23},{15,22},{0,8... | collective-permute-start | bytes 393224 | tf_op jit(solution)/shard_map/ppermute | solution.py:420
  28.2 0.5 %step_1_1.1 = (bf16[8,128,128]{2,1,0:T(8,128)(2,1)S(1)}, bf16[4,128,128]{2,1,0:T(8,128)(2,1)S(1)}, bf16[4,128,128]{2,1,0:T(8,128)(2,1)S(1)}) custom-call(s32[5]{0:T(128)S(1)} %stack.31.meta, bf16[8,128,256]{2,1,0:T(8,128)(2,1)S(1)} %get-tuple-element.55.own.refs_8_, bf16[2,128,256]{2,1,0:T(8,128)(2,1)S(1)} %collective-permute-done.5.even_in, ...), custom_call_target="tpu_custom_call" | custom-call | tf_op jit(solution)/shard_map/step_1_1/pallas_call | solution.py:508
  28.8 0.1 collective-permute-start.7
  28.9 0.4 collective-permute-done.10.even_b
  29.3 0.2 collective-permute-start.14
  29.6 0.0 collective-permute-done.11.odd_b
  29.6 0.7 %collective-permute-start.8 = (bf16[4,128,128]{2,1,0:T(8,128)(2,1)S(1)}, bf16[4,128,128]{2,1,0:T(8,128)(2,1)S(1)}, u32[]{:S(2)}, u32[]{:S(2)}) collective-permute-start(bf16[4,128,128]{2,1,0:T(8,128)(2,1)S(1)} %get-tuple-element.62), channel_id=1, source_target_pairs={{8,17},{9,16},{10,19},{11,18},{12,21},{13,20},{14,23},{15,22},{0,8... | collective-permute-start | bytes 393224 | tf_op jit(solution)/shard_map/ppermute | solution.py:420
  30.3 1.8 %collective-permute-done.13.refs_1_ = bf16[4,128,128]{2,1,0:T(8,128)(2,1)S(1)} collective-permute-done((bf16[4,128,128]{2,1,0:T(8,128)(2,1)S(1)}, bf16[4,128,128]{2,1,0:T(8,128)(2,1)S(1)}, u32[]{:S(2)}, u32[]{:S(2)}) %collective-permute-start.13) | collective-permute-done | bytes 131104 | tf_op jit(solution)/shard_map/ppermute | solution.py:420
  32.1 2.5 %collective-permute-start.9 = (bf16[4,128,128]{2,1,0:T(8,128)(2,1)S(1)}, bf16[4,128,128]{2,1,0:T(8,128)(2,1)S(1)}, u32[]{:S(2)}, u32[]{:S(2)}) collective-permute-start(bf16[4,128,128]{2,1,0:T(8,128)(2,1)S(1)} %get-tuple-element.63), channel_id=1, source_target_pairs={{8,16},{9,18},{10,17},{11,20},{12,19},{13,22},{14,21},{15,23},{0,8... | collective-permute-start | bytes 393224 | tf_op jit(solution)/shard_map/ppermute | solution.py:420
  34.6 0.6 %order.1.refs_3_.refs_4_ = bf16[2,14,128,128]{3,2,1,0:T(8,128)(2,1)S(1)} custom-call(s32[5]{0:T(128)S(1)} %stack.31.meta, bf16[4,128,128]{2,1,0:T(8,128)(2,1)S(1)} %collective-permute-done.even_in.even_a, bf16[4,128,128]{2,1,0:T(8,128)(2,1)S(1)} %collective-permute-done.1.odd_in.odd_a, bf16[10,128,128]{2,1,0:T(8,128)(2,1)S(1)} %collective-permute-done.10.even_b, ...), custom_call_target="tpu_custom_call" | custom-call | tf_op jit(solution)/shard_map/order/pallas_call | solution.py:491
  35.2 1.1 %collective-permute-done.14.refs_2_ = bf16[4,128,128]{2,1,0:T(8,128)(2,1)S(1)} collective-permute-done((bf16[4,128,128]{2,1,0:T(8,128)(2,1)S(1)}, bf16[4,128,128]{2,1,0:T(8,128)(2,1)S(1)}, u32[]{:S(2)}, u32[]{:S(2)}) %collective-permute-start.14) | collective-permute-done | bytes 131104 | tf_op jit(solution)/shard_map/ppermute | solution.py:420
  36.3 0.6 %step_2_0.1 = (bf16[2,8,128,256]{3,2,1,0:T(8,128)(2,1)}, bf16[8,128,128]{2,1,0:T(8,128)(2,1)S(1)}, bf16[8,128,128]{2,1,0:T(8,128)(2,1)S(1)}, bf16[4,128,128]{2,1...) custom-call(s32[5]{0:T(128)S(1)} %stack.31.meta, ...), custom_call_target="tpu_custom_call", output_to_operand_aliasing={{0}: (11, {})} | custom-call | tf_op jit(solution)/shard_map/step_2_0/pallas_call | solution.py:527
  36.9 1.6 %collective-permute-start.19 = (bf16[4,128,128]{2,1,0:T(8,128)(2,1)S(1)}, bf16[4,128,128]{2,1,0:T(8,128)(2,1)S(1)}, u32[]{:S(2)}, u32[]{:S(2)}) collective-permute-start(bf16[4,128,128]{2,1,0:T(8,128)(2,1)S(1)} %get-tuple-element.79), channel_id=1, source_target_pairs={{0,8},{1,9},{2,10},{3,11},{4,12},{5,13},{6,14},{7,15},{8,0},{9,1},... | collective-permute-start | bytes 393224 | tf_op jit(solution)/shard_map/ppermute | solution.py:420
  38.5 0.1 collective-permute-start.20
  38.6 2.9 %collective-permute-start.21 = (bf16[4,128,128]{2,1,0:T(8,128)(2,1)S(1)}, bf16[4,128,128]{2,1,0:T(8,128)(2,1)S(1)}, u32[]{:S(2)}, u32[]{:S(2)}) collective-permute-start(bf16[4,128,128]{2,1,0:T(8,128)(2,1)S(1)} %get-tuple-element.81), channel_id=1, source_target_pairs={{0,8},{1,9},{2,10},{3,11},{4,12},{5,13},{6,14},{7,15},{8,0},{9,1},... | collective-permute-start | bytes 393224 | tf_op jit(solution)/shard_map/ppermute | solution.py:419
  41.5 0.0 collective-permute-done.7.refs_0_
  41.5 0.6 %step_2_1.1 = (bf16[2,8,128,256]{3,2,1,0:T(8,128)(2,1)}, bf16[8,128,128]{2,1,0:T(8,128)(2,1)S(1)}, bf16[8,128,128]{2,1,0:T(8,128)(2,1)S(1)}, bf16[4,128,128]{2,1...) custom-call(s32[5]{0:T(128)S(1)} %stack.31.meta, ...), custom_call_target="tpu_custom_call", output_to_operand_aliasing={{0}: (11, {})} | custom-call | tf_op jit(solution)/shard_map/step_2_1/pallas_call | solution.py:527
  42.0 1.5 %collective-permute-start.15 = (bf16[4,128,128]{2,1,0:T(8,128)(2,1)S(1)}, bf16[4,128,128]{2,1,0:T(8,128)(2,1)S(1)}, u32[]{:S(2)}, u32[]{:S(2)}) collective-permute-start(bf16[4,128,128]{2,1,0:T(8,128)(2,1)S(1)} %get-tuple-element.73), channel_id=1, source_target_pairs={{0,8},{1,9},{2,10},{3,11},{4,12},{5,13},{6,14},{7,15},{8,0},{9,1},... | collective-permute-start | bytes 393224 | tf_op jit(solution)/shard_map/ppermute | solution.py:420
  43.5 0.1 collective-permute-start.22
  43.6 0.4 collective-permute-start.16
  44.0 0.1 collective-permute-start.17
  44.2 0.4 collective-permute-start.18
  44.5 0.3 collective-permute-done.22.refs_3_
  44.9 1.9 %step_3_0.1 = (bf16[2,8,128,256]{3,2,1,0:T(8,128)(2,1)}, bf16[8,128,128]{2,1,0:T(8,128)(2,1)S(1)}, bf16[8,128,128]{2,1,0:T(8,128)(2,1)S(1)}) custom-call(s32[5]{0:T(128)S(1)} %stack.31.meta, bf16[4,128,128]{2,1,0:T(8,128)(2,1)S(1)} %collective-permute-done.19.refs_0_, ...), custom_call_target="tpu_custom_call", output_to_operand_aliasing={{0}: (12, {})} | custom-call | tf_op jit(solution)/shard_map/step_3_0/pallas_call | solution.py:527
  46.8 2.1 %collective-permute-done.16.refs_1_ = bf16[4,128,128]{2,1,0:T(8,128)(2,1)S(1)} collective-permute-done((bf16[4,128,128]{2,1,0:T(8,128)(2,1)S(1)}, bf16[4,128,128]{2,1,0:T(8,128)(2,1)S(1)}, u32[]{:S(2)}, u32[]{:S(2)}) %collective-permute-start.16) | collective-permute-done | bytes 131104 | tf_op jit(solution)/shard_map/ppermute | solution.py:420
  48.9 2.9 %step_3_1.1 = bf16[2,8,128,256]{3,2,1,0:T(8,128)(2,1)} custom-call(s32[5]{0:T(128)S(1)} %stack.31.meta, bf16[4,128,128]{2,1,0:T(8,128)(2,1)S(1)} %collective-permute-done.15.refs_0_, bf16[4,128,128]{2,1,0:T(8,128)(2,1)S(1)} %collective-permute-done.16.refs_1_, ...), custom_call_target="tpu_custom_call", output_to_operand_aliasing={{}: (14, {})} | custom-call | tf_op jit(solution)/shard_map/step_3_1/pallas_call | solution.py:527
  (11 shorter events, 0.0 us)
Async XLA Ops:
  3.1 6.1 %collective-permute-start = (bf16[4,128,128]{2,1,0:T(8,128)(2,1)S(1)}, bf16[4,128,128]{2,1,0:T(8,128)(2,1)S(1)}, u32[]{:S(2)}, u32[]{:S(2)}) collective-permute-start(bf16[4,128,128]{2,1,0:T(8,128)(2,1)S(1)} %get-tuple-element.48), channel_id=1, source_target_pairs={{0,1},{16,17},{24,25},{8,10},{1,0},{17,16},{25,24},{9,11},{2,3},{1... | collective-permute-start | bytes 393224 | tf_op jit(solution)/shard_map/ppermute | solution.py:412
  4.4 4.8 %collective-permute-start.1 = (bf16[4,128,128]{2,1,0:T(8,128)(2,1)S(1)}, bf16[4,128,128]{2,1,0:T(8,128)(2,1)S(1)}, u32[]{:S(2)}, u32[]{:S(2)}) collective-permute-start(bf16[4,128,128]{2,1,0:T(8,128)(2,1)S(1)} %get-tuple-element.49), channel_id=1, source_target_pairs={{0,8},{8,0},{16,24},{24,16},{1,2},{17,18},{25,26},{9,11},{2,1},{18... | collective-permute-start | bytes 393224 | tf_op jit(solution)/shard_map/ppermute | solution.py:412
  9.8 4.6 %collective-permute-start.2 = (bf16[8,128,256]{2,1,0:T(8,128)(2,1)S(1)}, bf16[8,128,256]{2,1,0:T(8,128)(2,1)S(1)}, u32[]{:S(2)}, u32[]{:S(2)}) collective-permute-start(bf16[8,128,256]{2,1,0:T(8,128)(2,1)S(1)} %get-tuple-element.52.old_b), channel_id=1, source_target_pairs={{0,8},{1,9},{2,10},{3,11},{4,12},{5,13},{6,14},{7,15},{8,0},{9,1},... | collective-permute-start | bytes 1572872 | tf_op jit(solution)/shard_map/ppermute | solution.py:419
  12.5 1.8 %collective-permute-start.3 = (bf16[2,128,256]{2,1,0:T(8,128)(2,1)S(1)}, bf16[2,128,256]{2,1,0:T(8,128)(2,1)S(1)}, u32[]{:S(2)}, u32[]{:S(2)}) collective-permute-start(bf16[2,128,256]{2,1,0:T(8,128)(2,1)S(1)} %get-tuple-element.53), channel_id=1, source_target_pairs={{0,9},{1,8},{2,11},{3,10},{4,13},{5,12},{6,15},{7,14},{8,0},{9,1},... | collective-permute-start | bytes 393224 | tf_op jit(solution)/shard_map/ppermute | solution.py:420
  12.6 1.8 %collective-permute-start.4 = (bf16[2,128,256]{2,1,0:T(8,128)(2,1)S(1)}, bf16[2,128,256]{2,1,0:T(8,128)(2,1)S(1)}, u32[]{:S(2)}, u32[]{:S(2)}) collective-permute-start(bf16[2,128,256]{2,1,0:T(8,128)(2,1)S(1)} %get-tuple-element.54), channel_id=1, source_target_pairs={{0,8},{1,10},{2,9},{3,12},{4,11},{5,14},{6,13},{7,15},{8,0},{9,1},... | collective-permute-start | bytes 393224 | tf_op jit(solution)/shard_map/ppermute | solution.py:420
  13.0 16.3 %collective-permute-start.10 = (bf16[10,128,128]{2,1,0:T(8,128)(2,1)S(1)}, bf16[10,128,128]{2,1,0:T(8,128)(2,1)S(1)}, u32[]{:S(2)}, u32[]{:S(2)}) collective-permute-start(bf16[10,128,128]{2,1,0:T(8,128)(2,1)S(1)} %get-tuple-element.66), channel_id=1, source_target_pairs={{16,17},{24,25},{0,8},{8,0},{17,16},{25,24},{1,9},{9,1},{18,19},{2... | collective-permute-start | bytes 983048 | tf_op jit(solution)/shard_map/ppermute | solution.py:412
  14.3 15.3 %collective-permute-start.11 = (bf16[10,128,128]{2,1,0:T(8,128)(2,1)S(1)}, bf16[10,128,128]{2,1,0:T(8,128)(2,1)S(1)}, u32[]{:S(2)}, u32[]{:S(2)}) collective-permute-start(bf16[10,128,128]{2,1,0:T(8,128)(2,1)S(1)} %get-tuple-element.67), channel_id=1, source_target_pairs={{0,8},{8,0},{16,24},{24,16},{17,18},{25,26},{1,9},{9,1},{18,17},{2... | collective-permute-start | bytes 983048 | tf_op jit(solution)/shard_map/ppermute | solution.py:412
  15.0 3.7 %collective-permute-start.5 = (bf16[2,128,256]{2,1,0:T(8,128)(2,1)S(1)}, bf16[2,128,256]{2,1,0:T(8,128)(2,1)S(1)}, u32[]{:S(2)}, u32[]{:S(2)}) collective-permute-start(bf16[2,128,256]{2,1,0:T(8,128)(2,1)S(1)} %get-tuple-element.56), channel_id=1, source_target_pairs={{8,9},{0,2},{16,24},{24,16},{9,8},{1,3},{17,25},{25,17},{10,11},{2... | collective-permute-start | bytes 393224 | tf_op jit(solution)/shard_map/ppermute | solution.py:412
  15.5 3.3 %collective-permute-start.6 = (bf16[2,128,256]{2,1,0:T(8,128)(2,1)S(1)}, bf16[2,128,256]{2,1,0:T(8,128)(2,1)S(1)}, u32[]{:S(2)}, u32[]{:S(2)}) collective-permute-start(bf16[2,128,256]{2,1,0:T(8,128)(2,1)S(1)} %get-tuple-element.57), channel_id=1, source_target_pairs={{0,8},{8,0},{16,24},{24,16},{9,10},{1,3},{17,25},{25,17},{10,9},{2... | collective-permute-start | bytes 393224 | tf_op jit(solution)/shard_map/ppermute | solution.py:412
  19.3 17.0 %collective-permute-start.12 = (bf16[8,128,128]{2,1,0:T(8,128)(2,1)S(1)}, bf16[8,128,128]{2,1,0:T(8,128)(2,1)S(1)}, u32[]{:S(2)}, u32[]{:S(2)}) collective-permute-start(bf16[8,128,128]{2,1,0:T(8,128)(2,1)S(1)} %get-tuple-element.68.refs_9_), channel_id=1, source_target_pairs={{8,16},{9,17},{10,18},{11,19},{12,20},{13,21},{14,22},{15,23},{0,8... | collective-permute-start | bytes 786440 | tf_op jit(solution)/shard_map/ppermute | solution.py:419
  27.4 4.7 %collective-permute-start.13 = (bf16[4,128,128]{2,1,0:T(8,128)(2,1)S(1)}, bf16[4,128,128]{2,1,0:T(8,128)(2,1)S(1)}, u32[]{:S(2)}, u32[]{:S(2)}) collective-permute-start(bf16[4,128,128]{2,1,0:T(8,128)(2,1)S(1)} %get-tuple-element.69), channel_id=1, source_target_pairs={{8,17},{9,16},{10,19},{11,18},{12,21},{13,20},{14,23},{15,22},{0,8... | collective-permute-start | bytes 393224 | tf_op jit(solution)/shard_map/ppermute | solution.py:420
  28.8 12.7 %collective-permute-start.7 = (bf16[8,128,128]{2,1,0:T(8,128)(2,1)S(1)}, bf16[8,128,128]{2,1,0:T(8,128)(2,1)S(1)}, u32[]{:S(2)}, u32[]{:S(2)}) collective-permute-start(bf16[8,128,128]{2,1,0:T(8,128)(2,1)S(1)} %get-tuple-element.61.refs_9_), channel_id=1, source_target_pairs={{8,16},{9,17},{10,18},{11,19},{12,20},{13,21},{14,22},{15,23},{0,8... | collective-permute-start | bytes 786440 | tf_op jit(solution)/shard_map/ppermute | solution.py:419
  29.3 7.0 %collective-permute-start.14 = (bf16[4,128,128]{2,1,0:T(8,128)(2,1)S(1)}, bf16[4,128,128]{2,1,0:T(8,128)(2,1)S(1)}, u32[]{:S(2)}, u32[]{:S(2)}) collective-permute-start(bf16[4,128,128]{2,1,0:T(8,128)(2,1)S(1)} %get-tuple-element.70), channel_id=1, source_target_pairs={{8,16},{9,18},{10,17},{11,20},{12,19},{13,22},{14,21},{15,23},{0,8... | collective-permute-start | bytes 393224 | tf_op jit(solution)/shard_map/ppermute | solution.py:420
  29.6 9.0 %collective-permute-start.8 = (bf16[4,128,128]{2,1,0:T(8,128)(2,1)S(1)}, bf16[4,128,128]{2,1,0:T(8,128)(2,1)S(1)}, u32[]{:S(2)}, u32[]{:S(2)}) collective-permute-start(bf16[4,128,128]{2,1,0:T(8,128)(2,1)S(1)} %get-tuple-element.62), channel_id=1, source_target_pairs={{8,17},{9,16},{10,19},{11,18},{12,21},{13,20},{14,23},{15,22},{0,8... | collective-permute-start | bytes 393224 | tf_op jit(solution)/shard_map/ppermute | solution.py:420
  32.1 9.3 %collective-permute-start.9 = (bf16[4,128,128]{2,1,0:T(8,128)(2,1)S(1)}, bf16[4,128,128]{2,1,0:T(8,128)(2,1)S(1)}, u32[]{:S(2)}, u32[]{:S(2)}) collective-permute-start(bf16[4,128,128]{2,1,0:T(8,128)(2,1)S(1)} %get-tuple-element.63), channel_id=1, source_target_pairs={{8,16},{9,18},{10,17},{11,20},{12,19},{13,22},{14,21},{15,23},{0,8... | collective-permute-start | bytes 393224 | tf_op jit(solution)/shard_map/ppermute | solution.py:420
  36.9 6.7 %collective-permute-start.19 = (bf16[4,128,128]{2,1,0:T(8,128)(2,1)S(1)}, bf16[4,128,128]{2,1,0:T(8,128)(2,1)S(1)}, u32[]{:S(2)}, u32[]{:S(2)}) collective-permute-start(bf16[4,128,128]{2,1,0:T(8,128)(2,1)S(1)} %get-tuple-element.79), channel_id=1, source_target_pairs={{0,8},{1,9},{2,10},{3,11},{4,12},{5,13},{6,14},{7,15},{8,0},{9,1},... | collective-permute-start | bytes 393224 | tf_op jit(solution)/shard_map/ppermute | solution.py:420
  38.5 5.5 %collective-permute-start.20 = (bf16[4,128,128]{2,1,0:T(8,128)(2,1)S(1)}, bf16[4,128,128]{2,1,0:T(8,128)(2,1)S(1)}, u32[]{:S(2)}, u32[]{:S(2)}) collective-permute-start(bf16[4,128,128]{2,1,0:T(8,128)(2,1)S(1)} %get-tuple-element.80), channel_id=1, source_target_pairs={{0,8},{1,9},{2,10},{3,11},{4,12},{5,13},{6,14},{7,15},{8,0},{9,1},... | collective-permute-start | bytes 393224 | tf_op jit(solution)/shard_map/ppermute | solution.py:420
  38.6 5.6 %collective-permute-start.21 = (bf16[4,128,128]{2,1,0:T(8,128)(2,1)S(1)}, bf16[4,128,128]{2,1,0:T(8,128)(2,1)S(1)}, u32[]{:S(2)}, u32[]{:S(2)}) collective-permute-start(bf16[4,128,128]{2,1,0:T(8,128)(2,1)S(1)} %get-tuple-element.81), channel_id=1, source_target_pairs={{0,8},{1,9},{2,10},{3,11},{4,12},{5,13},{6,14},{7,15},{8,0},{9,1},... | collective-permute-start | bytes 393224 | tf_op jit(solution)/shard_map/ppermute | solution.py:419
  42.0 4.8 %collective-permute-start.15 = (bf16[4,128,128]{2,1,0:T(8,128)(2,1)S(1)}, bf16[4,128,128]{2,1,0:T(8,128)(2,1)S(1)}, u32[]{:S(2)}, u32[]{:S(2)}) collective-permute-start(bf16[4,128,128]{2,1,0:T(8,128)(2,1)S(1)} %get-tuple-element.73), channel_id=1, source_target_pairs={{0,8},{1,9},{2,10},{3,11},{4,12},{5,13},{6,14},{7,15},{8,0},{9,1},... | collective-permute-start | bytes 393224 | tf_op jit(solution)/shard_map/ppermute | solution.py:420
  43.5 1.3 %collective-permute-start.22 = (bf16[4,128,128]{2,1,0:T(8,128)(2,1)S(1)}, bf16[4,128,128]{2,1,0:T(8,128)(2,1)S(1)}, u32[]{:S(2)}, u32[]{:S(2)}) collective-permute-start(bf16[4,128,128]{2,1,0:T(8,128)(2,1)S(1)} %get-tuple-element.82), channel_id=1, source_target_pairs={{0,8},{1,9},{2,10},{3,11},{4,12},{5,13},{6,14},{7,15},{8,0},{9,1},... | collective-permute-start | bytes 393224 | tf_op jit(solution)/shard_map/ppermute | solution.py:419
  43.6 5.3 %collective-permute-start.16 = (bf16[4,128,128]{2,1,0:T(8,128)(2,1)S(1)}, bf16[4,128,128]{2,1,0:T(8,128)(2,1)S(1)}, u32[]{:S(2)}, u32[]{:S(2)}) collective-permute-start(bf16[4,128,128]{2,1,0:T(8,128)(2,1)S(1)} %get-tuple-element.74), channel_id=1, source_target_pairs={{0,8},{1,9},{2,10},{3,11},{4,12},{5,13},{6,14},{7,15},{8,0},{9,1},... | collective-permute-start | bytes 393224 | tf_op jit(solution)/shard_map/ppermute | solution.py:420
  44.0 4.9 %collective-permute-start.17 = (bf16[4,128,128]{2,1,0:T(8,128)(2,1)S(1)}, bf16[4,128,128]{2,1,0:T(8,128)(2,1)S(1)}, u32[]{:S(2)}, u32[]{:S(2)}) collective-permute-start(bf16[4,128,128]{2,1,0:T(8,128)(2,1)S(1)} %get-tuple-element.75), channel_id=1, source_target_pairs={{0,8},{1,9},{2,10},{3,11},{4,12},{5,13},{6,14},{7,15},{8,0},{9,1},... | collective-permute-start | bytes 393224 | tf_op jit(solution)/shard_map/ppermute | solution.py:419
  44.2 4.7 %collective-permute-start.18 = (bf16[4,128,128]{2,1,0:T(8,128)(2,1)S(1)}, bf16[4,128,128]{2,1,0:T(8,128)(2,1)S(1)}, u32[]{:S(2)}, u32[]{:S(2)}) collective-permute-start(bf16[4,128,128]{2,1,0:T(8,128)(2,1)S(1)} %get-tuple-element.76), channel_id=1, source_target_pairs={{0,8},{1,9},{2,10},{3,11},{4,12},{5,13},{6,14},{7,15},{8,0},{9,1},... | collective-permute-start | bytes 393224 | tf_op jit(solution)/shard_map/ppermute | solution.py:419

commit v14 on v13

--- a/solution.py
+++ b/solution.py
@@ -271,7 +271,9 @@
         copy.wait()
 
 
-def exchanged_step(group, chunk, meta, own, even_in, odd_in, wide_b, base_b, solved, even_out, odd_out, level_a):
+def exchanged_step(group, chunk, meta, own, even_in, odd_in, wide_b, base_b, solved, even_out, odd_out, *rest):
+    *halves, level_a = rest
+
     @pl.when(meta[0] == group)
     def _():
         at = columns(chunk, solved.shape[-1])
@@ -290,6 +292,8 @@
         clear_beyond(meta, level_a, REACH)
         second_of_group(wide_b, base_b, level_a, solved, at)
         emit_sends(meta[1], solved, (even_out, odd_out))
+        for i, part in enumerate(halves):
+            part[...] = solved[i * part.shape[0] : (i + 1) * part.shape[0]]
 
 
 def level_step(group, meta, centre, even_in, odd_in, first, wide_a, old_b, out, solved, even_out, odd_out, window, sems):
@@ -310,7 +314,7 @@
 
 def later_step(group, chunk, final, meta, *refs):
     stages = final and chunk == CHUNKS - 1
-    if final:
+    if final or group == 2:
         even_in, odd_in, low, high, *rest = refs
         centre = [low, high]
     else:
@@ -509,7 +513,7 @@
                 functools.partial(exchanged_step, 1, chunk),
                 f"step_1_{chunk}",
                 [SMEM] + [VMEM] * 5,
-                [half, half_edge, half_edge],
+                [half] + [half_edge] * 4,
                 scratch_shapes=[padded_half],
             )(meta, own, *sides, wide_b, base_b)
         )

time: 52.2 us -> 53.6 us (1.027)
  starting transfers between devices: 25.8 us -> 26.6 us
  waiting for transfers between devices: 7.57 us -> 8.36 us
    ppermute x10, starting transfers between devices: 8.33 us -> 19.2 us  [travel(): lax.ppermute(value, AXES, hop_pairs(group, mate, chain, rows))]
    ppermute x7 -> x9, starting transfers between devices: 14.3 us -> 4.26 us  [travel(): lax.ppermute(value, AXES, hop_pairs(group, same_row, chain, rows))]
    ppermute x6, waiting for transfers between devices: 2.02 us -> 5.4 us  [exchange(): lax.ppermute(value, AXES, inner_pairs(groups, mate, chain, rows, idle))]
    ppermute x10, waiting for transfers between devices: 5.22 us -> 2.94 us  [travel(): lax.ppermute(value, AXES, hop_pairs(group, mate, chain, rows))]
  transfers between devices with their start and end apart: 23 -> 25, of which waited for: 7 -> 5; matrix products, arithmetic and copies ran while one was open for 0% -> 0% of each run, Pallas kernels for 23% -> 22%
where the time goes in v14:
time: 53.6 us; the launch traced here: 53.4 us
  starting transfers between devices  26.6 us (50%)
  Pallas kernels  18.1 us (34%)
  waiting for transfers between devices  8.36 us (16%)
    ppermute x10, starting transfers between devices, travel(): lax.ppermute(value, AXES, hop_pairs(group, mate, chain, rows))  19.2 us
    pallas_call x2, Pallas kernels, prepare(): call(functools.partial(prepare_kernel, turn), f'prepare_{turn}', [SMEM] +...  6.33 us
    pallas_call x4, Pallas kernels, per_device(): call(functools.partial(later_step, group, chunk, final), f'step_{group}_{...  5.93 us
    ppermute x6, waiting for transfers between devices, exchange(): lax.ppermute(value, AXES, inner_pairs(groups, mate, chain, rows, idle))  5.4 us
    ppermute x9, starting transfers between devices, travel(): lax.ppermute(value, AXES, hop_pairs(group, same_row, chain, rows))  4.26 us
    ppermute x6, starting transfers between devices, exchange(): lax.ppermute(value, AXES, inner_pairs(groups, mate, chain, rows, idle))  3.2 us
    pallas_call x1, Pallas kernels, per_device(): call(first_kernel, 'first_level', [SMEM] + [HBM] * 5, [whole, *(shape for...  3.04 us
    ppermute x10, waiting for transfers between devices, travel(): lax.ppermute(value, AXES, hop_pairs(group, mate, chain, rows))  2.94 us
  transfers between devices with their start and end apart: 25, of which 5 were waited for; matrix products, arithmetic and copies ran while one was open for 0% of the time, Pallas kernels for 22%

profile of v14, /device:TPU:11, one launch (start us, length us, event | category | flops | bytes accessed | tf_op | source)
XLA Modules:
  0.0 53.4 jit_solution(7020478017958105578)
XLA Ops:
  0.0 0.1 stack.31.meta
  0.1 3.0 %first_level.1 = (bf16[8,128,256]{2,1,0:T(8,128)(2,1)S(1)}, bf16[4,128,128]{2,1,0:T(8,128)(2,1)S(1)}, bf16[4,128,128]{2,1,0:T(8,128)(2,1)S(1)}, bf16[10,128,128]...) custom-call(s32[5]{0:T(128)S(1)} %stack.31.meta, s32[6,2,8]{2,1,0:T(2,128)} %bitcast.7, f32[6,2,8]{2,1,0:T(2,128)} %bitcast.10, ...), custom_call_target="tpu_custom_call" | custom-call | tf_op jit(solution)/shard_map/first_level/pallas_call | solution.py:444
  3.1 1.3 %collective-permute-start = (bf16[4,128,128]{2,1,0:T(8,128)(2,1)S(1)}, bf16[4,128,128]{2,1,0:T(8,128)(2,1)S(1)}, u32[]{:S(2)}, u32[]{:S(2)}) collective-permute-start(bf16[4,128,128]{2,1,0:T(8,128)(2,1)S(1)} %get-tuple-element.52), channel_id=1, source_target_pairs={{0,1},{16,17},{24,25},{8,10},{1,0},{17,16},{25,24},{9,11},{2,3},{1... | collective-permute-start | bytes 393224 | tf_op jit(solution)/shard_map/ppermute | solution.py:416
  4.4 0.1 collective-permute-start.1
  4.5 3.2 %prepare_0.1 = (bf16[4,256,768]{2,1,0:T(8,128)(2,1)S(1)}, f32[8,128,256]{2,1,0:T(8,128)S(1)}) custom-call(s32[5]{0:T(128)S(1)} %stack.31.meta, s32[6,2,8]{2,1,0:T(2,128)} %bitcast.8, f32[6,2,8]{2,1,0:T(2,128)} %bitcast.11, bf16[2,8,6,128,128]{4,3,2,1,0:T(8,128)(2,1)} %lower_hbm.5, bf16[2,8,128,128]{3,2,1,0:T(8,128)(2,1)} %inverse_hbm.5, ...), custom_call_target="tpu_custom_call" | custom-call | tf_op jit(solution)/shard_map/prepare_0/pallas_call | solution.py:465
  7.7 1.5 %collective-permute-done.even_in.even_a = bf16[4,128,128]{2,1,0:T(8,128)(2,1)S(1)} collective-permute-done((bf16[4,128,128]{2,1,0:T(8,128)(2,1)S(1)}, bf16[4,128,128]{2,1,0:T(8,128)(2,1)S(1)}, u32[]{:S(2)}, u32[]{:S(2)}) %collective-permute-start) | collective-permute-done | bytes 131104 | tf_op jit(solution)/shard_map/ppermute | solution.py:416
  9.3 0.5 %step_0.1 = (bf16[8,128,256]{2,1,0:T(8,128)(2,1)S(1)}, bf16[2,128,256]{2,1,0:T(8,128)(2,1)S(1)}, bf16[2,128,256]{2,1,0:T(8,128)(2,1)S(1)}) custom-call(s32[5]{0:T(128)S(1)} %stack.31.meta, bf16[8,128,256]{2,1,0:T(8,128)(2,1)S(1)} %get-tuple-element.51.own.first.refs_5_, bf16[4,128,128]{2,1,0:T(8,128)(2,1)S(1)} %collective-permute-done.even_in.even_a, ...), custom_call_target="tpu_custom_call" | custom-call | tf_op jit(solution)/shard_map/step_0/pallas_call | solution.py:484
  9.8 2.7 %collective-permute-start.2 = (bf16[8,128,256]{2,1,0:T(8,128)(2,1)S(1)}, bf16[8,128,256]{2,1,0:T(8,128)(2,1)S(1)}, u32[]{:S(2)}, u32[]{:S(2)}) collective-permute-start(bf16[8,128,256]{2,1,0:T(8,128)(2,1)S(1)} %get-tuple-element.56.old_b), channel_id=1, source_target_pairs={{0,8},{1,9},{2,10},{3,11},{4,12},{5,13},{6,14},{7,15},{8,0},{9,1},... | collective-permute-start | bytes 1572872 | tf_op jit(solution)/shard_map/ppermute | solution.py:423
  12.5 0.1 collective-permute-start.3
  12.6 0.4 collective-permute-start.4
  13.0 1.2 %collective-permute-start.11 = (bf16[10,128,128]{2,1,0:T(8,128)(2,1)S(1)}, bf16[10,128,128]{2,1,0:T(8,128)(2,1)S(1)}, u32[]{:S(2)}, u32[]{:S(2)}) collective-permute-start(bf16[10,128,128]{2,1,0:T(8,128)(2,1)S(1)} %get-tuple-element.71), channel_id=1, source_target_pairs={{16,17},{24,25},{0,8},{8,0},{17,16},{25,24},{1,9},{9,1},{18,19},{2... | collective-permute-start | bytes 983048 | tf_op jit(solution)/shard_map/ppermute | solution.py:416
  14.3 0.2 collective-permute-done.4.odd_in
  14.4 0.6 %step_1.1 = (bf16[2,8,128,256]{3,2,1,0:T(8,128)(2,1)}, bf16[8,128,256]{2,1,0:T(8,128)(2,1)S(1)}, bf16[2,128,256]{2,1,0:T(8,128)(2,1)S(1)}, bf16[2,128,256]{2,1,0:T(8,128)(2,1)S(1)}) custom-call(s32[5]{0:T(128)S(1)} %stack.31.meta, bf16[8,128,256]{2,1,0:T(8,128)(2,1)S(1)} %collective-permute-done.2.centre, ...), custom_call_target="tpu_custom_call" | custom-call | tf_op jit(solution)/shard_map/step_1/pallas_call | solution.py:499
  15.0 0.4 collective-permute-start.5
  15.5 0.1 collective-permute-start.6
  15.6 3.2 %prepare_1.1 = (bf16[4,256,768]{2,1,0:T(8,128)(2,1)S(1)}, f32[8,128,256]{2,1,0:T(8,128)S(1)}) custom-call(s32[5]{0:T(128)S(1)} %stack.31.meta, s32[6,2,8]{2,1,0:T(2,128)} %bitcast.9, f32[6,2,8]{2,1,0:T(2,128)} %bitcast.12, bf16[2,8,6,128,128]{4,3,2,1,0:T(8,128)(2,1)} %lower_hbm.5, bf16[2,8,128,128]{3,2,1,0:T(8,128)(2,1)} %inverse_hbm.5, ...), custom_call_target="tpu_custom_call" | custom-call | tf_op jit(solution)/shard_map/prepare_1/pallas_call | solution.py:465
  18.8 0.0 collective-permute-done.6.odd_in
  18.8 0.6 %step_1_0.1 = (bf16[8,128,128]{2,1,0:T(8,128)(2,1)S(1)}, bf16[4,128,128]{2,1,0:T(8,128)(2,1)S(1)}, bf16[4,128,128]{2,1,0:T(8,128)(2,1)S(1)}, bf16[4,128,128]{2,1,0:T(8,128)(2,1)S(1)}, bf16[4,128,128]{2,1,0:T(8,128)(2,1)S(1)}) custom-call(s32[5]{0:T(128)S(1)} %stack.31.meta, bf16[8,128,256]{2,1,0:T(8,128)(2,1)S(1)} %get-tuple-element.59.own.refs_9_, ...), custom_call_target="tpu_custom_call" | custom-call | tf_op jit(solution)/shard_map/step_1_0/pallas_call | solution.py:512
  19.3 8.0 %collective-permute-start.13 = (bf16[4,128,128]{2,1,0:T(8,128)(2,1)S(1)}, bf16[4,128,128]{2,1,0:T(8,128)(2,1)S(1)}, u32[]{:S(2)}, u32[]{:S(2)}) collective-permute-start(bf16[4,128,128]{2,1,0:T(8,128)(2,1)S(1)} %get-tuple-element.74), channel_id=1, source_target_pairs={{8,17},{9,16},{10,19},{11,18},{12,21},{13,20},{14,23},{15,22},{0,8... | collective-permute-start | bytes 393224 | tf_op jit(solution)/shard_map/ppermute | solution.py:424
  27.4 0.9 %collective-permute-start.14 = (bf16[4,128,128]{2,1,0:T(8,128)(2,1)S(1)}, bf16[4,128,128]{2,1,0:T(8,128)(2,1)S(1)}, u32[]{:S(2)}, u32[]{:S(2)}) collective-permute-start(bf16[4,128,128]{2,1,0:T(8,128)(2,1)S(1)} %get-tuple-element.75), channel_id=1, source_target_pairs={{8,16},{9,18},{10,17},{11,20},{12,19},{13,22},{14,21},{15,23},{0,8... | collective-permute-start | bytes 393224 | tf_op jit(solution)/shard_map/ppermute | solution.py:424
  28.2 0.1 collective-permute-start.15
  28.3 3.8 %collective-permute-done.11.even_b = bf16[10,128,128]{2,1,0:T(8,128)(2,1)S(1)} collective-permute-done((bf16[10,128,128]{2,1,0:T(8,128)(2,1)S(1)}, bf16[10,128,128]{2,1,0:T(8,128)(2,1)S(1)}, u32[]{:S(2)}, u32[]{:S(2)}) %collective-permute-start.11) | collective-permute-done | bytes 327712 | tf_op jit(solution)/shard_map/ppermute | solution.py:416
  32.1 0.5 %step_1_1.1 = (bf16[8,128,128]{2,1,0:T(8,128)(2,1)S(1)}, bf16[4,128,128]{2,1,0:T(8,128)(2,1)S(1)}, bf16[4,128,128]{2,1,0:T(8,128)(2,1)S(1)}, bf16[4,128,128]{2,1,0:T(8,128)(2,1)S(1)}, bf16[4,128,128]{2,1,0:T(8,128)(2,1)S(1)}) custom-call(s32[5]{0:T(128)S(1)} %stack.31.meta, bf16[8,128,256]{2,1,0:T(8,128)(2,1)S(1)} %get-tuple-element.59.own.refs_9_, ...), custom_call_target="tpu_custom_call" | custom-call | tf_op jit(solution)/shard_map/step_1_1/pallas_call | solution.py:512
  32.7 0.1 collective-permute-start.7
  32.8 0.0 collective-permute-done.13.refs_0_
  32.8 3.2 %collective-permute-start.8 = (bf16[4,128,128]{2,1,0:T(8,128)(2,1)S(1)}, bf16[4,128,128]{2,1,0:T(8,128)(2,1)S(1)}, u32[]{:S(2)}, u32[]{:S(2)}) collective-permute-start(bf16[4,128,128]{2,1,0:T(8,128)(2,1)S(1)} %get-tuple-element.66), channel_id=1, source_target_pairs={{8,16},{9,18},{10,17},{11,20},{12,19},{13,22},{14,21},{15,23},{0,8... | collective-permute-start | bytes 393224 | tf_op jit(solution)/shard_map/ppermute | solution.py:424
  36.0 0.6 %order.1.refs_4_ = bf16[2,14,128,128]{3,2,1,0:T(8,128)(2,1)S(1)} custom-call(s32[5]{0:T(128)S(1)} %stack.31.meta, bf16[4,128,128]{2,1,0:T(8,128)(2,1)S(1)} %collective-permute-done.even_in.even_a, bf16[4,128,128]{2,1,0:T(8,128)(2,1)S(1)} %collective-permute-done.1.odd_in.odd_a, bf16[10,128,128]{2,1,0:T(8,128)(2,1)S(1)} %collective-permute-done.11.even_b, ...), custom_call_target="tpu_custom_call" | custom-call | tf_op jit(solution)/shard_map/order/pallas_call | solution.py:495
  36.7 0.3 collective-permute-start.9
  36.9 0.1 collective-permute-start.10
  37.0 0.6 %step_2_0.1 = (bf16[2,8,128,256]{3,2,1,0:T(8,128)(2,1)}, bf16[8,128,128]{2,1,0:T(8,128)(2,1)S(1)}, bf16[8,128,128]{2,1,0:T(8,128)(2,1)S(1)}, bf16[4,128,128]{2,1...) custom-call(s32[5]{0:T(128)S(1)} %stack.31.meta, ...), custom_call_target="tpu_custom_call", output_to_operand_aliasing={{0}: (12, {})} | custom-call | tf_op jit(solution)/shard_map/step_2_0/pallas_call | solution.py:531
  37.6 1.9 %collective-permute-start.21 = (bf16[4,128,128]{2,1,0:T(8,128)(2,1)S(1)}, bf16[4,128,128]{2,1,0:T(8,128)(2,1)S(1)}, u32[]{:S(2)}, u32[]{:S(2)}) collective-permute-start(bf16[4,128,128]{2,1,0:T(8,128)(2,1)S(1)} %get-tuple-element.87), channel_id=1, source_target_pairs={{0,8},{1,9},{2,10},{3,11},{4,12},{5,13},{6,14},{7,15},{8,0},{9,1},... | collective-permute-start | bytes 393224 | tf_op jit(solution)/shard_map/ppermute | solution.py:424
  39.5 1.7 %collective-permute-start.22 = (bf16[4,128,128]{2,1,0:T(8,128)(2,1)S(1)}, bf16[4,128,128]{2,1,0:T(8,128)(2,1)S(1)}, u32[]{:S(2)}, u32[]{:S(2)}) collective-permute-start(bf16[4,128,128]{2,1,0:T(8,128)(2,1)S(1)} %get-tuple-element.88), channel_id=1, source_target_pairs={{0,8},{1,9},{2,10},{3,11},{4,12},{5,13},{6,14},{7,15},{8,0},{9,1},... | collective-permute-start | bytes 393224 | tf_op jit(solution)/shard_map/ppermute | solution.py:424
  41.2 0.0 collective-permute-start.23
  41.2 0.0 collective-permute-done.9.refs_2_
  41.2 0.6 %collective-permute-start.24 = (bf16[4,128,128]{2,1,0:T(8,128)(2,1)S(1)}, bf16[4,128,128]{2,1,0:T(8,128)(2,1)S(1)}, u32[]{:S(2)}, u32[]{:S(2)}) collective-permute-start(bf16[4,128,128]{2,1,0:T(8,128)(2,1)S(1)} %get-tuple-element.90), channel_id=1, source_target_pairs={{0,8},{1,9},{2,10},{3,11},{4,12},{5,13},{6,14},{7,15},{8,0},{9,1},... | collective-permute-start | bytes 393224 | tf_op jit(solution)/shard_map/ppermute | solution.py:423
  41.8 0.0 collective-permute-done.10.refs_3_
  41.8 0.6 %step_2_1.1 = (bf16[2,8,128,256]{3,2,1,0:T(8,128)(2,1)}, bf16[8,128,128]{2,1,0:T(8,128)(2,1)S(1)}, bf16[8,128,128]{2,1,0:T(8,128)(2,1)S(1)}, bf16[4,128,128]{2,1...) custom-call(s32[5]{0:T(128)S(1)} %stack.31.meta, ...), custom_call_target="tpu_custom_call", output_to_operand_aliasing={{0}: (12, {})} | custom-call | tf_op jit(solution)/shard_map/step_2_1/pallas_call | solution.py:531
  42.4 2.9 %collective-permute-start.17 = (bf16[4,128,128]{2,1,0:T(8,128)(2,1)S(1)}, bf16[4,128,128]{2,1,0:T(8,128)(2,1)S(1)}, u32[]{:S(2)}, u32[]{:S(2)}) collective-permute-start(bf16[4,128,128]{2,1,0:T(8,128)(2,1)S(1)} %get-tuple-element.81), channel_id=1, source_target_pairs={{0,8},{1,9},{2,10},{3,11},{4,12},{5,13},{6,14},{7,15},{8,0},{9,1},... | collective-permute-start | bytes 393224 | tf_op jit(solution)/shard_map/ppermute | solution.py:424
  45.2 0.0 collective-permute-done.21.refs_0_
  45.2 0.1 collective-permute-start.18
  45.3 0.0 collective-permute-done.22.refs_1_
  45.3 0.1 collective-permute-start.19
  45.4 0.4 collective-permute-start.20
  45.8 0.0 collective-permute-done.24.refs_3_
  45.8 1.9 %step_3_0.1 = (bf16[2,8,128,256]{3,2,1,0:T(8,128)(2,1)}, bf16[8,128,128]{2,1,0:T(8,128)(2,1)S(1)}, bf16[8,128,128]{2,1,0:T(8,128)(2,1)S(1)}) custom-call(s32[5]{0:T(128)S(1)} %stack.31.meta, bf16[4,128,128]{2,1,0:T(8,128)(2,1)S(1)} %collective-permute-done.21.refs_0_, ...), custom_call_target="tpu_custom_call", output_to_operand_aliasing={{0}: (12, {})} | custom-call | tf_op jit(solution)/shard_map/step_3_0/pallas_call | solution.py:531
  47.7 1.1 %collective-permute-done.17.refs_0_ = bf16[4,128,128]{2,1,0:T(8,128)(2,1)S(1)} collective-permute-done((bf16[4,128,128]{2,1,0:T(8,128)(2,1)S(1)}, bf16[4,128,128]{2,1,0:T(8,128)(2,1)S(1)}, u32[]{:S(2)}, u32[]{:S(2)}) %collective-permute-start.17) | collective-permute-done | bytes 131104 | tf_op jit(solution)/shard_map/ppermute | solution.py:424
  48.8 1.7 %collective-permute-done.18.refs_1_ = bf16[4,128,128]{2,1,0:T(8,128)(2,1)S(1)} collective-permute-done((bf16[4,128,128]{2,1,0:T(8,128)(2,1)S(1)}, bf16[4,128,128]{2,1,0:T(8,128)(2,1)S(1)}, u32[]{:S(2)}, u32[]{:S(2)}) %collective-permute-start.18) | collective-permute-done | bytes 131104 | tf_op jit(solution)/shard_map/ppermute | solution.py:424
  50.5 2.9 %step_3_1.1 = bf16[2,8,128,256]{3,2,1,0:T(8,128)(2,1)} custom-call(s32[5]{0:T(128)S(1)} %stack.31.meta, bf16[4,128,128]{2,1,0:T(8,128)(2,1)S(1)} %collective-permute-done.17.refs_0_, bf16[4,128,128]{2,1,0:T(8,128)(2,1)S(1)} %collective-permute-done.18.refs_1_, ...), custom_call_target="tpu_custom_call", output_to_operand_aliasing={{}: (14, {})} | custom-call | tf_op jit(solution)/shard_map/step_3_1/pallas_call | solution.py:531
  (15 shorter events, 0.0 us)
Async XLA Ops:
  3.1 6.1 %collective-permute-start = (bf16[4,128,128]{2,1,0:T(8,128)(2,1)S(1)}, bf16[4,128,128]{2,1,0:T(8,128)(2,1)S(1)}, u32[]{:S(2)}, u32[]{:S(2)}) collective-permute-start(bf16[4,128,128]{2,1,0:T(8,128)(2,1)S(1)} %get-tuple-element.52), channel_id=1, source_target_pairs={{0,1},{16,17},{24,25},{8,10},{1,0},{17,16},{25,24},{9,11},{2,3},{1... | collective-permute-start | bytes 393224 | tf_op jit(solution)/shard_map/ppermute | solution.py:416
  4.4 4.8 %collective-permute-start.1 = (bf16[4,128,128]{2,1,0:T(8,128)(2,1)S(1)}, bf16[4,128,128]{2,1,0:T(8,128)(2,1)S(1)}, u32[]{:S(2)}, u32[]{:S(2)}) collective-permute-start(bf16[4,128,128]{2,1,0:T(8,128)(2,1)S(1)} %get-tuple-element.53), channel_id=1, source_target_pairs={{0,8},{8,0},{16,24},{24,16},{1,2},{17,18},{25,26},{9,11},{2,1},{18... | collective-permute-start | bytes 393224 | tf_op jit(solution)/shard_map/ppermute | solution.py:416
  9.8 4.6 %collective-permute-start.2 = (bf16[8,128,256]{2,1,0:T(8,128)(2,1)S(1)}, bf16[8,128,256]{2,1,0:T(8,128)(2,1)S(1)}, u32[]{:S(2)}, u32[]{:S(2)}) collective-permute-start(bf16[8,128,256]{2,1,0:T(8,128)(2,1)S(1)} %get-tuple-element.56.old_b), channel_id=1, source_target_pairs={{0,8},{1,9},{2,10},{3,11},{4,12},{5,13},{6,14},{7,15},{8,0},{9,1},... | collective-permute-start | bytes 1572872 | tf_op jit(solution)/shard_map/ppermute | solution.py:423
  12.5 1.8 %collective-permute-start.3 = (bf16[2,128,256]{2,1,0:T(8,128)(2,1)S(1)}, bf16[2,128,256]{2,1,0:T(8,128)(2,1)S(1)}, u32[]{:S(2)}, u32[]{:S(2)}) collective-permute-start(bf16[2,128,256]{2,1,0:T(8,128)(2,1)S(1)} %get-tuple-element.57), channel_id=1, source_target_pairs={{0,9},{1,8},{2,11},{3,10},{4,13},{5,12},{6,15},{7,14},{8,0},{9,1},... | collective-permute-start | bytes 393224 | tf_op jit(solution)/shard_map/ppermute | solution.py:424
  12.6 1.8 %collective-permute-start.4 = (bf16[2,128,256]{2,1,0:T(8,128)(2,1)S(1)}, bf16[2,128,256]{2,1,0:T(8,128)(2,1)S(1)}, u32[]{:S(2)}, u32[]{:S(2)}) collective-permute-start(bf16[2,128,256]{2,1,0:T(8,128)(2,1)S(1)} %get-tuple-element.58), channel_id=1, source_target_pairs={{0,8},{1,10},{2,9},{3,12},{4,11},{5,14},{6,13},{7,15},{8,0},{9,1},... | collective-permute-start | bytes 393224 | tf_op jit(solution)/shard_map/ppermute | solution.py:424
  13.0 19.1 %collective-permute-start.11 = (bf16[10,128,128]{2,1,0:T(8,128)(2,1)S(1)}, bf16[10,128,128]{2,1,0:T(8,128)(2,1)S(1)}, u32[]{:S(2)}, u32[]{:S(2)}) collective-permute-start(bf16[10,128,128]{2,1,0:T(8,128)(2,1)S(1)} %get-tuple-element.71), channel_id=1, source_target_pairs={{16,17},{24,25},{0,8},{8,0},{17,16},{25,24},{1,9},{9,1},{18,19},{2... | collective-permute-start | bytes 983048 | tf_op jit(solution)/shard_map/ppermute | solution.py:416
  14.3 18.4 %collective-permute-start.12 = (bf16[10,128,128]{2,1,0:T(8,128)(2,1)S(1)}, bf16[10,128,128]{2,1,0:T(8,128)(2,1)S(1)}, u32[]{:S(2)}, u32[]{:S(2)}) collective-permute-start(bf16[10,128,128]{2,1,0:T(8,128)(2,1)S(1)} %get-tuple-element.72), channel_id=1, source_target_pairs={{0,8},{8,0},{16,24},{24,16},{17,18},{25,26},{1,9},{9,1},{18,17},{2... | collective-permute-start | bytes 983048 | tf_op jit(solution)/shard_map/ppermute | solution.py:416
  15.0 3.7 %collective-permute-start.5 = (bf16[2,128,256]{2,1,0:T(8,128)(2,1)S(1)}, bf16[2,128,256]{2,1,0:T(8,128)(2,1)S(1)}, u32[]{:S(2)}, u32[]{:S(2)}) collective-permute-start(bf16[2,128,256]{2,1,0:T(8,128)(2,1)S(1)} %get-tuple-element.60), channel_id=1, source_target_pairs={{8,9},{0,2},{16,24},{24,16},{9,8},{1,3},{17,25},{25,17},{10,11},{2... | collective-permute-start | bytes 393224 | tf_op jit(solution)/shard_map/ppermute | solution.py:416
  15.5 3.3 %collective-permute-start.6 = (bf16[2,128,256]{2,1,0:T(8,128)(2,1)S(1)}, bf16[2,128,256]{2,1,0:T(8,128)(2,1)S(1)}, u32[]{:S(2)}, u32[]{:S(2)}) collective-permute-start(bf16[2,128,256]{2,1,0:T(8,128)(2,1)S(1)} %get-tuple-element.61), channel_id=1, source_target_pairs={{0,8},{8,0},{16,24},{24,16},{9,10},{1,3},{17,25},{25,17},{10,9},{2... | collective-permute-start | bytes 393224 | tf_op jit(solution)/shard_map/ppermute | solution.py:416
  19.3 13.4 %collective-permute-start.13 = (bf16[4,128,128]{2,1,0:T(8,128)(2,1)S(1)}, bf16[4,128,128]{2,1,0:T(8,128)(2,1)S(1)}, u32[]{:S(2)}, u32[]{:S(2)}) collective-permute-start(bf16[4,128,128]{2,1,0:T(8,128)(2,1)S(1)} %get-tuple-element.74), channel_id=1, source_target_pairs={{8,17},{9,16},{10,19},{11,18},{12,21},{13,20},{14,23},{15,22},{0,8... | collective-permute-start | bytes 393224 | tf_op jit(solution)/shard_map/ppermute | solution.py:424
  27.4 9.3 %collective-permute-start.14 = (bf16[4,128,128]{2,1,0:T(8,128)(2,1)S(1)}, bf16[4,128,128]{2,1,0:T(8,128)(2,1)S(1)}, u32[]{:S(2)}, u32[]{:S(2)}) collective-permute-start(bf16[4,128,128]{2,1,0:T(8,128)(2,1)S(1)} %get-tuple-element.75), channel_id=1, source_target_pairs={{8,16},{9,18},{10,17},{11,20},{12,19},{13,22},{14,21},{15,23},{0,8... | collective-permute-start | bytes 393224 | tf_op jit(solution)/shard_map/ppermute | solution.py:424
  28.2 8.7 %collective-permute-start.15 = (bf16[4,128,128]{2,1,0:T(8,128)(2,1)S(1)}, bf16[4,128,128]{2,1,0:T(8,128)(2,1)S(1)}, u32[]{:S(2)}, u32[]{:S(2)}) collective-permute-start(bf16[4,128,128]{2,1,0:T(8,128)(2,1)S(1)} %get-tuple-element.76), channel_id=1, source_target_pairs={{8,16},{9,17},{10,18},{11,19},{12,20},{13,21},{14,22},{15,23},{0,8... | collective-permute-start | bytes 393224 | tf_op jit(solution)/shard_map/ppermute | solution.py:423
  32.1 4.9 %collective-permute-start.16 = (bf16[4,128,128]{2,1,0:T(8,128)(2,1)S(1)}, bf16[4,128,128]{2,1,0:T(8,128)(2,1)S(1)}, u32[]{:S(2)}, u32[]{:S(2)}) collective-permute-start(bf16[4,128,128]{2,1,0:T(8,128)(2,1)S(1)} %get-tuple-element.77), channel_id=1, source_target_pairs={{8,16},{9,17},{10,18},{11,19},{12,20},{13,21},{14,22},{15,23},{0,8... | collective-permute-start | bytes 393224 | tf_op jit(solution)/shard_map/ppermute | solution.py:423
  32.7 6.8 %collective-permute-start.7 = (bf16[4,128,128]{2,1,0:T(8,128)(2,1)S(1)}, bf16[4,128,128]{2,1,0:T(8,128)(2,1)S(1)}, u32[]{:S(2)}, u32[]{:S(2)}) collective-permute-start(bf16[4,128,128]{2,1,0:T(8,128)(2,1)S(1)} %get-tuple-element.65), channel_id=1, source_target_pairs={{8,17},{9,16},{10,19},{11,18},{12,21},{13,20},{14,23},{15,22},{0,8... | collective-permute-start | bytes 393224 | tf_op jit(solution)/shard_map/ppermute | solution.py:424
  32.8 8.4 %collective-permute-start.8 = (bf16[4,128,128]{2,1,0:T(8,128)(2,1)S(1)}, bf16[4,128,128]{2,1,0:T(8,128)(2,1)S(1)}, u32[]{:S(2)}, u32[]{:S(2)}) collective-permute-start(bf16[4,128,128]{2,1,0:T(8,128)(2,1)S(1)} %get-tuple-element.66), channel_id=1, source_target_pairs={{8,16},{9,18},{10,17},{11,20},{12,19},{13,22},{14,21},{15,23},{0,8... | collective-permute-start | bytes 393224 | tf_op jit(solution)/shard_map/ppermute | solution.py:424
  36.7 4.5 %collective-permute-start.9 = (bf16[4,128,128]{2,1,0:T(8,128)(2,1)S(1)}, bf16[4,128,128]{2,1,0:T(8,128)(2,1)S(1)}, u32[]{:S(2)}, u32[]{:S(2)}) collective-permute-start(bf16[4,128,128]{2,1,0:T(8,128)(2,1)S(1)} %get-tuple-element.67), channel_id=1, source_target_pairs={{8,16},{9,17},{10,18},{11,19},{12,20},{13,21},{14,22},{15,23},{0,8... | collective-permute-start | bytes 393224 | tf_op jit(solution)/shard_map/ppermute | solution.py:423
  36.9 4.8 %collective-permute-start.10 = (bf16[4,128,128]{2,1,0:T(8,128)(2,1)S(1)}, bf16[4,128,128]{2,1,0:T(8,128)(2,1)S(1)}, u32[]{:S(2)}, u32[]{:S(2)}) collective-permute-start(bf16[4,128,128]{2,1,0:T(8,128)(2,1)S(1)} %get-tuple-element.68), channel_id=1, source_target_pairs={{8,16},{9,17},{10,18},{11,19},{12,20},{13,21},{14,22},{15,23},{0,8... | collective-permute-start | bytes 393224 | tf_op jit(solution)/shard_map/ppermute | solution.py:423
  37.6 7.6 %collective-permute-start.21 = (bf16[4,128,128]{2,1,0:T(8,128)(2,1)S(1)}, bf16[4,128,128]{2,1,0:T(8,128)(2,1)S(1)}, u32[]{:S(2)}, u32[]{:S(2)}) collective-permute-start(bf16[4,128,128]{2,1,0:T(8,128)(2,1)S(1)} %get-tuple-element.87), channel_id=1, source_target_pairs={{0,8},{1,9},{2,10},{3,11},{4,12},{5,13},{6,14},{7,15},{8,0},{9,1},... | collective-permute-start | bytes 393224 | tf_op jit(solution)/shard_map/ppermute | solution.py:424
  39.5 5.8 %collective-permute-start.22 = (bf16[4,128,128]{2,1,0:T(8,128)(2,1)S(1)}, bf16[4,128,128]{2,1,0:T(8,128)(2,1)S(1)}, u32[]{:S(2)}, u32[]{:S(2)}) collective-permute-start(bf16[4,128,128]{2,1,0:T(8,128)(2,1)S(1)} %get-tuple-element.88), channel_id=1, source_target_pairs={{0,8},{1,9},{2,10},{3,11},{4,12},{5,13},{6,14},{7,15},{8,0},{9,1},... | collective-permute-start | bytes 393224 | tf_op jit(solution)/shard_map/ppermute | solution.py:424
  41.2 4.2 %collective-permute-start.23 = (bf16[4,128,128]{2,1,0:T(8,128)(2,1)S(1)}, bf16[4,128,128]{2,1,0:T(8,128)(2,1)S(1)}, u32[]{:S(2)}, u32[]{:S(2)}) collective-permute-start(bf16[4,128,128]{2,1,0:T(8,128)(2,1)S(1)} %get-tuple-element.89), channel_id=1, source_target_pairs={{0,8},{1,9},{2,10},{3,11},{4,12},{5,13},{6,14},{7,15},{8,0},{9,1},... | collective-permute-start | bytes 393224 | tf_op jit(solution)/shard_map/ppermute | solution.py:423
  41.2 4.6 %collective-permute-start.24 = (bf16[4,128,128]{2,1,0:T(8,128)(2,1)S(1)}, bf16[4,128,128]{2,1,0:T(8,128)(2,1)S(1)}, u32[]{:S(2)}, u32[]{:S(2)}) collective-permute-start(bf16[4,128,128]{2,1,0:T(8,128)(2,1)S(1)} %get-tuple-element.90), channel_id=1, source_target_pairs={{0,8},{1,9},{2,10},{3,11},{4,12},{5,13},{6,14},{7,15},{8,0},{9,1},... | collective-permute-start | bytes 393224 | tf_op jit(solution)/shard_map/ppermute | solution.py:423
  42.4 6.5 %collective-permute-start.17 = (bf16[4,128,128]{2,1,0:T(8,128)(2,1)S(1)}, bf16[4,128,128]{2,1,0:T(8,128)(2,1)S(1)}, u32[]{:S(2)}, u32[]{:S(2)}) collective-permute-start(bf16[4,128,128]{2,1,0:T(8,128)(2,1)S(1)} %get-tuple-element.81), channel_id=1, source_target_pairs={{0,8},{1,9},{2,10},{3,11},{4,12},{5,13},{6,14},{7,15},{8,0},{9,1},... | collective-permute-start | bytes 393224 | tf_op jit(solution)/shard_map/ppermute | solution.py:424
  45.2 5.3 %collective-permute-start.18 = (bf16[4,128,128]{2,1,0:T(8,128)(2,1)S(1)}, bf16[4,128,128]{2,1,0:T(8,128)(2,1)S(1)}, u32[]{:S(2)}, u32[]{:S(2)}) collective-permute-start(bf16[4,128,128]{2,1,0:T(8,128)(2,1)S(1)} %get-tuple-element.82), channel_id=1, source_target_pairs={{0,8},{1,9},{2,10},{3,11},{4,12},{5,13},{6,14},{7,15},{8,0},{9,1},... | collective-permute-start | bytes 393224 | tf_op jit(solution)/shard_map/ppermute | solution.py:424
  45.3 5.2 %collective-permute-start.19 = (bf16[4,128,128]{2,1,0:T(8,128)(2,1)S(1)}, bf16[4,128,128]{2,1,0:T(8,128)(2,1)S(1)}, u32[]{:S(2)}, u32[]{:S(2)}) collective-permute-start(bf16[4,128,128]{2,1,0:T(8,128)(2,1)S(1)} %get-tuple-element.83), channel_id=1, source_target_pairs={{0,8},{1,9},{2,10},{3,11},{4,12},{5,13},{6,14},{7,15},{8,0},{9,1},... | collective-permute-start | bytes 393224 | tf_op jit(solution)/shard_map/ppermute | solution.py:423
  45.4 5.1 %collective-permute-start.20 = (bf16[4,128,128]{2,1,0:T(8,128)(2,1)S(1)}, bf16[4,128,128]{2,1,0:T(8,128)(2,1)S(1)}, u32[]{:S(2)}, u32[]{:S(2)}) collective-permute-start(bf16[4,128,128]{2,1,0:T(8,128)(2,1)S(1)} %get-tuple-element.84), channel_id=1, source_target_pairs={{0,8},{1,9},{2,10},{3,11},{4,12},{5,13},{6,14},{7,15},{8,0},{9,1},... | collective-permute-start | bytes 393224 | tf_op jit(solution)/shard_map/ppermute | solution.py:423

commit v15 on v13

--- a/solution.py
+++ b/solution.py
@@ -38,6 +38,8 @@
 def hop_pairs(group, mate, chain, rows):
     if group % 2 == 0:
         moves = swap_groups(chain)
+        if group and mate is not same_row:
+            moves.update({group + 1: group - 1, group - 1: group - 2, group - 2: group})
     else:
         moves = swap_groups(chain, range(group - 1, group + 3))
         moves.update({group: group + 1, group - 1: group, group + 1: group + 2, group + 2: group - 1})

time: 52.2 us -> 52.4 us (level)
  waiting for transfers between devices: 7.57 us -> 6.85 us
    ppermute x10, starting transfers between devices: 8.33 us -> 9.49 us  [travel(): lax.ppermute(value, AXES, hop_pairs(group, mate, chain, rows))]
    ppermute x7, starting transfers between devices: 14.3 us -> 13.5 us  [travel(): lax.ppermute(value, AXES, hop_pairs(group, same_row, chain, rows))]
  transfers between devices with their start and end apart: 23 -> 23, of which waited for: 7 -> 6; matrix products, arithmetic and copies ran while one was open for 0% -> 0% of each run, Pallas kernels for 23% -> 23%
where the time goes in v15:
time: 52.4 us; the launch traced here: 51.4 us
  starting transfers between devices  26.2 us (50%)
  Pallas kernels  18.1 us (35%)
  waiting for transfers between devices  6.85 us (13%)
    ppermute x7, starting transfers between devices, travel(): lax.ppermute(value, AXES, hop_pairs(group, same_row, chain, rows))  13.5 us
    ppermute x10, starting transfers between devices, travel(): lax.ppermute(value, AXES, hop_pairs(group, mate, chain, rows))  9.49 us
    pallas_call x2, Pallas kernels, prepare(): call(functools.partial(prepare_kernel, turn), f'prepare_{turn}', [SMEM] +...  6.33 us
    pallas_call x4, Pallas kernels, per_device(): call(functools.partial(later_step, group, chunk, final), f'step_{group}_{...  5.93 us
    ppermute x10, waiting for transfers between devices, travel(): lax.ppermute(value, AXES, hop_pairs(group, mate, chain, rows))  4.84 us
    ppermute x6, starting transfers between devices, exchange(): lax.ppermute(value, AXES, inner_pairs(groups, mate, chain, rows, idle))  3.19 us
    pallas_call x1, Pallas kernels, per_device(): call(first_kernel, 'first_level', [SMEM] + [HBM] * 5, [whole, *(shape for...  3.04 us
    ppermute x6, waiting for transfers between devices, exchange(): lax.ppermute(value, AXES, inner_pairs(groups, mate, chain, rows, idle))  2 us
  transfers between devices with their start and end apart: 23, of which 6 were waited for; matrix products, arithmetic and copies ran while one was open for 0% of the time, Pallas kernels for 23%

profile of v15, /device:TPU:11, one launch (start us, length us, event | category | flops | bytes accessed | tf_op | source)
XLA Modules:
  0.0 51.4 jit_solution(17149305159297364154)
XLA Ops:
  0.0 0.1 stack.31.meta
  0.1 3.0 %first_level.1 = (bf16[8,128,256]{2,1,0:T(8,128)(2,1)S(1)}, bf16[4,128,128]{2,1,0:T(8,128)(2,1)S(1)}, bf16[4,128,128]{2,1,0:T(8,128)(2,1)S(1)}, bf16[10,128,128]...) custom-call(s32[5]{0:T(128)S(1)} %stack.31.meta, s32[6,2,8]{2,1,0:T(2,128)} %bitcast.7, f32[6,2,8]{2,1,0:T(2,128)} %bitcast.10, ...), custom_call_target="tpu_custom_call" | custom-call | tf_op jit(solution)/shard_map/first_level/pallas_call | solution.py:442
  3.1 1.3 %collective-permute-start = (bf16[4,128,128]{2,1,0:T(8,128)(2,1)S(1)}, bf16[4,128,128]{2,1,0:T(8,128)(2,1)S(1)}, u32[]{:S(2)}, u32[]{:S(2)}) collective-permute-start(bf16[4,128,128]{2,1,0:T(8,128)(2,1)S(1)} %get-tuple-element.48), channel_id=1, source_target_pairs={{0,1},{16,17},{24,25},{8,10},{1,0},{17,16},{25,24},{9,11},{2,3},{1... | collective-permute-start | bytes 393224 | tf_op jit(solution)/shard_map/ppermute | solution.py:414
  4.4 0.1 collective-permute-start.1
  4.5 3.2 %prepare_0.1 = (bf16[4,256,768]{2,1,0:T(8,128)(2,1)S(1)}, f32[8,128,256]{2,1,0:T(8,128)S(1)}) custom-call(s32[5]{0:T(128)S(1)} %stack.31.meta, s32[6,2,8]{2,1,0:T(2,128)} %bitcast.8, f32[6,2,8]{2,1,0:T(2,128)} %bitcast.11, bf16[2,8,6,128,128]{4,3,2,1,0:T(8,128)(2,1)} %lower_hbm.5, bf16[2,8,128,128]{3,2,1,0:T(8,128)(2,1)} %inverse_hbm.5, ...), custom_call_target="tpu_custom_call" | custom-call | tf_op jit(solution)/shard_map/prepare_0/pallas_call | solution.py:463
  7.7 1.5 %collective-permute-done.even_in.even_a = bf16[4,128,128]{2,1,0:T(8,128)(2,1)S(1)} collective-permute-done((bf16[4,128,128]{2,1,0:T(8,128)(2,1)S(1)}, bf16[4,128,128]{2,1,0:T(8,128)(2,1)S(1)}, u32[]{:S(2)}, u32[]{:S(2)}) %collective-permute-start) | collective-permute-done | bytes 131104 | tf_op jit(solution)/shard_map/ppermute | solution.py:414
  9.2 0.0 collective-permute-done.1.odd_in.odd_a
  9.3 0.5 %step_0.1 = (bf16[8,128,256]{2,1,0:T(8,128)(2,1)S(1)}, bf16[2,128,256]{2,1,0:T(8,128)(2,1)S(1)}, bf16[2,128,256]{2,1,0:T(8,128)(2,1)S(1)}) custom-call(s32[5]{0:T(128)S(1)} %stack.31.meta, bf16[8,128,256]{2,1,0:T(8,128)(2,1)S(1)} %get-tuple-element.47.own.first.refs_4_.refs_5_, bf16[4,128,128]{2,1,0:T(8,128)(2,1)S(1)} %collective-permute-done.even_in.even_a, ...), custom_call_target="tpu_custom_call" | custom-call | tf_op jit(solution)/shard_map/step_0/pallas_call | solution.py:482
  9.8 2.7 %collective-permute-start.2 = (bf16[8,128,256]{2,1,0:T(8,128)(2,1)S(1)}, bf16[8,128,256]{2,1,0:T(8,128)(2,1)S(1)}, u32[]{:S(2)}, u32[]{:S(2)}) collective-permute-start(bf16[8,128,256]{2,1,0:T(8,128)(2,1)S(1)} %get-tuple-element.52.old_b), channel_id=1, source_target_pairs={{0,8},{1,9},{2,10},{3,11},{4,12},{5,13},{6,14},{7,15},{8,0},{9,1},... | collective-permute-start | bytes 1572872 | tf_op jit(solution)/shard_map/ppermute | solution.py:421
  12.5 0.1 collective-permute-start.3
  12.6 0.4 collective-permute-start.4
  13.0 1.2 %collective-permute-start.10 = (bf16[10,128,128]{2,1,0:T(8,128)(2,1)S(1)}, bf16[10,128,128]{2,1,0:T(8,128)(2,1)S(1)}, u32[]{:S(2)}, u32[]{:S(2)}) collective-permute-start(bf16[10,128,128]{2,1,0:T(8,128)(2,1)S(1)} %get-tuple-element.66), channel_id=1, source_target_pairs={{16,17},{24,25},{0,8},{8,0},{17,16},{25,24},{1,9},{9,1},{18,19},{2... | collective-permute-start | bytes 983048 | tf_op jit(solution)/shard_map/ppermute | solution.py:414
  14.3 0.2 collective-permute-done.4.odd_in
  14.5 0.6 %step_1.1 = (bf16[2,8,128,256]{3,2,1,0:T(8,128)(2,1)}, bf16[8,128,256]{2,1,0:T(8,128)(2,1)S(1)}, bf16[2,128,256]{2,1,0:T(8,128)(2,1)S(1)}, bf16[2,128,256]{2,1,0:T(8,128)(2,1)S(1)}) custom-call(s32[5]{0:T(128)S(1)} %stack.31.meta, bf16[8,128,256]{2,1,0:T(8,128)(2,1)S(1)} %collective-permute-done.2.centre, ...), custom_call_target="tpu_custom_call" | custom-call | tf_op jit(solution)/shard_map/step_1/pallas_call | solution.py:497
  15.0 0.4 collective-permute-start.5
  15.5 0.1 collective-permute-start.6
  15.6 3.2 %prepare_1.1 = (bf16[4,256,768]{2,1,0:T(8,128)(2,1)S(1)}, f32[8,128,256]{2,1,0:T(8,128)S(1)}) custom-call(s32[5]{0:T(128)S(1)} %stack.31.meta, s32[6,2,8]{2,1,0:T(2,128)} %bitcast.9, f32[6,2,8]{2,1,0:T(2,128)} %bitcast.12, bf16[2,8,6,128,128]{4,3,2,1,0:T(8,128)(2,1)} %lower_hbm.5, bf16[2,8,128,128]{3,2,1,0:T(8,128)(2,1)} %inverse_hbm.5, ...), custom_call_target="tpu_custom_call" | custom-call | tf_op jit(solution)/shard_map/prepare_1/pallas_call | solution.py:463
  18.8 0.0 collective-permute-done.5.even_in
  18.8 0.0 collective-permute-done.6.odd_in
  18.8 0.6 %step_1_0.1 = (bf16[8,128,128]{2,1,0:T(8,128)(2,1)S(1)}, bf16[4,128,128]{2,1,0:T(8,128)(2,1)S(1)}, bf16[4,128,128]{2,1,0:T(8,128)(2,1)S(1)}) custom-call(s32[5]{0:T(128)S(1)} %stack.31.meta, bf16[8,128,256]{2,1,0:T(8,128)(2,1)S(1)} %get-tuple-element.55.own.refs_8_, bf16[2,128,256]{2,1,0:T(8,128)(2,1)S(1)} %collective-permute-done.5.even_in, ...), custom_call_target="tpu_custom_call" | custom-call | tf_op jit(solution)/shard_map/step_1_0/pallas_call | solution.py:510
  19.3 8.0 %collective-permute-start.12 = (bf16[8,128,128]{2,1,0:T(8,128)(2,1)S(1)}, bf16[8,128,128]{2,1,0:T(8,128)(2,1)S(1)}, u32[]{:S(2)}, u32[]{:S(2)}) collective-permute-start(bf16[8,128,128]{2,1,0:T(8,128)(2,1)S(1)} %get-tuple-element.68.refs_9_), channel_id=1, source_target_pairs={{8,16},{9,17},{10,18},{11,19},{12,20},{13,21},{14,22},{15,23},{0,8... | collective-permute-start | bytes 786440 | tf_op jit(solution)/shard_map/ppermute | solution.py:421
  27.4 0.8 %collective-permute-start.13 = (bf16[4,128,128]{2,1,0:T(8,128)(2,1)S(1)}, bf16[4,128,128]{2,1,0:T(8,128)(2,1)S(1)}, u32[]{:S(2)}, u32[]{:S(2)}) collective-permute-start(bf16[4,128,128]{2,1,0:T(8,128)(2,1)S(1)} %get-tuple-element.69), channel_id=1, source_target_pairs={{8,17},{9,16},{10,19},{11,18},{12,21},{13,20},{14,23},{15,22},{0,8... | collective-permute-start | bytes 393224 | tf_op jit(solution)/shard_map/ppermute | solution.py:422
  28.2 0.5 %step_1_1.1 = (bf16[8,128,128]{2,1,0:T(8,128)(2,1)S(1)}, bf16[4,128,128]{2,1,0:T(8,128)(2,1)S(1)}, bf16[4,128,128]{2,1,0:T(8,128)(2,1)S(1)}) custom-call(s32[5]{0:T(128)S(1)} %stack.31.meta, bf16[8,128,256]{2,1,0:T(8,128)(2,1)S(1)} %get-tuple-element.55.own.refs_8_, bf16[2,128,256]{2,1,0:T(8,128)(2,1)S(1)} %collective-permute-done.5.even_in, ...), custom_call_target="tpu_custom_call" | custom-call | tf_op jit(solution)/shard_map/step_1_1/pallas_call | solution.py:510
  28.8 0.1 collective-permute-start.7
  28.9 0.4 collective-permute-done.10.even_b
  29.3 0.2 collective-permute-start.14
  29.6 0.7 %collective-permute-start.8 = (bf16[4,128,128]{2,1,0:T(8,128)(2,1)S(1)}, bf16[4,128,128]{2,1,0:T(8,128)(2,1)S(1)}, u32[]{:S(2)}, u32[]{:S(2)}) collective-permute-start(bf16[4,128,128]{2,1,0:T(8,128)(2,1)S(1)} %get-tuple-element.62), channel_id=1, source_target_pairs={{8,17},{9,16},{10,19},{11,18},{12,21},{13,20},{14,23},{15,22},{0,8... | collective-permute-start | bytes 393224 | tf_op jit(solution)/shard_map/ppermute | solution.py:422
  30.3 1.8 %collective-permute-done.13.refs_1_ = bf16[4,128,128]{2,1,0:T(8,128)(2,1)S(1)} collective-permute-done((bf16[4,128,128]{2,1,0:T(8,128)(2,1)S(1)}, bf16[4,128,128]{2,1,0:T(8,128)(2,1)S(1)}, u32[]{:S(2)}, u32[]{:S(2)}) %collective-permute-start.13) | collective-permute-done | bytes 131104 | tf_op jit(solution)/shard_map/ppermute | solution.py:422
  32.1 2.5 %collective-permute-start.9 = (bf16[4,128,128]{2,1,0:T(8,128)(2,1)S(1)}, bf16[4,128,128]{2,1,0:T(8,128)(2,1)S(1)}, u32[]{:S(2)}, u32[]{:S(2)}) collective-permute-start(bf16[4,128,128]{2,1,0:T(8,128)(2,1)S(1)} %get-tuple-element.63), channel_id=1, source_target_pairs={{8,16},{9,18},{10,17},{11,20},{12,19},{13,22},{14,21},{15,23},{0,8... | collective-permute-start | bytes 393224 | tf_op jit(solution)/shard_map/ppermute | solution.py:422
  34.6 0.6 %order.1.refs_3_.refs_4_ = bf16[2,14,128,128]{3,2,1,0:T(8,128)(2,1)S(1)} custom-call(s32[5]{0:T(128)S(1)} %stack.31.meta, bf16[4,128,128]{2,1,0:T(8,128)(2,1)S(1)} %collective-permute-done.even_in.even_a, bf16[4,128,128]{2,1,0:T(8,128)(2,1)S(1)} %collective-permute-done.1.odd_in.odd_a, bf16[10,128,128]{2,1,0:T(8,128)(2,1)S(1)} %collective-permute-done.10.even_b, ...), custom_call_target="tpu_custom_call" | custom-call | tf_op jit(solution)/shard_map/order/pallas_call | solution.py:493
  35.2 1.1 %collective-permute-done.14.refs_2_ = bf16[4,128,128]{2,1,0:T(8,128)(2,1)S(1)} collective-permute-done((bf16[4,128,128]{2,1,0:T(8,128)(2,1)S(1)}, bf16[4,128,128]{2,1,0:T(8,128)(2,1)S(1)}, u32[]{:S(2)}, u32[]{:S(2)}) %collective-permute-start.14) | collective-permute-done | bytes 131104 | tf_op jit(solution)/shard_map/ppermute | solution.py:422
  36.3 0.0 collective-permute-done.12.refs_0_
  36.3 0.6 %step_2_0.1 = (bf16[2,8,128,256]{3,2,1,0:T(8,128)(2,1)}, bf16[8,128,128]{2,1,0:T(8,128)(2,1)S(1)}, bf16[8,128,128]{2,1,0:T(8,128)(2,1)S(1)}, bf16[4,128,128]{2,1...) custom-call(s32[5]{0:T(128)S(1)} %stack.31.meta, ...), custom_call_target="tpu_custom_call", output_to_operand_aliasing={{0}: (11, {})} | custom-call | tf_op jit(solution)/shard_map/step_2_0/pallas_call | solution.py:529
  36.9 0.3 collective-permute-start.19
  37.2 2.4 %collective-permute-start.20 = (bf16[4,128,128]{2,1,0:T(8,128)(2,1)S(1)}, bf16[4,128,128]{2,1,0:T(8,128)(2,1)S(1)}, u32[]{:S(2)}, u32[]{:S(2)}) collective-permute-start(bf16[4,128,128]{2,1,0:T(8,128)(2,1)S(1)} %get-tuple-element.80), channel_id=1, source_target_pairs={{0,16},{1,17},{2,18},{3,19},{4,20},{5,21},{6,22},{7,23},{8,0},{9,1... | collective-permute-start | bytes 393224 | tf_op jit(solution)/shard_map/ppermute | solution.py:422
  39.6 0.0 collective-permute-done.8.refs_1_
  39.6 0.9 %collective-permute-start.21 = (bf16[4,128,128]{2,1,0:T(8,128)(2,1)S(1)}, bf16[4,128,128]{2,1,0:T(8,128)(2,1)S(1)}, u32[]{:S(2)}, u32[]{:S(2)}) collective-permute-start(bf16[4,128,128]{2,1,0:T(8,128)(2,1)S(1)} %get-tuple-element.81), channel_id=1, source_target_pairs={{0,8},{1,9},{2,10},{3,11},{4,12},{5,13},{6,14},{7,15},{8,0},{9,1},... | collective-permute-start | bytes 393224 | tf_op jit(solution)/shard_map/ppermute | solution.py:421
  40.5 0.0 collective-permute-done.9.refs_2_
  40.5 0.0 collective-permute-done.7.refs_0_
  40.5 0.6 %step_2_1.1 = (bf16[2,8,128,256]{3,2,1,0:T(8,128)(2,1)}, bf16[8,128,128]{2,1,0:T(8,128)(2,1)S(1)}, bf16[8,128,128]{2,1,0:T(8,128)(2,1)S(1)}, bf16[4,128,128]{2,1...) custom-call(s32[5]{0:T(128)S(1)} %stack.31.meta, ...), custom_call_target="tpu_custom_call", output_to_operand_aliasing={{0}: (11, {})} | custom-call | tf_op jit(solution)/shard_map/step_2_1/pallas_call | solution.py:529
  41.1 0.7 %collective-permute-start.15 = (bf16[4,128,128]{2,1,0:T(8,128)(2,1)S(1)}, bf16[4,128,128]{2,1,0:T(8,128)(2,1)S(1)}, u32[]{:S(2)}, u32[]{:S(2)}) collective-permute-start(bf16[4,128,128]{2,1,0:T(8,128)(2,1)S(1)} %get-tuple-element.73), channel_id=1, source_target_pairs={{0,16},{1,17},{2,18},{3,19},{4,20},{5,21},{6,22},{7,23},{8,0},{9,1... | collective-permute-start | bytes 393224 | tf_op jit(solution)/shard_map/ppermute | solution.py:422
  41.8 1.1 %collective-permute-start.22 = (bf16[4,128,128]{2,1,0:T(8,128)(2,1)S(1)}, bf16[4,128,128]{2,1,0:T(8,128)(2,1)S(1)}, u32[]{:S(2)}, u32[]{:S(2)}) collective-permute-start(bf16[4,128,128]{2,1,0:T(8,128)(2,1)S(1)} %get-tuple-element.82), channel_id=1, source_target_pairs={{0,8},{1,9},{2,10},{3,11},{4,12},{5,13},{6,14},{7,15},{8,0},{9,1},... | collective-permute-start | bytes 393224 | tf_op jit(solution)/shard_map/ppermute | solution.py:421
  42.9 1.4 %collective-permute-start.16 = (bf16[4,128,128]{2,1,0:T(8,128)(2,1)S(1)}, bf16[4,128,128]{2,1,0:T(8,128)(2,1)S(1)}, u32[]{:S(2)}, u32[]{:S(2)}) collective-permute-start(bf16[4,128,128]{2,1,0:T(8,128)(2,1)S(1)} %get-tuple-element.74), channel_id=1, source_target_pairs={{0,16},{1,17},{2,18},{3,19},{4,20},{5,21},{6,22},{7,23},{8,0},{9,1... | collective-permute-start | bytes 393224 | tf_op jit(solution)/shard_map/ppermute | solution.py:422
  44.3 0.6 %collective-permute-start.17 = (bf16[4,128,128]{2,1,0:T(8,128)(2,1)S(1)}, bf16[4,128,128]{2,1,0:T(8,128)(2,1)S(1)}, u32[]{:S(2)}, u32[]{:S(2)}) collective-permute-start(bf16[4,128,128]{2,1,0:T(8,128)(2,1)S(1)} %get-tuple-element.75), channel_id=1, source_target_pairs={{0,8},{1,9},{2,10},{3,11},{4,12},{5,13},{6,14},{7,15},{8,0},{9,1},... | collective-permute-start | bytes 393224 | tf_op jit(solution)/shard_map/ppermute | solution.py:421
  44.9 0.0 collective-permute-start.18
  44.9 1.9 %step_3_0.1 = (bf16[2,8,128,256]{3,2,1,0:T(8,128)(2,1)}, bf16[8,128,128]{2,1,0:T(8,128)(2,1)S(1)}, bf16[8,128,128]{2,1,0:T(8,128)(2,1)S(1)}) custom-call(s32[5]{0:T(128)S(1)} %stack.31.meta, bf16[4,128,128]{2,1,0:T(8,128)(2,1)S(1)} %collective-permute-done.19.refs_0_, ...), custom_call_target="tpu_custom_call", output_to_operand_aliasing={{0}: (12, {})} | custom-call | tf_op jit(solution)/shard_map/step_3_0/pallas_call | solution.py:529
  46.9 1.7 %collective-permute-done.16.refs_1_ = bf16[4,128,128]{2,1,0:T(8,128)(2,1)S(1)} collective-permute-done((bf16[4,128,128]{2,1,0:T(8,128)(2,1)S(1)}, bf16[4,128,128]{2,1,0:T(8,128)(2,1)S(1)}, u32[]{:S(2)}, u32[]{:S(2)}) %collective-permute-start.16) | collective-permute-done | bytes 131104 | tf_op jit(solution)/shard_map/ppermute | solution.py:422
  48.6 2.9 %step_3_1.1 = bf16[2,8,128,256]{3,2,1,0:T(8,128)(2,1)} custom-call(s32[5]{0:T(128)S(1)} %stack.31.meta, bf16[4,128,128]{2,1,0:T(8,128)(2,1)S(1)} %collective-permute-done.15.refs_0_, bf16[4,128,128]{2,1,0:T(8,128)(2,1)S(1)} %collective-permute-done.16.refs_1_, ...), custom_call_target="tpu_custom_call", output_to_operand_aliasing={{}: (14, {})} | custom-call | tf_op jit(solution)/shard_map/step_3_1/pallas_call | solution.py:529
  (11 shorter events, 0.0 us)
Async XLA Ops:
  3.1 6.1 %collective-permute-start = (bf16[4,128,128]{2,1,0:T(8,128)(2,1)S(1)}, bf16[4,128,128]{2,1,0:T(8,128)(2,1)S(1)}, u32[]{:S(2)}, u32[]{:S(2)}) collective-permute-start(bf16[4,128,128]{2,1,0:T(8,128)(2,1)S(1)} %get-tuple-element.48), channel_id=1, source_target_pairs={{0,1},{16,17},{24,25},{8,10},{1,0},{17,16},{25,24},{9,11},{2,3},{1... | collective-permute-start | bytes 393224 | tf_op jit(solution)/shard_map/ppermute | solution.py:414
  4.4 4.8 %collective-permute-start.1 = (bf16[4,128,128]{2,1,0:T(8,128)(2,1)S(1)}, bf16[4,128,128]{2,1,0:T(8,128)(2,1)S(1)}, u32[]{:S(2)}, u32[]{:S(2)}) collective-permute-start(bf16[4,128,128]{2,1,0:T(8,128)(2,1)S(1)} %get-tuple-element.49), channel_id=1, source_target_pairs={{0,8},{8,0},{16,24},{24,16},{1,2},{17,18},{25,26},{9,11},{2,1},{18... | collective-permute-start | bytes 393224 | tf_op jit(solution)/shard_map/ppermute | solution.py:414
  9.8 4.6 %collective-permute-start.2 = (bf16[8,128,256]{2,1,0:T(8,128)(2,1)S(1)}, bf16[8,128,256]{2,1,0:T(8,128)(2,1)S(1)}, u32[]{:S(2)}, u32[]{:S(2)}) collective-permute-start(bf16[8,128,256]{2,1,0:T(8,128)(2,1)S(1)} %get-tuple-element.52.old_b), channel_id=1, source_target_pairs={{0,8},{1,9},{2,10},{3,11},{4,12},{5,13},{6,14},{7,15},{8,0},{9,1},... | collective-permute-start | bytes 1572872 | tf_op jit(solution)/shard_map/ppermute | solution.py:421
  12.5 1.7 %collective-permute-start.3 = (bf16[2,128,256]{2,1,0:T(8,128)(2,1)S(1)}, bf16[2,128,256]{2,1,0:T(8,128)(2,1)S(1)}, u32[]{:S(2)}, u32[]{:S(2)}) collective-permute-start(bf16[2,128,256]{2,1,0:T(8,128)(2,1)S(1)} %get-tuple-element.53), channel_id=1, source_target_pairs={{0,9},{1,8},{2,11},{3,10},{4,13},{5,12},{6,15},{7,14},{8,0},{9,1},... | collective-permute-start | bytes 393224 | tf_op jit(solution)/shard_map/ppermute | solution.py:422
  12.6 1.8 %collective-permute-start.4 = (bf16[2,128,256]{2,1,0:T(8,128)(2,1)S(1)}, bf16[2,128,256]{2,1,0:T(8,128)(2,1)S(1)}, u32[]{:S(2)}, u32[]{:S(2)}) collective-permute-start(bf16[2,128,256]{2,1,0:T(8,128)(2,1)S(1)} %get-tuple-element.54), channel_id=1, source_target_pairs={{0,8},{1,10},{2,9},{3,12},{4,11},{5,14},{6,13},{7,15},{8,0},{9,1},... | collective-permute-start | bytes 393224 | tf_op jit(solution)/shard_map/ppermute | solution.py:422
  13.0 16.3 %collective-permute-start.10 = (bf16[10,128,128]{2,1,0:T(8,128)(2,1)S(1)}, bf16[10,128,128]{2,1,0:T(8,128)(2,1)S(1)}, u32[]{:S(2)}, u32[]{:S(2)}) collective-permute-start(bf16[10,128,128]{2,1,0:T(8,128)(2,1)S(1)} %get-tuple-element.66), channel_id=1, source_target_pairs={{16,17},{24,25},{0,8},{8,0},{17,16},{25,24},{1,9},{9,1},{18,19},{2... | collective-permute-start | bytes 983048 | tf_op jit(solution)/shard_map/ppermute | solution.py:414
  14.3 15.3 %collective-permute-start.11 = (bf16[10,128,128]{2,1,0:T(8,128)(2,1)S(1)}, bf16[10,128,128]{2,1,0:T(8,128)(2,1)S(1)}, u32[]{:S(2)}, u32[]{:S(2)}) collective-permute-start(bf16[10,128,128]{2,1,0:T(8,128)(2,1)S(1)} %get-tuple-element.67), channel_id=1, source_target_pairs={{0,8},{8,0},{16,24},{24,16},{17,18},{25,26},{1,9},{9,1},{18,17},{2... | collective-permute-start | bytes 983048 | tf_op jit(solution)/shard_map/ppermute | solution.py:414
  15.0 3.7 %collective-permute-start.5 = (bf16[2,128,256]{2,1,0:T(8,128)(2,1)S(1)}, bf16[2,128,256]{2,1,0:T(8,128)(2,1)S(1)}, u32[]{:S(2)}, u32[]{:S(2)}) collective-permute-start(bf16[2,128,256]{2,1,0:T(8,128)(2,1)S(1)} %get-tuple-element.56), channel_id=1, source_target_pairs={{8,9},{0,2},{16,24},{24,16},{9,8},{1,3},{17,25},{25,17},{10,11},{2... | collective-permute-start | bytes 393224 | tf_op jit(solution)/shard_map/ppermute | solution.py:414
  15.5 3.3 %collective-permute-start.6 = (bf16[2,128,256]{2,1,0:T(8,128)(2,1)S(1)}, bf16[2,128,256]{2,1,0:T(8,128)(2,1)S(1)}, u32[]{:S(2)}, u32[]{:S(2)}) collective-permute-start(bf16[2,128,256]{2,1,0:T(8,128)(2,1)S(1)} %get-tuple-element.57), channel_id=1, source_target_pairs={{0,8},{8,0},{16,24},{24,16},{9,10},{1,3},{17,25},{25,17},{10,9},{2... | collective-permute-start | bytes 393224 | tf_op jit(solution)/shard_map/ppermute | solution.py:414
  19.3 17.0 %collective-permute-start.12 = (bf16[8,128,128]{2,1,0:T(8,128)(2,1)S(1)}, bf16[8,128,128]{2,1,0:T(8,128)(2,1)S(1)}, u32[]{:S(2)}, u32[]{:S(2)}) collective-permute-start(bf16[8,128,128]{2,1,0:T(8,128)(2,1)S(1)} %get-tuple-element.68.refs_9_), channel_id=1, source_target_pairs={{8,16},{9,17},{10,18},{11,19},{12,20},{13,21},{14,22},{15,23},{0,8... | collective-permute-start | bytes 786440 | tf_op jit(solution)/shard_map/ppermute | solution.py:421
  27.4 4.7 %collective-permute-start.13 = (bf16[4,128,128]{2,1,0:T(8,128)(2,1)S(1)}, bf16[4,128,128]{2,1,0:T(8,128)(2,1)S(1)}, u32[]{:S(2)}, u32[]{:S(2)}) collective-permute-start(bf16[4,128,128]{2,1,0:T(8,128)(2,1)S(1)} %get-tuple-element.69), channel_id=1, source_target_pairs={{8,17},{9,16},{10,19},{11,18},{12,21},{13,20},{14,23},{15,22},{0,8... | collective-permute-start | bytes 393224 | tf_op jit(solution)/shard_map/ppermute | solution.py:422
  28.8 11.7 %collective-permute-start.7 = (bf16[8,128,128]{2,1,0:T(8,128)(2,1)S(1)}, bf16[8,128,128]{2,1,0:T(8,128)(2,1)S(1)}, u32[]{:S(2)}, u32[]{:S(2)}) collective-permute-start(bf16[8,128,128]{2,1,0:T(8,128)(2,1)S(1)} %get-tuple-element.61.refs_9_), channel_id=1, source_target_pairs={{8,16},{9,17},{10,18},{11,19},{12,20},{13,21},{14,22},{15,23},{0,8... | collective-permute-start | bytes 786440 | tf_op jit(solution)/shard_map/ppermute | solution.py:421
  29.3 7.0 %collective-permute-start.14 = (bf16[4,128,128]{2,1,0:T(8,128)(2,1)S(1)}, bf16[4,128,128]{2,1,0:T(8,128)(2,1)S(1)}, u32[]{:S(2)}, u32[]{:S(2)}) collective-permute-start(bf16[4,128,128]{2,1,0:T(8,128)(2,1)S(1)} %get-tuple-element.70), channel_id=1, source_target_pairs={{8,16},{9,18},{10,17},{11,20},{12,19},{13,22},{14,21},{15,23},{0,8... | collective-permute-start | bytes 393224 | tf_op jit(solution)/shard_map/ppermute | solution.py:422
  29.6 10.0 %collective-permute-start.8 = (bf16[4,128,128]{2,1,0:T(8,128)(2,1)S(1)}, bf16[4,128,128]{2,1,0:T(8,128)(2,1)S(1)}, u32[]{:S(2)}, u32[]{:S(2)}) collective-permute-start(bf16[4,128,128]{2,1,0:T(8,128)(2,1)S(1)} %get-tuple-element.62), channel_id=1, source_target_pairs={{8,17},{9,16},{10,19},{11,18},{12,21},{13,20},{14,23},{15,22},{0,8... | collective-permute-start | bytes 393224 | tf_op jit(solution)/shard_map/ppermute | solution.py:422
  32.1 8.4 %collective-permute-start.9 = (bf16[4,128,128]{2,1,0:T(8,128)(2,1)S(1)}, bf16[4,128,128]{2,1,0:T(8,128)(2,1)S(1)}, u32[]{:S(2)}, u32[]{:S(2)}) collective-permute-start(bf16[4,128,128]{2,1,0:T(8,128)(2,1)S(1)} %get-tuple-element.63), channel_id=1, source_target_pairs={{8,16},{9,18},{10,17},{11,20},{12,19},{13,22},{14,21},{15,23},{0,8... | collective-permute-start | bytes 393224 | tf_op jit(solution)/shard_map/ppermute | solution.py:422
  36.9 6.0 %collective-permute-start.19 = (bf16[4,128,128]{2,1,0:T(8,128)(2,1)S(1)}, bf16[4,128,128]{2,1,0:T(8,128)(2,1)S(1)}, u32[]{:S(2)}, u32[]{:S(2)}) collective-permute-start(bf16[4,128,128]{2,1,0:T(8,128)(2,1)S(1)} %get-tuple-element.79), channel_id=1, source_target_pairs={{0,16},{1,17},{2,18},{3,19},{4,20},{5,21},{6,22},{7,23},{8,0},{9,1... | collective-permute-start | bytes 393224 | tf_op jit(solution)/shard_map/ppermute | solution.py:422
  37.2 7.2 %collective-permute-start.20 = (bf16[4,128,128]{2,1,0:T(8,128)(2,1)S(1)}, bf16[4,128,128]{2,1,0:T(8,128)(2,1)S(1)}, u32[]{:S(2)}, u32[]{:S(2)}) collective-permute-start(bf16[4,128,128]{2,1,0:T(8,128)(2,1)S(1)} %get-tuple-element.80), channel_id=1, source_target_pairs={{0,16},{1,17},{2,18},{3,19},{4,20},{5,21},{6,22},{7,23},{8,0},{9,1... | collective-permute-start | bytes 393224 | tf_op jit(solution)/shard_map/ppermute | solution.py:422
  39.6 5.4 %collective-permute-start.21 = (bf16[4,128,128]{2,1,0:T(8,128)(2,1)S(1)}, bf16[4,128,128]{2,1,0:T(8,128)(2,1)S(1)}, u32[]{:S(2)}, u32[]{:S(2)}) collective-permute-start(bf16[4,128,128]{2,1,0:T(8,128)(2,1)S(1)} %get-tuple-element.81), channel_id=1, source_target_pairs={{0,8},{1,9},{2,10},{3,11},{4,12},{5,13},{6,14},{7,15},{8,0},{9,1},... | collective-permute-start | bytes 393224 | tf_op jit(solution)/shard_map/ppermute | solution.py:421
  41.1 5.8 %collective-permute-start.15 = (bf16[4,128,128]{2,1,0:T(8,128)(2,1)S(1)}, bf16[4,128,128]{2,1,0:T(8,128)(2,1)S(1)}, u32[]{:S(2)}, u32[]{:S(2)}) collective-permute-start(bf16[4,128,128]{2,1,0:T(8,128)(2,1)S(1)} %get-tuple-element.73), channel_id=1, source_target_pairs={{0,16},{1,17},{2,18},{3,19},{4,20},{5,21},{6,22},{7,23},{8,0},{9,1... | collective-permute-start | bytes 393224 | tf_op jit(solution)/shard_map/ppermute | solution.py:422
  41.8 3.1 %collective-permute-start.22 = (bf16[4,128,128]{2,1,0:T(8,128)(2,1)S(1)}, bf16[4,128,128]{2,1,0:T(8,128)(2,1)S(1)}, u32[]{:S(2)}, u32[]{:S(2)}) collective-permute-start(bf16[4,128,128]{2,1,0:T(8,128)(2,1)S(1)} %get-tuple-element.82), channel_id=1, source_target_pairs={{0,8},{1,9},{2,10},{3,11},{4,12},{5,13},{6,14},{7,15},{8,0},{9,1},... | collective-permute-start | bytes 393224 | tf_op jit(solution)/shard_map/ppermute | solution.py:421
  42.9 5.6 %collective-permute-start.16 = (bf16[4,128,128]{2,1,0:T(8,128)(2,1)S(1)}, bf16[4,128,128]{2,1,0:T(8,128)(2,1)S(1)}, u32[]{:S(2)}, u32[]{:S(2)}) collective-permute-start(bf16[4,128,128]{2,1,0:T(8,128)(2,1)S(1)} %get-tuple-element.74), channel_id=1, source_target_pairs={{0,16},{1,17},{2,18},{3,19},{4,20},{5,21},{6,22},{7,23},{8,0},{9,1... | collective-permute-start | bytes 393224 | tf_op jit(solution)/shard_map/ppermute | solution.py:422
  44.3 4.2 %collective-permute-start.17 = (bf16[4,128,128]{2,1,0:T(8,128)(2,1)S(1)}, bf16[4,128,128]{2,1,0:T(8,128)(2,1)S(1)}, u32[]{:S(2)}, u32[]{:S(2)}) collective-permute-start(bf16[4,128,128]{2,1,0:T(8,128)(2,1)S(1)} %get-tuple-element.75), channel_id=1, source_target_pairs={{0,8},{1,9},{2,10},{3,11},{4,12},{5,13},{6,14},{7,15},{8,0},{9,1},... | collective-permute-start | bytes 393224 | tf_op jit(solution)/shard_map/ppermute | solution.py:421
  44.9 3.7 %collective-permute-start.18 = (bf16[4,128,128]{2,1,0:T(8,128)(2,1)S(1)}, bf16[4,128,128]{2,1,0:T(8,128)(2,1)S(1)}, u32[]{:S(2)}, u32[]{:S(2)}) collective-permute-start(bf16[4,128,128]{2,1,0:T(8,128)(2,1)S(1)} %get-tuple-element.76), channel_id=1, source_target_pairs={{0,8},{1,9},{2,10},{3,11},{4,12},{5,13},{6,14},{7,15},{8,0},{9,1},... | collective-permute-start | bytes 393224 | tf_op jit(solution)/shard_map/ppermute | solution.py:421

commit v16 on v15

--- a/solution.py
+++ b/solution.py
@@ -35,10 +35,10 @@
     return {g: g ^ 1 for g in range(chain) if g not in taken}
 
 
-def hop_pairs(group, mate, chain, rows):
+def hop_pairs(group, mate, chain, rows, ahead=False):
     if group % 2 == 0:
         moves = swap_groups(chain)
-        if group and mate is not same_row:
+        if group and ahead:
             moves.update({group + 1: group - 1, group - 1: group - 2, group - 2: group})
     else:
         moves = swap_groups(chain, range(group - 1, group + 3))
@@ -415,11 +415,11 @@
             for value, mate in zip(values, mates)
         ]
 
-    def travel(group, centre, sides):
+    def travel(group, centre, sides, ahead):
         *sides, = sides
         centres = sides[2:] or [centre]
         kinds = [lax.ppermute(value, AXES, hop_pairs(group, same_row, chain, rows)) for value in centres]
-        kinds += [lax.ppermute(value, AXES, hop_pairs(group, mate, chain, rows)) for value, mate in zip(sides, mates)]
+        kinds += [lax.ppermute(value, AXES, hop_pairs(group, mate, chain, rows, ahead)) for value, mate in zip(sides, mates)]
         return [kinds[i] for i in (2, 3, 0, 1)] if len(kinds) > 3 else kinds
 
     def call(kernel, name, in_specs, out_shape, out_specs=None, **more):
@@ -487,7 +487,7 @@
         scratch_shapes=[padded],
     )(meta, first, *sides, wide_a, base_0)
     wide_b, base_b = prepare(1, after(meta, solved))
-    arrived = travel(0, solved, sends)
+    arrived = travel(0, solved, sends, False)
 
     later_w = exchange(range(2, chain), after(edge_w[2:], sides))
     edges, = call(
@@ -518,7 +518,7 @@
 
     for group in range(2, chain):
         final = group == chain - 1
-        arrived = [travel(group - 1, solved, sends) for solved, *sends in sent]
+        arrived = [travel(group - 1, solved, sends, i == 0) for i, (solved, *sends) in enumerate(sent)]
         made = []
         for chunk in range(CHUNKS):
             stages = final and chunk == CHUNKS - 1

time: 52.4 us -> 52.4 us (level)
  transfers between devices with their start and end apart: 23 -> 23, of which waited for: 6 -> 7; matrix products, arithmetic and copies ran while one was open for 0% -> 0% of each run, Pallas kernels for 23% -> 23%
where the time goes in v16:
time: 52.4 us; the launch traced here: 51.4 us
  starting transfers between devices  26 us (50%)
  Pallas kernels  18.1 us (35%)
  waiting for transfers between devices  7.07 us (13%)
    ppermute x7, starting transfers between devices, travel(): lax.ppermute(value, AXES, hop_pairs(group, same_row, chain, rows))  13.4 us
    ppermute x10, starting transfers between devices, travel(): lax.ppermute(value, AXES, hop_pairs(group, mate, chain, rows, ahead))  9.45 us
    pallas_call x2, Pallas kernels, prepare(): call(functools.partial(prepare_kernel, turn), f'prepare_{turn}', [SMEM] +...  6.32 us
    pallas_call x4, Pallas kernels, per_device(): call(functools.partial(later_step, group, chunk, final), f'step_{group}_{...  5.93 us
    ppermute x10, waiting for transfers between devices, travel(): lax.ppermute(value, AXES, hop_pairs(group, mate, chain, rows, ahead))  5.05 us
    ppermute x6, starting transfers between devices, exchange(): lax.ppermute(value, AXES, inner_pairs(groups, mate, chain, rows, idle))  3.19 us
    pallas_call x1, Pallas kernels, per_device(): call(first_kernel, 'first_level', [SMEM] + [HBM] * 5, [whole, *(shape for...  3.05 us
    ppermute x6, waiting for transfers between devices, exchange(): lax.ppermute(value, AXES, inner_pairs(groups, mate, chain, rows, idle))  2.01 us
  transfers between devices with their start and end apart: 23, of which 7 were waited for; matrix products, arithmetic and copies ran while one was open for 0% of the time, Pallas kernels for 23%

profile of v16, /device:TPU:11, one launch (start us, length us, event | category | flops | bytes accessed | tf_op | source)
XLA Modules:
  0.0 51.4 jit_solution(8065564245478037841)
XLA Ops:
  0.0 0.1 stack.31.meta
  0.1 3.0 %first_level.1 = (bf16[8,128,256]{2,1,0:T(8,128)(2,1)S(1)}, bf16[4,128,128]{2,1,0:T(8,128)(2,1)S(1)}, bf16[4,128,128]{2,1,0:T(8,128)(2,1)S(1)}, bf16[10,128,128]...) custom-call(s32[5]{0:T(128)S(1)} %stack.31.meta, s32[6,2,8]{2,1,0:T(2,128)} %bitcast.7, f32[6,2,8]{2,1,0:T(2,128)} %bitcast.10, ...), custom_call_target="tpu_custom_call" | custom-call | tf_op jit(solution)/shard_map/first_level/pallas_call | solution.py:442
  3.1 1.3 %collective-permute-start = (bf16[4,128,128]{2,1,0:T(8,128)(2,1)S(1)}, bf16[4,128,128]{2,1,0:T(8,128)(2,1)S(1)}, u32[]{:S(2)}, u32[]{:S(2)}) collective-permute-start(bf16[4,128,128]{2,1,0:T(8,128)(2,1)S(1)} %get-tuple-element.48), channel_id=1, source_target_pairs={{0,1},{16,17},{24,25},{8,10},{1,0},{17,16},{25,24},{9,11},{2,3},{1... | collective-permute-start | bytes 393224 | tf_op jit(solution)/shard_map/ppermute | solution.py:414
  4.4 0.1 collective-permute-start.1
  4.5 3.2 %prepare_0.1 = (bf16[4,256,768]{2,1,0:T(8,128)(2,1)S(1)}, f32[8,128,256]{2,1,0:T(8,128)S(1)}) custom-call(s32[5]{0:T(128)S(1)} %stack.31.meta, s32[6,2,8]{2,1,0:T(2,128)} %bitcast.8, f32[6,2,8]{2,1,0:T(2,128)} %bitcast.11, bf16[2,8,6,128,128]{4,3,2,1,0:T(8,128)(2,1)} %lower_hbm.5, bf16[2,8,128,128]{3,2,1,0:T(8,128)(2,1)} %inverse_hbm.5, ...), custom_call_target="tpu_custom_call" | custom-call | tf_op jit(solution)/shard_map/prepare_0/pallas_call | solution.py:463
  7.7 1.6 %collective-permute-done.even_in.even_a = bf16[4,128,128]{2,1,0:T(8,128)(2,1)S(1)} collective-permute-done((bf16[4,128,128]{2,1,0:T(8,128)(2,1)S(1)}, bf16[4,128,128]{2,1,0:T(8,128)(2,1)S(1)}, u32[]{:S(2)}, u32[]{:S(2)}) %collective-permute-start) | collective-permute-done | bytes 131104 | tf_op jit(solution)/shard_map/ppermute | solution.py:414
  9.3 0.5 %step_0.1 = (bf16[8,128,256]{2,1,0:T(8,128)(2,1)S(1)}, bf16[2,128,256]{2,1,0:T(8,128)(2,1)S(1)}, bf16[2,128,256]{2,1,0:T(8,128)(2,1)S(1)}) custom-call(s32[5]{0:T(128)S(1)} %stack.31.meta, bf16[8,128,256]{2,1,0:T(8,128)(2,1)S(1)} %get-tuple-element.47.own.first.refs_4_.refs_5_, bf16[4,128,128]{2,1,0:T(8,128)(2,1)S(1)} %collective-permute-done.even_in.even_a, ...), custom_call_target="tpu_custom_call" | custom-call | tf_op jit(solution)/shard_map/step_0/pallas_call | solution.py:482
  9.8 2.7 %collective-permute-start.2 = (bf16[8,128,256]{2,1,0:T(8,128)(2,1)S(1)}, bf16[8,128,256]{2,1,0:T(8,128)(2,1)S(1)}, u32[]{:S(2)}, u32[]{:S(2)}) collective-permute-start(bf16[8,128,256]{2,1,0:T(8,128)(2,1)S(1)} %get-tuple-element.52.old_b), channel_id=1, source_target_pairs={{0,8},{1,9},{2,10},{3,11},{4,12},{5,13},{6,14},{7,15},{8,0},{9,1},... | collective-permute-start | bytes 1572872 | tf_op jit(solution)/shard_map/ppermute | solution.py:421
  12.5 0.1 collective-permute-start.3
  12.6 0.4 collective-permute-start.4
  13.0 1.2 %collective-permute-start.10 = (bf16[10,128,128]{2,1,0:T(8,128)(2,1)S(1)}, bf16[10,128,128]{2,1,0:T(8,128)(2,1)S(1)}, u32[]{:S(2)}, u32[]{:S(2)}) collective-permute-start(bf16[10,128,128]{2,1,0:T(8,128)(2,1)S(1)} %get-tuple-element.66), channel_id=1, source_target_pairs={{16,17},{24,25},{0,8},{8,0},{17,16},{25,24},{1,9},{9,1},{18,19},{2... | collective-permute-start | bytes 983048 | tf_op jit(solution)/shard_map/ppermute | solution.py:414
  14.3 0.0 collective-permute-start.11
  14.3 0.0 collective-permute-done.3.even_in
  14.3 0.2 collective-permute-done.4.odd_in
  14.4 0.0 collective-permute-done.2.centre
  14.5 0.6 %step_1.1 = (bf16[2,8,128,256]{3,2,1,0:T(8,128)(2,1)}, bf16[8,128,256]{2,1,0:T(8,128)(2,1)S(1)}, bf16[2,128,256]{2,1,0:T(8,128)(2,1)S(1)}, bf16[2,128,256]{2,1,0:T(8,128)(2,1)S(1)}) custom-call(s32[5]{0:T(128)S(1)} %stack.31.meta, bf16[8,128,256]{2,1,0:T(8,128)(2,1)S(1)} %collective-permute-done.2.centre, ...), custom_call_target="tpu_custom_call" | custom-call | tf_op jit(solution)/shard_map/step_1/pallas_call | solution.py:497
  15.0 0.4 collective-permute-start.5
  15.5 0.1 collective-permute-start.6
  15.6 3.2 %prepare_1.1 = (bf16[4,256,768]{2,1,0:T(8,128)(2,1)S(1)}, f32[8,128,256]{2,1,0:T(8,128)S(1)}) custom-call(s32[5]{0:T(128)S(1)} %stack.31.meta, s32[6,2,8]{2,1,0:T(2,128)} %bitcast.9, f32[6,2,8]{2,1,0:T(2,128)} %bitcast.12, bf16[2,8,6,128,128]{4,3,2,1,0:T(8,128)(2,1)} %lower_hbm.5, bf16[2,8,128,128]{3,2,1,0:T(8,128)(2,1)} %inverse_hbm.5, ...), custom_call_target="tpu_custom_call" | custom-call | tf_op jit(solution)/shard_map/prepare_1/pallas_call | solution.py:463
  18.8 0.0 collective-permute-done.5.even_in
  18.8 0.6 %step_1_0.1 = (bf16[8,128,128]{2,1,0:T(8,128)(2,1)S(1)}, bf16[4,128,128]{2,1,0:T(8,128)(2,1)S(1)}, bf16[4,128,128]{2,1,0:T(8,128)(2,1)S(1)}) custom-call(s32[5]{0:T(128)S(1)} %stack.31.meta, bf16[8,128,256]{2,1,0:T(8,128)(2,1)S(1)} %get-tuple-element.55.own.refs_8_, bf16[2,128,256]{2,1,0:T(8,128)(2,1)S(1)} %collective-permute-done.5.even_in, ...), custom_call_target="tpu_custom_call" | custom-call | tf_op jit(solution)/shard_map/step_1_0/pallas_call | solution.py:510
  19.3 8.0 %collective-permute-start.12 = (bf16[8,128,128]{2,1,0:T(8,128)(2,1)S(1)}, bf16[8,128,128]{2,1,0:T(8,128)(2,1)S(1)}, u32[]{:S(2)}, u32[]{:S(2)}) collective-permute-start(bf16[8,128,128]{2,1,0:T(8,128)(2,1)S(1)} %get-tuple-element.68.refs_9_), channel_id=1, source_target_pairs={{8,16},{9,17},{10,18},{11,19},{12,20},{13,21},{14,22},{15,23},{0,8... | collective-permute-start | bytes 786440 | tf_op jit(solution)/shard_map/ppermute | solution.py:421
  27.4 0.8 %collective-permute-start.13 = (bf16[4,128,128]{2,1,0:T(8,128)(2,1)S(1)}, bf16[4,128,128]{2,1,0:T(8,128)(2,1)S(1)}, u32[]{:S(2)}, u32[]{:S(2)}) collective-permute-start(bf16[4,128,128]{2,1,0:T(8,128)(2,1)S(1)} %get-tuple-element.69), channel_id=1, source_target_pairs={{8,17},{9,16},{10,19},{11,18},{12,21},{13,20},{14,23},{15,22},{0,8... | collective-permute-start | bytes 393224 | tf_op jit(solution)/shard_map/ppermute | solution.py:422
  28.2 0.5 %step_1_1.1 = (bf16[8,128,128]{2,1,0:T(8,128)(2,1)S(1)}, bf16[4,128,128]{2,1,0:T(8,128)(2,1)S(1)}, bf16[4,128,128]{2,1,0:T(8,128)(2,1)S(1)}) custom-call(s32[5]{0:T(128)S(1)} %stack.31.meta, bf16[8,128,256]{2,1,0:T(8,128)(2,1)S(1)} %get-tuple-element.55.own.refs_8_, bf16[2,128,256]{2,1,0:T(8,128)(2,1)S(1)} %collective-permute-done.5.even_in, ...), custom_call_target="tpu_custom_call" | custom-call | tf_op jit(solution)/shard_map/step_1_1/pallas_call | solution.py:510
  28.8 0.1 collective-permute-start.7
  28.9 0.4 collective-permute-done.10.even_b
  29.3 0.2 collective-permute-start.14
  29.6 0.7 %collective-permute-start.8 = (bf16[4,128,128]{2,1,0:T(8,128)(2,1)S(1)}, bf16[4,128,128]{2,1,0:T(8,128)(2,1)S(1)}, u32[]{:S(2)}, u32[]{:S(2)}) collective-permute-start(bf16[4,128,128]{2,1,0:T(8,128)(2,1)S(1)} %get-tuple-element.62), channel_id=1, source_target_pairs={{8,17},{9,16},{10,19},{11,18},{12,21},{13,20},{14,23},{15,22},{0,8... | collective-permute-start | bytes 393224 | tf_op jit(solution)/shard_map/ppermute | solution.py:422
  30.3 1.8 %collective-permute-done.13.refs_1_ = bf16[4,128,128]{2,1,0:T(8,128)(2,1)S(1)} collective-permute-done((bf16[4,128,128]{2,1,0:T(8,128)(2,1)S(1)}, bf16[4,128,128]{2,1,0:T(8,128)(2,1)S(1)}, u32[]{:S(2)}, u32[]{:S(2)}) %collective-permute-start.13) | collective-permute-done | bytes 131104 | tf_op jit(solution)/shard_map/ppermute | solution.py:422
  32.1 2.5 %collective-permute-start.9 = (bf16[4,128,128]{2,1,0:T(8,128)(2,1)S(1)}, bf16[4,128,128]{2,1,0:T(8,128)(2,1)S(1)}, u32[]{:S(2)}, u32[]{:S(2)}) collective-permute-start(bf16[4,128,128]{2,1,0:T(8,128)(2,1)S(1)} %get-tuple-element.63), channel_id=1, source_target_pairs={{8,16},{9,18},{10,17},{11,20},{12,19},{13,22},{14,21},{15,23},{0,8... | collective-permute-start | bytes 393224 | tf_op jit(solution)/shard_map/ppermute | solution.py:422
  34.6 0.6 %order.1.refs_3_.refs_4_ = bf16[2,14,128,128]{3,2,1,0:T(8,128)(2,1)S(1)} custom-call(s32[5]{0:T(128)S(1)} %stack.31.meta, bf16[4,128,128]{2,1,0:T(8,128)(2,1)S(1)} %collective-permute-done.even_in.even_a, bf16[4,128,128]{2,1,0:T(8,128)(2,1)S(1)} %collective-permute-done.1.odd_in.odd_a, bf16[10,128,128]{2,1,0:T(8,128)(2,1)S(1)} %collective-permute-done.10.even_b, ...), custom_call_target="tpu_custom_call" | custom-call | tf_op jit(solution)/shard_map/order/pallas_call | solution.py:493
  35.2 1.1 %collective-permute-done.14.refs_2_ = bf16[4,128,128]{2,1,0:T(8,128)(2,1)S(1)} collective-permute-done((bf16[4,128,128]{2,1,0:T(8,128)(2,1)S(1)}, bf16[4,128,128]{2,1,0:T(8,128)(2,1)S(1)}, u32[]{:S(2)}, u32[]{:S(2)}) %collective-permute-start.14) | collective-permute-done | bytes 131104 | tf_op jit(solution)/shard_map/ppermute | solution.py:422
  36.3 0.0 collective-permute-done.12.refs_0_
  36.3 0.6 %step_2_0.1 = (bf16[2,8,128,256]{3,2,1,0:T(8,128)(2,1)}, bf16[8,128,128]{2,1,0:T(8,128)(2,1)S(1)}, bf16[8,128,128]{2,1,0:T(8,128)(2,1)S(1)}, bf16[4,128,128]{2,1...) custom-call(s32[5]{0:T(128)S(1)} %stack.31.meta, ...), custom_call_target="tpu_custom_call", output_to_operand_aliasing={{0}: (11, {})} | custom-call | tf_op jit(solution)/shard_map/step_2_0/pallas_call | solution.py:529
  36.9 0.3 collective-permute-start.19
  37.2 2.4 %collective-permute-start.20 = (bf16[4,128,128]{2,1,0:T(8,128)(2,1)S(1)}, bf16[4,128,128]{2,1,0:T(8,128)(2,1)S(1)}, u32[]{:S(2)}, u32[]{:S(2)}) collective-permute-start(bf16[4,128,128]{2,1,0:T(8,128)(2,1)S(1)} %get-tuple-element.80), channel_id=1, source_target_pairs={{0,16},{1,17},{2,18},{3,19},{4,20},{5,21},{6,22},{7,23},{8,0},{9,1... | collective-permute-start | bytes 393224 | tf_op jit(solution)/shard_map/ppermute | solution.py:422
  39.6 0.0 collective-permute-done.8.refs_1_
  39.6 0.9 %collective-permute-start.21 = (bf16[4,128,128]{2,1,0:T(8,128)(2,1)S(1)}, bf16[4,128,128]{2,1,0:T(8,128)(2,1)S(1)}, u32[]{:S(2)}, u32[]{:S(2)}) collective-permute-start(bf16[4,128,128]{2,1,0:T(8,128)(2,1)S(1)} %get-tuple-element.81), channel_id=1, source_target_pairs={{0,8},{1,9},{2,10},{3,11},{4,12},{5,13},{6,14},{7,15},{8,0},{9,1},... | collective-permute-start | bytes 393224 | tf_op jit(solution)/shard_map/ppermute | solution.py:421
  40.5 0.6 %step_2_1.1 = (bf16[2,8,128,256]{3,2,1,0:T(8,128)(2,1)}, bf16[8,128,128]{2,1,0:T(8,128)(2,1)S(1)}, bf16[8,128,128]{2,1,0:T(8,128)(2,1)S(1)}, bf16[4,128,128]{2,1...) custom-call(s32[5]{0:T(128)S(1)} %stack.31.meta, ...), custom_call_target="tpu_custom_call", output_to_operand_aliasing={{0}: (11, {})} | custom-call | tf_op jit(solution)/shard_map/step_2_1/pallas_call | solution.py:529
  41.1 1.5 %collective-permute-start.15 = (bf16[4,128,128]{2,1,0:T(8,128)(2,1)S(1)}, bf16[4,128,128]{2,1,0:T(8,128)(2,1)S(1)}, u32[]{:S(2)}, u32[]{:S(2)}) collective-permute-start(bf16[4,128,128]{2,1,0:T(8,128)(2,1)S(1)} %get-tuple-element.73), channel_id=1, source_target_pairs={{0,8},{1,9},{2,10},{3,11},{4,12},{5,13},{6,14},{7,15},{8,0},{9,1},... | collective-permute-start | bytes 393224 | tf_op jit(solution)/shard_map/ppermute | solution.py:422
  42.6 0.4 collective-permute-start.22
  42.9 0.6 %collective-permute-start.16 = (bf16[4,128,128]{2,1,0:T(8,128)(2,1)S(1)}, bf16[4,128,128]{2,1,0:T(8,128)(2,1)S(1)}, u32[]{:S(2)}, u32[]{:S(2)}) collective-permute-start(bf16[4,128,128]{2,1,0:T(8,128)(2,1)S(1)} %get-tuple-element.74), channel_id=1, source_target_pairs={{0,8},{1,9},{2,10},{3,11},{4,12},{5,13},{6,14},{7,15},{8,0},{9,1},... | collective-permute-start | bytes 393224 | tf_op jit(solution)/shard_map/ppermute | solution.py:422
  43.5 0.2 collective-permute-done.20.refs_1_
  43.7 1.2 %collective-permute-start.17 = (bf16[4,128,128]{2,1,0:T(8,128)(2,1)S(1)}, bf16[4,128,128]{2,1,0:T(8,128)(2,1)S(1)}, u32[]{:S(2)}, u32[]{:S(2)}) collective-permute-start(bf16[4,128,128]{2,1,0:T(8,128)(2,1)S(1)} %get-tuple-element.75), channel_id=1, source_target_pairs={{0,8},{1,9},{2,10},{3,11},{4,12},{5,13},{6,14},{7,15},{8,0},{9,1},... | collective-permute-start | bytes 393224 | tf_op jit(solution)/shard_map/ppermute | solution.py:421
  44.9 0.0 collective-permute-start.18
  44.9 1.9 %step_3_0.1 = (bf16[2,8,128,256]{3,2,1,0:T(8,128)(2,1)}, bf16[8,128,128]{2,1,0:T(8,128)(2,1)S(1)}, bf16[8,128,128]{2,1,0:T(8,128)(2,1)S(1)}) custom-call(s32[5]{0:T(128)S(1)} %stack.31.meta, bf16[4,128,128]{2,1,0:T(8,128)(2,1)S(1)} %collective-permute-done.19.refs_0_, ...), custom_call_target="tpu_custom_call", output_to_operand_aliasing={{0}: (12, {})} | custom-call | tf_op jit(solution)/shard_map/step_3_0/pallas_call | solution.py:529
  46.9 1.7 %collective-permute-done.16.refs_1_ = bf16[4,128,128]{2,1,0:T(8,128)(2,1)S(1)} collective-permute-done((bf16[4,128,128]{2,1,0:T(8,128)(2,1)S(1)}, bf16[4,128,128]{2,1,0:T(8,128)(2,1)S(1)}, u32[]{:S(2)}, u32[]{:S(2)}) %collective-permute-start.16) | collective-permute-done | bytes 131104 | tf_op jit(solution)/shard_map/ppermute | solution.py:422
  48.6 2.9 %step_3_1.1 = bf16[2,8,128,256]{3,2,1,0:T(8,128)(2,1)} custom-call(s32[5]{0:T(128)S(1)} %stack.31.meta, bf16[4,128,128]{2,1,0:T(8,128)(2,1)S(1)} %collective-permute-done.15.refs_0_, bf16[4,128,128]{2,1,0:T(8,128)(2,1)S(1)} %collective-permute-done.16.refs_1_, ...), custom_call_target="tpu_custom_call", output_to_operand_aliasing={{}: (14, {})} | custom-call | tf_op jit(solution)/shard_map/step_3_1/pallas_call | solution.py:529
  (11 shorter events, 0.0 us)
Async XLA Ops:
  3.1 6.1 %collective-permute-start = (bf16[4,128,128]{2,1,0:T(8,128)(2,1)S(1)}, bf16[4,128,128]{2,1,0:T(8,128)(2,1)S(1)}, u32[]{:S(2)}, u32[]{:S(2)}) collective-permute-start(bf16[4,128,128]{2,1,0:T(8,128)(2,1)S(1)} %get-tuple-element.48), channel_id=1, source_target_pairs={{0,1},{16,17},{24,25},{8,10},{1,0},{17,16},{25,24},{9,11},{2,3},{1... | collective-permute-start | bytes 393224 | tf_op jit(solution)/shard_map/ppermute | solution.py:414
  4.4 4.8 %collective-permute-start.1 = (bf16[4,128,128]{2,1,0:T(8,128)(2,1)S(1)}, bf16[4,128,128]{2,1,0:T(8,128)(2,1)S(1)}, u32[]{:S(2)}, u32[]{:S(2)}) collective-permute-start(bf16[4,128,128]{2,1,0:T(8,128)(2,1)S(1)} %get-tuple-element.49), channel_id=1, source_target_pairs={{0,8},{8,0},{16,24},{24,16},{1,2},{17,18},{25,26},{9,11},{2,1},{18... | collective-permute-start | bytes 393224 | tf_op jit(solution)/shard_map/ppermute | solution.py:414
  9.8 4.6 %collective-permute-start.2 = (bf16[8,128,256]{2,1,0:T(8,128)(2,1)S(1)}, bf16[8,128,256]{2,1,0:T(8,128)(2,1)S(1)}, u32[]{:S(2)}, u32[]{:S(2)}) collective-permute-start(bf16[8,128,256]{2,1,0:T(8,128)(2,1)S(1)} %get-tuple-element.52.old_b), channel_id=1, source_target_pairs={{0,8},{1,9},{2,10},{3,11},{4,12},{5,13},{6,14},{7,15},{8,0},{9,1},... | collective-permute-start | bytes 1572872 | tf_op jit(solution)/shard_map/ppermute | solution.py:421
  12.5 1.8 %collective-permute-start.3 = (bf16[2,128,256]{2,1,0:T(8,128)(2,1)S(1)}, bf16[2,128,256]{2,1,0:T(8,128)(2,1)S(1)}, u32[]{:S(2)}, u32[]{:S(2)}) collective-permute-start(bf16[2,128,256]{2,1,0:T(8,128)(2,1)S(1)} %get-tuple-element.53), channel_id=1, source_target_pairs={{0,9},{1,8},{2,11},{3,10},{4,13},{5,12},{6,15},{7,14},{8,0},{9,1},... | collective-permute-start | bytes 393224 | tf_op jit(solution)/shard_map/ppermute | solution.py:422
  12.6 1.8 %collective-permute-start.4 = (bf16[2,128,256]{2,1,0:T(8,128)(2,1)S(1)}, bf16[2,128,256]{2,1,0:T(8,128)(2,1)S(1)}, u32[]{:S(2)}, u32[]{:S(2)}) collective-permute-start(bf16[2,128,256]{2,1,0:T(8,128)(2,1)S(1)} %get-tuple-element.54), channel_id=1, source_target_pairs={{0,8},{1,10},{2,9},{3,12},{4,11},{5,14},{6,13},{7,15},{8,0},{9,1},... | collective-permute-start | bytes 393224 | tf_op jit(solution)/shard_map/ppermute | solution.py:422
  13.0 16.3 %collective-permute-start.10 = (bf16[10,128,128]{2,1,0:T(8,128)(2,1)S(1)}, bf16[10,128,128]{2,1,0:T(8,128)(2,1)S(1)}, u32[]{:S(2)}, u32[]{:S(2)}) collective-permute-start(bf16[10,128,128]{2,1,0:T(8,128)(2,1)S(1)} %get-tuple-element.66), channel_id=1, source_target_pairs={{16,17},{24,25},{0,8},{8,0},{17,16},{25,24},{1,9},{9,1},{18,19},{2... | collective-permute-start | bytes 983048 | tf_op jit(solution)/shard_map/ppermute | solution.py:414
  14.3 15.3 %collective-permute-start.11 = (bf16[10,128,128]{2,1,0:T(8,128)(2,1)S(1)}, bf16[10,128,128]{2,1,0:T(8,128)(2,1)S(1)}, u32[]{:S(2)}, u32[]{:S(2)}) collective-permute-start(bf16[10,128,128]{2,1,0:T(8,128)(2,1)S(1)} %get-tuple-element.67), channel_id=1, source_target_pairs={{0,8},{8,0},{16,24},{24,16},{17,18},{25,26},{1,9},{9,1},{18,17},{2... | collective-permute-start | bytes 983048 | tf_op jit(solution)/shard_map/ppermute | solution.py:414
  15.0 3.7 %collective-permute-start.5 = (bf16[2,128,256]{2,1,0:T(8,128)(2,1)S(1)}, bf16[2,128,256]{2,1,0:T(8,128)(2,1)S(1)}, u32[]{:S(2)}, u32[]{:S(2)}) collective-permute-start(bf16[2,128,256]{2,1,0:T(8,128)(2,1)S(1)} %get-tuple-element.56), channel_id=1, source_target_pairs={{8,9},{0,2},{16,24},{24,16},{9,8},{1,3},{17,25},{25,17},{10,11},{2... | collective-permute-start | bytes 393224 | tf_op jit(solution)/shard_map/ppermute | solution.py:414
  15.5 3.3 %collective-permute-start.6 = (bf16[2,128,256]{2,1,0:T(8,128)(2,1)S(1)}, bf16[2,128,256]{2,1,0:T(8,128)(2,1)S(1)}, u32[]{:S(2)}, u32[]{:S(2)}) collective-permute-start(bf16[2,128,256]{2,1,0:T(8,128)(2,1)S(1)} %get-tuple-element.57), channel_id=1, source_target_pairs={{0,8},{8,0},{16,24},{24,16},{9,10},{1,3},{17,25},{25,17},{10,9},{2... | collective-permute-start | bytes 393224 | tf_op jit(solution)/shard_map/ppermute | solution.py:414
  19.3 17.0 %collective-permute-start.12 = (bf16[8,128,128]{2,1,0:T(8,128)(2,1)S(1)}, bf16[8,128,128]{2,1,0:T(8,128)(2,1)S(1)}, u32[]{:S(2)}, u32[]{:S(2)}) collective-permute-start(bf16[8,128,128]{2,1,0:T(8,128)(2,1)S(1)} %get-tuple-element.68.refs_9_), channel_id=1, source_target_pairs={{8,16},{9,17},{10,18},{11,19},{12,20},{13,21},{14,22},{15,23},{0,8... | collective-permute-start | bytes 786440 | tf_op jit(solution)/shard_map/ppermute | solution.py:421
  27.4 4.7 %collective-permute-start.13 = (bf16[4,128,128]{2,1,0:T(8,128)(2,1)S(1)}, bf16[4,128,128]{2,1,0:T(8,128)(2,1)S(1)}, u32[]{:S(2)}, u32[]{:S(2)}) collective-permute-start(bf16[4,128,128]{2,1,0:T(8,128)(2,1)S(1)} %get-tuple-element.69), channel_id=1, source_target_pairs={{8,17},{9,16},{10,19},{11,18},{12,21},{13,20},{14,23},{15,22},{0,8... | collective-permute-start | bytes 393224 | tf_op jit(solution)/shard_map/ppermute | solution.py:422
  28.8 11.7 %collective-permute-start.7 = (bf16[8,128,128]{2,1,0:T(8,128)(2,1)S(1)}, bf16[8,128,128]{2,1,0:T(8,128)(2,1)S(1)}, u32[]{:S(2)}, u32[]{:S(2)}) collective-permute-start(bf16[8,128,128]{2,1,0:T(8,128)(2,1)S(1)} %get-tuple-element.61.refs_9_), channel_id=1, source_target_pairs={{8,16},{9,17},{10,18},{11,19},{12,20},{13,21},{14,22},{15,23},{0,8... | collective-permute-start | bytes 786440 | tf_op jit(solution)/shard_map/ppermute | solution.py:421
  29.3 7.0 %collective-permute-start.14 = (bf16[4,128,128]{2,1,0:T(8,128)(2,1)S(1)}, bf16[4,128,128]{2,1,0:T(8,128)(2,1)S(1)}, u32[]{:S(2)}, u32[]{:S(2)}) collective-permute-start(bf16[4,128,128]{2,1,0:T(8,128)(2,1)S(1)} %get-tuple-element.70), channel_id=1, source_target_pairs={{8,16},{9,18},{10,17},{11,20},{12,19},{13,22},{14,21},{15,23},{0,8... | collective-permute-start | bytes 393224 | tf_op jit(solution)/shard_map/ppermute | solution.py:422
  29.6 10.0 %collective-permute-start.8 = (bf16[4,128,128]{2,1,0:T(8,128)(2,1)S(1)}, bf16[4,128,128]{2,1,0:T(8,128)(2,1)S(1)}, u32[]{:S(2)}, u32[]{:S(2)}) collective-permute-start(bf16[4,128,128]{2,1,0:T(8,128)(2,1)S(1)} %get-tuple-element.62), channel_id=1, source_target_pairs={{8,17},{9,16},{10,19},{11,18},{12,21},{13,20},{14,23},{15,22},{0,8... | collective-permute-start | bytes 393224 | tf_op jit(solution)/shard_map/ppermute | solution.py:422
  32.1 8.4 %collective-permute-start.9 = (bf16[4,128,128]{2,1,0:T(8,128)(2,1)S(1)}, bf16[4,128,128]{2,1,0:T(8,128)(2,1)S(1)}, u32[]{:S(2)}, u32[]{:S(2)}) collective-permute-start(bf16[4,128,128]{2,1,0:T(8,128)(2,1)S(1)} %get-tuple-element.63), channel_id=1, source_target_pairs={{8,16},{9,18},{10,17},{11,20},{12,19},{13,22},{14,21},{15,23},{0,8... | collective-permute-start | bytes 393224 | tf_op jit(solution)/shard_map/ppermute | solution.py:422
  36.9 6.0 %collective-permute-start.19 = (bf16[4,128,128]{2,1,0:T(8,128)(2,1)S(1)}, bf16[4,128,128]{2,1,0:T(8,128)(2,1)S(1)}, u32[]{:S(2)}, u32[]{:S(2)}) collective-permute-start(bf16[4,128,128]{2,1,0:T(8,128)(2,1)S(1)} %get-tuple-element.79), channel_id=1, source_target_pairs={{0,16},{1,17},{2,18},{3,19},{4,20},{5,21},{6,22},{7,23},{8,0},{9,1... | collective-permute-start | bytes 393224 | tf_op jit(solution)/shard_map/ppermute | solution.py:422
  37.2 6.6 %collective-permute-start.20 = (bf16[4,128,128]{2,1,0:T(8,128)(2,1)S(1)}, bf16[4,128,128]{2,1,0:T(8,128)(2,1)S(1)}, u32[]{:S(2)}, u32[]{:S(2)}) collective-permute-start(bf16[4,128,128]{2,1,0:T(8,128)(2,1)S(1)} %get-tuple-element.80), channel_id=1, source_target_pairs={{0,16},{1,17},{2,18},{3,19},{4,20},{5,21},{6,22},{7,23},{8,0},{9,1... | collective-permute-start | bytes 393224 | tf_op jit(solution)/shard_map/ppermute | solution.py:422
  39.6 5.4 %collective-permute-start.21 = (bf16[4,128,128]{2,1,0:T(8,128)(2,1)S(1)}, bf16[4,128,128]{2,1,0:T(8,128)(2,1)S(1)}, u32[]{:S(2)}, u32[]{:S(2)}) collective-permute-start(bf16[4,128,128]{2,1,0:T(8,128)(2,1)S(1)} %get-tuple-element.81), channel_id=1, source_target_pairs={{0,8},{1,9},{2,10},{3,11},{4,12},{5,13},{6,14},{7,15},{8,0},{9,1},... | collective-permute-start | bytes 393224 | tf_op jit(solution)/shard_map/ppermute | solution.py:421
  41.1 5.8 %collective-permute-start.15 = (bf16[4,128,128]{2,1,0:T(8,128)(2,1)S(1)}, bf16[4,128,128]{2,1,0:T(8,128)(2,1)S(1)}, u32[]{:S(2)}, u32[]{:S(2)}) collective-permute-start(bf16[4,128,128]{2,1,0:T(8,128)(2,1)S(1)} %get-tuple-element.73), channel_id=1, source_target_pairs={{0,8},{1,9},{2,10},{3,11},{4,12},{5,13},{6,14},{7,15},{8,0},{9,1},... | collective-permute-start | bytes 393224 | tf_op jit(solution)/shard_map/ppermute | solution.py:422
  42.6 2.4 %collective-permute-start.22 = (bf16[4,128,128]{2,1,0:T(8,128)(2,1)S(1)}, bf16[4,128,128]{2,1,0:T(8,128)(2,1)S(1)}, u32[]{:S(2)}, u32[]{:S(2)}) collective-permute-start(bf16[4,128,128]{2,1,0:T(8,128)(2,1)S(1)} %get-tuple-element.82), channel_id=1, source_target_pairs={{0,8},{1,9},{2,10},{3,11},{4,12},{5,13},{6,14},{7,15},{8,0},{9,1},... | collective-permute-start | bytes 393224 | tf_op jit(solution)/shard_map/ppermute | solution.py:421
  42.9 5.6 %collective-permute-start.16 = (bf16[4,128,128]{2,1,0:T(8,128)(2,1)S(1)}, bf16[4,128,128]{2,1,0:T(8,128)(2,1)S(1)}, u32[]{:S(2)}, u32[]{:S(2)}) collective-permute-start(bf16[4,128,128]{2,1,0:T(8,128)(2,1)S(1)} %get-tuple-element.74), channel_id=1, source_target_pairs={{0,8},{1,9},{2,10},{3,11},{4,12},{5,13},{6,14},{7,15},{8,0},{9,1},... | collective-permute-start | bytes 393224 | tf_op jit(solution)/shard_map/ppermute | solution.py:422
  43.7 4.8 %collective-permute-start.17 = (bf16[4,128,128]{2,1,0:T(8,128)(2,1)S(1)}, bf16[4,128,128]{2,1,0:T(8,128)(2,1)S(1)}, u32[]{:S(2)}, u32[]{:S(2)}) collective-permute-start(bf16[4,128,128]{2,1,0:T(8,128)(2,1)S(1)} %get-tuple-element.75), channel_id=1, source_target_pairs={{0,8},{1,9},{2,10},{3,11},{4,12},{5,13},{6,14},{7,15},{8,0},{9,1},... | collective-permute-start | bytes 393224 | tf_op jit(solution)/shard_map/ppermute | solution.py:421
  44.9 3.7 %collective-permute-start.18 = (bf16[4,128,128]{2,1,0:T(8,128)(2,1)S(1)}, bf16[4,128,128]{2,1,0:T(8,128)(2,1)S(1)}, u32[]{:S(2)}, u32[]{:S(2)}) collective-permute-start(bf16[4,128,128]{2,1,0:T(8,128)(2,1)S(1)} %get-tuple-element.76), channel_id=1, source_target_pairs={{0,8},{1,9},{2,10},{3,11},{4,12},{5,13},{6,14},{7,15},{8,0},{9,1},... | collective-permute-start | bytes 393224 | tf_op jit(solution)/shard_map/ppermute | solution.py:421
